TPU v7x, 128 devices: a whole 4x4x4 slice. The times are simulated.
128 devices in a mesh: song: 16 (over x_lo, z, core), tensor: 8 (over x_hi, y).
Axes of the slice: x: 4 (x_hi: 2, x_lo: 2; x = x_hi * 2 + x_lo), y: 4, z: 4, core: 2. Of those that a mesh axis runs over, the one named last changes fastest.
Arguments:
- upper_codes: int32 [4096], P('song'), may hold values from 0 to 2047
- middle_codes: int32 [16384], P('song'), may hold values from 0 to 2047
- upper_table: bfloat16 [2048, 1024], P(None, 'tensor'), may hold values from -6 to 6
- dilated_weight: bfloat16 [4, 3, 1024, 1024], P(None, None, 'tensor'), may hold values from -0.109375 to 0.109375
- mixing_weight: bfloat16 [4, 1024, 1024], P(None, None, 'tensor'), may hold values from -0.1875 to 0.1875
- upsample_weight: bfloat16 [1024, 7680], P('tensor'), may hold values from -0.1875 to 0.1875
- middle_table: bfloat16 [2048, 1920], P('tensor'), may hold values from -6 to 6
- norm_gain: float32 [1920], replicated, may hold values from 0.1 to 1.9
- qkv_weight: bfloat16 [1920, 16, 384], P(None, 'tensor'), may hold values from -4 to 4
Outputs:
- context: bfloat16 [16384, 2048], P('song', 'tensor')
All inputs are finite; a program needn't handle non-finite values.
Results may differ from a plain program's by a relative error of at most 0.0145.
Values may be sent and summed in bfloat16 or wider, within the bound.
No kernel may reach another device: no remote copies, remote signals or barrier semaphores. Data moves between devices by JAX's collectives and lax.ppermute only.
A program may use at most 128 MiB of HBM per device.

v0:
```python
import functools

import jax
import jax.numpy as jnp
from jax import lax
from jax.experimental import pallas as pl
from jax.experimental.pallas import tpu as pltpu
from jax.sharding import PartitionSpec as P

BF = jnp.bfloat16
F32 = jnp.float32
D = 1920
C = 1024
VOCAB = 2048
UPPER = 4096
HALF = 128
HALO = (40, 39, 36, 27, 0)
ROWS = (208, 208, 208, 192, 128)
VMEM_LIMIT = 60 << 20

Y_GROUPS = [[0, 1, 2, 3], [4, 5, 6, 7]]


def params(**kw):
    return pltpu.CompilerParams(vmem_limit_bytes=VMEM_LIMIT, **kw)


def cost(flops, nbytes, trans=0):
    return pl.CostEstimate(flops=flops, bytes_accessed=nbytes, transcendentals=trans)


def dot(a, b):
    return jnp.dot(a, b, preferred_element_type=F32)


def dilated_copies(level, info, dil_hbm, got_hbm, sib_hbm, near_ref, away_ref, sems):
    own = pl.multiple_of(info[0] * 512, 512)
    other = pl.multiple_of((1 - info[0]) * 512, 512)
    pairs = []
    for ref, hbm, begin in ((near_ref, got_hbm, own), (away_ref, sib_hbm, other)):
        part = hbm if level == 0 else hbm.at[level - 1]
        pairs.append((dil_hbm.at[level, :, :, pl.ds(begin, 512)], ref.at[:, pl.ds(0, 128), :]))
        for tap in range(3):
            pairs.append((part.at[pl.ds(tap * 128, 128), :], ref.at[tap, pl.ds(128, 128), :]))
    return [pltpu.make_async_copy(a, b, sems.at[i]) for i, (a, b) in enumerate(pairs)]


def mixing_copies(level, info, mix_hbm, got_hbm, sib_hbm, mix_ref, sems):
    pairs = []
    for half, hbm in enumerate((got_hbm, sib_hbm)):
        part = hbm if level == 0 else hbm.at[level - 1]
        begin = info[0] if half == 0 else 1 - info[0]
        rows = pl.ds(pl.multiple_of(begin * 512, 512), 512)
        pairs.append((mix_hbm.at[level, rows, :], mix_ref.at[half, :, pl.ds(0, 128)]))
        for y in range(4):
            pairs.append(
                (
                    part.at[pl.ds(384, 128), pl.ds(y * 128, 128)],
                    mix_ref.at[half, pl.ds(y * 128, 128), pl.ds(128, 128)],
                )
            )
    return [pltpu.make_async_copy(a, b, sems.at[i]) for i, (a, b) in enumerate(pairs)]


def send_terms(level, info, h_ref, near_ref, away_ref, out_ref):
    step = 3**level
    count = HALF + 2 * HALO[level + 1]
    padded = out_ref.shape[1]
    rows = h_ref.shape[0]
    first = info[1] - HALO[level]
    pos = first + lax.broadcasted_iota(jnp.int32, (rows, 1), 0)
    inside = (pos >= 0) & (pos < UPPER)
    h_ref[...] = jnp.where(inside, jnp.maximum(h_ref[...], 0.0), 0.0)
    taps = [h_ref[tap * step : tap * step + count, :].astype(BF) for tap in range(3)]
    for half, ref in enumerate((near_ref, away_ref)):
        total = dot(taps[0], ref[0]) + dot(taps[1], ref[1]) + dot(taps[2], ref[2])
        total = total.astype(BF)
        for y in range(4):
            out_ref[y, :count, half * 128 : half * 128 + 128] = total[:, y * 128 : y * 128 + 128]
    if padded > count:
        for y in range(4):
            out_ref[y, count:, :] = jnp.zeros((padded - count, 256), BF)


def start(copies):
    for copy in copies:
        copy.start()


def finish(copies):
    for copy in copies:
        copy.wait()


DILATED = [pltpu.VMEM((3, 256, 512), BF), pltpu.VMEM((3, 256, 512), BF), pltpu.SemaphoreType.DMA((8,))]
MIXING = [pltpu.VMEM((2, 512, 256), BF), pltpu.SemaphoreType.DMA((10,))]


def first_kernel(info, codes_ref, table_ref, dil_hbm, got_ref, sib_ref, h_ref, out_ref, near_ref, away_ref, sems, work):
    copies = dilated_copies(0, info, dil_hbm, got_ref, sib_ref, near_ref, away_ref, sems)
    start(copies)
    codes = codes_ref[...]
    rows = codes.shape[0]
    lane = lax.broadcasted_iota(jnp.int32, (rows, 1024), 1)
    core = info[0]
    one = jnp.ones((), BF)
    zero = jnp.zeros((), BF)
    h_own = jnp.zeros((rows, 128), F32)
    h_oth = jnp.zeros((rows, 128), F32)
    for src, begin in ((got_ref, core * 1024), (sib_ref, (1 - core) * 1024)):
        hot = jnp.where(codes - begin == lane, one, zero)
        h_own += dot(hot, table_ref[pl.ds(pl.multiple_of(begin, 1024), 1024), :])
        for q in range(4):
            h_oth += dot(hot[:, q * 256 : q * 256 + 256], src[512:768, q * 128 : q * 128 + 128])
    work[:, :128] = h_own
    work[:, 128:] = h_oth
    h_ref[...] = work[...]
    finish(copies)
    send_terms(0, info, work, near_ref, away_ref, out_ref)


def mixed(level, r_ref, h_ref, mix_ref):
    step = 3**level
    count = HALF + 2 * HALO[level + 1]
    h = h_ref[step : step + count, :]
    for half in range(2):
        r = jnp.concatenate([r_ref[y, :, half * 128 : half * 128 + 128] for y in range(4)], axis=1)
        h += dot(r, mix_ref[half])[:count]
    return h


def middle_kernel(level, info, r_ref, h_ref, mix_hbm, got_hbm, sib_hbm, dil_hbm, got1_hbm, sib1_hbm, new_ref, out_ref, mix_ref, mix_sems, near_ref, away_ref, sems, work):
    first = mixing_copies(level, info, mix_hbm, got_hbm, sib_hbm, mix_ref, mix_sems)
    then = dilated_copies(level + 1, info, dil_hbm, got1_hbm, sib1_hbm, near_ref, away_ref, sems)
    start(first)
    start(then)
    finish(first)
    count = HALF + 2 * HALO[level + 1]
    if work.shape[0] > count:
        work[count:, :] = jnp.zeros((work.shape[0] - count, 256), F32)
    work[:count, :] = mixed(level, r_ref, h_ref, mix_ref)
    new_ref[...] = work[...]
    finish(then)
    send_terms(level + 1, info, work, near_ref, away_ref, out_ref)


def last_kernel(info, r_ref, h_ref, mix_hbm, got_hbm, sib_hbm, out_ref, mix_ref, mix_sems):
    copies = mixing_copies(3, info, mix_hbm, got_hbm, sib_hbm, mix_ref, mix_sems)
    start(copies)
    finish(copies)
    h = mixed(3, r_ref, h_ref, mix_ref).astype(BF)
    for peer in range(8):
        out_ref[peer] = h


def call(body, outs, scratch=(), smem=1, n=0, hbm=0, after=0, flops=10**9, name=None):
    def spec(space):
        return pl.BlockSpec(memory_space=space)

    specs = [spec(pltpu.SMEM)] * smem + [spec(pltpu.VMEM)] * n
    specs += [spec(pl.ANY)] * hbm + [spec(pltpu.VMEM)] * after
    return pl.pallas_call(
        body,
        out_shape=outs,
        in_specs=specs,
        out_specs=jax.tree.map(lambda _: spec(pltpu.VMEM), outs),
        scratch_shapes=list(scratch),
        compiler_params=params(),
        cost_estimate=cost(flops, 4 << 20),
        name=name,
    )


def shape(*dims, dtype=BF):
    return jax.ShapeDtypeStruct(dims, dtype)


CHUNKS = ((0, 512), (512, 512), (1024, 512), (1536, 384))


def embed_kernel(codes_ref, full_ref, out_ref, table, hot, sems):
    def fetch(i):
        begin, size = CHUNKS[i]
        return pltpu.make_async_copy(
            full_ref.at[:, :, :, :, pl.ds(2 * D + begin, size)],
            table.at[:, :, :, :, pl.ds(begin, size)],
            sems.at[i],
        )

    start([fetch(i) for i in range(4)])
    lane = lax.broadcasted_iota(jnp.int32, (256, VOCAB), 1)

    def body(m, carry):
        lines = pl.ds(pl.multiple_of(m * 256, 256), 256)
        hot[...] = jnp.where(codes_ref[lines, :] == lane, jnp.ones((), BF), jnp.zeros((), BF))
        for i, (begin, size) in enumerate(CHUNKS):
            cols = slice(begin, begin + size)

            @pl.when(m == 0)
            def _():
                fetch(i).wait()

            out_ref[lines, cols] = dot(hot[...], table[:, :, :, :, cols].reshape(VOCAB, size)).astype(BF)
        return carry

    lax.fori_loop(0, 4, body, 0)


def embed(codes, full):
    return pl.pallas_call(
        embed_kernel,
        out_shape=shape(1024, D),
        in_specs=[pl.BlockSpec(memory_space=pltpu.VMEM), pl.BlockSpec(memory_space=pltpu.HBM)],
        out_specs=pl.BlockSpec(memory_space=pltpu.VMEM),
        scratch_shapes=[
            pltpu.VMEM((8, 2, 8, 16, D), BF),
            pltpu.VMEM((256, VOCAB), BF),
            pltpu.SemaphoreType.DMA((4,)),
        ],
        compiler_params=params(),
        cost_estimate=cost(8 * 10**9, 12 << 20),
        name="embed",
    )(codes, full)


def frames_kernel(pair, emb_ref, hf_ref, gain_ref, qkv_ref, full_ref, q_ref, kv_ref, weights, emb, hf, x, xn, sems, emb_sem):
    def weight_copy(phase, t):
        cols = pl.ds(pl.multiple_of(phase * D, 128), D)
        return pltpu.make_async_copy(
            full_ref.at[:, pair, t, :, cols], weights.at[phase, t], sems.at[phase, t]
        )

    fetch = pltpu.make_async_copy(emb_ref.at[pl.ds(pair * 512, 512), :], emb, emb_sem)
    fetch.start()
    for phase in range(2):
        start([weight_copy(phase, t) for t in range(8)])
    for half in range(2):
        for j in range(8):
            at = 0 if j // 4 == half else 128
            hf[half * 128 : half * 128 + 128, j * 128 : j * 128 + 128] = hf_ref[
                half * 4 + j % 4, :, at : at + 128
            ]
    fetch.wait()

    def body(phase, carry):
        finish([weight_copy(phase, t) for t in range(8)])
        lines = pl.ds(pl.multiple_of(phase * 256, 256), 256)
        total = jnp.zeros((256, 1), F32)
        for begin, size in CHUNKS:
            cols = slice(begin, begin + size)
            y = dot(hf[...], weights[phase, :, :, :, cols].reshape(C, size))
            y += emb[lines, cols].astype(F32)
            x[:, cols] = y
            total += jnp.sum(y, axis=1, keepdims=True)
        mean = total * (1.0 / D)
        square = jnp.zeros((256, 1), F32)
        for begin, size in CHUNKS:
            y = x[:, begin : begin + size] - mean
            square += jnp.sum(y * y, axis=1, keepdims=True)
        factor = lax.rsqrt(square * (1.0 / D) + 1e-5)
        for begin, size in CHUNKS:
            cols = slice(begin, begin + size)
            xn[:, cols] = ((x[:, cols] - mean) * factor * gain_ref[:, cols]).astype(BF)
        y = dot(xn[...], qkv_ref[...]).astype(BF)
        for head in range(2):
            at = head * 384
            cols = slice(head * 128, head * 128 + 128)
            q_ref[lines, cols] = y[:, at : at + 128]
            kv_ref[lines, cols] = y[:, at + 128 : at + 256]
            kv_ref[lines, 256 + head * 128 : 384 + head * 128] = y[:, at + 256 : at + 384]
        return carry

    lax.fori_loop(0, 2, body, 0)


def frames(pair, emb, hf, gain, qkv, full):
    vm = pl.BlockSpec(memory_space=pltpu.VMEM)
    return pl.pallas_call(
        functools.partial(frames_kernel, pair),
        out_shape=(shape(512, 256), shape(512, 512)),
        in_specs=[pl.BlockSpec(memory_space=pl.ANY), vm, vm, vm, pl.BlockSpec(memory_space=pltpu.HBM)],
        out_specs=(vm, vm),
        scratch_shapes=[
            pltpu.VMEM((2, 8, 8, 16, D), BF),
            pltpu.VMEM((512, D), BF),
            pltpu.VMEM((256, C), BF),
            pltpu.VMEM((256, D), F32),
            pltpu.VMEM((256, D), BF),
            pltpu.SemaphoreType.DMA((2, 8)),
            pltpu.SemaphoreType.DMA,
        ],
        compiler_params=params(),
        cost_estimate=cost(4 * 10**9, 12 << 20),
        name="frames",
    )(emb, hf, gain, qkv, full)


SCALE = 128**-0.5 * 1.4426950408889634


def scores_of(q, k):
    return lax.dot_general(q, k, (((1,), (1,)), ((), ())), preferred_element_type=F32) * SCALE


def gather_rows(dest, first, second):
    dest[:512, :] = first[...]
    dest[512:, :] = second[...]


def own_kernel(q0_ref, q1_ref, kv0_ref, kv1_ref, acc_ref, top_ref, sum_ref, q_all):
    gather_rows(q_all, q0_ref, q1_ref)
    for part in range(2):
        keys = part * 128 + 128
        wide = (slice(0, keys), slice(256, 256 + keys))
        kv = jnp.concatenate([ref[at, :] for ref in (kv0_ref, kv1_ref) for at in wide], axis=0)
        col = lax.broadcasted_iota(jnp.int32, (128, 4 * keys), 1)
        col = col % keys * 4 + col // keys
        row = (part * 128 + lax.broadcasted_iota(jnp.int32, (128, 4 * keys), 0)) * 4

        def body(phase, carry):
            lines = pl.ds(pl.multiple_of(phase * 256 + part * 128, 128), 128)
            seen = col <= row + phase
            for head in range(2):
                cols = slice(head * 128, head * 128 + 128)
                vals = slice(256 + head * 128, 384 + head * 128)
                s = jnp.where(seen, scores_of(q_all[lines, cols], kv[:, cols]), -1e30)
                top = jnp.max(s, axis=1, keepdims=True)
                p = jnp.exp2(s - top)
                top_ref[lines, head : head + 1] = top
                sum_ref[lines, head : head + 1] = jnp.sum(p, axis=1, keepdims=True)
                acc_ref[lines, cols] = dot(p.astype(BF), kv[:, vals])
            return carry

        lax.fori_loop(0, 4, body, 0)


def past_kernel(last, info, q0_ref, q1_ref, far_ref, near_ref, acc_ref, top_ref, sum_ref, *refs):
    if last:
        out_ref, acc, tops, sums, q_all, wide = refs
    else:
        acc, tops, sums, q_all = refs
    gather_rows(q_all, q0_ref, q1_ref)
    acc[...] = acc_ref[...]
    tops[...] = top_ref[...]
    sums[...] = sum_ref[...]

    def fold(kv_ref):
        def body(phase, carry):
            lines = pl.ds(pl.multiple_of(phase * 256, 256), 256)
            for head in range(2):
                cols = slice(head * 128, head * 128 + 128)
                vals = slice(256 + head * 128, 384 + head * 128)
                one = slice(head, head + 1)
                s = scores_of(q_all[lines, cols], kv_ref[:, cols])
                old = tops[lines, one]
                top = jnp.maximum(old, jnp.max(s, axis=1, keepdims=True))
                p = jnp.exp2(s - top)
                keep = jnp.exp2(old - top)
                tops[lines, one] = top
                sums[lines, one] = keep * sums[lines, one] + jnp.sum(p, axis=1, keepdims=True)
                acc[lines, cols] = keep * acc[lines, cols] + dot(p.astype(BF), kv_ref[:, vals])
            return carry

        lax.fori_loop(0, 4, body, 0)

    @pl.when(info[2] >= 2)
    def _():
        fold(far_ref)

    @pl.when(info[2] >= 1)
    def _():
        fold(near_ref)

    if last:
        for head in range(2):
            cols = slice(head * 128, head * 128 + 128)
            for phase in range(4):
                lines = slice(phase * 256, phase * 256 + 256)
                wide[pl.ds(phase, 256, stride=4), :] = acc[lines, cols] / sums[lines, head : head + 1]
            out_ref[:, cols] = wide[...].astype(BF)


EVERY = ("song", "tensor")


def other_half():
    pairs = []
    for song in range(16):
        for rank in range(8):
            pairs.append((song * 8 + rank, (song ^ 8) * 8 + (rank ^ 4)))
    return pairs


def to_sibling(value):
    return lax.ppermute(value, "song", [(i, i ^ 1) for i in range(16)])


def exchange(value, axis="tensor", groups=None):
    return lax.all_to_all(value, axis, 0, 0, axis_index_groups=groups, tiled=True)


def on_device(
    upper_codes,
    middle_codes,
    upper_table,
    dilated_weight,
    mixing_weight,
    upsample_weight,
    middle_table,
    norm_gain,
    qkv_weight,
):
    song = lax.axis_index("song")
    rank = lax.axis_index("tensor")
    core = song % 2
    x_hi = rank // 4
    begin = song * 256 + x_hi * HALF
    info = jnp.stack([core, begin, song]).astype(jnp.int32)

    after = lax.ppermute(upper_codes[-40:], "song", [(i, i + 1) for i in range(15)])
    before = lax.ppermute(upper_codes[:40], "song", [(i + 1, i) for i in range(15)])
    codes = jnp.concatenate([after, upper_codes, before])
    codes = lax.dynamic_slice_in_dim(codes, x_hi * HALF, HALF + 80)[:, None]

    dil_half = lax.dynamic_slice_in_dim(dilated_weight, core * 512, 512, 3)
    mix_half = lax.dynamic_slice_in_dim(mixing_weight, core * 512, 512, 1)
    mix_pack = jnp.concatenate([mix_half[:, i * 128 : i * 128 + 128] for i in range(4)], axis=2)
    tab_half = lax.dynamic_slice_in_dim(upper_table, core * 1024, 1024, 0)
    tab_pack = jnp.concatenate([tab_half[i * 256 : i * 256 + 256] for i in range(4)], axis=1)
    pack0 = jnp.concatenate([dil_half[0].reshape(384, 512), mix_pack[0], tab_pack], axis=0)
    got0 = lax.ppermute(pack0, EVERY, other_half())

    up_part = lax.dynamic_slice(upsample_weight, (song // 2 * 16, core * 2 * D), (16, 2 * D))
    mid_part = lax.dynamic_slice_in_dim(middle_table, song * 16, 16, 0)
    part = jnp.concatenate([up_part, mid_part], axis=1)
    parts = lax.all_gather(part, "tensor", axis=0, tiled=False)

    sib0 = to_sibling(got0)
    pack1 = jnp.concatenate([dil_half[1:].reshape(3, 384, 512), mix_pack[1:]], axis=1)
    pack1, got0 = lax.optimization_barrier((pack1, got0))
    got1 = lax.ppermute(pack1, EVERY, other_half())

    h, terms = call(
        first_kernel,
        (shape(ROWS[0], 256, dtype=F32), shape(4, ROWS[1], 256)),
        [*DILATED, pltpu.VMEM((ROWS[0], 256), F32)],
        n=2,
        hbm=1,
        after=2,
        name="cond0",
    )(info, codes, upper_table, dilated_weight, got0, sib0)
    for level in range(4):
        terms = exchange(terms, groups=Y_GROUPS)
        if level == 0:
            parts, got1, terms = lax.optimization_barrier((parts, got1, terms))
            full = lax.all_gather(parts, "song", axis=0, tiled=False).reshape(8, 2, 8, 16, 3 * D)
            sib1 = to_sibling(got1)
        total = terms[0].astype(F32)
        for y in range(1, 4):
            total = total + terms[y].astype(F32)
        r = jnp.maximum(total, 0.0).astype(BF)
        r = exchange(jnp.broadcast_to(r[None], terms.shape), groups=Y_GROUPS)
        old = (got0, sib0) if level == 0 else (got1, sib1)
        if level < 3:
            h, terms = call(
                functools.partial(middle_kernel, level),
                (shape(ROWS[level + 1], 256, dtype=F32), shape(4, ROWS[level + 2], 256)),
                [*MIXING, *DILATED, pltpu.VMEM((ROWS[level + 1], 256), F32)],
                n=2,
                hbm=6,
                name="cond",
            )(info, r, h, mixing_weight, *old, dilated_weight, got1, sib1)
        else:
            spread = call(
                last_kernel, shape(8, HALF, 256), MIXING, n=2, hbm=3, name="cond_end"
            )(info, r, h, mixing_weight, *old)
    hf = exchange(spread)

    mid = middle_codes.reshape(256, 4).T.reshape(1024, 1)
    mid = (mid % 256) // 16 * 128 + mid // 256 * 16 + mid % 16
    gain = norm_gain[None]
    qkv = qkv_weight.reshape(D, 768)

    def from_two_back(value):
        return lax.ppermute(value, "song", [(i, i + 2) for i in range(14)])

    emb = embed(mid, full)
    q0, kv0 = frames(0, emb, hf, gain, qkv, full)
    far0 = from_two_back(kv0)
    q1, kv1 = frames(1, emb, hf, gain, qkv, full)
    far1 = from_two_back(kv1)
    near0 = to_sibling(jnp.where(core == 0, kv0, far0))
    state = (shape(1024, 256, dtype=F32), shape(1024, 2, dtype=F32), shape(1024, 2, dtype=F32))
    work = [pltpu.VMEM((1024, 256), F32), pltpu.VMEM((1024, 2), F32), pltpu.VMEM((1024, 2), F32)]
    queries = pltpu.VMEM((1024, 256), BF)
    kept = call(own_kernel, state, [queries], smem=0, n=4, flops=10**9, name="own")(q0, q1, kv0, kv1)
    kept = call(
        functools.partial(past_kernel, False), state, [queries], n=7, flops=2 * 10**9, name="past"
    )(info, q0, q1, far0, near0, *kept)
    near1 = to_sibling(jnp.where(core == 0, kv1, far1))
    return call(
        functools.partial(past_kernel, True),
        shape(1024, 256),
        [*work, queries, pltpu.VMEM((1024, 128), F32)],
        n=7,
        flops=2 * 10**9,
        name="past_end",
    )(info, q0, q1, far1, near1, *kept)


def solution(mesh):
    placed = (
        P("song"),
        P("song"),
        P(None, "tensor"),
        P(None, None, "tensor", None),
        P(None, None, "tensor"),
        P("tensor", None),
        P("tensor", None),
        P(),
        P(None, "tensor", None),
    )
    return jax.shard_map(
        on_device, mesh=mesh, in_specs=placed, out_specs=P("song", "tensor"), check_vma=False
    )
```

profile of v0, /device:TPU:3, one launch (start us, length us, event | category | flops | bytes accessed | tf_op | source)
XLA Modules:
  0.0 311.4 jit_solution(15414153069613025495)
XLA Ops:
  14.8 16.5 %collective-permute-done.got_ref.got_hbm = bf16[768,512]{1,0:T(8,128)(2,1)S(1)} collective-permute-done((bf16[768,512]{1,0:T(8,128)(2,1)S(1)}, bf16[768,512]{1,0:T(8,128)(2,1)S(1)}, u32[]{:S(2)}, u32[]{:S(2)}) %collective-permute-start) | collective-permute-done | bytes 786464 | tf_op jit(solution)/shard_map/ppermute | solution.py:431
  34.3 3.4 %collective-permute-start.2 = (s32[40]{0:T(128)S(1)}, s32[40]{0:T(128)S(1)}, u32[]{:S(2)}, u32[]{:S(2)}) collective-permute-start(s32[40]{0:T(128)S(1)} %get-tuple-element.59), channel_id=1, source_target_pairs={{0,8},{8,16},{16,24},{24,32},{32,40},{40,48},{48,56},{56,64},{64,7... | collective-permute-start | bytes 488 | tf_op jit(solution)/shard_map/ppermute | solution.py:420
  40.3 2.6 collective-permute-done.3
  44.7 4.7 %cond0.1 = (f32[208,256]{1,0:T(8,128)}, bf16[4,208,256]{2,1,0:T(8,128)(2,1)}) custom-call(s32[3]{0:T(128)} %pad_add_fusion.1.info, s32[208,1]{1,0:T(8,128)} %copy.21.codes_ref, bf16[2048,128]{1,0:T(8,128)(2,1)} %table_ref.1, bf16[4,3,128,1024]{3,2,1,0:T(8,128)(2,1)} %dil_hbm.7, bf16[768,512]{1,0:T(8,128)(2,1)} %copy-done.6, bf16[768,512]{1,0:T(8,128)(2,1)} %copy-done.7), custom_call_target="tpu_custom_call" | custom-call | flops 1000000000 | bytes 4194304 | tf_op jit(solution)/shard_map/cond0/pallas_call | solution.py:443
  49.4 12.7 %all_to_all.45 = bf16[4,208,256]{2,1,0:T(8,128)(2,1)S(1)} all-to-all(bf16[4,208,256]{2,1,0:T(8,128)(2,1)} %get-tuple-element.30), channel_id=1, replica_groups={{0,1,2,3},{4,5,6,7},{8,9,10,11},{12,13,14,15},{16,17,18,19},{20,21,22,2..., dimensions={0} | all-to-all | bytes 851968 | tf_op jit(solution)/shard_map/all_to_all | solution.py:399
  62.1 11.7 %collective-permute-done.1.got1_hbm.got_hbm = bf16[3,512,512]{2,1,0:T(8,128)(2,1)S(1)} collective-permute-done((bf16[3,512,512]{2,1,0:T(8,128)(2,1)}, bf16[3,512,512]{2,1,0:T(8,128)(2,1)S(1)}, u32[]{:S(2)}, u32[]{:S(2)}) %collective-permute-start.1) | collective-permute-done | bytes 1572896 | tf_op jit(solution)/shard_map/ppermute | solution.py:441
  73.9 2.4 collective-permute-start.5
  76.4 11.9 %all_to_all.46.r_ref = bf16[4,208,256]{2,1,0:T(8,128)(2,1)} all-to-all(bf16[4,208,256]{2,1,0:T(8,128)(2,1)S(1)} %broadcast_in_dim.40), channel_id=1, replica_groups={{0,1,2,3},{4,5,6,7},{8,9,10,11},{12,13,14,15},{16,17,18,19},{20,21,22,2..., dimensions={0} | all-to-all | bytes 851968 | tf_op jit(solution)/shard_map/all_to_all | solution.py:399
  89.5 4.4 %cond.3 = (f32[208,256]{1,0:T(8,128)}, bf16[4,208,256]{2,1,0:T(8,128)(2,1)}) custom-call(s32[3]{0:T(128)} %pad_add_fusion.1.info, bf16[4,208,256]{2,1,0:T(8,128)(2,1)} %all_to_all.46.r_ref, f32[208,256]{1,0:T(8,128)} %get-tuple-element.33.h_ref, bf16[4,1024,128]{2,1,0:T(8,128)(2,1)} %mix_hbm.7, bf16[768,512]{1,0:T(8,128)(2,1)} %copy-done.6, ...), custom_call_target="tpu_custom_call" | custom-call | flops 1000000000 | bytes 4194304 | tf_op jit(solution)/shard_map/cond/pallas_call | solution.py:465
  93.9 10.7 %all_to_all.47 = bf16[4,208,256]{2,1,0:T(8,128)(2,1)S(1)} all-to-all(bf16[4,208,256]{2,1,0:T(8,128)(2,1)} %get-tuple-element.35), channel_id=1, replica_groups={{0,1,2,3},{4,5,6,7},{8,9,10,11},{12,13,14,15},{16,17,18,19},{20,21,22,2..., dimensions={0} | all-to-all | bytes 851968 | tf_op jit(solution)/shard_map/all_to_all | solution.py:399
  104.7 9.5 %all_to_all.48.r_ref = bf16[4,208,256]{2,1,0:T(8,128)(2,1)} all-to-all(bf16[4,208,256]{2,1,0:T(8,128)(2,1)S(1)} %broadcast_in_dim.42), channel_id=1, replica_groups={{0,1,2,3},{4,5,6,7},{8,9,10,11},{12,13,14,15},{16,17,18,19},{20,21,22,2..., dimensions={0} | all-to-all | bytes 851968 | tf_op jit(solution)/shard_map/all_to_all | solution.py:399
  114.2 4.2 %cond.4 = (f32[208,256]{1,0:T(8,128)}, bf16[4,192,256]{2,1,0:T(8,128)(2,1)}) custom-call(s32[3]{0:T(128)} %pad_add_fusion.1.info, bf16[4,208,256]{2,1,0:T(8,128)(2,1)} %all_to_all.48.r_ref, f32[208,256]{1,0:T(8,128)} %get-tuple-element.36.h_ref, bf16[4,1024,128]{2,1,0:T(8,128)(2,1)} %mix_hbm.7, bf16[3,512,512]{2,1,0:T(8,128)(2,1)} %copy-done.2, ...), custom_call_target="tpu_custom_call" | custom-call | flops 1000000000 | bytes 4194304 | tf_op jit(solution)/shard_map/cond/pallas_call | solution.py:465
  118.4 9.7 %all_to_all.49 = bf16[4,192,256]{2,1,0:T(8,128)(2,1)S(1)} all-to-all(bf16[4,192,256]{2,1,0:T(8,128)(2,1)} %get-tuple-element.37), channel_id=1, replica_groups={{0,1,2,3},{4,5,6,7},{8,9,10,11},{12,13,14,15},{16,17,18,19},{20,21,22,2..., dimensions={0} | all-to-all | bytes 786432 | tf_op jit(solution)/shard_map/all_to_all | solution.py:399
  128.2 9.3 %all_to_all.50.r_ref = bf16[4,192,256]{2,1,0:T(8,128)(2,1)} all-to-all(bf16[4,192,256]{2,1,0:T(8,128)(2,1)S(1)} %broadcast_in_dim.44), channel_id=1, replica_groups={{0,1,2,3},{4,5,6,7},{8,9,10,11},{12,13,14,15},{16,17,18,19},{20,21,22,2..., dimensions={0} | all-to-all | bytes 786432 | tf_op jit(solution)/shard_map/all_to_all | solution.py:399
  137.5 4.1 %cond.5 = (f32[192,256]{1,0:T(8,128)}, bf16[4,128,256]{2,1,0:T(8,128)(2,1)}) custom-call(s32[3]{0:T(128)} %pad_add_fusion.1.info, bf16[4,192,256]{2,1,0:T(8,128)(2,1)} %all_to_all.50.r_ref, f32[208,256]{1,0:T(8,128)} %get-tuple-element.38.h_ref, bf16[4,1024,128]{2,1,0:T(8,128)(2,1)} %mix_hbm.7, bf16[3,512,512]{2,1,0:T(8,128)(2,1)} %copy-done.2, ...), custom_call_target="tpu_custom_call" | custom-call | flops 1000000000 | bytes 4194304 | tf_op jit(solution)/shard_map/cond/pallas_call | solution.py:465
  141.6 3.4 %all-to-all-start.6 = ((bf16[4,128,256]{2,1,0:T(8,128)(2,1)}), bf16[4,128,256]{2,1,0:T(8,128)(2,1)S(1)}, u32[]{:S(2)}, u32[]{:S(2)}) async-start(bf16[4,128,256]{2,1,0:T(8,128)(2,1)} %get-tuple-element.39), calls=%async_computation.6 | async-start | bytes 524288 | tf_op jit(solution)/shard_map/all_to_all | solution.py:399
  145.5 4.2 %copy.24 = bf16[240,8,2,384]{3,1,2,0:T(8,128)(2,1)} copy(bf16[240,8,2,384]{3,2,1,0:T(2,128)(2,1)} %bitcast.56) | data formatting | bytes 5898240
  151.3 4.0 %all-to-all-start.7 = ((bf16[4,128,256]{2,1,0:T(8,128)(2,1)}), bf16[4,128,256]{2,1,0:T(8,128)(2,1)S(1)}, u32[]{:S(2)}, u32[]{:S(2)}) async-start(bf16[4,128,256]{2,1,0:T(8,128)(2,1)} %broadcast_in_dim.46), calls=%async_computation.7 | async-start | bytes 524288 | tf_op jit(solution)/shard_map/all_to_all | solution.py:399
  157.0 3.8 %all-to-all-done.7.r_ref = bf16[4,128,256]{2,1,0:T(8,128)(2,1)S(1)} async-done(((bf16[4,128,256]{2,1,0:T(8,128)(2,1)}), bf16[4,128,256]{2,1,0:T(8,128)(2,1)S(1)}, u32[]{:S(2)}, u32[]{:S(2)}) %all-to-all-start.7) | async-done | bytes 262176 | tf_op jit(solution)/shard_map/all_to_all | solution.py:399
  161.5 3.3 %cond_end.1 = bf16[8,128,256]{2,1,0:T(8,128)(2,1)} custom-call(s32[3]{0:T(128)} %pad_add_fusion.1.info, bf16[4,128,256]{2,1,0:T(8,128)(2,1)} %copy-done.9, f32[192,256]{1,0:T(8,128)} %get-tuple-element.40.h_ref, bf16[4,1024,128]{2,1,0:T(8,128)(2,1)} %mix_hbm.7, bf16[3,512,512]{2,1,0:T(8,128)(2,1)} %copy-done.2, bf16[3,512,512]{2,1,0:T(8,128)(2,1)} %copy-done.3), custom_call_target="tpu_custom_call" | custom-call | flops 1000000000 | bytes 4194304 | tf_op jit(solution)/shard_map/cond_end/pallas_call | solution.py:474
  164.8 5.2 %all-to-all-start.8 = ((bf16[8,128,256]{2,1,0:T(8,128)(2,1)}), bf16[8,128,256]{2,1,0:T(8,128)(2,1)S(1)}, u32[]{:S(2)}, u32[]{:S(2)}) async-start(bf16[8,128,256]{2,1,0:T(8,128)(2,1)} %cond_end.1), calls=%async_computation.8 | async-start | bytes 1048576 | tf_op jit(solution)/shard_map/all_to_all | solution.py:399
  170.0 38.7 %all-gather.7.cloned.1.call-done = bf16[128,16,5760]{2,1,0:T(8,128)(2,1)} async-done(((bf16[8,16,5760]{2,1,0:T(8,128)(2,1)}), bf16[128,16,5760]{2,1,0:T(8,128)(2,1)}) %all-gather.7.cloned.1.call-update) | async-done | bytes 23592976 | tf_op jit(solution)/shard_map/all_gather | solution.py:456
  208.7 16.6 %embed.1.emb_ref = bf16[1024,1920]{1,0:T(8,128)(2,1)} custom-call(s32[1024,1]{1,0:T(8,128)} %fusion.3.codes_ref, bf16[8,2,8,16,5760]{4,3,2,1,0:T(8,128)(2,1)} %bitcast.50), custom_call_target="tpu_custom_call" | custom-call | flops 8000000000 | bytes 12582912 | tf_op jit(solution)/shard_map/embed/pallas_call | solution.py:210
  226.1 11.8 %frames.2 = (bf16[512,256]{1,0:T(8,128)(2,1)}, bf16[512,512]{1,0:T(8,128)(2,1)}) custom-call(bf16[1024,1920]{1,0:T(8,128)(2,1)} %embed.1.emb_ref, bf16[8,128,256]{2,1,0:T(8,128)(2,1)} %copy-done.5, f32[1,1920]{1,0:T(1,128)} %broadcast_in_dim.47.gain_ref, bf16[1920,768]{1,0:T(8,128)(2,1)} %bitcast.53, bf16[8,2,8,16,5760]{4,3,2,1,0:T(8,128)(2,1)} %bitcast.51), custom_call_target="tpu_custom_call" | custom-call | flops 4000000000 | bytes 12582912 | tf_op jit(solution)/shard_map/frames/pallas_call | solution.py:278
  237.9 2.1 collective-permute-start.8
  240.0 11.8 %frames.3 = (bf16[512,256]{1,0:T(8,128)(2,1)}, bf16[512,512]{1,0:T(8,128)(2,1)}) custom-call(bf16[1024,1920]{1,0:T(8,128)(2,1)} %embed.1.emb_ref, bf16[8,128,256]{2,1,0:T(8,128)(2,1)} %copy-done.5, f32[1,1920]{1,0:T(1,128)} %broadcast_in_dim.47.gain_ref, bf16[1920,768]{1,0:T(8,128)(2,1)} %bitcast.54, bf16[8,2,8,16,5760]{4,3,2,1,0:T(8,128)(2,1)} %bitcast.52), custom_call_target="tpu_custom_call" | custom-call | flops 4000000000 | bytes 12582912 | tf_op jit(solution)/shard_map/frames/pallas_call | solution.py:278
  251.8 2.1 collective-permute-start.6
  253.9 2.2 collective-permute-done.8.far_ref
  257.0 12.9 %collective-permute-done.6.far_ref = bf16[512,512]{1,0:T(8,128)(2,1)S(1)} collective-permute-done((bf16[512,512]{1,0:T(8,128)(2,1)}, bf16[512,512]{1,0:T(8,128)(2,1)S(1)}, u32[]{:S(2)}, u32[]{:S(2)}) %collective-permute-start.6) | collective-permute-done | bytes 524320 | tf_op jit(solution)/shard_map/ppermute | solution.py:485
  270.9 8.8 %own.1 = (f32[1024,256]{1,0:T(8,128)}, f32[1024,2]{1,0:T(8,128)}, f32[1024,2]{1,0:T(8,128)}) custom-call(bf16[512,256]{1,0:T(8,128)(2,1)} %get-tuple-element.41.q0_ref, bf16[512,256]{1,0:T(8,128)(2,1)} %get-tuple-element.42.q1_ref, bf16[512,512]{1,0:T(8,128)(2,1)} %get-tuple-element.44.kv0_ref, bf16[512,512]{1,0:T(8,128)(2,1)} %get-tuple-element.43.kv1_ref), custom_call_target="tpu_custom_call" | custom-call | flops 1000000000 | bytes 4194304 | tf_op jit(solution)/shard_map/own/pallas_call | solution.py:496
  280.5 11.6 %past.1 = (f32[1024,256]{1,0:T(8,128)}, f32[1024,2]{1,0:T(8,128)}, f32[1024,2]{1,0:T(8,128)}) custom-call(s32[3]{0:T(128)} %pad_add_fusion.1.info, bf16[512,256]{1,0:T(8,128)(2,1)} %get-tuple-element.41.q0_ref, bf16[512,256]{1,0:T(8,128)(2,1)} %get-tuple-element.42.q1_ref, bf16[512,512]{1,0:T(8,128)(2,1)} %copy-done.11, bf16[512,512]{1,0:T(8,128)(2,1)} %copy-done.18, ...), custom_call_target="tpu_custom_call" | custom-call | flops 2000000000 | bytes 4194304 | tf_op jit(solution)/shard_map/past/pallas_call | solution.py:497
  293.0 11.6 %past_end.1 = bf16[1024,256]{1,0:T(8,128)(2,1)} custom-call(s32[3]{0:T(128)} %pad_add_fusion.1.info, bf16[512,256]{1,0:T(8,128)(2,1)} %get-tuple-element.41.q0_ref, bf16[512,256]{1,0:T(8,128)(2,1)} %get-tuple-element.42.q1_ref, bf16[512,512]{1,0:T(8,128)(2,1)} %copy-done.10, bf16[512,512]{1,0:T(8,128)(2,1)} %copy-done.17, ...), custom_call_target="tpu_custom_call" | custom-call | flops 2000000000 | bytes 4194304 | tf_op jit(solution)/shard_map/past_end/pallas_call | solution.py:501
  (89 shorter events, 25.7 us)
Async XLA Ops:
  6.5 1.2 copy-start
  6.5 3.9 %copy-start.4 = (bf16[4,1024,128]{2,1,0:T(8,128)(2,1)S(1)}, bf16[4,1024,128]{2,1,0:T(8,128)(2,1)}, u32[]{:S(2)}) copy-start(bf16[4,1024,128]{2,1,0:T(8,128)(2,1)} %mix_hbm.7) | copy-start | bytes 3145732
  6.5 4.0 %copy-start.8 = (bf16[2048,128]{1,0:T(8,128)(2,1)S(1)}, bf16[2048,128]{1,0:T(8,128)(2,1)}, u32[]{:S(2)}) copy-start(bf16[2048,128]{1,0:T(8,128)(2,1)} %table_ref.1) | copy-start | bytes 1572868
  6.5 67.3 %all-gather.5.cloned.1.call-start = ((), (), s32[]{:S(2)}) async-start(), calls=%async_computation.9 | async-start | bytes 1658880 | tf_op jit(solution)/shard_map/all_gather | solution.py:436
  9.4 199.3 %all-gather.7.cloned.1.call-start = ((), (), s32[]{:S(2)}) async-start(), calls=%async_computation.10 | async-start | bytes 25067520 | tf_op jit(solution)/shard_map/all_gather | solution.py:456
  10.7 20.6 %collective-permute-start = (bf16[768,512]{1,0:T(8,128)(2,1)S(1)}, bf16[768,512]{1,0:T(8,128)(2,1)S(1)}, u32[]{:S(2)}, u32[]{:S(2)}) collective-permute-start(bf16[768,512]{1,0:T(8,128)(2,1)S(1)} %maximum_maximum_fusion), channel_id=1, source_target_pairs={{0,68},{1,69},{2,70},{3,71},{4,64},{5,65},{6,66},{7,67},{8,76},{9,... | collective-permute-start | bytes 2359304 | tf_op jit(solution)/shard_map/ppermute | solution.py:431
  13.5 20.7 %copy-start.16 = (s32[256]{0:T(256)S(1)}, s32[256]{0:T(256)}, u32[]{:S(2)}) copy-start(s32[256]{0:T(256)} %param.9) | copy-start | bytes 3076
  31.3 12.5 %copy-start.6 = (bf16[768,512]{1,0:T(8,128)(2,1)}, bf16[768,512]{1,0:T(8,128)(2,1)S(1)}, u32[]{:S(2)}) copy-start(bf16[768,512]{1,0:T(8,128)(2,1)S(1)} %collective-permute-done.got_ref.got_hbm) | copy-start | bytes 2359300
  31.3 42.6 %collective-permute-start.1 = (bf16[3,512,512]{2,1,0:T(8,128)(2,1)}, bf16[3,512,512]{2,1,0:T(8,128)(2,1)S(1)}, u32[]{:S(2)}, u32[]{:S(2)}) collective-permute-start(bf16[3,512,512]{2,1,0:T(8,128)(2,1)} %pad_maximum_fusion), channel_id=1, source_target_pairs={{0,68},{1,69},{2,70},{3,71},{4,64},{5,65},{6,66},{7,67},{8,76},{9,... | collective-permute-start | bytes 4718600 | tf_op jit(solution)/shard_map/ppermute | solution.py:441
  32.4 11.4 %collective-permute-start.4 = (bf16[768,512]{1,0:T(8,128)(2,1)S(1)}, bf16[768,512]{1,0:T(8,128)(2,1)S(1)}, u32[]{:S(2)}, u32[]{:S(2)}) collective-permute-start(bf16[768,512]{1,0:T(8,128)(2,1)S(1)} %collective-permute-done.got_ref.got_hbm), channel_id=1, source_target_pairs={{0,8},{8,0},{16,24},{24,16},{32,40},{40,32},{48,56},{56,48},{64,72... | collective-permute-start | bytes 2359304 | tf_op jit(solution)/shard_map/ppermute | solution.py:395
  34.3 6.0 %collective-permute-start.2 = (s32[40]{0:T(128)S(1)}, s32[40]{0:T(128)S(1)}, u32[]{:S(2)}, u32[]{:S(2)}) collective-permute-start(s32[40]{0:T(128)S(1)} %get-tuple-element.59), channel_id=1, source_target_pairs={{0,8},{8,16},{16,24},{24,32},{32,40},{40,48},{48,56},{56,64},{64,7... | collective-permute-start | bytes 488 | tf_op jit(solution)/shard_map/ppermute | solution.py:420
  37.7 5.2 %collective-permute-start.3 = (s32[40]{0:T(128)S(1)}, s32[40]{0:T(128)S(1)}, u32[]{:S(2)}, u32[]{:S(2)}) collective-permute-start(s32[40]{0:T(128)S(1)} %get-tuple-element.60), channel_id=1, source_target_pairs={{8,0},{16,8},{24,16},{32,24},{40,32},{48,40},{56,48},{64,56},{72,6... | collective-permute-start | bytes 488 | tf_op jit(solution)/shard_map/ppermute | solution.py:421
  43.8 0.9 copy-start.7
  73.8 14.5 %copy-start.2 = (bf16[3,512,512]{2,1,0:T(8,128)(2,1)}, bf16[3,512,512]{2,1,0:T(8,128)(2,1)S(1)}, u32[]{:S(2)}) copy-start(bf16[3,512,512]{2,1,0:T(8,128)(2,1)S(1)} %collective-permute-done.1.got1_hbm.got_hbm) | copy-start | bytes 4718596
  73.9 14.5 %collective-permute-start.5 = (bf16[3,512,512]{2,1,0:T(8,128)(2,1)S(1)}, bf16[3,512,512]{2,1,0:T(8,128)(2,1)S(1)}, u32[]{:S(2)}, u32[]{:S(2)}) collective-permute-start(bf16[3,512,512]{2,1,0:T(8,128)(2,1)S(1)} %collective-permute-done.1.got1_hbm.got_hbm), channel_id=1, source_target_pairs={{0,8},{8,0},{16,24},{24,16},{32,40},{40,32},{48,56},{56,48},{64,72... | collective-permute-start | bytes 4718600 | tf_op jit(solution)/shard_map/ppermute | solution.py:395
  88.4 1.1 copy-start.3
  137.5 7.5 %copy-start.15 = (s32[1024]{0:T(1024)S(1)}, s32[1024]{0:T(1024)}, u32[]{:S(2)}) copy-start(s32[1024]{0:T(1024)} %param.10) | copy-start | bytes 12292
  141.6 8.9 %all-to-all-start.6 = ((bf16[4,128,256]{2,1,0:T(8,128)(2,1)}), bf16[4,128,256]{2,1,0:T(8,128)(2,1)S(1)}, u32[]{:S(2)}, u32[]{:S(2)}) async-start(bf16[4,128,256]{2,1,0:T(8,128)(2,1)} %get-tuple-element.39), calls=%async_computation.6 | async-start | bytes 524288 | tf_op jit(solution)/shard_map/all_to_all | solution.py:399
  145.5 4.2 %copy-start.14 = (f32[1920]{0:T(1024)S(1)}, f32[1920]{0:T(1024)}, u32[]{:S(2)}) copy-start(f32[1920]{0:T(1024)} %param.16) | copy-start | bytes 23044
  151.3 9.5 %all-to-all-start.7 = ((bf16[4,128,256]{2,1,0:T(8,128)(2,1)}), bf16[4,128,256]{2,1,0:T(8,128)(2,1)S(1)}, u32[]{:S(2)}, u32[]{:S(2)}) async-start(bf16[4,128,256]{2,1,0:T(8,128)(2,1)} %broadcast_in_dim.46), calls=%async_computation.7 | async-start | bytes 524288 | tf_op jit(solution)/shard_map/all_to_all | solution.py:399
  164.8 60.5 %all-to-all-start.8 = ((bf16[8,128,256]{2,1,0:T(8,128)(2,1)}), bf16[8,128,256]{2,1,0:T(8,128)(2,1)S(1)}, u32[]{:S(2)}, u32[]{:S(2)}) async-start(bf16[8,128,256]{2,1,0:T(8,128)(2,1)} %cond_end.1), calls=%async_computation.8 | async-start | bytes 1048576 | tf_op jit(solution)/shard_map/all_to_all | solution.py:399
  237.9 18.2 %copy-start.12 = (bf16[512,512]{1,0:T(8,128)(2,1)S(1)}, bf16[512,512]{1,0:T(8,128)(2,1)}, u32[]{:S(2)}) copy-start(bf16[512,512]{1,0:T(8,128)(2,1)} %get-tuple-element.44.kv0_ref) | copy-start | bytes 1572868
  237.9 18.1 %collective-permute-start.8 = (bf16[512,512]{1,0:T(8,128)(2,1)}, bf16[512,512]{1,0:T(8,128)(2,1)S(1)}, u32[]{:S(2)}, u32[]{:S(2)}) collective-permute-start(bf16[512,512]{1,0:T(8,128)(2,1)} %get-tuple-element.44.kv0_ref), channel_id=1, source_target_pairs={{0,16},{8,24},{16,32},{24,40},{32,48},{40,56},{48,64},{56,72},{64,... | collective-permute-start | bytes 1572872 | tf_op jit(solution)/shard_map/ppermute | solution.py:485
  251.8 18.2 %copy-start.13 = (bf16[512,512]{1,0:T(8,128)(2,1)S(1)}, bf16[512,512]{1,0:T(8,128)(2,1)}, u32[]{:S(2)}) copy-start(bf16[512,512]{1,0:T(8,128)(2,1)} %get-tuple-element.43.kv1_ref) | copy-start | bytes 1572868
  251.8 18.1 %collective-permute-start.6 = (bf16[512,512]{1,0:T(8,128)(2,1)}, bf16[512,512]{1,0:T(8,128)(2,1)S(1)}, u32[]{:S(2)}, u32[]{:S(2)}) collective-permute-start(bf16[512,512]{1,0:T(8,128)(2,1)} %get-tuple-element.43.kv1_ref), channel_id=1, source_target_pairs={{0,16},{8,24},{16,32},{24,40},{32,48},{40,56},{48,64},{56,72},{64,... | collective-permute-start | bytes 1572872 | tf_op jit(solution)/shard_map/ppermute | solution.py:485
  256.1 13.9 %copy-start.11 = (bf16[512,512]{1,0:T(8,128)(2,1)}, bf16[512,512]{1,0:T(8,128)(2,1)S(1)}, u32[]{:S(2)}) copy-start(bf16[512,512]{1,0:T(8,128)(2,1)S(1)} %collective-permute-done.8.far_ref) | copy-start | bytes 1572868
  256.2 23.5 %collective-permute-start.9 = (bf16[512,512]{1,0:T(8,128)(2,1)S(1)}, bf16[512,512]{1,0:T(8,128)(2,1)S(1)}, u32[]{:S(2)}, u32[]{:S(2)}) collective-permute-start(bf16[512,512]{1,0:T(8,128)(2,1)S(1)} %broadcast_select_fusion), channel_id=1, source_target_pairs={{0,8},{8,0},{16,24},{24,16},{32,40},{40,32},{48,56},{56,48},{64,72... | collective-permute-start | bytes 1572872 | tf_op jit(solution)/shard_map/ppermute | solution.py:395
  269.9 9.7 %copy-start.10 = (bf16[512,512]{1,0:T(8,128)(2,1)}, bf16[512,512]{1,0:T(8,128)(2,1)S(1)}, u32[]{:S(2)}) copy-start(bf16[512,512]{1,0:T(8,128)(2,1)S(1)} %collective-permute-done.6.far_ref) | copy-start | bytes 1572868
  270.0 22.1 %collective-permute-start.7 = (bf16[512,512]{1,0:T(8,128)(2,1)S(1)}, bf16[512,512]{1,0:T(8,128)(2,1)S(1)}, u32[]{:S(2)}, u32[]{:S(2)}) collective-permute-start(bf16[512,512]{1,0:T(8,128)(2,1)S(1)} %broadcast_select_fusion.1), channel_id=1, source_target_pairs={{0,8},{8,0},{16,24},{24,16},{32,40},{40,32},{48,56},{56,48},{64,72... | collective-permute-start | bytes 1572872 | tf_op jit(solution)/shard_map/ppermute | solution.py:395
  279.7 0.8 copy-start.18
  292.1 0.8 copy-start.17
  293.0 11.6 %copy-start.1 = (bf16[256,1920]{1,0:T(8,128)(2,1)S(1)}, bf16[256,1920]{1,0:T(8,128)(2,1)}, u32[]{:S(2)}) copy-start(bf16[256,1920]{1,0:T(8,128)(2,1)} %param.15) | copy-start | bytes 2949124
  (2 other events, 1.5 us)
Sparse Core Ops, SparseCore 0:
  9.7 51.4 all-gather.4
  74.0 134.6 all-gather.6
where the time goes:
time: 313 us; the launch traced here: 311 us
  Pallas kernels  92.9 us (30%)
  waiting for transfers between devices  88.6 us (28%)
  blocking collectives  63.9 us (20%)
  starting transfers between devices  30.5 us (10%)
  local copies, waits for them, and re-layouts  16.8 us (5%)
  between operations  13.8 us (4%)
  other arithmetic  4.92 us (2%)
    all_to_all x6, blocking collectives, exchange(): lax.all_to_all(value, axis, 0, 0, axis_index_groups=groups, tiled=True)  63.9 us
    all_gather x1, waiting for transfers between devices, on_device(): lax.all_gather(parts, 'song', axis=0, tiled=False)  38.7 us
    pallas_call x2, Pallas kernels, frames(): pl.pallas_call(functools.partial(frames_kernel, pair), out_shape=(shape(5...  23.6 us
    pallas_call x1, Pallas kernels, embed(): pl.pallas_call(embed_kernel, out_shape=shape(1024, D), in_specs=[pl.Block...  16.6 us
    ppermute x1, waiting for transfers between devices, on_device(): got0 = lax.ppermute(pack0, EVERY, other_half())  16.5 us
    ppermute x2, waiting for transfers between devices, from_two_back(): return lax.ppermute(value, 'song', [(i, i + 2) for i in range(14)])  15.2 us
    pallas_call x3, Pallas kernels, on_device(): call(functools.partial(middle_kernel, level), (shape(ROWS[level + 1], 256...  12.7 us
    all_to_all x3, starting transfers between devices, exchange(): lax.all_to_all(value, axis, 0, 0, axis_index_groups=groups, tiled=True)  12.6 us
  transfers between devices with their start and end apart: 15, of which 8 were waited for; matrix products, arithmetic and copies ran while one was open for 4% of the time, Pallas kernels for 22%

commit v1 on v0

v1 whole, which is shorter than its diff:
```python
import functools

import jax
import jax.numpy as jnp
from jax import lax
from jax.experimental import pallas as pl
from jax.experimental.pallas import tpu as pltpu
from jax.sharding import PartitionSpec as P

BF = jnp.bfloat16
F32 = jnp.float32
D = 1920
C = 1024
VOCAB = 2048
UPPER = 4096
HALF = 128
HALO = (40, 39, 36, 27, 0)
ROWS = (208, 208, 208, 192, 128)
VMEM_LIMIT = 60 << 20

Y_GROUPS = [[0, 1, 2, 3], [4, 5, 6, 7]]


def params(**kw):
    return pltpu.CompilerParams(vmem_limit_bytes=VMEM_LIMIT, **kw)


def cost(flops, nbytes, trans=0):
    return pl.CostEstimate(flops=flops, bytes_accessed=nbytes, transcendentals=trans)


def dot(a, b):
    return jnp.dot(a, b, preferred_element_type=F32)


def dilated_copies(level, info, dil_hbm, got_hbm, sib_hbm, near_ref, away_ref, sems):
    own = pl.multiple_of(info[0] * 512, 512)
    other = pl.multiple_of((1 - info[0]) * 512, 512)
    pairs = []
    for ref, hbm, begin in ((near_ref, got_hbm, own), (away_ref, sib_hbm, other)):
        part = hbm if level < 2 else hbm.at[level - 2]
        pairs.append((dil_hbm.at[level, :, :, pl.ds(begin, 512)], ref.at[:, pl.ds(0, 128), :]))
        for tap in range(3):
            pairs.append((part.at[pl.ds(tap * 128, 128), :], ref.at[tap, pl.ds(128, 128), :]))
    return [pltpu.make_async_copy(a, b, sems.at[i]) for i, (a, b) in enumerate(pairs)]


def mixing_copies(level, info, mix_hbm, got_hbm, sib_hbm, mix_ref, sems):
    pairs = []
    for half, hbm in enumerate((got_hbm, sib_hbm)):
        part = hbm if level < 2 else hbm.at[level - 2]
        begin = info[0] if half == 0 else 1 - info[0]
        rows = pl.ds(pl.multiple_of(begin * 512, 512), 512)
        pairs.append((mix_hbm.at[level, rows, :], mix_ref.at[half, :, pl.ds(0, 128)]))
        for y in range(4):
            pairs.append(
                (
                    part.at[pl.ds(384, 128), pl.ds(y * 128, 128)],
                    mix_ref.at[half, pl.ds(y * 128, 128), pl.ds(128, 128)],
                )
            )
    return [pltpu.make_async_copy(a, b, sems.at[i]) for i, (a, b) in enumerate(pairs)]


def send_terms(level, info, h_ref, near_ref, away_ref, out_ref):
    step = 3**level
    count = HALF + 2 * HALO[level + 1]
    padded = out_ref.shape[1]
    rows = h_ref.shape[0]
    first = info[1] - HALO[level]
    pos = first + lax.broadcasted_iota(jnp.int32, (rows, 1), 0)
    inside = (pos >= 0) & (pos < UPPER)
    h_ref[...] = jnp.where(inside, jnp.maximum(h_ref[...], 0.0), 0.0)
    taps = [h_ref[tap * step : tap * step + count, :].astype(BF) for tap in range(3)]
    for half, ref in enumerate((near_ref, away_ref)):
        total = dot(taps[0], ref[0]) + dot(taps[1], ref[1]) + dot(taps[2], ref[2])
        total = total.astype(BF)
        for y in range(4):
            out_ref[y, :count, half * 128 : half * 128 + 128] = total[:, y * 128 : y * 128 + 128]
    if padded > count:
        for y in range(4):
            out_ref[y, count:, :] = jnp.zeros((padded - count, 256), BF)


def start(copies):
    for copy in copies:
        copy.start()


def finish(copies):
    for copy in copies:
        copy.wait()


DILATED = [pltpu.VMEM((3, 256, 512), BF), pltpu.VMEM((3, 256, 512), BF), pltpu.SemaphoreType.DMA((8,))]
MIXING = [pltpu.VMEM((2, 512, 256), BF), pltpu.SemaphoreType.DMA((10,))]


def first_kernel(info, codes_ref, table_ref, dil_hbm, got_ref, sib_ref, h_ref, out_ref, near_ref, away_ref, sems, work):
    copies = dilated_copies(0, info, dil_hbm, got_ref, sib_ref, near_ref, away_ref, sems)
    start(copies)
    codes = codes_ref[...]
    rows = codes.shape[0]
    lane = lax.broadcasted_iota(jnp.int32, (rows, 1024), 1)
    core = info[0]
    one = jnp.ones((), BF)
    zero = jnp.zeros((), BF)
    h_own = jnp.zeros((rows, 128), F32)
    h_oth = jnp.zeros((rows, 128), F32)
    for src, begin in ((got_ref, core * 1024), (sib_ref, (1 - core) * 1024)):
        hot = jnp.where(codes - begin == lane, one, zero)
        h_own += dot(hot, table_ref[pl.ds(pl.multiple_of(begin, 1024), 1024), :])
        for q in range(4):
            h_oth += dot(hot[:, q * 256 : q * 256 + 256], src[512:768, q * 128 : q * 128 + 128])
    work[:, :128] = h_own
    work[:, 128:] = h_oth
    h_ref[...] = work[...]
    finish(copies)
    send_terms(0, info, work, near_ref, away_ref, out_ref)


def mixed(level, r_ref, h_ref, mix_ref):
    step = 3**level
    count = HALF + 2 * HALO[level + 1]
    h = h_ref[step : step + count, :]
    for half in range(2):
        r = jnp.concatenate([r_ref[y, :, half * 128 : half * 128 + 128] for y in range(4)], axis=1)
        h += dot(r, mix_ref[half])[:count]
    return h


def middle_kernel(level, info, r_ref, h_ref, mix_hbm, got_hbm, sib_hbm, dil_hbm, got1_hbm, sib1_hbm, new_ref, out_ref, mix_ref, mix_sems, near_ref, away_ref, sems, work):
    first = mixing_copies(level, info, mix_hbm, got_hbm, sib_hbm, mix_ref, mix_sems)
    then = dilated_copies(level + 1, info, dil_hbm, got1_hbm, sib1_hbm, near_ref, away_ref, sems)
    start(first)
    start(then)
    finish(first)
    count = HALF + 2 * HALO[level + 1]
    if work.shape[0] > count:
        work[count:, :] = jnp.zeros((work.shape[0] - count, 256), F32)
    work[:count, :] = mixed(level, r_ref, h_ref, mix_ref)
    new_ref[...] = work[...]
    finish(then)
    send_terms(level + 1, info, work, near_ref, away_ref, out_ref)


def last_kernel(info, r_ref, h_ref, mix_hbm, got_hbm, sib_hbm, out_ref, mix_ref, mix_sems):
    copies = mixing_copies(3, info, mix_hbm, got_hbm, sib_hbm, mix_ref, mix_sems)
    start(copies)
    finish(copies)
    h = mixed(3, r_ref, h_ref, mix_ref).astype(BF)
    for peer in range(8):
        out_ref[peer] = h


def call(body, outs, scratch=(), smem=1, n=0, hbm=0, after=0, flops=10**9, name=None):
    def spec(space):
        return pl.BlockSpec(memory_space=space)

    specs = [spec(pltpu.SMEM)] * smem + [spec(pltpu.VMEM)] * n
    specs += [spec(pl.ANY)] * hbm + [spec(pltpu.VMEM)] * after
    return pl.pallas_call(
        body,
        out_shape=outs,
        in_specs=specs,
        out_specs=jax.tree.map(lambda _: spec(pltpu.VMEM), outs),
        scratch_shapes=list(scratch),
        compiler_params=params(),
        cost_estimate=cost(flops, 4 << 20),
        name=name,
    )


def shape(*dims, dtype=BF):
    return jax.ShapeDtypeStruct(dims, dtype)


BLOCKS = D // 128
UP_BLOCKS = 2 * BLOCKS
PART = UP_BLOCKS + 16
CHUNKS = ((0, 4), (4, 4), (8, 4), (12, 3))


def frames_kernel(pair, info, codes_ref, hf_ref, gain_ref, qkv_ref, full_ref, q_ref, kv_ref, weights, table, hf, rows, x, xn, sems, table_sems):
    def weight_copies(phase):
        return [
            pltpu.make_async_copy(
                full_ref.at[pl.ds(part * 4 ^ info[3], 4), pair, t ^ info[3], pl.ds(phase * BLOCKS, BLOCKS)],
                weights.at[phase, t, pl.ds(part * 4, 4)],
                sems.at[phase, part, t],
            )
            for part in range(2)
            for t in range(8)
        ]

    table_copies = [
        pltpu.make_async_copy(
            full_ref.at[:, part, :, pl.ds(UP_BLOCKS, 16)], table.at[:, part], table_sems.at[part]
        )
        for part in range(2)
    ]
    start(weight_copies(0))
    start(table_copies)
    start(weight_copies(1))
    for half in range(2):
        for j in range(8):
            at = 0 if j // 4 == half else 128
            hf[half * 128 : half * 128 + 128, j * 128 : j * 128 + 128] = hf_ref[
                half * 4 + j % 4, :, at : at + 128
            ]
    flat = table.reshape(VOCAB, 16, 128)
    for phase in range(2):
        finish(weight_copies(phase))
        for first, size in CHUNKS:
            w = [weights[phase, :, :, block].reshape(C, 128) for block in range(first, first + size)]
            x[:, first * 128 : (first + size) * 128] = dot(hf[...], jnp.concatenate(w, axis=1))
        if phase == 0:
            finish(table_copies)

        def look_up(i, carry):
            for j in range(8):
                row = i * 8 + j
                rows[row] = flat[codes_ref[(pair * 2 + phase) * 256 + row]].astype(F32)
            return carry

        lax.fori_loop(0, 32, look_up, 0)
        total = jnp.zeros((256, 128), F32)
        for block in range(BLOCKS):
            cols = slice(block * 128, block * 128 + 128)
            y = x[:, cols] + rows[:, block, :]
            x[:, cols] = y
            total += y
        mean = jnp.sum(total, axis=1, keepdims=True) * (1.0 / D)
        square = jnp.zeros((256, 128), F32)
        for block in range(BLOCKS):
            y = x[:, block * 128 : block * 128 + 128] - mean
            square += y * y
        factor = lax.rsqrt(jnp.sum(square, axis=1, keepdims=True) * (1.0 / D) + 1e-5)
        for block in range(BLOCKS):
            cols = slice(block * 128, block * 128 + 128)
            xn[:, cols] = ((x[:, cols] - mean) * factor * gain_ref[:, cols]).astype(BF)
        y = dot(xn[...], qkv_ref[...]).astype(BF)
        lines = slice(phase * 256, phase * 256 + 256)
        for head in range(2):
            at = head * 384
            cols = slice(head * 128, head * 128 + 128)
            q_ref[lines, cols] = y[:, at : at + 128]
            kv_ref[lines, cols] = y[:, at + 128 : at + 256]
            kv_ref[lines, 256 + head * 128 : 384 + head * 128] = y[:, at + 256 : at + 384]


def frames(pair, info, codes, hf, gain, qkv, full):
    vm = pl.BlockSpec(memory_space=pltpu.VMEM)
    sm = pl.BlockSpec(memory_space=pltpu.SMEM)
    return pl.pallas_call(
        functools.partial(frames_kernel, pair),
        out_shape=(shape(512, 256), shape(512, 512)),
        in_specs=[sm, sm, vm, vm, vm, pl.BlockSpec(memory_space=pltpu.HBM)],
        out_specs=(vm, vm),
        scratch_shapes=[
            pltpu.VMEM((2, 8, 8, BLOCKS, 16, 128), BF),
            pltpu.VMEM((8, 2, 8, 16, 16, 128), BF),
            pltpu.VMEM((256, C), BF),
            pltpu.VMEM((256, 16, 128), F32),
            pltpu.VMEM((256, D), F32),
            pltpu.VMEM((256, D), BF),
            pltpu.SemaphoreType.DMA((2, 2, 8)),
            pltpu.SemaphoreType.DMA((2,)),
        ],
        compiler_params=params(),
        cost_estimate=cost(4 * 10**9, 20 << 20),
        name="frames",
    )(info, codes, hf, gain, qkv, full)


SCALE = 128**-0.5 * 1.4426950408889634


def scores_of(q, k):
    return lax.dot_general(q, k, (((1,), (1,)), ((), ())), preferred_element_type=F32)


def fold(q_refs, kv_refs, seen_of, old_of, put):
    kv = jnp.concatenate([ref[...] for ref in kv_refs], axis=0)
    ones = jnp.ones((kv.shape[0], 128), BF)
    for head in range(2):
        k = kv[:, head * 128 : head * 128 + 128]
        v = jnp.concatenate([kv[:, 256 + head * 128 : 384 + head * 128], ones], axis=1)
        for phase in range(4):
            lines = slice(phase % 2 * 256, phase % 2 * 256 + 256)
            s = scores_of(q_refs[phase // 2][lines, head * 128 : head * 128 + 128], k)
            s = jnp.where(seen_of(phase), s, -1e30)
            top = jnp.max(s, axis=1, keepdims=True)
            old = old_of(head, phase)
            if old is None:
                put(head, phase, top, dot(jnp.exp2((s - top) * SCALE).astype(BF), v))
            else:
                top = jnp.maximum(old[0], top)
                p = jnp.exp2((s - top) * SCALE).astype(BF)
                put(head, phase, top, old[1] * jnp.exp2((old[0] - top) * SCALE) + dot(p, v))


def at_tile(head, phase):
    lines = slice(phase * 256, phase * 256 + 256)
    return (lines, slice(head, head + 1)), (lines, slice(head * 256, head * 256 + 256))


def own_kernel(q0_ref, q1_ref, kv0_ref, kv1_ref, acc_ref, top_ref):
    col = lax.broadcasted_iota(jnp.int32, (256, 1024), 1)
    ahead = (col & 255) * 4 + (col >> 8) - 4 * lax.broadcasted_iota(jnp.int32, (256, 1024), 0)

    def put(head, phase, top, acc):
        one, both = at_tile(head, phase)
        top_ref[one] = top
        acc_ref[both] = acc

    fold((q0_ref, q1_ref), (kv0_ref, kv1_ref), lambda p: ahead <= p, lambda head, phase: None, put)


def past_kernel(last, info, q0_ref, q1_ref, far_ref, near_ref, acc_ref, top_ref, *refs):
    if last:
        out_ref, acc, tops, wide = refs
    else:
        acc, tops = refs
    song = info[2]

    @pl.when(song == 0)
    def _():
        acc[...] = acc_ref[...]
        tops[...] = top_ref[...]

    @pl.when(song > 0)
    def _():
        col = lax.broadcasted_iota(jnp.int32, (256, 1024), 1)
        seen = col >= jnp.where(song == 1, 512, 0)

        def old_of(head, phase):
            one, both = at_tile(head, phase)
            return top_ref[one], acc_ref[both]

        def put(head, phase, top, total):
            one, both = at_tile(head, phase)
            tops[one] = top
            acc[both] = total

        fold((q0_ref, q1_ref), (far_ref, near_ref), lambda p: seen, old_of, put)

    if last:
        for head in range(2):
            for phase in range(4):
                both = acc[at_tile(head, phase)[1]]
                wide[pl.ds(phase, 256, stride=4), :] = both[:, :128] / both[:, 128:]
            out_ref[:, head * 128 : head * 128 + 128] = wide[...].astype(BF)


EVERY = ("song", "tensor")


def other_half():
    pairs = []
    for song in range(16):
        for rank in range(8):
            pairs.append((song * 8 + rank, (song ^ 8) * 8 + (rank ^ 4)))
    return pairs


def to_sibling(value):
    return lax.ppermute(value, "song", [(i, i ^ 1) for i in range(16)])


def exchange(value, axis="tensor", groups=None):
    return lax.all_to_all(value, axis, 0, 0, axis_index_groups=groups, tiled=True)


def on_device(
    upper_codes,
    middle_codes,
    upper_table,
    dilated_weight,
    mixing_weight,
    upsample_weight,
    middle_table,
    norm_gain,
    qkv_weight,
):
    song = lax.axis_index("song")
    rank = lax.axis_index("tensor")
    core = song % 2
    x_hi = rank // 4
    begin = song * 256 + x_hi * HALF
    info = jnp.stack([core, begin, song, x_hi * 4]).astype(jnp.int32)

    after = lax.ppermute(upper_codes[-40:], "song", [(i, i + 1) for i in range(15)])
    before = lax.ppermute(upper_codes[:40], "song", [(i + 1, i) for i in range(15)])
    codes = jnp.concatenate([after, upper_codes, before])
    codes = lax.dynamic_slice_in_dim(codes, x_hi * HALF, HALF + 80)[:, None]

    dil_half = lax.dynamic_slice_in_dim(dilated_weight, core * 512, 512, 3)
    mix_half = lax.dynamic_slice_in_dim(mixing_weight, core * 512, 512, 1)
    mix_pack = jnp.concatenate([mix_half[:, i * 128 : i * 128 + 128] for i in range(4)], axis=2)
    tab_half = lax.dynamic_slice_in_dim(upper_table, core * 1024, 1024, 0)
    tab_pack = jnp.concatenate([tab_half[i * 256 : i * 256 + 256] for i in range(4)], axis=1)
    pack0 = jnp.concatenate([dil_half[0].reshape(384, 512), mix_pack[0], tab_pack], axis=0)
    pack1 = jnp.concatenate([dil_half[1].reshape(384, 512), mix_pack[1]], axis=0)
    pack2 = jnp.concatenate([dil_half[2:].reshape(2, 384, 512), mix_pack[2:]], axis=1)
    got0 = lax.ppermute(pack0, EVERY, other_half())

    share = song ^ (8 * x_hi)
    up_part = lax.dynamic_slice(upsample_weight, (share // 2 * 16, core * 2 * D), (16, 2 * D))
    mid_part = lax.dynamic_slice_in_dim(middle_table, share * 16, 16, 0)
    up_part = up_part.reshape(16, UP_BLOCKS, 128).transpose(1, 0, 2)
    mid_part = jnp.pad(mid_part.reshape(16, BLOCKS, 128), ((0, 0), (0, 1), (0, 0)))
    part = jnp.concatenate([up_part, mid_part])
    part, pack0 = lax.optimization_barrier((part, pack0))
    mine = exchange(jnp.broadcast_to(part[None], (4, PART, 16, 128)), groups=Y_GROUPS)
    mine, got0 = lax.optimization_barrier((mine, got0))
    sib0 = to_sibling(got0)
    others = lax.ppermute(mine, EVERY, other_half())

    h, terms = call(
        first_kernel,
        (shape(ROWS[0], 256, dtype=F32), shape(4, ROWS[1], 256)),
        [*DILATED, pltpu.VMEM((ROWS[0], 256), F32)],
        n=2,
        hbm=1,
        after=2,
        name="cond0",
    )(info, codes, upper_table, dilated_weight, got0, sib0)
    for level in range(4):
        terms = exchange(terms, groups=Y_GROUPS)
        if level == 0:
            others, pack1, terms = lax.optimization_barrier((others, pack1, terms))
            full = lax.all_gather(jnp.concatenate([mine, others]), "song", axis=0, tiled=False)
            full = full.reshape(8, 2, 8, PART, 16, 128)
            got1 = lax.ppermute(pack1, EVERY, other_half())
        total = terms[0].astype(F32)
        for y in range(1, 4):
            total = total + terms[y].astype(F32)
        r = jnp.maximum(total, 0.0).astype(BF)
        r = exchange(jnp.broadcast_to(r[None], terms.shape), groups=Y_GROUPS)
        if level == 0:
            got1, pack2, r = lax.optimization_barrier((got1, pack2, r))
            sib1 = to_sibling(got1)
            got2 = lax.ppermute(pack2, EVERY, other_half())
            stacks = [(got0, sib0), (got1, sib1)]
        if level == 1:
            got2, r = lax.optimization_barrier((got2, r))
            stacks += [(got2, to_sibling(got2))] * 2
        if level < 3:
            h, terms = call(
                functools.partial(middle_kernel, level),
                (shape(ROWS[level + 1], 256, dtype=F32), shape(4, ROWS[level + 2], 256)),
                [*MIXING, *DILATED, pltpu.VMEM((ROWS[level + 1], 256), F32)],
                n=2,
                hbm=6,
                name="cond",
            )(info, r, h, mixing_weight, *stacks[level], dilated_weight, *stacks[level + 1])
        else:
            spread = call(
                last_kernel, shape(8, HALF, 256), MIXING, n=2, hbm=3, name="cond_end"
            )(info, r, h, mixing_weight, *stacks[level])
    hf = exchange(spread)

    mid = middle_codes.reshape(256, 4).T.reshape(1024)
    mid = ((mid % 256) // 16 * 128 + mid // 256 * 16 + mid % 16) ^ (x_hi * (8 * 128 + 4 * 16))
    gain = norm_gain[None]
    qkv = qkv_weight.reshape(D, 768)

    def from_two_back(value):
        return lax.ppermute(value, "song", [(i, i + 2) for i in range(14)])

    q0, kv0 = frames(0, info, mid, hf, gain, qkv, full)
    far0 = from_two_back(kv0)
    q1, kv1 = frames(1, info, mid, hf, gain, qkv, full)
    far1 = from_two_back(kv1)
    state = (shape(1024, 512, dtype=F32), shape(1024, 2, dtype=F32))
    kept = call(own_kernel, state, smem=0, n=4, flops=10**9, name="own")(q0, q1, kv0, kv1)
    near0 = to_sibling(jnp.where(core == 0, kv0, far0))
    far1, kept = lax.optimization_barrier((far1, kept))
    kept = call(functools.partial(past_kernel, False), state, n=6, flops=2 * 10**9, name="past")(
        info, q0, q1, far0, near0, *kept
    )
    near1 = to_sibling(jnp.where(core == 0, kv1, far1))
    return call(
        functools.partial(past_kernel, True),
        shape(1024, 256),
        [pltpu.VMEM((1024, 512), F32), pltpu.VMEM((1024, 2), F32), pltpu.VMEM((1024, 128), F32)],
        n=6,
        flops=2 * 10**9,
        name="past_end",
    )(info, q0, q1, far1, near1, *kept)


def solution(mesh):
    placed = (
        P("song"),
        P("song"),
        P(None, "tensor"),
        P(None, None, "tensor", None),
        P(None, None, "tensor"),
        P("tensor", None),
        P("tensor", None),
        P(),
        P(None, "tensor", None),
    )
    return jax.shard_map(
        on_device, mesh=mesh, in_specs=placed, out_specs=P("song", "tensor"), check_vma=False
    )
```

time: 313 us -> 270 us (0.86)
  waiting for transfers between devices: 88.6 us -> 51.6 us
  Pallas kernels: 92.9 us -> 71.8 us
  starting transfers between devices: 30.5 us -> 40.5 us
    pallas_call x4 -> x3, Pallas kernels: 48.6 us -> 19.8 us  [the longest x1 7.17 us: on_device(): call(functools.partial(past_kernel, False), state, n=6, flops=2 * 10 ** 9...]
    all_gather x2 -> x1, waiting for transfers between devices: 38.7 us -> 11.4 us  [on_device(): lax.all_gather(jnp.concatenate([mine, others]), 'song', axis=0, tiled=False)]
    all_to_all x3 -> x4, waiting for transfers between devices: 4 us -> 23.2 us  [exchange(): lax.all_to_all(value, axis, 0, 0, axis_index_groups=groups, tiled=True)]
    ppermute x1, waiting for transfers between devices: 16.5 us -> 0.01 us  [on_device(): got0 = lax.ppermute(pack0, EVERY, other_half())]
    ppermute x1, waiting for transfers between devices: 11.7 us -> 0.01 us  [on_device(): got1 = lax.ppermute(pack1, EVERY, other_half())]
    pallas_call x2, Pallas kernels: 23.6 us -> 31.6 us  [frames(): pl.pallas_call(functools.partial(frames_kernel, pair), out_shape=(shape(5...]
    ppermute x2, waiting for transfers between devices: 15.2 us -> 9.52 us  [from_two_back(): return lax.ppermute(value, 'song', [(i, i + 2) for i in range(14)])]
    all_to_all x3 -> x4, starting transfers between devices: 12.6 us -> 16.7 us  [exchange(): lax.all_to_all(value, axis, 0, 0, axis_index_groups=groups, tiled=True)]
  transfers between devices with their start and end apart: 15 -> 18, of which waited for: 8 -> 9; matrix products, arithmetic and copies ran while one was open for 4% -> 6% of each run, Pallas kernels for 22% -> 18%
where the time goes in v1:
time: 270 us; the launch traced here: 268 us
  Pallas kernels  71.8 us (27%)
  blocking collectives  64.9 us (24%)
  waiting for transfers between devices  51.6 us (19%)
  starting transfers between devices  40.5 us (15%)
  local copies, waits for them, and re-layouts  18.7 us (7%)
  between operations  13.7 us (5%)
  other arithmetic  6.73 us (2%)
    all_to_all x6, blocking collectives, exchange(): lax.all_to_all(value, axis, 0, 0, axis_index_groups=groups, tiled=True)  64.9 us
    pallas_call x2, Pallas kernels, frames(): pl.pallas_call(functools.partial(frames_kernel, pair), out_shape=(shape(5...  31.6 us
    all_to_all x4, waiting for transfers between devices, exchange(): lax.all_to_all(value, axis, 0, 0, axis_index_groups=groups, tiled=True)  23.2 us
    all_to_all x4, starting transfers between devices, exchange(): lax.all_to_all(value, axis, 0, 0, axis_index_groups=groups, tiled=True)  16.7 us
    pallas_call x3, Pallas kernels, on_device(): call(functools.partial(middle_kernel, level), (shape(ROWS[level + 1], 256...  12.5 us
    all_gather x1, waiting for transfers between devices, on_device(): lax.all_gather(jnp.concatenate([mine, others]), 'song', axis=0, tiled=False)  11.4 us
    ppermute x2, waiting for transfers between devices, from_two_back(): return lax.ppermute(value, 'song', [(i, i + 2) for i in range(14)])  9.52 us
    ppermute x5, starting transfers between devices, to_sibling(): return lax.ppermute(value, 'song', [(i, i ^ 1) for i in range(16)])  9.04 us
  transfers between devices with their start and end apart: 18, of which 9 were waited for; matrix products, arithmetic and copies ran while one was open for 6% of the time, Pallas kernels for 18%

profile of v1, /device:TPU:3, one launch (start us, length us, event | category | flops | bytes accessed | tf_op | source)
XLA Modules:
  0.0 268.1 jit_solution(6965074376613477085)
XLA Ops:
  15.3 14.4 %all_to_all.50 = bf16[4,46,16,128]{3,2,1,0:T(8,128)(2,1)S(1)} all-to-all(bf16[4,46,16,128]{3,2,1,0:T(8,128)(2,1)S(1)} %broadcast_in_dim.44), channel_id=1, replica_groups={{0,1,2,3},{4,5,6,7},{8,9,10,11},{12,13,14,15},{16,17,18,19},{20,21,22,2..., dimensions={0} | all-to-all | bytes 1507328 | tf_op jit(solution)/shard_map/all_to_all | solution.py:372
  32.5 3.8 %collective-permute-start.2 = (s32[40]{0:T(128)S(1)}, s32[40]{0:T(128)S(1)}, u32[]{:S(2)}, u32[]{:S(2)}) collective-permute-start(s32[40]{0:T(128)S(1)} %get-tuple-element.77), channel_id=1, source_target_pairs={{0,8},{8,16},{16,24},{24,32},{32,40},{40,48},{48,56},{56,64},{64,7... | collective-permute-start | bytes 488 | tf_op jit(solution)/shard_map/ppermute | solution.py:393
  38.9 2.7 %collective-permute-done.3 = s32[40]{0:T(128)S(1)} collective-permute-done((s32[40]{0:T(128)S(1)}, s32[40]{0:T(128)S(1)}, u32[]{:S(2)}, u32[]{:S(2)}) %collective-permute-start.3) | collective-permute-done | bytes 192 | tf_op jit(solution)/shard_map/ppermute | solution.py:394
  43.4 4.7 %cond0.1 = (f32[208,256]{1,0:T(8,128)}, bf16[4,208,256]{2,1,0:T(8,128)(2,1)}) custom-call(s32[4]{0:T(128)} %pad_add_fusion.1.info, s32[208,1]{1,0:T(8,128)} %copy.17.codes_ref, bf16[2048,128]{1,0:T(8,128)(2,1)} %table_ref.1, bf16[4,3,128,1024]{3,2,1,0:T(8,128)(2,1)} %dil_hbm.7, bf16[768,512]{1,0:T(8,128)(2,1)} %copy-done.6, bf16[768,512]{1,0:T(8,128)(2,1)} %copy-done.7), custom_call_target="tpu_custom_call" | custom-call | flops 1000000000 | bytes 4194304 | tf_op jit(solution)/shard_map/cond0/pallas_call | solution.py:420
  48.1 3.5 %all-to-all-start.1 = ((bf16[4,208,256]{2,1,0:T(8,128)(2,1)}), bf16[4,208,256]{2,1,0:T(8,128)(2,1)S(1)}, u32[]{:S(2)}, u32[]{:S(2)}) async-start(bf16[4,208,256]{2,1,0:T(8,128)(2,1)} %get-tuple-element.38), calls=%async_computation.1 | async-start | bytes 851968 | tf_op jit(solution)/shard_map/all_to_all | solution.py:372
  52.5 5.5 %all-to-all-done.1 = bf16[4,208,256]{2,1,0:T(8,128)(2,1)S(1)} async-done(((bf16[4,208,256]{2,1,0:T(8,128)(2,1)}), bf16[4,208,256]{2,1,0:T(8,128)(2,1)S(1)}, u32[]{:S(2)}, u32[]{:S(2)}) %all-to-all-start.1) | async-done | bytes 426016 | tf_op jit(solution)/shard_map/all_to_all | solution.py:372
  63.1 3.5 %all-to-all-start.2 = ((bf16[4,208,256]{2,1,0:T(8,128)(2,1)}), bf16[4,208,256]{2,1,0:T(8,128)(2,1)S(1)}, u32[]{:S(2)}, u32[]{:S(2)}) async-start(bf16[4,208,256]{2,1,0:T(8,128)(2,1)} %broadcast_in_dim.47), calls=%async_computation.2 | async-start | bytes 851968 | tf_op jit(solution)/shard_map/all_to_all | solution.py:372
  67.8 5.2 %all-to-all-done.2.r_ref = bf16[4,208,256]{2,1,0:T(8,128)(2,1)S(1)} async-done(((bf16[4,208,256]{2,1,0:T(8,128)(2,1)}), bf16[4,208,256]{2,1,0:T(8,128)(2,1)S(1)}, u32[]{:S(2)}, u32[]{:S(2)}) %all-to-all-start.2) | async-done | bytes 426016 | tf_op jit(solution)/shard_map/all_to_all | solution.py:372
  73.1 2.9 %collective-permute-start.7 = (bf16[512,512]{1,0:T(8,128)(2,1)S(1)}, bf16[512,512]{1,0:T(8,128)(2,1)S(1)}, u32[]{:S(2)}, u32[]{:S(2)}) collective-permute-start(bf16[512,512]{1,0:T(8,128)(2,1)S(1)} %collective-permute-done.5.got1_hbm.got_hbm), channel_id=1, source_target_pairs={{0,8},{8,0},{16,24},{24,16},{32,40},{40,32},{48,56},{56,48},{64,72... | collective-permute-start | bytes 1572872 | tf_op jit(solution)/shard_map/ppermute | solution.py:368
  78.3 4.2 %cond.3 = (f32[208,256]{1,0:T(8,128)}, bf16[4,208,256]{2,1,0:T(8,128)(2,1)}) custom-call(s32[4]{0:T(128)} %pad_add_fusion.1.info, bf16[4,208,256]{2,1,0:T(8,128)(2,1)} %copy-done.10, f32[208,256]{1,0:T(8,128)} %get-tuple-element.43.h_ref, bf16[4,1024,128]{2,1,0:T(8,128)(2,1)} %mix_hbm.7, bf16[768,512]{1,0:T(8,128)(2,1)} %copy-done.6, ...), custom_call_target="tpu_custom_call" | custom-call | flops 1000000000 | bytes 4194304 | tf_op jit(solution)/shard_map/cond/pallas_call | solution.py:450
  82.5 11.5 %all_to_all.51 = bf16[4,208,256]{2,1,0:T(8,128)(2,1)S(1)} all-to-all(bf16[4,208,256]{2,1,0:T(8,128)(2,1)} %get-tuple-element.45), channel_id=1, replica_groups={{0,1,2,3},{4,5,6,7},{8,9,10,11},{12,13,14,15},{16,17,18,19},{20,21,22,2..., dimensions={0} | all-to-all | bytes 851968 | tf_op jit(solution)/shard_map/all_to_all | solution.py:372
  94.9 3.5 %all-to-all-start.4 = ((bf16[4,208,256]{2,1,0:T(8,128)(2,1)}), bf16[4,208,256]{2,1,0:T(8,128)(2,1)S(1)}, u32[]{:S(2)}, u32[]{:S(2)}) async-start(bf16[4,208,256]{2,1,0:T(8,128)(2,1)} %broadcast_in_dim.49), calls=%async_computation.4 | async-start | bytes 851968 | tf_op jit(solution)/shard_map/all_to_all | solution.py:372
  98.4 2.5 collective-permute-done.6.got1_hbm.got_hbm
  100.9 4.3 %all-to-all-done.4.r_ref = bf16[4,208,256]{2,1,0:T(8,128)(2,1)S(1)} async-done(((bf16[4,208,256]{2,1,0:T(8,128)(2,1)}), bf16[4,208,256]{2,1,0:T(8,128)(2,1)S(1)}, u32[]{:S(2)}, u32[]{:S(2)}) %all-to-all-start.4) | async-done | bytes 426016 | tf_op jit(solution)/shard_map/all_to_all | solution.py:372
  105.2 2.5 collective-permute-start.8
  111.1 4.2 %cond.4 = (f32[208,256]{1,0:T(8,128)}, bf16[4,192,256]{2,1,0:T(8,128)(2,1)}) custom-call(s32[4]{0:T(128)} %pad_add_fusion.1.info, bf16[4,208,256]{2,1,0:T(8,128)(2,1)} %copy-done.11, f32[208,256]{1,0:T(8,128)} %get-tuple-element.47.h_ref, bf16[4,1024,128]{2,1,0:T(8,128)(2,1)} %mix_hbm.7, bf16[512,512]{1,0:T(8,128)(2,1)} %copy-done.8, ...), custom_call_target="tpu_custom_call" | custom-call | flops 1000000000 | bytes 4194304 | tf_op jit(solution)/shard_map/cond/pallas_call | solution.py:450
  115.3 11.3 %all_to_all.52 = bf16[4,192,256]{2,1,0:T(8,128)(2,1)S(1)} all-to-all(bf16[4,192,256]{2,1,0:T(8,128)(2,1)} %get-tuple-element.49), channel_id=1, replica_groups={{0,1,2,3},{4,5,6,7},{8,9,10,11},{12,13,14,15},{16,17,18,19},{20,21,22,2..., dimensions={0} | all-to-all | bytes 786432 | tf_op jit(solution)/shard_map/all_to_all | solution.py:372
  126.7 10.0 %all_to_all.53.r_ref = bf16[4,192,256]{2,1,0:T(8,128)(2,1)} all-to-all(bf16[4,192,256]{2,1,0:T(8,128)(2,1)S(1)} %broadcast_in_dim.51), channel_id=1, replica_groups={{0,1,2,3},{4,5,6,7},{8,9,10,11},{12,13,14,15},{16,17,18,19},{20,21,22,2..., dimensions={0} | all-to-all | bytes 786432 | tf_op jit(solution)/shard_map/all_to_all | solution.py:372
  136.7 4.1 %cond.5 = (f32[192,256]{1,0:T(8,128)}, bf16[4,128,256]{2,1,0:T(8,128)(2,1)}) custom-call(s32[4]{0:T(128)} %pad_add_fusion.1.info, bf16[4,192,256]{2,1,0:T(8,128)(2,1)} %all_to_all.53.r_ref, f32[208,256]{1,0:T(8,128)} %get-tuple-element.50.h_ref, bf16[4,1024,128]{2,1,0:T(8,128)(2,1)} %mix_hbm.7, bf16[2,512,512]{2,1,0:T(8,128)(2,1)} %copy-done.3, ...), custom_call_target="tpu_custom_call" | custom-call | flops 1000000000 | bytes 4194304 | tf_op jit(solution)/shard_map/cond/pallas_call | solution.py:450
  140.8 8.9 %all_to_all.54 = bf16[4,128,256]{2,1,0:T(8,128)(2,1)S(1)} all-to-all(bf16[4,128,256]{2,1,0:T(8,128)(2,1)} %get-tuple-element.51), channel_id=1, replica_groups={{0,1,2,3},{4,5,6,7},{8,9,10,11},{12,13,14,15},{16,17,18,19},{20,21,22,2..., dimensions={0} | all-to-all | bytes 524288 | tf_op jit(solution)/shard_map/all_to_all | solution.py:372
  149.8 8.6 %all_to_all.55.r_ref = bf16[4,128,256]{2,1,0:T(8,128)(2,1)} all-to-all(bf16[4,128,256]{2,1,0:T(8,128)(2,1)S(1)} %broadcast_in_dim.53), channel_id=1, replica_groups={{0,1,2,3},{4,5,6,7},{8,9,10,11},{12,13,14,15},{16,17,18,19},{20,21,22,2..., dimensions={0} | all-to-all | bytes 524288 | tf_op jit(solution)/shard_map/all_to_all | solution.py:372
  158.4 3.3 %cond_end.1 = bf16[8,128,256]{2,1,0:T(8,128)(2,1)} custom-call(s32[4]{0:T(128)} %pad_add_fusion.1.info, bf16[4,128,256]{2,1,0:T(8,128)(2,1)} %all_to_all.55.r_ref, f32[192,256]{1,0:T(8,128)} %get-tuple-element.52.h_ref, bf16[4,1024,128]{2,1,0:T(8,128)(2,1)} %mix_hbm.7, bf16[2,512,512]{2,1,0:T(8,128)(2,1)} %copy-done.3, bf16[2,512,512]{2,1,0:T(8,128)(2,1)} %copy-done.4), custom_call_target="tpu_custom_call" | custom-call | flops 1000000000 | bytes 4194304 | tf_op jit(solution)/shard_map/cond_end/pallas_call | solution.py:459
  161.7 6.3 %all-to-all-start.9 = ((bf16[8,128,256]{2,1,0:T(8,128)(2,1)}), bf16[8,128,256]{2,1,0:T(8,128)(2,1)S(1)}, u32[]{:S(2)}, u32[]{:S(2)}) async-start(bf16[8,128,256]{2,1,0:T(8,128)(2,1)} %cond_end.1), calls=%async_computation.9 | async-start | bytes 1048576 | tf_op jit(solution)/shard_map/all_to_all | solution.py:372
  168.8 4.1 %copy.20 = bf16[240,8,2,384]{3,1,2,0:T(8,128)(2,1)} copy(bf16[240,8,2,384]{3,2,1,0:T(2,128)(2,1)} %bitcast.37) | data formatting | bytes 5898240
  173.6 8.2 %all-to-all-done.9.hf_ref = bf16[8,128,256]{2,1,0:T(8,128)(2,1)S(1)} async-done(((bf16[8,128,256]{2,1,0:T(8,128)(2,1)}), bf16[8,128,256]{2,1,0:T(8,128)(2,1)S(1)}, u32[]{:S(2)}, u32[]{:S(2)}) %all-to-all-start.9) | async-done | bytes 524320 | tf_op jit(solution)/shard_map/all_to_all | solution.py:372
  181.7 11.4 %all-gather.3.cloned.1.call-done = bf16[128,46,16,128]{3,2,1,0:T(8,128)(2,1)} async-done(((bf16[8,46,16,128]{3,2,1,0:T(8,128)(2,1)}), bf16[128,46,16,128]{3,2,1,0:T(8,128)(2,1)}) %all-gather.3.cloned.1.call-update) | async-done | bytes 24117264 | tf_op jit(solution)/shard_map/all_gather | solution.py:433
  193.1 15.8 %frames.2 = (bf16[512,256]{1,0:T(8,128)(2,1)}, bf16[512,512]{1,0:T(8,128)(2,1)}) custom-call(s32[4]{0:T(128)} %pad_add_fusion.1.info, s32[1024]{0:T(1024)} %fusion.11.codes_ref, bf16[8,128,256]{2,1,0:T(8,128)(2,1)} %copy-done.5, f32[1,1920]{1,0:T(1,128)} %broadcast_in_dim.54.gain_ref, bf16[1920,768]{1,0:T(8,128)(2,1)} %bitcast.34, ...), custom_call_target="tpu_custom_call" | custom-call | flops 4000000000 | bytes 20971520 | tf_op jit(solution)/shard_map/frames/pallas_call | solution.py:255
  211.1 15.8 %frames.3 = (bf16[512,256]{1,0:T(8,128)(2,1)}, bf16[512,512]{1,0:T(8,128)(2,1)}) custom-call(s32[4]{0:T(128)} %pad_add_fusion.1.info, s32[1024]{0:T(1024)} %fusion.11.codes_ref, bf16[8,128,256]{2,1,0:T(8,128)(2,1)} %copy-done.5, f32[1,1920]{1,0:T(1,128)} %broadcast_in_dim.54.gain_ref, bf16[1920,768]{1,0:T(8,128)(2,1)} %bitcast.35, ...), custom_call_target="tpu_custom_call" | custom-call | flops 4000000000 | bytes 20971520 | tf_op jit(solution)/shard_map/frames/pallas_call | solution.py:255
  229.0 6.2 %own.1 = (f32[1024,512]{1,0:T(8,128)}, f32[1024,2]{1,0:T(8,128)}) custom-call(bf16[512,256]{1,0:T(8,128)(2,1)} %get-tuple-element.54.q0_ref, bf16[512,256]{1,0:T(8,128)(2,1)} %get-tuple-element.55.q1_ref, bf16[512,512]{1,0:T(8,128)(2,1)} %get-tuple-element.57.kv0_ref, bf16[512,512]{1,0:T(8,128)(2,1)} %get-tuple-element.56.kv1_ref), custom_call_target="tpu_custom_call" | custom-call | flops 1000000000 | bytes 4194304 | tf_op jit(solution)/shard_map/own/pallas_call | solution.py:477
  235.5 9.5 %collective-permute-done.9.far_ref = bf16[512,512]{1,0:T(8,128)(2,1)S(1)} collective-permute-done((bf16[512,512]{1,0:T(8,128)(2,1)}, bf16[512,512]{1,0:T(8,128)(2,1)S(1)}, u32[]{:S(2)}, u32[]{:S(2)}) %collective-permute-start.9) | collective-permute-done | bytes 524320 | tf_op jit(solution)/shard_map/ppermute | solution.py:470
  246.8 7.2 %past.1 = (f32[1024,512]{1,0:T(8,128)}, f32[1024,2]{1,0:T(8,128)}) custom-call(s32[4]{0:T(128)} %pad_add_fusion.1.info, bf16[512,256]{1,0:T(8,128)(2,1)} %get-tuple-element.54.q0_ref, bf16[512,256]{1,0:T(8,128)(2,1)} %get-tuple-element.55.q1_ref, bf16[512,512]{1,0:T(8,128)(2,1)} %copy-done.13, bf16[512,512]{1,0:T(8,128)(2,1)} %copy-done.20, ...), custom_call_target="tpu_custom_call" | custom-call | flops 2000000000 | bytes 4194304 | tf_op jit(solution)/shard_map/past/pallas_call | solution.py:480
  254.7 6.5 %past_end.1 = bf16[1024,256]{1,0:T(8,128)(2,1)} custom-call(s32[4]{0:T(128)} %pad_add_fusion.1.info, bf16[512,256]{1,0:T(8,128)(2,1)} %get-tuple-element.54.q0_ref, bf16[512,256]{1,0:T(8,128)(2,1)} %get-tuple-element.55.q1_ref, bf16[512,512]{1,0:T(8,128)(2,1)} %copy-done.12, bf16[512,512]{1,0:T(8,128)(2,1)} %copy-done.21, ...), custom_call_target="tpu_custom_call" | custom-call | flops 2000000000 | bytes 4194304 | tf_op jit(solution)/shard_map/past_end/pallas_call | solution.py:484
  (101 shorter events, 38.3 us)
Async XLA Ops:
  6.5 7.6 %copy-start = (bf16[256,1920]{1,0:T(8,128)(2,1)S(1)}, bf16[256,1920]{1,0:T(8,128)(2,1)}, u32[]{:S(2)}) copy-start(bf16[256,1920]{1,0:T(8,128)(2,1)} %param.15) | copy-start | bytes 2949124
  9.7 22.8 %copy-start.19 = (s32[256]{0:T(256)S(1)}, s32[256]{0:T(256)}, u32[]{:S(2)}) copy-start(s32[256]{0:T(256)} %param.9) | copy-start | bytes 3076
  9.7 20.1 %collective-permute-start = (bf16[768,512]{1,0:T(8,128)(2,1)S(1)}, bf16[768,512]{1,0:T(8,128)(2,1)S(1)}, u32[]{:S(2)}, u32[]{:S(2)}) collective-permute-start(bf16[768,512]{1,0:T(8,128)(2,1)S(1)} %maximum_maximum_fusion), channel_id=1, source_target_pairs={{0,68},{1,69},{2,70},{3,71},{4,64},{5,65},{6,66},{7,67},{8,76},{9,... | collective-permute-start | bytes 2359304 | tf_op jit(solution)/shard_map/ppermute | solution.py:406
  29.7 12.8 %copy-start.6 = (bf16[768,512]{1,0:T(8,128)(2,1)}, bf16[768,512]{1,0:T(8,128)(2,1)S(1)}, u32[]{:S(2)}) copy-start(bf16[768,512]{1,0:T(8,128)(2,1)S(1)} %collective-permute-done.got_ref.got_hbm) | copy-start | bytes 2359300
  29.7 12.8 %collective-permute-start.4 = (bf16[768,512]{1,0:T(8,128)(2,1)S(1)}, bf16[768,512]{1,0:T(8,128)(2,1)S(1)}, u32[]{:S(2)}, u32[]{:S(2)}) collective-permute-start(bf16[768,512]{1,0:T(8,128)(2,1)S(1)} %collective-permute-done.got_ref.got_hbm), channel_id=1, source_target_pairs={{0,8},{8,0},{16,24},{24,16},{32,40},{40,32},{48,56},{56,48},{64,72... | collective-permute-start | bytes 2359304 | tf_op jit(solution)/shard_map/ppermute | solution.py:368
  32.2 20.3 %collective-permute-start.1 = (bf16[4,46,16,128]{3,2,1,0:T(8,128)(2,1)S(1)}, bf16[4,46,16,128]{3,2,1,0:T(8,128)(2,1)}, u32[]{:S(2)}, u32[]{:S(2)}) collective-permute-start(bf16[4,46,16,128]{3,2,1,0:T(8,128)(2,1)S(1)} %all_to_all.50), channel_id=1, source_target_pairs={{0,68},{1,69},{2,70},{3,71},{4,64},{5,65},{6,66},{7,67},{8,76},{9,... | collective-permute-start | bytes 2261000 | tf_op jit(solution)/shard_map/ppermute | solution.py:418
  32.5 6.3 %collective-permute-start.2 = (s32[40]{0:T(128)S(1)}, s32[40]{0:T(128)S(1)}, u32[]{:S(2)}, u32[]{:S(2)}) collective-permute-start(s32[40]{0:T(128)S(1)} %get-tuple-element.77), channel_id=1, source_target_pairs={{0,8},{8,16},{16,24},{24,32},{32,40},{40,48},{48,56},{56,64},{64,7... | collective-permute-start | bytes 488 | tf_op jit(solution)/shard_map/ppermute | solution.py:393
  36.3 5.3 %collective-permute-start.3 = (s32[40]{0:T(128)S(1)}, s32[40]{0:T(128)S(1)}, u32[]{:S(2)}, u32[]{:S(2)}) collective-permute-start(s32[40]{0:T(128)S(1)} %get-tuple-element.78), channel_id=1, source_target_pairs={{8,0},{16,8},{24,16},{32,24},{40,32},{48,40},{56,48},{64,56},{72,6... | collective-permute-start | bytes 488 | tf_op jit(solution)/shard_map/ppermute | solution.py:394
  42.5 9.1 %copy-start.16 = (bf16[128,512]{1,0:T(8,128)(2,1)S(1)}, bf16[128,512]{1,0:T(8,128)(2,1)}, u32[]{:S(2)}) copy-start(bf16[128,512]{1,0:T(8,128)(2,1)} %get-tuple-element.71) | copy-start | bytes 393220
  48.1 9.9 %all-to-all-start.1 = ((bf16[4,208,256]{2,1,0:T(8,128)(2,1)}), bf16[4,208,256]{2,1,0:T(8,128)(2,1)S(1)}, u32[]{:S(2)}, u32[]{:S(2)}) async-start(bf16[4,208,256]{2,1,0:T(8,128)(2,1)} %get-tuple-element.38), calls=%async_computation.1 | async-start | bytes 851968 | tf_op jit(solution)/shard_map/all_to_all | solution.py:372
  51.6 141.6 %all-gather.3.cloned.1.call-start = ((), (), s32[]{:S(2)}) async-start(), calls=%async_computation.10 | async-start | bytes 25624576 | tf_op jit(solution)/shard_map/all_gather | solution.py:433
  60.4 12.6 %collective-permute-start.5 = (bf16[512,512]{1,0:T(8,128)(2,1)}, bf16[512,512]{1,0:T(8,128)(2,1)S(1)}, u32[]{:S(2)}, u32[]{:S(2)}) collective-permute-start(bf16[512,512]{1,0:T(8,128)(2,1)} %pad_maximum_fusion.4), channel_id=1, source_target_pairs={{0,68},{1,69},{2,70},{3,71},{4,64},{5,65},{6,66},{7,67},{8,76},{9,... | collective-permute-start | bytes 1572872 | tf_op jit(solution)/shard_map/ppermute | solution.py:435
  63.1 10.0 %all-to-all-start.2 = ((bf16[4,208,256]{2,1,0:T(8,128)(2,1)}), bf16[4,208,256]{2,1,0:T(8,128)(2,1)S(1)}, u32[]{:S(2)}, u32[]{:S(2)}) async-start(bf16[4,208,256]{2,1,0:T(8,128)(2,1)} %broadcast_in_dim.47), calls=%async_computation.2 | async-start | bytes 851968 | tf_op jit(solution)/shard_map/all_to_all | solution.py:372
  73.1 4.4 %collective-permute-start.7 = (bf16[512,512]{1,0:T(8,128)(2,1)S(1)}, bf16[512,512]{1,0:T(8,128)(2,1)S(1)}, u32[]{:S(2)}, u32[]{:S(2)}) collective-permute-start(bf16[512,512]{1,0:T(8,128)(2,1)S(1)} %collective-permute-done.5.got1_hbm.got_hbm), channel_id=1, source_target_pairs={{0,8},{8,0},{16,24},{24,16},{32,40},{40,32},{48,56},{56,48},{64,72... | collective-permute-start | bytes 1572872 | tf_op jit(solution)/shard_map/ppermute | solution.py:368
  76.0 24.9 %collective-permute-start.6 = (bf16[2,512,512]{2,1,0:T(8,128)(2,1)S(1)}, bf16[2,512,512]{2,1,0:T(8,128)(2,1)S(1)}, u32[]{:S(2)}, u32[]{:S(2)}) collective-permute-start(bf16[2,512,512]{2,1,0:T(8,128)(2,1)S(1)} %fusion), channel_id=1, source_target_pairs={{0,68},{1,69},{2,70},{3,71},{4,64},{5,65},{6,66},{7,67},{8,76},{9,... | collective-permute-start | bytes 3145736 | tf_op jit(solution)/shard_map/ppermute | solution.py:444
  94.9 10.3 %all-to-all-start.4 = ((bf16[4,208,256]{2,1,0:T(8,128)(2,1)}), bf16[4,208,256]{2,1,0:T(8,128)(2,1)S(1)}, u32[]{:S(2)}, u32[]{:S(2)}) async-start(bf16[4,208,256]{2,1,0:T(8,128)(2,1)} %broadcast_in_dim.49), calls=%async_computation.4 | async-start | bytes 851968 | tf_op jit(solution)/shard_map/all_to_all | solution.py:372
  100.9 9.1 %copy-start.3 = (bf16[2,512,512]{2,1,0:T(8,128)(2,1)}, bf16[2,512,512]{2,1,0:T(8,128)(2,1)S(1)}, u32[]{:S(2)}) copy-start(bf16[2,512,512]{2,1,0:T(8,128)(2,1)S(1)} %collective-permute-done.6.got1_hbm.got_hbm) | copy-start | bytes 3145732
  105.2 4.8 %copy-start.11 = (bf16[4,208,256]{2,1,0:T(8,128)(2,1)}, bf16[4,208,256]{2,1,0:T(8,128)(2,1)S(1)}, u32[]{:S(2)}) copy-start(bf16[4,208,256]{2,1,0:T(8,128)(2,1)S(1)} %all-to-all-done.4.r_ref) | copy-start | bytes 1277956
  105.2 4.8 %collective-permute-start.8 = (bf16[2,512,512]{2,1,0:T(8,128)(2,1)S(1)}, bf16[2,512,512]{2,1,0:T(8,128)(2,1)S(1)}, u32[]{:S(2)}, u32[]{:S(2)}) collective-permute-start(bf16[2,512,512]{2,1,0:T(8,128)(2,1)S(1)} %collective-permute-done.6.got1_hbm.got_hbm), channel_id=1, source_target_pairs={{0,8},{8,0},{16,24},{24,16},{32,40},{40,32},{48,56},{56,48},{64,72... | collective-permute-start | bytes 3145736 | tf_op jit(solution)/shard_map/ppermute | solution.py:368
  158.4 9.6 %copy-start.17 = (f32[1920]{0:T(1024)S(1)}, f32[1920]{0:T(1024)}, u32[]{:S(2)}) copy-start(f32[1920]{0:T(1024)} %param.16) | copy-start | bytes 23044
  158.4 10.2 %copy-start.18 = (s32[1024]{0:T(1024)S(1)}, s32[1024]{0:T(1024)}, u32[]{:S(2)}) copy-start(s32[1024]{0:T(1024)} %param.10) | copy-start | bytes 12292
  161.7 20.0 %all-to-all-start.9 = ((bf16[8,128,256]{2,1,0:T(8,128)(2,1)}), bf16[8,128,256]{2,1,0:T(8,128)(2,1)S(1)}, u32[]{:S(2)}, u32[]{:S(2)}) async-start(bf16[8,128,256]{2,1,0:T(8,128)(2,1)} %cond_end.1), calls=%async_computation.9 | async-start | bytes 1048576 | tf_op jit(solution)/shard_map/all_to_all | solution.py:372
  181.7 11.4 %copy-start.5 = (bf16[8,128,256]{2,1,0:T(8,128)(2,1)}, bf16[8,128,256]{2,1,0:T(8,128)(2,1)S(1)}, u32[]{:S(2)}) copy-start(bf16[8,128,256]{2,1,0:T(8,128)(2,1)S(1)} %all-to-all-done.9.hf_ref) | copy-start | bytes 1572868
  208.9 26.2 %collective-permute-start.11 = (bf16[512,512]{1,0:T(8,128)(2,1)}, bf16[512,512]{1,0:T(8,128)(2,1)S(1)}, u32[]{:S(2)}, u32[]{:S(2)}) collective-permute-start(bf16[512,512]{1,0:T(8,128)(2,1)} %get-tuple-element.57.kv0_ref), channel_id=1, source_target_pairs={{0,16},{8,24},{16,32},{24,40},{32,48},{40,56},{48,64},{56,72},{64,... | collective-permute-start | bytes 1572872 | tf_op jit(solution)/shard_map/ppermute | solution.py:470
  226.9 8.2 %copy-start.15 = (bf16[512,512]{1,0:T(8,128)(2,1)S(1)}, bf16[512,512]{1,0:T(8,128)(2,1)}, u32[]{:S(2)}) copy-start(bf16[512,512]{1,0:T(8,128)(2,1)} %get-tuple-element.57.kv0_ref) | copy-start | bytes 1572868
  226.9 18.2 %collective-permute-start.9 = (bf16[512,512]{1,0:T(8,128)(2,1)}, bf16[512,512]{1,0:T(8,128)(2,1)S(1)}, u32[]{:S(2)}, u32[]{:S(2)}) collective-permute-start(bf16[512,512]{1,0:T(8,128)(2,1)} %get-tuple-element.56.kv1_ref), channel_id=1, source_target_pairs={{0,16},{8,24},{16,32},{24,40},{32,48},{40,56},{48,64},{56,72},{64,... | collective-permute-start | bytes 1572872 | tf_op jit(solution)/shard_map/ppermute | solution.py:470
  228.9 16.1 %copy-start.14 = (bf16[512,512]{1,0:T(8,128)(2,1)S(1)}, bf16[512,512]{1,0:T(8,128)(2,1)}, u32[]{:S(2)}) copy-start(bf16[512,512]{1,0:T(8,128)(2,1)} %get-tuple-element.56.kv1_ref) | copy-start | bytes 1572868
  235.1 10.8 %copy-start.13 = (bf16[512,512]{1,0:T(8,128)(2,1)}, bf16[512,512]{1,0:T(8,128)(2,1)S(1)}, u32[]{:S(2)}) copy-start(bf16[512,512]{1,0:T(8,128)(2,1)S(1)} %collective-permute-done.11.far_ref) | copy-start | bytes 1572868
  235.2 10.8 %collective-permute-start.12 = (bf16[512,512]{1,0:T(8,128)(2,1)S(1)}, bf16[512,512]{1,0:T(8,128)(2,1)S(1)}, u32[]{:S(2)}, u32[]{:S(2)}) collective-permute-start(bf16[512,512]{1,0:T(8,128)(2,1)S(1)} %broadcast_select_fusion), channel_id=1, source_target_pairs={{0,8},{8,0},{16,24},{24,16},{32,40},{40,32},{48,56},{56,48},{64,72... | collective-permute-start | bytes 1572872 | tf_op jit(solution)/shard_map/ppermute | solution.py:368
  245.0 8.9 %copy-start.12 = (bf16[512,512]{1,0:T(8,128)(2,1)}, bf16[512,512]{1,0:T(8,128)(2,1)S(1)}, u32[]{:S(2)}) copy-start(bf16[512,512]{1,0:T(8,128)(2,1)S(1)} %collective-permute-done.9.far_ref) | copy-start | bytes 1572868
  245.1 8.9 %collective-permute-start.10 = (bf16[512,512]{1,0:T(8,128)(2,1)S(1)}, bf16[512,512]{1,0:T(8,128)(2,1)S(1)}, u32[]{:S(2)}, u32[]{:S(2)}) collective-permute-start(bf16[512,512]{1,0:T(8,128)(2,1)S(1)} %broadcast_select_fusion.1), channel_id=1, source_target_pairs={{0,8},{8,0},{16,24},{24,16},{32,40},{40,32},{48,56},{56,48},{64,72... | collective-permute-start | bytes 1572872 | tf_op jit(solution)/shard_map/ppermute | solution.py:368
  254.0 7.2 %copy-start.1 = (bf16[256,1920]{1,0:T(8,128)(2,1)S(1)}, bf16[256,1920]{1,0:T(8,128)(2,1)}, u32[]{:S(2)}) copy-start(bf16[256,1920]{1,0:T(8,128)(2,1)} %param.15) | copy-start | bytes 2949124
  (8 other events, 15.5 us)
Sparse Core Ops, SparseCore 0:
  60.6 132.5 all-gather.2

commit v2 on v1

--- a/solution.py
+++ b/solution.py
@@ -17,6 +17,10 @@
 HALO = (40, 39, 36, 27, 0)
 ROWS = (208, 208, 208, 192, 128)
 VMEM_LIMIT = 60 << 20
+
+BLOCKS = D // 128
+UP_BLOCKS = 2 * BLOCKS
+PART = UP_BLOCKS + 16
 
 Y_GROUPS = [[0, 1, 2, 3], [4, 5, 6, 7]]
 
@@ -153,6 +157,57 @@
         out_ref[peer] = h
 
 
+def pack_kernel(info, dil_hbm, mix_hbm, tab_hbm, up_hbm, mid_hbm, pack0, pack1, pack2, part_ref, up, mid, wide, sems):
+    cols = pl.ds(pl.multiple_of(info[0] * 512, 512), 512)
+    pairs = [
+        (up_hbm.at[pl.ds(info[4] * 16, 16), pl.ds(pl.multiple_of(info[0] * 2 * D, 128), 2 * D)], up),
+        (mid_hbm.at[pl.ds(info[5] * 16, 16), :], mid),
+    ]
+    for level in range(4):
+        dest = (pack0, pack1, pack2.at[0], pack2.at[1])[level]
+        for tap in range(3):
+            pairs.append((dil_hbm.at[level, tap, :, cols], dest.at[pl.ds(tap * 128, 128), :]))
+        for i in range(4):
+            rows = pl.ds(pl.multiple_of(info[0] * 512 + i * 128, 128), 128)
+            pairs.append((mix_hbm.at[level, rows, :], dest.at[pl.ds(384, 128), pl.ds(i * 128, 128)]))
+    for i in range(4):
+        rows = pl.ds(pl.multiple_of(info[0] * 1024 + i * 256, 256), 256)
+        pairs.append((tab_hbm.at[rows, :], pack0.at[pl.ds(512, 256), pl.ds(i * 128, 128)]))
+    copies = [pltpu.make_async_copy(a, b, sems.at[i]) for i, (a, b) in enumerate(pairs)]
+    start(copies)
+    finish(copies[:2])
+    wide[...] = jnp.zeros_like(wide)
+    for block in range(BLOCKS):
+        wide[:, block, :] = mid[:, block * 128 : block * 128 + 128].astype(F32)
+    for y in range(4):
+        for block in range(UP_BLOCKS):
+            part_ref[y, block] = up[:, block * 128 : block * 128 + 128]
+        part_ref[y, UP_BLOCKS:] = wide[...].astype(BF)
+    finish(copies[2:])
+
+
+def join_kernel(mine, others, out, sems):
+    copies = [
+        pltpu.make_async_copy(ref, out.at[pl.ds(i * 4, 4)], sems.at[i]) for i, ref in enumerate((mine, others))
+    ]
+    start(copies)
+    finish(copies)
+
+
+def join(mine, others):
+    space = pl.BlockSpec(memory_space=pl.ANY)
+    return pl.pallas_call(
+        join_kernel,
+        out_shape=shape(8, PART, 16, 128),
+        in_specs=[space, space],
+        out_specs=space,
+        scratch_shapes=[pltpu.SemaphoreType.DMA((2,))],
+        compiler_params=params(),
+        cost_estimate=cost(0, 3 << 20),
+        name="join",
+    )(mine, others)
+
+
 def call(body, outs, scratch=(), smem=1, n=0, hbm=0, after=0, flops=10**9, name=None):
     def spec(space):
         return pl.BlockSpec(memory_space=space)
@@ -175,13 +230,10 @@
     return jax.ShapeDtypeStruct(dims, dtype)
 
 
-BLOCKS = D // 128
-UP_BLOCKS = 2 * BLOCKS
-PART = UP_BLOCKS + 16
 CHUNKS = ((0, 4), (4, 4), (8, 4), (12, 3))
 
 
-def frames_kernel(pair, info, codes_ref, hf_ref, gain_ref, qkv_ref, full_ref, q_ref, kv_ref, weights, table, hf, rows, x, xn, sems, table_sems):
+def frames_kernel(pair, info, codes_ref, hf_ref, gain_ref, qkv_hbm, full_ref, q_ref, kv_ref, weights, table, qkv, hf, rows, x, xn, sems, table_sems, qkv_sem):
     def weight_copies(phase):
         return [
             pltpu.make_async_copy(
@@ -193,15 +245,49 @@
             for t in range(8)
         ]
 
+    def product(phase):
+        for first, size in CHUNKS:
+            w = [weights[phase, :, :, block].reshape(C, 128) for block in range(first, first + size)]
+            x[phase, :, first * 128 : (first + size) * 128] = dot(hf[...], jnp.concatenate(w, axis=1))
+
+    def norm(phase):
+        total = jnp.zeros((256, 128), F32)
+        for block in range(BLOCKS):
+            cols = slice(block * 128, block * 128 + 128)
+            y = x[phase, :, cols] + rows[pl.ds(phase * 256, 256), block, :]
+            x[phase, :, cols] = y
+            total += y
+        mean = jnp.sum(total, axis=1, keepdims=True) * (1.0 / D)
+        square = jnp.zeros((256, 128), F32)
+        for block in range(BLOCKS):
+            y = x[phase, :, block * 128 : block * 128 + 128] - mean
+            square += y * y
+        factor = lax.rsqrt(jnp.sum(square, axis=1, keepdims=True) * (1.0 / D) + 1e-5)
+        for block in range(BLOCKS):
+            cols = slice(block * 128, block * 128 + 128)
+            xn[phase, :, cols] = ((x[phase, :, cols] - mean) * factor * gain_ref[:, cols]).astype(BF)
+
+    def project(phase):
+        y = dot(xn[phase], qkv[...]).astype(BF)
+        lines = slice(phase * 256, phase * 256 + 256)
+        for head in range(2):
+            at = head * 384
+            cols = slice(head * 128, head * 128 + 128)
+            q_ref[lines, cols] = y[:, at : at + 128]
+            kv_ref[lines, cols] = y[:, at + 128 : at + 256]
+            kv_ref[lines, 256 + head * 128 : 384 + head * 128] = y[:, at + 256 : at + 384]
+
     table_copies = [
         pltpu.make_async_copy(
             full_ref.at[:, part, :, pl.ds(UP_BLOCKS, 16)], table.at[:, part], table_sems.at[part]
         )
         for part in range(2)
     ]
+    qkv_copy = pltpu.make_async_copy(qkv_hbm, qkv, qkv_sem)
+    start(table_copies)
     start(weight_copies(0))
-    start(table_copies)
     start(weight_copies(1))
+    qkv_copy.start()
     for half in range(2):
         for j in range(8):
             at = 0 if j // 4 == half else 128
@@ -209,44 +295,24 @@
                 half * 4 + j % 4, :, at : at + 128
             ]
     flat = table.reshape(VOCAB, 16, 128)
-    for phase in range(2):
-        finish(weight_copies(phase))
-        for first, size in CHUNKS:
-            w = [weights[phase, :, :, block].reshape(C, 128) for block in range(first, first + size)]
-            x[:, first * 128 : (first + size) * 128] = dot(hf[...], jnp.concatenate(w, axis=1))
-        if phase == 0:
-            finish(table_copies)
-
-        def look_up(i, carry):
-            for j in range(8):
-                row = i * 8 + j
-                rows[row] = flat[codes_ref[(pair * 2 + phase) * 256 + row]].astype(F32)
-            return carry
-
-        lax.fori_loop(0, 32, look_up, 0)
-        total = jnp.zeros((256, 128), F32)
-        for block in range(BLOCKS):
-            cols = slice(block * 128, block * 128 + 128)
-            y = x[:, cols] + rows[:, block, :]
-            x[:, cols] = y
-            total += y
-        mean = jnp.sum(total, axis=1, keepdims=True) * (1.0 / D)
-        square = jnp.zeros((256, 128), F32)
-        for block in range(BLOCKS):
-            y = x[:, block * 128 : block * 128 + 128] - mean
-            square += y * y
-        factor = lax.rsqrt(jnp.sum(square, axis=1, keepdims=True) * (1.0 / D) + 1e-5)
-        for block in range(BLOCKS):
-            cols = slice(block * 128, block * 128 + 128)
-            xn[:, cols] = ((x[:, cols] - mean) * factor * gain_ref[:, cols]).astype(BF)
-        y = dot(xn[...], qkv_ref[...]).astype(BF)
-        lines = slice(phase * 256, phase * 256 + 256)
-        for head in range(2):
-            at = head * 384
-            cols = slice(head * 128, head * 128 + 128)
-            q_ref[lines, cols] = y[:, at : at + 128]
-            kv_ref[lines, cols] = y[:, at + 128 : at + 256]
-            kv_ref[lines, 256 + head * 128 : 384 + head * 128] = y[:, at + 256 : at + 384]
+    finish(table_copies)
+
+    def look_up(i, carry):
+        for j in range(8):
+            row = i * 8 + j
+            rows[row] = flat[codes_ref[pair * 512 + row]].astype(F32)
+        return carry
+
+    lax.fori_loop(0, 64, look_up, 0)
+    finish(weight_copies(0))
+    product(0)
+    finish(weight_copies(1))
+    qkv_copy.wait()
+    norm(0)
+    product(1)
+    project(0)
+    norm(1)
+    project(1)
 
 
 def frames(pair, info, codes, hf, gain, qkv, full):
@@ -255,17 +321,19 @@
     return pl.pallas_call(
         functools.partial(frames_kernel, pair),
         out_shape=(shape(512, 256), shape(512, 512)),
-        in_specs=[sm, sm, vm, vm, vm, pl.BlockSpec(memory_space=pltpu.HBM)],
+        in_specs=[sm, sm, vm, vm, pl.BlockSpec(memory_space=pl.ANY), pl.BlockSpec(memory_space=pltpu.HBM)],
         out_specs=(vm, vm),
         scratch_shapes=[
             pltpu.VMEM((2, 8, 8, BLOCKS, 16, 128), BF),
             pltpu.VMEM((8, 2, 8, 16, 16, 128), BF),
+            pltpu.VMEM((D, 768), BF),
             pltpu.VMEM((256, C), BF),
-            pltpu.VMEM((256, 16, 128), F32),
-            pltpu.VMEM((256, D), F32),
-            pltpu.VMEM((256, D), BF),
+            pltpu.VMEM((512, 16, 128), F32),
+            pltpu.VMEM((2, 256, D), F32),
+            pltpu.VMEM((2, 256, D), BF),
             pltpu.SemaphoreType.DMA((2, 2, 8)),
             pltpu.SemaphoreType.DMA((2,)),
+            pltpu.SemaphoreType.DMA,
         ],
         compiler_params=params(),
         cost_estimate=cost(4 * 10**9, 20 << 20),
@@ -364,6 +432,12 @@
     return pairs
 
 
+def song_neighbours():
+    first = [(song * 8 + rank, song * 8 + 8 + rank) for song in range(15) for rank in range(4)]
+    second = [(song * 8 + 8 + rank, song * 8 + rank) for song in range(15) for rank in range(4, 8)]
+    return first + second
+
+
 def to_sibling(value):
     return lax.ppermute(value, "song", [(i, i ^ 1) for i in range(16)])
 
@@ -388,34 +462,34 @@
     core = song % 2
     x_hi = rank // 4
     begin = song * 256 + x_hi * HALF
-    info = jnp.stack([core, begin, song, x_hi * 4]).astype(jnp.int32)
-
-    after = lax.ppermute(upper_codes[-40:], "song", [(i, i + 1) for i in range(15)])
-    before = lax.ppermute(upper_codes[:40], "song", [(i + 1, i) for i in range(15)])
-    codes = jnp.concatenate([after, upper_codes, before])
-    codes = lax.dynamic_slice_in_dim(codes, x_hi * HALF, HALF + 80)[:, None]
-
-    dil_half = lax.dynamic_slice_in_dim(dilated_weight, core * 512, 512, 3)
-    mix_half = lax.dynamic_slice_in_dim(mixing_weight, core * 512, 512, 1)
-    mix_pack = jnp.concatenate([mix_half[:, i * 128 : i * 128 + 128] for i in range(4)], axis=2)
-    tab_half = lax.dynamic_slice_in_dim(upper_table, core * 1024, 1024, 0)
-    tab_pack = jnp.concatenate([tab_half[i * 256 : i * 256 + 256] for i in range(4)], axis=1)
-    pack0 = jnp.concatenate([dil_half[0].reshape(384, 512), mix_pack[0], tab_pack], axis=0)
-    pack1 = jnp.concatenate([dil_half[1].reshape(384, 512), mix_pack[1]], axis=0)
-    pack2 = jnp.concatenate([dil_half[2:].reshape(2, 384, 512), mix_pack[2:]], axis=1)
+    share = song ^ (8 * x_hi)
+    info = jnp.stack([core, begin, song, x_hi * 4, share // 2, share]).astype(jnp.int32)
+
+    pack0, pack1, pack2, part = call(
+        pack_kernel,
+        (shape(768, 512), shape(512, 512), shape(2, 512, 512), shape(4, PART, 16, 128)),
+        [
+            pltpu.VMEM((16, 2 * D), BF),
+            pltpu.VMEM((16, D), BF),
+            pltpu.VMEM((16, 16, 128), F32),
+            pltpu.SemaphoreType.DMA((34,)),
+        ],
+        hbm=5,
+        name="pack",
+    )(info, dilated_weight, mixing_weight, upper_table, upsample_weight, middle_table)
     got0 = lax.ppermute(pack0, EVERY, other_half())
-
-    share = song ^ (8 * x_hi)
-    up_part = lax.dynamic_slice(upsample_weight, (share // 2 * 16, core * 2 * D), (16, 2 * D))
-    mid_part = lax.dynamic_slice_in_dim(middle_table, share * 16, 16, 0)
-    up_part = up_part.reshape(16, UP_BLOCKS, 128).transpose(1, 0, 2)
-    mid_part = jnp.pad(mid_part.reshape(16, BLOCKS, 128), ((0, 0), (0, 1), (0, 0)))
-    part = jnp.concatenate([up_part, mid_part])
-    part, pack0 = lax.optimization_barrier((part, pack0))
-    mine = exchange(jnp.broadcast_to(part[None], (4, PART, 16, 128)), groups=Y_GROUPS)
+    mine = exchange(part, groups=Y_GROUPS)
     mine, got0 = lax.optimization_barrier((mine, got0))
     sib0 = to_sibling(got0)
     others = lax.ppermute(mine, EVERY, other_half())
+
+    edge = jnp.where(x_hi == 0, upper_codes[-40:], upper_codes[:40])
+    edge = lax.ppermute(edge, EVERY, song_neighbours())
+    codes = jnp.where(
+        x_hi == 0,
+        jnp.concatenate([edge, upper_codes[: HALF + 40]]),
+        jnp.concatenate([upper_codes[HALF - 40 :], edge]),
+    )[:, None]
 
     h, terms = call(
         first_kernel,
@@ -426,13 +500,12 @@
         after=2,
         name="cond0",
     )(info, codes, upper_table, dilated_weight, got0, sib0)
+    others, pack1, terms = lax.optimization_barrier((others, pack1, terms))
+    full = lax.all_gather(join(mine, others), "song", axis=0, tiled=False)
+    full = full.reshape(8, 2, 8, PART, 16, 128)
+    got1 = lax.ppermute(pack1, EVERY, other_half())
     for level in range(4):
         terms = exchange(terms, groups=Y_GROUPS)
-        if level == 0:
-            others, pack1, terms = lax.optimization_barrier((others, pack1, terms))
-            full = lax.all_gather(jnp.concatenate([mine, others]), "song", axis=0, tiled=False)
-            full = full.reshape(8, 2, 8, PART, 16, 128)
-            got1 = lax.ppermute(pack1, EVERY, other_half())
         total = terms[0].astype(F32)
         for y in range(1, 4):
             total = total + terms[y].astype(F32)
@@ -476,10 +549,10 @@
     state = (shape(1024, 512, dtype=F32), shape(1024, 2, dtype=F32))
     kept = call(own_kernel, state, smem=0, n=4, flops=10**9, name="own")(q0, q1, kv0, kv1)
     near0 = to_sibling(jnp.where(core == 0, kv0, far0))
-    far1, kept = lax.optimization_barrier((far1, kept))
     kept = call(functools.partial(past_kernel, False), state, n=6, flops=2 * 10**9, name="past")(
         info, q0, q1, far0, near0, *kept
     )
+    far1, kept = lax.optimization_barrier((far1, kept))
     near1 = to_sibling(jnp.where(core == 0, kv1, far1))
     return call(
         functools.partial(past_kernel, True),

time: 270 us -> 318 us (1.18)
  Pallas kernels: 71.8 us -> 120 us
  waiting for transfers between devices: 51.6 us -> 71.5 us
  blocking collectives: 64.9 us -> 50.1 us
  starting transfers between devices: 40.5 us -> 47.5 us
  local copies, waits for them, and re-layouts: 18.7 us -> 12.5 us
  other arithmetic: 6.73 us -> 1.77 us
    pallas_call x0 -> x2, Pallas kernels: none -> 51.2 us  [the longest x1 46.8 us: join(): pl.pallas_call(join_kernel, out_shape=shape(8, PART, 16, 128), in_specs=[...]
    all_to_all x6 -> x5, blocking collectives: 64.9 us -> 50.1 us  [exchange(): lax.all_to_all(value, axis, 0, 0, axis_index_groups=groups, tiled=True)]
    all_to_all x4 -> x5, waiting for transfers between devices: 23.2 us -> 34.5 us  [exchange(): lax.all_to_all(value, axis, 0, 0, axis_index_groups=groups, tiled=True)]
    all_gather x1, waiting for transfers between devices: 11.4 us -> 4.46 us  [on_device(): full = lax.all_gather(join(mine, others), 'song', axis=0, tiled=False)]
    ppermute x1, waiting for transfers between devices: 0.01 us -> 6.13 us  [on_device(): others = lax.ppermute(mine, EVERY, other_half())]
    ppermute x2, waiting for transfers between devices: 9.52 us -> 15.5 us  [from_two_back(): return lax.ppermute(value, 'song', [(i, i + 2) for i in range(14)])]
    all_to_all x4 -> x5, starting transfers between devices: 16.7 us -> 22.2 us  [exchange(): lax.all_to_all(value, axis, 0, 0, axis_index_groups=groups, tiled=True)]
    concatenate x6 -> x1, other arithmetic: 4.47 us -> 0.07 us  [on_device(): jnp.concatenate([upper_codes[HALF - 40:], edge])]
  transfers between devices with their start and end apart: 18 -> 18, of which waited for: 9 -> 16; matrix products, arithmetic and copies ran while one was open for 6% -> 3% of each run, Pallas kernels for 18% -> 15%
where the time goes in v2:
time: 318 us; the launch traced here: 317 us
  Pallas kernels  120 us (38%)
  waiting for transfers between devices  71.5 us (22%)
  blocking collectives  50.1 us (16%)
  starting transfers between devices  47.5 us (15%)
  between operations  13.6 us (4%)
  local copies, waits for them, and re-layouts  12.5 us (4%)
    all_to_all x5, blocking collectives, exchange(): lax.all_to_all(value, axis, 0, 0, axis_index_groups=groups, tiled=True)  50.1 us
    pallas_call x1, Pallas kernels, join(): pl.pallas_call(join_kernel, out_shape=shape(8, PART, 16, 128), in_specs=[...  46.8 us
    all_to_all x5, waiting for transfers between devices, exchange(): lax.all_to_all(value, axis, 0, 0, axis_index_groups=groups, tiled=True)  34.5 us
    pallas_call x2, Pallas kernels, frames(): pl.pallas_call(functools.partial(frames_kernel, pair), out_shape=(shape(5...  28.2 us
    all_to_all x5, starting transfers between devices, exchange(): lax.all_to_all(value, axis, 0, 0, axis_index_groups=groups, tiled=True)  22.2 us
    ppermute x2, waiting for transfers between devices, from_two_back(): return lax.ppermute(value, 'song', [(i, i + 2) for i in range(14)])  15.5 us
    ppermute x5, starting transfers between devices, to_sibling(): return lax.ppermute(value, 'song', [(i, i ^ 1) for i in range(16)])  12.8 us
    pallas_call x3, Pallas kernels, on_device(): call(functools.partial(middle_kernel, level), (shape(ROWS[level + 1], 256...  12.3 us
  transfers between devices with their start and end apart: 18, of which 16 were waited for; matrix products, arithmetic and copies ran while one was open for 3% of the time, Pallas kernels for 15%

profile of v2, /device:TPU:3, one launch (start us, length us, event | category | flops | bytes accessed | tf_op | source)
XLA Modules:
  0.0 316.6 jit_solution(15364932182913206296)
XLA Ops:
  7.2 4.5 %pack.1 = (bf16[768,512]{1,0:T(8,128)(2,1)}, bf16[512,512]{1,0:T(8,128)(2,1)}, bf16[2,512,512]{2,1,0:T(8,128)(2,1)}, bf16[4,46,16,128]{3,2,1,0:T(8,128)(2,1)}) custom-call(s32[6]{0:T(128)} %stack.27.info, bf16[4,3,128,1024]{3,2,1,0:T(8,128)(2,1)} %dil_hbm.9, bf16[4,1024,128]{2,1,0:T(8,128)(2,1)} %mix_hbm.9, bf16[2048,128]{1,0:T(8,128)(2,1)} %table_ref.1, ...), custom_call_target="tpu_custom_call" | custom-call | flops 1000000000 | bytes 4194304 | tf_op jit(solution)/shard_map/pack/pallas_call | solution.py:468
  13.0 4.2 %all-to-all-start = ((bf16[4,46,16,128]{3,2,1,0:T(8,128)(2,1)}), bf16[4,46,16,128]{3,2,1,0:T(8,128)(2,1)S(1)}, u32[]{:S(2)}, u32[]{:S(2)}) async-start(bf16[4,46,16,128]{3,2,1,0:T(8,128)(2,1)} %get-tuple-element.38), calls=%async_computation | async-start | bytes 1507328 | tf_op jit(solution)/shard_map/all_to_all | solution.py:446
  17.2 10.7 %all-to-all-done.mine = bf16[4,46,16,128]{3,2,1,0:T(8,128)(2,1)S(1)} async-done(((bf16[4,46,16,128]{3,2,1,0:T(8,128)(2,1)}), bf16[4,46,16,128]{3,2,1,0:T(8,128)(2,1)S(1)}, u32[]{:S(2)}, u32[]{:S(2)}) %all-to-all-start) | async-done | bytes 753696 | tf_op jit(solution)/shard_map/all_to_all | solution.py:446
  33.2 3.7 %collective-permute-start.2 = (s32[40]{0:T(128)S(1)}, s32[40]{0:T(128)S(1)}, u32[]{:S(2)}, u32[]{:S(2)}) collective-permute-start(s32[40]{0:T(128)S(1)} %broadcast_select_fusion.3), channel_id=1, source_target_pairs={{0,8},{1,9},{2,10},{3,11},{8,16},{9,17},{10,18},{11,19},{16,24},{1... | collective-permute-start | bytes 488 | tf_op jit(solution)/shard_map/ppermute | solution.py:487
  39.5 4.7 %cond0.1 = (f32[208,256]{1,0:T(8,128)}, bf16[4,208,256]{2,1,0:T(8,128)(2,1)}) custom-call(s32[6]{0:T(128)} %stack.27.info, s32[208,1]{1,0:T(8,128)} %broadcast_select_fusion.2.codes_ref, bf16[2048,128]{1,0:T(8,128)(2,1)} %table_ref.1, bf16[4,3,128,1024]{3,2,1,0:T(8,128)(2,1)} %dil_hbm.9, bf16[768,512]{1,0:T(8,128)(2,1)} %copy-done.3, bf16[768,512]{1,0:T(8,128)(2,1)} %copy-done.4), custom_call_target="tpu_custom_call" | custom-call | flops 1000000000 | bytes 4194304 | tf_op jit(solution)/shard_map/cond0/pallas_call | solution.py:494
  44.3 6.1 %collective-permute-done.1.others = bf16[4,46,16,128]{3,2,1,0:T(8,128)(2,1)S(1)} collective-permute-done((bf16[4,46,16,128]{3,2,1,0:T(8,128)(2,1)S(1)}, bf16[4,46,16,128]{3,2,1,0:T(8,128)(2,1)S(1)}, u32[]{:S(2)}, u32[]{:S(2)}) %collective-permute-start.1) | collective-permute-done | bytes 753696 | tf_op jit(solution)/shard_map/ppermute | solution.py:484
  51.3 46.8 %join.1 = bf16[8,46,16,128]{3,2,1,0:T(8,128)(2,1)} custom-call(bf16[4,46,16,128]{3,2,1,0:T(8,128)(2,1)} %copy-done.5, bf16[4,46,16,128]{3,2,1,0:T(8,128)(2,1)} %copy-done.11), custom_call_target="tpu_custom_call" | custom-call | bytes 3145728 | tf_op jit(solution)/shard_map/join/pallas_call | solution.py:199
  98.1 4.2 %all-to-all-start.1 = ((bf16[4,208,256]{2,1,0:T(8,128)(2,1)}), bf16[4,208,256]{2,1,0:T(8,128)(2,1)S(1)}, u32[]{:S(2)}, u32[]{:S(2)}) async-start(bf16[4,208,256]{2,1,0:T(8,128)(2,1)} %get-tuple-element.46), calls=%async_computation.1 | async-start | bytes 851968 | tf_op jit(solution)/shard_map/all_to_all | solution.py:446
  103.5 5.9 %all-to-all-done.1 = bf16[4,208,256]{2,1,0:T(8,128)(2,1)S(1)} async-done(((bf16[4,208,256]{2,1,0:T(8,128)(2,1)}), bf16[4,208,256]{2,1,0:T(8,128)(2,1)S(1)}, u32[]{:S(2)}, u32[]{:S(2)}) %all-to-all-start.1) | async-done | bytes 426016 | tf_op jit(solution)/shard_map/all_to_all | solution.py:446
  110.3 3.5 %all-to-all-start.2 = ((bf16[4,208,256]{2,1,0:T(8,128)(2,1)}), bf16[4,208,256]{2,1,0:T(8,128)(2,1)S(1)}, u32[]{:S(2)}, u32[]{:S(2)}) async-start(bf16[4,208,256]{2,1,0:T(8,128)(2,1)} %broadcast_in_dim.37), calls=%async_computation.2 | async-start | bytes 851968 | tf_op jit(solution)/shard_map/all_to_all | solution.py:446
  115.0 5.2 %all-to-all-done.2.r_ref = bf16[4,208,256]{2,1,0:T(8,128)(2,1)S(1)} async-done(((bf16[4,208,256]{2,1,0:T(8,128)(2,1)}), bf16[4,208,256]{2,1,0:T(8,128)(2,1)S(1)}, u32[]{:S(2)}, u32[]{:S(2)}) %all-to-all-start.2) | async-done | bytes 426016 | tf_op jit(solution)/shard_map/all_to_all | solution.py:446
  120.2 3.4 %collective-permute-start.6 = (bf16[512,512]{1,0:T(8,128)(2,1)S(1)}, bf16[512,512]{1,0:T(8,128)(2,1)S(1)}, u32[]{:S(2)}, u32[]{:S(2)}) collective-permute-start(bf16[512,512]{1,0:T(8,128)(2,1)S(1)} %collective-permute-done.4.got1_hbm.got_hbm), channel_id=1, source_target_pairs={{0,8},{8,0},{16,24},{24,16},{32,40},{40,32},{48,56},{56,48},{64,72... | collective-permute-start | bytes 1572872 | tf_op jit(solution)/shard_map/ppermute | solution.py:442
  125.9 4.2 %cond.3 = (f32[208,256]{1,0:T(8,128)}, bf16[4,208,256]{2,1,0:T(8,128)(2,1)}) custom-call(s32[6]{0:T(128)} %stack.27.info, bf16[4,208,256]{2,1,0:T(8,128)(2,1)} %copy-done.9, f32[208,256]{1,0:T(8,128)} %get-tuple-element.49.h_ref, bf16[4,1024,128]{2,1,0:T(8,128)(2,1)} %mix_hbm.9, bf16[768,512]{1,0:T(8,128)(2,1)} %copy-done.3, bf16[768,512]{1,0:T(8,128)(2,1)} %copy-done.4, ...), custom_call_target="tpu_custom_call" | custom-call | flops 1000000000 | bytes 4194304 | tf_op jit(solution)/shard_map/cond/pallas_call | solution.py:523
  130.1 11.5 %all_to_all.50 = bf16[4,208,256]{2,1,0:T(8,128)(2,1)S(1)} all-to-all(bf16[4,208,256]{2,1,0:T(8,128)(2,1)} %get-tuple-element.51), channel_id=1, replica_groups={{0,1,2,3},{4,5,6,7},{8,9,10,11},{12,13,14,15},{16,17,18,19},{20,21,22,2..., dimensions={0} | all-to-all | bytes 851968 | tf_op jit(solution)/shard_map/all_to_all | solution.py:446
  142.4 3.5 %all-to-all-start.4 = ((bf16[4,208,256]{2,1,0:T(8,128)(2,1)}), bf16[4,208,256]{2,1,0:T(8,128)(2,1)S(1)}, u32[]{:S(2)}, u32[]{:S(2)}) async-start(bf16[4,208,256]{2,1,0:T(8,128)(2,1)} %broadcast_in_dim.39), calls=%async_computation.4 | async-start | bytes 851968 | tf_op jit(solution)/shard_map/all_to_all | solution.py:446
  148.4 4.3 %all-to-all-done.4.r_ref = bf16[4,208,256]{2,1,0:T(8,128)(2,1)S(1)} async-done(((bf16[4,208,256]{2,1,0:T(8,128)(2,1)}), bf16[4,208,256]{2,1,0:T(8,128)(2,1)S(1)}, u32[]{:S(2)}, u32[]{:S(2)}) %all-to-all-start.4) | async-done | bytes 426016 | tf_op jit(solution)/shard_map/all_to_all | solution.py:446
  158.5 4.1 %cond.4 = (f32[208,256]{1,0:T(8,128)}, bf16[4,192,256]{2,1,0:T(8,128)(2,1)}) custom-call(s32[6]{0:T(128)} %stack.27.info, bf16[4,208,256]{2,1,0:T(8,128)(2,1)} %copy-done.10, f32[208,256]{1,0:T(8,128)} %get-tuple-element.53.h_ref, bf16[4,1024,128]{2,1,0:T(8,128)(2,1)} %mix_hbm.9, bf16[512,512]{1,0:T(8,128)(2,1)} %copy-done.7, bf16[512,512]{1,0:T(8,128)(2,1)} %copy-done.8, ...), custom_call_target="tpu_custom_call" | custom-call | flops 1000000000 | bytes 4194304 | tf_op jit(solution)/shard_map/cond/pallas_call | solution.py:523
  162.7 11.2 %all_to_all.51 = bf16[4,192,256]{2,1,0:T(8,128)(2,1)S(1)} all-to-all(bf16[4,192,256]{2,1,0:T(8,128)(2,1)} %get-tuple-element.55), channel_id=1, replica_groups={{0,1,2,3},{4,5,6,7},{8,9,10,11},{12,13,14,15},{16,17,18,19},{20,21,22,2..., dimensions={0} | all-to-all | bytes 786432 | tf_op jit(solution)/shard_map/all_to_all | solution.py:446
  174.0 9.6 %all_to_all.52.r_ref = bf16[4,192,256]{2,1,0:T(8,128)(2,1)} all-to-all(bf16[4,192,256]{2,1,0:T(8,128)(2,1)S(1)} %broadcast_in_dim.41), channel_id=1, replica_groups={{0,1,2,3},{4,5,6,7},{8,9,10,11},{12,13,14,15},{16,17,18,19},{20,21,22,2..., dimensions={0} | all-to-all | bytes 786432 | tf_op jit(solution)/shard_map/all_to_all | solution.py:446
  183.6 4.0 %cond.5 = (f32[192,256]{1,0:T(8,128)}, bf16[4,128,256]{2,1,0:T(8,128)(2,1)}) custom-call(s32[6]{0:T(128)} %stack.27.info, bf16[4,192,256]{2,1,0:T(8,128)(2,1)} %all_to_all.52.r_ref, f32[208,256]{1,0:T(8,128)} %get-tuple-element.56.h_ref, bf16[4,1024,128]{2,1,0:T(8,128)(2,1)} %mix_hbm.9, bf16[2,512,512]{2,1,0:T(8,128)(2,1)} %copy-done, ...), custom_call_target="tpu_custom_call" | custom-call | flops 1000000000 | bytes 4194304 | tf_op jit(solution)/shard_map/cond/pallas_call | solution.py:523
  187.6 8.9 %all_to_all.53 = bf16[4,128,256]{2,1,0:T(8,128)(2,1)S(1)} all-to-all(bf16[4,128,256]{2,1,0:T(8,128)(2,1)} %get-tuple-element.57), channel_id=1, replica_groups={{0,1,2,3},{4,5,6,7},{8,9,10,11},{12,13,14,15},{16,17,18,19},{20,21,22,2..., dimensions={0} | all-to-all | bytes 524288 | tf_op jit(solution)/shard_map/all_to_all | solution.py:446
  196.6 8.9 %all_to_all.54.r_ref = bf16[4,128,256]{2,1,0:T(8,128)(2,1)} all-to-all(bf16[4,128,256]{2,1,0:T(8,128)(2,1)S(1)} %broadcast_in_dim.43), channel_id=1, replica_groups={{0,1,2,3},{4,5,6,7},{8,9,10,11},{12,13,14,15},{16,17,18,19},{20,21,22,2..., dimensions={0} | all-to-all | bytes 524288 | tf_op jit(solution)/shard_map/all_to_all | solution.py:446
  208.7 6.9 %all-to-all-start.9 = ((bf16[8,128,256]{2,1,0:T(8,128)(2,1)}), bf16[8,128,256]{2,1,0:T(8,128)(2,1)S(1)}, u32[]{:S(2)}, u32[]{:S(2)}) async-start(bf16[8,128,256]{2,1,0:T(8,128)(2,1)} %cond_end.1), calls=%async_computation.9 | async-start | bytes 1048576 | tf_op jit(solution)/shard_map/all_to_all | solution.py:446
  220.8 8.4 %all-to-all-done.9.hf_ref = bf16[8,128,256]{2,1,0:T(8,128)(2,1)S(1)} async-done(((bf16[8,128,256]{2,1,0:T(8,128)(2,1)}), bf16[8,128,256]{2,1,0:T(8,128)(2,1)S(1)}, u32[]{:S(2)}, u32[]{:S(2)}) %all-to-all-start.9) | async-done | bytes 524320 | tf_op jit(solution)/shard_map/all_to_all | solution.py:446
  229.2 4.5 %all-gather.3.cloned.1.call-done = bf16[128,46,16,128]{3,2,1,0:T(8,128)(2,1)} async-done(((bf16[8,46,16,128]{3,2,1,0:T(8,128)(2,1)}), bf16[128,46,16,128]{3,2,1,0:T(8,128)(2,1)}) %all-gather.3.cloned.1.call-update) | async-done | bytes 24117264 | tf_op jit(solution)/shard_map/all_gather | solution.py:504
  233.7 14.1 %frames.2 = (bf16[512,256]{1,0:T(8,128)(2,1)}, bf16[512,512]{1,0:T(8,128)(2,1)}) custom-call(s32[6]{0:T(128)} %stack.27.info, s32[1024]{0:T(1024)} %fusion.8.codes_ref, bf16[8,128,256]{2,1,0:T(8,128)(2,1)} %copy-done.2, f32[1,1920]{1,0:T(1,128)} %broadcast_in_dim.44.gain_ref, bf16[1920,768]{1,0:T(8,128)(2,1)} %bitcast.25, ...), custom_call_target="tpu_custom_call" | custom-call | flops 4000000000 | bytes 20971520 | tf_op jit(solution)/shard_map/frames/pallas_call | solution.py:321
  249.7 13.8 %collective-permute-done.9.far_ref = bf16[512,512]{1,0:T(8,128)(2,1)S(1)} collective-permute-done((bf16[512,512]{1,0:T(8,128)(2,1)}, bf16[512,512]{1,0:T(8,128)(2,1)S(1)}, u32[]{:S(2)}, u32[]{:S(2)}) %collective-permute-start.9) | collective-permute-done | bytes 524320 | tf_op jit(solution)/shard_map/ppermute | solution.py:543
  263.6 4.5 %collective-permute-start.10 = (bf16[512,512]{1,0:T(8,128)(2,1)S(1)}, bf16[512,512]{1,0:T(8,128)(2,1)S(1)}, u32[]{:S(2)}, u32[]{:S(2)}) collective-permute-start(bf16[512,512]{1,0:T(8,128)(2,1)S(1)} %broadcast_select_fusion.1), channel_id=1, source_target_pairs={{0,8},{8,0},{16,24},{24,16},{32,40},{40,32},{48,56},{56,48},{64,72... | collective-permute-start | bytes 1572872 | tf_op jit(solution)/shard_map/ppermute | solution.py:442
  268.1 14.1 %frames.3 = (bf16[512,256]{1,0:T(8,128)(2,1)}, bf16[512,512]{1,0:T(8,128)(2,1)}) custom-call(s32[6]{0:T(128)} %stack.27.info, s32[1024]{0:T(1024)} %fusion.8.codes_ref, bf16[8,128,256]{2,1,0:T(8,128)(2,1)} %copy-done.2, f32[1,1920]{1,0:T(1,128)} %broadcast_in_dim.44.gain_ref, bf16[1920,768]{1,0:T(8,128)(2,1)} %bitcast.26, ...), custom_call_target="tpu_custom_call" | custom-call | flops 4000000000 | bytes 20971520 | tf_op jit(solution)/shard_map/frames/pallas_call | solution.py:321
  284.1 6.1 %own.1 = (f32[1024,512]{1,0:T(8,128)}, f32[1024,2]{1,0:T(8,128)}) custom-call(bf16[512,256]{1,0:T(8,128)(2,1)} %get-tuple-element.60.q0_ref, bf16[512,256]{1,0:T(8,128)(2,1)} %get-tuple-element.61.q1_ref, bf16[512,512]{1,0:T(8,128)(2,1)} %get-tuple-element.63.kv0_ref, bf16[512,512]{1,0:T(8,128)(2,1)} %get-tuple-element.62.kv1_ref), custom_call_target="tpu_custom_call" | custom-call | flops 1000000000 | bytes 4194304 | tf_op jit(solution)/shard_map/own/pallas_call | solution.py:550
  291.0 7.3 %past.1 = (f32[1024,512]{1,0:T(8,128)}, f32[1024,2]{1,0:T(8,128)}) custom-call(s32[6]{0:T(128)} %stack.27.info, bf16[512,256]{1,0:T(8,128)(2,1)} %get-tuple-element.60.q0_ref, bf16[512,256]{1,0:T(8,128)(2,1)} %get-tuple-element.61.q1_ref, bf16[512,512]{1,0:T(8,128)(2,1)} %copy-done.12, bf16[512,512]{1,0:T(8,128)(2,1)} %copy-done.19, ...), custom_call_target="tpu_custom_call" | custom-call | flops 2000000000 | bytes 4194304 | tf_op jit(solution)/shard_map/past/pallas_call | solution.py:552
  303.3 6.5 %past_end.1 = bf16[1024,256]{1,0:T(8,128)(2,1)} custom-call(s32[6]{0:T(128)} %stack.27.info, bf16[512,256]{1,0:T(8,128)(2,1)} %get-tuple-element.60.q0_ref, bf16[512,256]{1,0:T(8,128)(2,1)} %get-tuple-element.61.q1_ref, bf16[512,512]{1,0:T(8,128)(2,1)} %copy-done.13, bf16[512,512]{1,0:T(8,128)(2,1)} %copy-done.20, f32[1024,512]{1,0:T(8,128)} %get-tuple-element.69.acc_ref, ...), custom_call_target="tpu_custom_call" | custom-call | flops 2000000000 | bytes 4194304 | tf_op jit(solution)/shard_map/past_end/pallas_call | solution.py:557
  (87 shorter events, 43.8 us)
Async XLA Ops:
  7.2 25.9 %copy-start.15 = (s32[256]{0:T(256)S(1)}, s32[256]{0:T(256)}, u32[]{:S(2)}) copy-start(s32[256]{0:T(256)} %param.9) | copy-start | bytes 3076
  11.7 18.7 %collective-permute-start = (bf16[768,512]{1,0:T(8,128)(2,1)}, bf16[768,512]{1,0:T(8,128)(2,1)S(1)}, u32[]{:S(2)}, u32[]{:S(2)}) collective-permute-start(bf16[768,512]{1,0:T(8,128)(2,1)} %get-tuple-element.39), channel_id=1, source_target_pairs={{0,68},{1,69},{2,70},{3,71},{4,64},{5,65},{6,66},{7,67},{8,76},{9,... | collective-permute-start | bytes 2359304 | tf_op jit(solution)/shard_map/ppermute | solution.py:480
  13.0 14.9 %all-to-all-start = ((bf16[4,46,16,128]{3,2,1,0:T(8,128)(2,1)}), bf16[4,46,16,128]{3,2,1,0:T(8,128)(2,1)S(1)}, u32[]{:S(2)}, u32[]{:S(2)}) async-start(bf16[4,46,16,128]{3,2,1,0:T(8,128)(2,1)} %get-tuple-element.38), calls=%async_computation | async-start | bytes 1507328 | tf_op jit(solution)/shard_map/all_to_all | solution.py:446
  17.2 216.5 %all-gather.3.cloned.1.call-start = ((), (), s32[]{:S(2)}) async-start(), calls=%async_computation.10 | async-start | bytes 25624576 | tf_op jit(solution)/shard_map/all_gather | solution.py:504
  27.9 22.5 %copy-start.5 = (bf16[4,46,16,128]{3,2,1,0:T(8,128)(2,1)}, bf16[4,46,16,128]{3,2,1,0:T(8,128)(2,1)S(1)}, u32[]{:S(2)}) copy-start(bf16[4,46,16,128]{3,2,1,0:T(8,128)(2,1)S(1)} %all-to-all-done.mine) | copy-start | bytes 2260996
  30.4 8.3 %copy-start.3 = (bf16[768,512]{1,0:T(8,128)(2,1)}, bf16[768,512]{1,0:T(8,128)(2,1)S(1)}, u32[]{:S(2)}) copy-start(bf16[768,512]{1,0:T(8,128)(2,1)S(1)} %collective-permute-done.got_ref.got_hbm) | copy-start | bytes 2359300
  30.4 8.3 %collective-permute-start.3 = (bf16[768,512]{1,0:T(8,128)(2,1)S(1)}, bf16[768,512]{1,0:T(8,128)(2,1)S(1)}, u32[]{:S(2)}, u32[]{:S(2)}) collective-permute-start(bf16[768,512]{1,0:T(8,128)(2,1)S(1)} %collective-permute-done.got_ref.got_hbm), channel_id=1, source_target_pairs={{0,8},{8,0},{16,24},{24,16},{32,40},{40,32},{48,56},{56,48},{64,72... | collective-permute-start | bytes 2359304 | tf_op jit(solution)/shard_map/ppermute | solution.py:442
  31.9 18.5 %collective-permute-start.1 = (bf16[4,46,16,128]{3,2,1,0:T(8,128)(2,1)S(1)}, bf16[4,46,16,128]{3,2,1,0:T(8,128)(2,1)S(1)}, u32[]{:S(2)}, u32[]{:S(2)}) collective-permute-start(bf16[4,46,16,128]{3,2,1,0:T(8,128)(2,1)S(1)} %all-to-all-done.mine), channel_id=1, source_target_pairs={{0,68},{1,69},{2,70},{3,71},{4,64},{5,65},{6,66},{7,67},{8,76},{9,... | collective-permute-start | bytes 2261000 | tf_op jit(solution)/shard_map/ppermute | solution.py:484
  33.2 4.4 %collective-permute-start.2 = (s32[40]{0:T(128)S(1)}, s32[40]{0:T(128)S(1)}, u32[]{:S(2)}, u32[]{:S(2)}) collective-permute-start(s32[40]{0:T(128)S(1)} %broadcast_select_fusion.3), channel_id=1, source_target_pairs={{0,8},{1,9},{2,10},{3,11},{8,16},{9,17},{10,18},{11,19},{16,24},{1... | collective-permute-start | bytes 488 | tf_op jit(solution)/shard_map/ppermute | solution.py:487
  51.3 72.3 %copy-start.18 = (bf16[2,512,512]{2,1,0:T(8,128)(2,1)S(1)}, bf16[2,512,512]{2,1,0:T(8,128)(2,1)}, u32[]{:S(2)}) copy-start(bf16[2,512,512]{2,1,0:T(8,128)(2,1)} %get-tuple-element.47) | copy-start | bytes 3145732
  98.1 11.3 %all-to-all-start.1 = ((bf16[4,208,256]{2,1,0:T(8,128)(2,1)}), bf16[4,208,256]{2,1,0:T(8,128)(2,1)S(1)}, u32[]{:S(2)}, u32[]{:S(2)}) async-start(bf16[4,208,256]{2,1,0:T(8,128)(2,1)} %get-tuple-element.46), calls=%async_computation.1 | async-start | bytes 851968 | tf_op jit(solution)/shard_map/all_to_all | solution.py:446
  102.3 12.7 %collective-permute-start.4 = (bf16[512,512]{1,0:T(8,128)(2,1)}, bf16[512,512]{1,0:T(8,128)(2,1)S(1)}, u32[]{:S(2)}, u32[]{:S(2)}) collective-permute-start(bf16[512,512]{1,0:T(8,128)(2,1)} %get-tuple-element.44), channel_id=1, source_target_pairs={{0,68},{1,69},{2,70},{3,71},{4,64},{5,65},{6,66},{7,67},{8,76},{9,... | collective-permute-start | bytes 1572872 | tf_op jit(solution)/shard_map/ppermute | solution.py:506
  110.3 9.9 %all-to-all-start.2 = ((bf16[4,208,256]{2,1,0:T(8,128)(2,1)}), bf16[4,208,256]{2,1,0:T(8,128)(2,1)S(1)}, u32[]{:S(2)}, u32[]{:S(2)}) async-start(bf16[4,208,256]{2,1,0:T(8,128)(2,1)} %broadcast_in_dim.37), calls=%async_computation.2 | async-start | bytes 851968 | tf_op jit(solution)/shard_map/all_to_all | solution.py:446
  115.0 10.1 %copy-start.7 = (bf16[512,512]{1,0:T(8,128)(2,1)}, bf16[512,512]{1,0:T(8,128)(2,1)S(1)}, u32[]{:S(2)}) copy-start(bf16[512,512]{1,0:T(8,128)(2,1)S(1)} %collective-permute-done.4.got1_hbm.got_hbm) | copy-start | bytes 1572868
  120.2 4.9 %copy-start.9 = (bf16[4,208,256]{2,1,0:T(8,128)(2,1)}, bf16[4,208,256]{2,1,0:T(8,128)(2,1)S(1)}, u32[]{:S(2)}) copy-start(bf16[4,208,256]{2,1,0:T(8,128)(2,1)S(1)} %all-to-all-done.2.r_ref) | copy-start | bytes 1277956
  120.2 4.9 %collective-permute-start.6 = (bf16[512,512]{1,0:T(8,128)(2,1)S(1)}, bf16[512,512]{1,0:T(8,128)(2,1)S(1)}, u32[]{:S(2)}, u32[]{:S(2)}) collective-permute-start(bf16[512,512]{1,0:T(8,128)(2,1)S(1)} %collective-permute-done.4.got1_hbm.got_hbm), channel_id=1, source_target_pairs={{0,8},{8,0},{16,24},{24,16},{32,40},{40,32},{48,56},{56,48},{64,72... | collective-permute-start | bytes 1572872 | tf_op jit(solution)/shard_map/ppermute | solution.py:442
  123.5 24.8 %collective-permute-start.5 = (bf16[2,512,512]{2,1,0:T(8,128)(2,1)S(1)}, bf16[2,512,512]{2,1,0:T(8,128)(2,1)S(1)}, u32[]{:S(2)}, u32[]{:S(2)}) collective-permute-start(bf16[2,512,512]{2,1,0:T(8,128)(2,1)S(1)} %copy-done.18), channel_id=1, source_target_pairs={{0,68},{1,69},{2,70},{3,71},{4,64},{5,65},{6,66},{7,67},{8,76},{9,... | collective-permute-start | bytes 3145736 | tf_op jit(solution)/shard_map/ppermute | solution.py:517
  142.4 10.3 %all-to-all-start.4 = ((bf16[4,208,256]{2,1,0:T(8,128)(2,1)}), bf16[4,208,256]{2,1,0:T(8,128)(2,1)S(1)}, u32[]{:S(2)}, u32[]{:S(2)}) async-start(bf16[4,208,256]{2,1,0:T(8,128)(2,1)} %broadcast_in_dim.39), calls=%async_computation.4 | async-start | bytes 851968 | tf_op jit(solution)/shard_map/all_to_all | solution.py:446
  148.4 9.2 %copy-start = (bf16[2,512,512]{2,1,0:T(8,128)(2,1)}, bf16[2,512,512]{2,1,0:T(8,128)(2,1)S(1)}, u32[]{:S(2)}) copy-start(bf16[2,512,512]{2,1,0:T(8,128)(2,1)S(1)} %collective-permute-done.5.got1_hbm.got_hbm) | copy-start | bytes 3145732
  152.7 4.9 %copy-start.10 = (bf16[4,208,256]{2,1,0:T(8,128)(2,1)}, bf16[4,208,256]{2,1,0:T(8,128)(2,1)S(1)}, u32[]{:S(2)}) copy-start(bf16[4,208,256]{2,1,0:T(8,128)(2,1)S(1)} %all-to-all-done.4.r_ref) | copy-start | bytes 1277956
  152.7 4.8 %collective-permute-start.7 = (bf16[2,512,512]{2,1,0:T(8,128)(2,1)S(1)}, bf16[2,512,512]{2,1,0:T(8,128)(2,1)S(1)}, u32[]{:S(2)}, u32[]{:S(2)}) collective-permute-start(bf16[2,512,512]{2,1,0:T(8,128)(2,1)S(1)} %collective-permute-done.5.got1_hbm.got_hbm), channel_id=1, source_target_pairs={{0,8},{8,0},{16,24},{24,16},{32,40},{40,32},{48,56},{56,48},{64,72... | collective-permute-start | bytes 3145736 | tf_op jit(solution)/shard_map/ppermute | solution.py:442
  196.5 19.0 %copy-start.17 = (s32[1024]{0:T(1024)S(1)}, s32[1024]{0:T(1024)}, u32[]{:S(2)}) copy-start(s32[1024]{0:T(1024)} %param.10) | copy-start | bytes 12292
  196.6 20.7 %copy-start.6 = (bf16[1920,2,384]{2,1,0:T(2,128)(2,1)S(1)}, bf16[1920,2,384]{2,1,0:T(2,128)(2,1)}, u32[]{:S(2)}) copy-start(bf16[1920,2,384]{2,1,0:T(2,128)(2,1)} %param.17) | copy-start | bytes 8847364
  208.7 20.5 %all-to-all-start.9 = ((bf16[8,128,256]{2,1,0:T(8,128)(2,1)}), bf16[8,128,256]{2,1,0:T(8,128)(2,1)S(1)}, u32[]{:S(2)}, u32[]{:S(2)}) async-start(bf16[8,128,256]{2,1,0:T(8,128)(2,1)} %cond_end.1), calls=%async_computation.9 | async-start | bytes 1048576 | tf_op jit(solution)/shard_map/all_to_all | solution.py:446
  229.2 4.5 %copy-start.2 = (bf16[8,128,256]{2,1,0:T(8,128)(2,1)}, bf16[8,128,256]{2,1,0:T(8,128)(2,1)S(1)}, u32[]{:S(2)}) copy-start(bf16[8,128,256]{2,1,0:T(8,128)(2,1)S(1)} %all-to-all-done.9.hf_ref) | copy-start | bytes 1572868
  247.8 15.8 %collective-permute-start.9 = (bf16[512,512]{1,0:T(8,128)(2,1)}, bf16[512,512]{1,0:T(8,128)(2,1)S(1)}, u32[]{:S(2)}, u32[]{:S(2)}) collective-permute-start(bf16[512,512]{1,0:T(8,128)(2,1)} %get-tuple-element.63.kv0_ref), channel_id=1, source_target_pairs={{0,16},{8,24},{16,32},{24,40},{32,48},{40,56},{48,64},{56,72},{64,... | collective-permute-start | bytes 1572872 | tf_op jit(solution)/shard_map/ppermute | solution.py:543
  263.5 18.6 %copy-start.12 = (bf16[512,512]{1,0:T(8,128)(2,1)}, bf16[512,512]{1,0:T(8,128)(2,1)S(1)}, u32[]{:S(2)}) copy-start(bf16[512,512]{1,0:T(8,128)(2,1)S(1)} %collective-permute-done.9.far_ref) | copy-start | bytes 1572868
  263.6 26.6 %collective-permute-start.10 = (bf16[512,512]{1,0:T(8,128)(2,1)S(1)}, bf16[512,512]{1,0:T(8,128)(2,1)S(1)}, u32[]{:S(2)}, u32[]{:S(2)}) collective-permute-start(bf16[512,512]{1,0:T(8,128)(2,1)S(1)} %broadcast_select_fusion.1), channel_id=1, source_target_pairs={{0,8},{8,0},{16,24},{24,16},{32,40},{40,32},{48,56},{56,48},{64,72... | collective-permute-start | bytes 1572872 | tf_op jit(solution)/shard_map/ppermute | solution.py:442
  282.2 17.8 %collective-permute-start.8 = (bf16[512,512]{1,0:T(8,128)(2,1)}, bf16[512,512]{1,0:T(8,128)(2,1)S(1)}, u32[]{:S(2)}, u32[]{:S(2)}) collective-permute-start(bf16[512,512]{1,0:T(8,128)(2,1)} %get-tuple-element.62.kv1_ref), channel_id=1, source_target_pairs={{0,16},{8,24},{16,32},{24,40},{32,48},{40,56},{48,64},{56,72},{64,... | collective-permute-start | bytes 1572872 | tf_op jit(solution)/shard_map/ppermute | solution.py:543
  291.0 8.9 %copy-start.14 = (bf16[512,512]{1,0:T(8,128)(2,1)S(1)}, bf16[512,512]{1,0:T(8,128)(2,1)}, u32[]{:S(2)}) copy-start(bf16[512,512]{1,0:T(8,128)(2,1)} %get-tuple-element.62.kv1_ref) | copy-start | bytes 1572868
  299.9 2.5 copy-start.13
  300.0 2.4 collective-permute-start.11
  (7 other events, 7.5 us)
Sparse Core Ops, SparseCore 0:
  98.2 135.3 all-gather.2

commit v3 on v2

--- a/solution.py
+++ b/solution.py
@@ -157,23 +157,29 @@
         out_ref[peer] = h
 
 
-def pack_kernel(info, dil_hbm, mix_hbm, tab_hbm, up_hbm, mid_hbm, pack0, pack1, pack2, part_ref, up, mid, wide, sems):
+def half_copies(info, level, dil_hbm, mix_hbm, dest):
     cols = pl.ds(pl.multiple_of(info[0] * 512, 512), 512)
+    pairs = [(dil_hbm.at[level, tap, :, cols], dest.at[pl.ds(tap * 128, 128), :]) for tap in range(3)]
+    for i in range(4):
+        rows = pl.ds(pl.multiple_of(info[0] * 512 + i * 128, 128), 128)
+        pairs.append((mix_hbm.at[level, rows, :], dest.at[pl.ds(384, 128), pl.ds(i * 128, 128)]))
+    return pairs
+
+
+def copies_of(pairs, sems):
+    return [pltpu.make_async_copy(a, b, sems.at[i]) for i, (a, b) in enumerate(pairs)]
+
+
+def pack_kernel(info, dil_hbm, mix_hbm, tab_hbm, up_hbm, mid_hbm, pack0, part_ref, up, mid, wide, sems):
     pairs = [
         (up_hbm.at[pl.ds(info[4] * 16, 16), pl.ds(pl.multiple_of(info[0] * 2 * D, 128), 2 * D)], up),
         (mid_hbm.at[pl.ds(info[5] * 16, 16), :], mid),
     ]
-    for level in range(4):
-        dest = (pack0, pack1, pack2.at[0], pack2.at[1])[level]
-        for tap in range(3):
-            pairs.append((dil_hbm.at[level, tap, :, cols], dest.at[pl.ds(tap * 128, 128), :]))
-        for i in range(4):
-            rows = pl.ds(pl.multiple_of(info[0] * 512 + i * 128, 128), 128)
-            pairs.append((mix_hbm.at[level, rows, :], dest.at[pl.ds(384, 128), pl.ds(i * 128, 128)]))
+    pairs += half_copies(info, 0, dil_hbm, mix_hbm, pack0)
     for i in range(4):
         rows = pl.ds(pl.multiple_of(info[0] * 1024 + i * 256, 256), 256)
         pairs.append((tab_hbm.at[rows, :], pack0.at[pl.ds(512, 256), pl.ds(i * 128, 128)]))
-    copies = [pltpu.make_async_copy(a, b, sems.at[i]) for i, (a, b) in enumerate(pairs)]
+    copies = copies_of(pairs, sems)
     start(copies)
     finish(copies[:2])
     wide[...] = jnp.zeros_like(wide)
@@ -186,26 +192,18 @@
     finish(copies[2:])
 
 
-def join_kernel(mine, others, out, sems):
-    copies = [
-        pltpu.make_async_copy(ref, out.at[pl.ds(i * 4, 4)], sems.at[i]) for i, ref in enumerate((mine, others))
-    ]
+def later_kernel(info, dil_hbm, mix_hbm, pack1, pack2, sems):
+    pairs = half_copies(info, 1, dil_hbm, mix_hbm, pack1)
+    for i in range(2):
+        pairs += half_copies(info, 2 + i, dil_hbm, mix_hbm, pack2.at[i])
+    copies = copies_of(pairs, sems)
     start(copies)
     finish(copies)
 
 
-def join(mine, others):
-    space = pl.BlockSpec(memory_space=pl.ANY)
-    return pl.pallas_call(
-        join_kernel,
-        out_shape=shape(8, PART, 16, 128),
-        in_specs=[space, space],
-        out_specs=space,
-        scratch_shapes=[pltpu.SemaphoreType.DMA((2,))],
-        compiler_params=params(),
-        cost_estimate=cost(0, 3 << 20),
-        name="join",
-    )(mine, others)
+def join_kernel(mine, others, out):
+    out[:4] = mine[...]
+    out[4:] = others[...]
 
 
 def call(body, outs, scratch=(), smem=1, n=0, hbm=0, after=0, flops=10**9, name=None):
@@ -348,15 +346,14 @@
     return lax.dot_general(q, k, (((1,), (1,)), ((), ())), preferred_element_type=F32)
 
 
-def fold(q_refs, kv_refs, seen_of, old_of, put):
-    kv = jnp.concatenate([ref[...] for ref in kv_refs], axis=0)
-    ones = jnp.ones((kv.shape[0], 128), BF)
-    for head in range(2):
-        k = kv[:, head * 128 : head * 128 + 128]
-        v = jnp.concatenate([kv[:, 256 + head * 128 : 384 + head * 128], ones], axis=1)
+def fold(q_refs, kv, seen_of, old_of, put):
+    def body(head, carry):
+        k = kv[:, pl.ds(pl.multiple_of(head * 128, 128), 128)]
+        v = kv[:, pl.ds(pl.multiple_of(256 + head * 128, 128), 128)]
+        v = jnp.concatenate([v, jnp.ones(v.shape, BF)], axis=1)
+        cols = pl.ds(pl.multiple_of(head * 128, 128), 128)
         for phase in range(4):
-            lines = slice(phase % 2 * 256, phase % 2 * 256 + 256)
-            s = scores_of(q_refs[phase // 2][lines, head * 128 : head * 128 + 128], k)
+            s = scores_of(q_refs[phase // 2][phase % 2 * 256 : phase % 2 * 256 + 256, cols], k)
             s = jnp.where(seen_of(phase), s, -1e30)
             top = jnp.max(s, axis=1, keepdims=True)
             old = old_of(head, phase)
@@ -366,30 +363,33 @@
                 top = jnp.maximum(old[0], top)
                 p = jnp.exp2((s - top) * SCALE).astype(BF)
                 put(head, phase, top, old[1] * jnp.exp2((old[0] - top) * SCALE) + dot(p, v))
-
-
-def at_tile(head, phase):
-    lines = slice(phase * 256, phase * 256 + 256)
-    return (lines, slice(head, head + 1)), (lines, slice(head * 256, head * 256 + 256))
-
-
-def own_kernel(q0_ref, q1_ref, kv0_ref, kv1_ref, acc_ref, top_ref):
+        return carry
+
+    lax.fori_loop(0, 2, body, 0)
+
+
+def join_keys(kv, first, second):
+    kv[:512] = first[...]
+    kv[512:] = second[...]
+
+
+def own_kernel(q0_ref, q1_ref, kv0_ref, kv1_ref, acc_ref, top_ref, kv):
+    join_keys(kv, kv0_ref, kv1_ref)
     col = lax.broadcasted_iota(jnp.int32, (256, 1024), 1)
     ahead = (col & 255) * 4 + (col >> 8) - 4 * lax.broadcasted_iota(jnp.int32, (256, 1024), 0)
 
     def put(head, phase, top, acc):
-        one, both = at_tile(head, phase)
-        top_ref[one] = top
-        acc_ref[both] = acc
-
-    fold((q0_ref, q1_ref), (kv0_ref, kv1_ref), lambda p: ahead <= p, lambda head, phase: None, put)
+        top_ref[head, phase] = top
+        acc_ref[head, phase] = acc
+
+    fold((q0_ref, q1_ref), kv, lambda p: ahead <= p, lambda head, phase: None, put)
 
 
 def past_kernel(last, info, q0_ref, q1_ref, far_ref, near_ref, acc_ref, top_ref, *refs):
     if last:
-        out_ref, acc, tops, wide = refs
+        out_ref, kv, acc, tops, wide = refs
     else:
-        acc, tops = refs
+        acc, tops, kv = refs
     song = info[2]
 
     @pl.when(song == 0)
@@ -399,24 +399,26 @@
 
     @pl.when(song > 0)
     def _():
+        join_keys(kv, far_ref, near_ref)
         col = lax.broadcasted_iota(jnp.int32, (256, 1024), 1)
         seen = col >= jnp.where(song == 1, 512, 0)
 
-        def old_of(head, phase):
-            one, both = at_tile(head, phase)
-            return top_ref[one], acc_ref[both]
-
         def put(head, phase, top, total):
-            one, both = at_tile(head, phase)
-            tops[one] = top
-            acc[both] = total
-
-        fold((q0_ref, q1_ref), (far_ref, near_ref), lambda p: seen, old_of, put)
+            tops[head, phase] = top
+            acc[head, phase] = total
+
+        fold(
+            (q0_ref, q1_ref),
+            kv,
+            lambda p: seen,
+            lambda head, phase: (top_ref[head, phase], acc_ref[head, phase]),
+            put,
+        )
 
     if last:
         for head in range(2):
             for phase in range(4):
-                both = acc[at_tile(head, phase)[1]]
+                both = acc[head, phase]
                 wide[pl.ds(phase, 256, stride=4), :] = both[:, :128] / both[:, 128:]
             out_ref[:, head * 128 : head * 128 + 128] = wide[...].astype(BF)
 
@@ -465,26 +467,25 @@
     share = song ^ (8 * x_hi)
     info = jnp.stack([core, begin, song, x_hi * 4, share // 2, share]).astype(jnp.int32)
 
-    pack0, pack1, pack2, part = call(
+    pack0, part = call(
         pack_kernel,
-        (shape(768, 512), shape(512, 512), shape(2, 512, 512), shape(4, PART, 16, 128)),
+        (shape(768, 512), shape(4, PART, 16, 128)),
         [
             pltpu.VMEM((16, 2 * D), BF),
             pltpu.VMEM((16, D), BF),
             pltpu.VMEM((16, 16, 128), F32),
-            pltpu.SemaphoreType.DMA((34,)),
+            pltpu.SemaphoreType.DMA((13,)),
         ],
         hbm=5,
         name="pack",
     )(info, dilated_weight, mixing_weight, upper_table, upsample_weight, middle_table)
     got0 = lax.ppermute(pack0, EVERY, other_half())
     mine = exchange(part, groups=Y_GROUPS)
-    mine, got0 = lax.optimization_barrier((mine, got0))
-    sib0 = to_sibling(got0)
-    others = lax.ppermute(mine, EVERY, other_half())
-
     edge = jnp.where(x_hi == 0, upper_codes[-40:], upper_codes[:40])
     edge = lax.ppermute(edge, EVERY, song_neighbours())
+    mine, got0, edge = lax.optimization_barrier((mine, got0, edge))
+    others = lax.ppermute(mine, EVERY, other_half())
+    sib0 = to_sibling(got0)
     codes = jnp.where(
         x_hi == 0,
         jnp.concatenate([edge, upper_codes[: HALF + 40]]),
@@ -500,8 +501,17 @@
         after=2,
         name="cond0",
     )(info, codes, upper_table, dilated_weight, got0, sib0)
+    pack1, pack2 = call(
+        later_kernel,
+        (shape(512, 512), shape(2, 512, 512)),
+        [pltpu.SemaphoreType.DMA((21,))],
+        hbm=2,
+        name="pack_later",
+    )(info, dilated_weight, mixing_weight)
+
     others, pack1, terms = lax.optimization_barrier((others, pack1, terms))
-    full = lax.all_gather(join(mine, others), "song", axis=0, tiled=False)
+    both = call(join_kernel, shape(8, PART, 16, 128), smem=0, n=2, name="join")(mine, others)
+    full = lax.all_gather(both, "song", axis=0, tiled=False)
     full = full.reshape(8, 2, 8, PART, 16, 128)
     got1 = lax.ppermute(pack1, EVERY, other_half())
     for level in range(4):
@@ -546,10 +556,12 @@
     far0 = from_two_back(kv0)
     q1, kv1 = frames(1, info, mid, hf, gain, qkv, full)
     far1 = from_two_back(kv1)
-    state = (shape(1024, 512, dtype=F32), shape(1024, 2, dtype=F32))
-    kept = call(own_kernel, state, smem=0, n=4, flops=10**9, name="own")(q0, q1, kv0, kv1)
+    state = (shape(2, 4, 256, 256, dtype=F32), shape(2, 4, 256, 1, dtype=F32))
+    keys = pltpu.VMEM((1024, 512), BF)
+    far0, q1 = lax.optimization_barrier((far0, q1))
+    kept = call(own_kernel, state, [keys], smem=0, n=4, flops=10**9, name="own")(q0, q1, kv0, kv1)
     near0 = to_sibling(jnp.where(core == 0, kv0, far0))
-    kept = call(functools.partial(past_kernel, False), state, n=6, flops=2 * 10**9, name="past")(
+    kept = call(functools.partial(past_kernel, False), state, [keys], n=6, flops=10**9, name="past")(
         info, q0, q1, far0, near0, *kept
     )
     far1, kept = lax.optimization_barrier((far1, kept))
@@ -557,7 +569,12 @@
     return call(
         functools.partial(past_kernel, True),
         shape(1024, 256),
-        [pltpu.VMEM((1024, 512), F32), pltpu.VMEM((1024, 2), F32), pltpu.VMEM((1024, 128), F32)],
+        [
+            keys,
+            pltpu.VMEM((2, 4, 256, 256), F32),
+            pltpu.VMEM((2, 4, 256, 1), F32),
+            pltpu.VMEM((1024, 128), F32),
+        ],
         n=6,
         flops=2 * 10**9,
         name="past_end",

time: 318 us -> 260 us (0.82)
  Pallas kernels: 120 us -> 80.3 us
  waiting for transfers between devices: 71.5 us -> 51.8 us
    pallas_call x5 -> x6, Pallas kernels: 71.1 us -> 31.7 us  [the longest x1 8.06 us: on_device(): call(functools.partial(past_kernel, False), state, [keys], n=6, flops=10...]
    ppermute x2, waiting for transfers between devices: 15.5 us -> 0.53 us  [from_two_back(): return lax.ppermute(value, 'song', [(i, i + 2) for i in range(14)])]
    all_to_all x5, waiting for transfers between devices: 34.5 us -> 29 us  [exchange(): lax.all_to_all(value, axis, 0, 0, axis_index_groups=groups, tiled=True)]
    unnamed x44 -> x46, local copies, waits for them, and re-layouts: 7.52 us -> 7.47 us
  transfers between devices with their start and end apart: 18 -> 18, of which waited for: 16 -> 15; matrix products, arithmetic and copies ran while one was open for 3% -> 3% of each run, Pallas kernels for 15% -> 21%
where the time goes in v3:
time: 260 us; the launch traced here: 257 us
  Pallas kernels  80.3 us (31%)
  waiting for transfers between devices  51.8 us (20%)
  blocking collectives  50.5 us (19%)
  starting transfers between devices  46.2 us (18%)
  between operations  13.7 us (5%)
  local copies, waits for them, and re-layouts  12.4 us (5%)
    all_to_all x5, blocking collectives, exchange(): lax.all_to_all(value, axis, 0, 0, axis_index_groups=groups, tiled=True)  50.5 us
    all_to_all x5, waiting for transfers between devices, exchange(): lax.all_to_all(value, axis, 0, 0, axis_index_groups=groups, tiled=True)  29 us
    pallas_call x2, Pallas kernels, frames(): pl.pallas_call(functools.partial(frames_kernel, pair), out_shape=(shape(5...  28.2 us
    all_to_all x5, starting transfers between devices, exchange(): lax.all_to_all(value, axis, 0, 0, axis_index_groups=groups, tiled=True)  21.8 us
    pallas_call x3, Pallas kernels, on_device(): call(functools.partial(middle_kernel, level), (shape(ROWS[level + 1], 256...  12.4 us
    ppermute x5, starting transfers between devices, to_sibling(): return lax.ppermute(value, 'song', [(i, i ^ 1) for i in range(16)])  10.8 us
    pallas_call x1, Pallas kernels, on_device(): call(functools.partial(past_kernel, False), state, [keys], n=6, flops=10...  8.06 us
    unnamed x46, local copies, waits for them, and re-layouts  7.47 us
  transfers between devices with their start and end apart: 18, of which 15 were waited for; matrix products, arithmetic and copies ran while one was open for 3% of the time, Pallas kernels for 21%

profile of v3, /device:TPU:3, one launch (start us, length us, event | category | flops | bytes accessed | tf_op | source)
XLA Modules:
  0.0 256.7 jit_solution(11894441413674606813)
XLA Ops:
  7.2 3.3 %pack.1 = (bf16[768,512]{1,0:T(8,128)(2,1)}, bf16[4,46,16,128]{3,2,1,0:T(8,128)(2,1)}) custom-call(s32[6]{0:T(128)} %stack.27.info, bf16[4,3,128,1024]{3,2,1,0:T(8,128)(2,1)} %dil_hbm.11, bf16[4,1024,128]{2,1,0:T(8,128)(2,1)} %mix_hbm.11, bf16[2048,128]{1,0:T(8,128)(2,1)} %table_ref.1, bf16[128,7680]{1,0:T(8,128)(2,1)} %up_hbm.1, bf16[256,1920]{1,0:T(8,128)(2,1)} %mid_hbm.1), custom_call_target="tpu_custom_call" | custom-call | flops 1000000000 | bytes 4194304 | tf_op jit(solution)/shard_map/pack/pallas_call | solution.py:470
  11.8 4.2 %all-to-all-start = ((bf16[4,46,16,128]{3,2,1,0:T(8,128)(2,1)}), bf16[4,46,16,128]{3,2,1,0:T(8,128)(2,1)S(1)}, u32[]{:S(2)}, u32[]{:S(2)}) async-start(bf16[4,46,16,128]{3,2,1,0:T(8,128)(2,1)} %get-tuple-element.41), calls=%async_computation | async-start | bytes 1507328 | tf_op jit(solution)/shard_map/all_to_all | solution.py:448
  16.0 4.7 %collective-permute-start.1 = (s32[40]{0:T(128)S(1)}, s32[40]{0:T(128)S(1)}, u32[]{:S(2)}, u32[]{:S(2)}) collective-permute-start(s32[40]{0:T(128)S(1)} %broadcast_select_fusion.3), channel_id=1, source_target_pairs={{0,8},{1,9},{2,10},{3,11},{8,16},{9,17},{10,18},{11,19},{16,24},{1... | collective-permute-start | bytes 488 | tf_op jit(solution)/shard_map/ppermute | solution.py:485
  21.4 5.3 %all-to-all-done.mine = bf16[4,46,16,128]{3,2,1,0:T(8,128)(2,1)S(1)} async-done(((bf16[4,46,16,128]{3,2,1,0:T(8,128)(2,1)}), bf16[4,46,16,128]{3,2,1,0:T(8,128)(2,1)S(1)}, u32[]{:S(2)}, u32[]{:S(2)}) %all-to-all-start) | async-done | bytes 753696 | tf_op jit(solution)/shard_map/all_to_all | solution.py:448
  31.9 3.4 %pack_later.1 = (bf16[512,512]{1,0:T(8,128)(2,1)}, bf16[2,512,512]{2,1,0:T(8,128)(2,1)}) custom-call(s32[6]{0:T(128)} %stack.27.info, bf16[4,3,128,1024]{3,2,1,0:T(8,128)(2,1)} %dil_hbm.11, bf16[4,1024,128]{2,1,0:T(8,128)(2,1)} %mix_hbm.11), custom_call_target="tpu_custom_call" | custom-call | flops 1000000000 | bytes 4194304 | tf_op jit(solution)/shard_map/pack_later/pallas_call | solution.py:504
  37.3 4.7 %cond0.1 = (f32[208,256]{1,0:T(8,128)}, bf16[4,208,256]{2,1,0:T(8,128)(2,1)}) custom-call(s32[6]{0:T(128)} %stack.27.info, s32[208,1]{1,0:T(8,128)} %broadcast_select_fusion.2.codes_ref, bf16[2048,128]{1,0:T(8,128)(2,1)} %table_ref.1, bf16[4,3,128,1024]{3,2,1,0:T(8,128)(2,1)} %dil_hbm.11, bf16[768,512]{1,0:T(8,128)(2,1)} %copy-done.3, bf16[768,512]{1,0:T(8,128)(2,1)} %copy-done.4), custom_call_target="tpu_custom_call" | custom-call | flops 1000000000 | bytes 4194304 | tf_op jit(solution)/shard_map/cond0/pallas_call | solution.py:495
  42.1 7.1 %collective-permute-done.2.others = bf16[4,46,16,128]{3,2,1,0:T(8,128)(2,1)S(1)} collective-permute-done((bf16[4,46,16,128]{3,2,1,0:T(8,128)(2,1)S(1)}, bf16[4,46,16,128]{3,2,1,0:T(8,128)(2,1)S(1)}, u32[]{:S(2)}, u32[]{:S(2)}) %collective-permute-start.2) | collective-permute-done | bytes 753696 | tf_op jit(solution)/shard_map/ppermute | solution.py:487
  50.1 2.7 %join.1 = bf16[8,46,16,128]{3,2,1,0:T(8,128)(2,1)} custom-call(bf16[4,46,16,128]{3,2,1,0:T(8,128)(2,1)} %copy-done.11, bf16[4,46,16,128]{3,2,1,0:T(8,128)(2,1)} %copy-done.20), custom_call_target="tpu_custom_call" | custom-call | flops 1000000000 | bytes 4194304 | tf_op jit(solution)/shard_map/join/pallas_call | solution.py:513
  52.8 4.3 %all-to-all-start.1 = ((bf16[4,208,256]{2,1,0:T(8,128)(2,1)}), bf16[4,208,256]{2,1,0:T(8,128)(2,1)S(1)}, u32[]{:S(2)}, u32[]{:S(2)}) async-start(bf16[4,208,256]{2,1,0:T(8,128)(2,1)} %get-tuple-element.50), calls=%async_computation.1 | async-start | bytes 851968 | tf_op jit(solution)/shard_map/all_to_all | solution.py:448
  58.3 5.9 %all-to-all-done.1 = bf16[4,208,256]{2,1,0:T(8,128)(2,1)S(1)} async-done(((bf16[4,208,256]{2,1,0:T(8,128)(2,1)}), bf16[4,208,256]{2,1,0:T(8,128)(2,1)S(1)}, u32[]{:S(2)}, u32[]{:S(2)}) %all-to-all-start.1) | async-done | bytes 426016 | tf_op jit(solution)/shard_map/all_to_all | solution.py:448
  65.1 3.5 %all-to-all-start.2 = ((bf16[4,208,256]{2,1,0:T(8,128)(2,1)}), bf16[4,208,256]{2,1,0:T(8,128)(2,1)S(1)}, u32[]{:S(2)}, u32[]{:S(2)}) async-start(bf16[4,208,256]{2,1,0:T(8,128)(2,1)} %broadcast_in_dim.37), calls=%async_computation.2 | async-start | bytes 851968 | tf_op jit(solution)/shard_map/all_to_all | solution.py:448
  69.8 5.2 %all-to-all-done.2.r_ref = bf16[4,208,256]{2,1,0:T(8,128)(2,1)S(1)} async-done(((bf16[4,208,256]{2,1,0:T(8,128)(2,1)}), bf16[4,208,256]{2,1,0:T(8,128)(2,1)S(1)}, u32[]{:S(2)}, u32[]{:S(2)}) %all-to-all-start.2) | async-done | bytes 426016 | tf_op jit(solution)/shard_map/all_to_all | solution.py:448
  74.9 3.4 %collective-permute-start.6 = (bf16[512,512]{1,0:T(8,128)(2,1)S(1)}, bf16[512,512]{1,0:T(8,128)(2,1)S(1)}, u32[]{:S(2)}, u32[]{:S(2)}) collective-permute-start(bf16[512,512]{1,0:T(8,128)(2,1)S(1)} %collective-permute-done.4.got1_hbm.got_hbm), channel_id=1, source_target_pairs={{0,8},{8,0},{16,24},{24,16},{32,40},{40,32},{48,56},{56,48},{64,72... | collective-permute-start | bytes 1572872 | tf_op jit(solution)/shard_map/ppermute | solution.py:444
  80.6 4.2 %cond.3 = (f32[208,256]{1,0:T(8,128)}, bf16[4,208,256]{2,1,0:T(8,128)(2,1)}) custom-call(s32[6]{0:T(128)} %stack.27.info, bf16[4,208,256]{2,1,0:T(8,128)(2,1)} %copy-done.9, f32[208,256]{1,0:T(8,128)} %get-tuple-element.53.h_ref, bf16[4,1024,128]{2,1,0:T(8,128)(2,1)} %mix_hbm.11, bf16[768,512]{1,0:T(8,128)(2,1)} %copy-done.3, bf16[768,512]{1,0:T(8,128)(2,1)} %copy-done.4, ...), custom_call_target="tpu_custom_call" | custom-call | flops 1000000000 | bytes 4194304 | tf_op jit(solution)/shard_map/cond/pallas_call | solution.py:533
  84.9 11.5 %all_to_all.50 = bf16[4,208,256]{2,1,0:T(8,128)(2,1)S(1)} all-to-all(bf16[4,208,256]{2,1,0:T(8,128)(2,1)} %get-tuple-element.55), channel_id=1, replica_groups={{0,1,2,3},{4,5,6,7},{8,9,10,11},{12,13,14,15},{16,17,18,19},{20,21,22,2..., dimensions={0} | all-to-all | bytes 851968 | tf_op jit(solution)/shard_map/all_to_all | solution.py:448
  97.2 3.5 %all-to-all-start.4 = ((bf16[4,208,256]{2,1,0:T(8,128)(2,1)}), bf16[4,208,256]{2,1,0:T(8,128)(2,1)S(1)}, u32[]{:S(2)}, u32[]{:S(2)}) async-start(bf16[4,208,256]{2,1,0:T(8,128)(2,1)} %broadcast_in_dim.39), calls=%async_computation.4 | async-start | bytes 851968 | tf_op jit(solution)/shard_map/all_to_all | solution.py:448
  103.2 4.3 %all-to-all-done.4.r_ref = bf16[4,208,256]{2,1,0:T(8,128)(2,1)S(1)} async-done(((bf16[4,208,256]{2,1,0:T(8,128)(2,1)}), bf16[4,208,256]{2,1,0:T(8,128)(2,1)S(1)}, u32[]{:S(2)}, u32[]{:S(2)}) %all-to-all-start.4) | async-done | bytes 426016 | tf_op jit(solution)/shard_map/all_to_all | solution.py:448
  113.3 4.2 %cond.4 = (f32[208,256]{1,0:T(8,128)}, bf16[4,192,256]{2,1,0:T(8,128)(2,1)}) custom-call(s32[6]{0:T(128)} %stack.27.info, bf16[4,208,256]{2,1,0:T(8,128)(2,1)} %copy-done.10, f32[208,256]{1,0:T(8,128)} %get-tuple-element.57.h_ref, bf16[4,1024,128]{2,1,0:T(8,128)(2,1)} %mix_hbm.11, bf16[512,512]{1,0:T(8,128)(2,1)} %copy-done.6, bf16[512,512]{1,0:T(8,128)(2,1)} %copy-done.7, ...), custom_call_target="tpu_custom_call" | custom-call | flops 1000000000 | bytes 4194304 | tf_op jit(solution)/shard_map/cond/pallas_call | solution.py:533
  117.5 11.3 %all_to_all.51 = bf16[4,192,256]{2,1,0:T(8,128)(2,1)S(1)} all-to-all(bf16[4,192,256]{2,1,0:T(8,128)(2,1)} %get-tuple-element.59), channel_id=1, replica_groups={{0,1,2,3},{4,5,6,7},{8,9,10,11},{12,13,14,15},{16,17,18,19},{20,21,22,2..., dimensions={0} | all-to-all | bytes 786432 | tf_op jit(solution)/shard_map/all_to_all | solution.py:448
  128.9 10.0 %all_to_all.52.r_ref = bf16[4,192,256]{2,1,0:T(8,128)(2,1)} all-to-all(bf16[4,192,256]{2,1,0:T(8,128)(2,1)S(1)} %broadcast_in_dim.41), channel_id=1, replica_groups={{0,1,2,3},{4,5,6,7},{8,9,10,11},{12,13,14,15},{16,17,18,19},{20,21,22,2..., dimensions={0} | all-to-all | bytes 786432 | tf_op jit(solution)/shard_map/all_to_all | solution.py:448
  138.8 4.0 %cond.5 = (f32[192,256]{1,0:T(8,128)}, bf16[4,128,256]{2,1,0:T(8,128)(2,1)}) custom-call(s32[6]{0:T(128)} %stack.27.info, bf16[4,192,256]{2,1,0:T(8,128)(2,1)} %all_to_all.52.r_ref, f32[208,256]{1,0:T(8,128)} %get-tuple-element.60.h_ref, bf16[4,1024,128]{2,1,0:T(8,128)(2,1)} %mix_hbm.11, bf16[2,512,512]{2,1,0:T(8,128)(2,1)} %copy-done, ...), custom_call_target="tpu_custom_call" | custom-call | flops 1000000000 | bytes 4194304 | tf_op jit(solution)/shard_map/cond/pallas_call | solution.py:533
  142.9 8.9 %all_to_all.53 = bf16[4,128,256]{2,1,0:T(8,128)(2,1)S(1)} all-to-all(bf16[4,128,256]{2,1,0:T(8,128)(2,1)} %get-tuple-element.61), channel_id=1, replica_groups={{0,1,2,3},{4,5,6,7},{8,9,10,11},{12,13,14,15},{16,17,18,19},{20,21,22,2..., dimensions={0} | all-to-all | bytes 524288 | tf_op jit(solution)/shard_map/all_to_all | solution.py:448
  151.9 8.8 %all_to_all.54.r_ref = bf16[4,128,256]{2,1,0:T(8,128)(2,1)} all-to-all(bf16[4,128,256]{2,1,0:T(8,128)(2,1)S(1)} %broadcast_in_dim.43), channel_id=1, replica_groups={{0,1,2,3},{4,5,6,7},{8,9,10,11},{12,13,14,15},{16,17,18,19},{20,21,22,2..., dimensions={0} | all-to-all | bytes 524288 | tf_op jit(solution)/shard_map/all_to_all | solution.py:448
  160.7 3.2 %cond_end.1 = bf16[8,128,256]{2,1,0:T(8,128)(2,1)} custom-call(s32[6]{0:T(128)} %stack.27.info, bf16[4,128,256]{2,1,0:T(8,128)(2,1)} %all_to_all.54.r_ref, f32[192,256]{1,0:T(8,128)} %get-tuple-element.62.h_ref, bf16[4,1024,128]{2,1,0:T(8,128)(2,1)} %mix_hbm.11, bf16[2,512,512]{2,1,0:T(8,128)(2,1)} %copy-done, bf16[2,512,512]{2,1,0:T(8,128)(2,1)} %copy-done.1), custom_call_target="tpu_custom_call" | custom-call | flops 1000000000 | bytes 4194304 | tf_op jit(solution)/shard_map/cond_end/pallas_call | solution.py:542
  164.0 6.3 %all-to-all-start.9 = ((bf16[8,128,256]{2,1,0:T(8,128)(2,1)}), bf16[8,128,256]{2,1,0:T(8,128)(2,1)S(1)}, u32[]{:S(2)}, u32[]{:S(2)}) async-start(bf16[8,128,256]{2,1,0:T(8,128)(2,1)} %cond_end.1), calls=%async_computation.9 | async-start | bytes 1048576 | tf_op jit(solution)/shard_map/all_to_all | solution.py:448
  175.6 8.4 %all-to-all-done.9.hf_ref = bf16[8,128,256]{2,1,0:T(8,128)(2,1)S(1)} async-done(((bf16[8,128,256]{2,1,0:T(8,128)(2,1)}), bf16[8,128,256]{2,1,0:T(8,128)(2,1)S(1)}, u32[]{:S(2)}, u32[]{:S(2)}) %all-to-all-start.9) | async-done | bytes 524320 | tf_op jit(solution)/shard_map/all_to_all | solution.py:448
  184.0 4.1 %all-gather.3.cloned.1.call-done = bf16[128,46,16,128]{3,2,1,0:T(8,128)(2,1)} async-done(((bf16[8,46,16,128]{3,2,1,0:T(8,128)(2,1)}), bf16[128,46,16,128]{3,2,1,0:T(8,128)(2,1)}) %all-gather.3.cloned.1.call-update) | async-done | bytes 24117264 | tf_op jit(solution)/shard_map/all_gather | solution.py:514
  188.1 14.1 %frames.2 = (bf16[512,256]{1,0:T(8,128)(2,1)}, bf16[512,512]{1,0:T(8,128)(2,1)}) custom-call(s32[6]{0:T(128)} %stack.27.info, s32[1024]{0:T(1024)} %fusion.8.codes_ref, bf16[8,128,256]{2,1,0:T(8,128)(2,1)} %copy-done.2, f32[1,1920]{1,0:T(1,128)} %broadcast_in_dim.44.gain_ref, bf16[1920,768]{1,0:T(8,128)(2,1)} %bitcast.25, ...), custom_call_target="tpu_custom_call" | custom-call | flops 4000000000 | bytes 20971520 | tf_op jit(solution)/shard_map/frames/pallas_call | solution.py:319
  204.4 14.2 %frames.3 = (bf16[512,256]{1,0:T(8,128)(2,1)}, bf16[512,512]{1,0:T(8,128)(2,1)}) custom-call(s32[6]{0:T(128)} %stack.27.info, s32[1024]{0:T(1024)} %fusion.8.codes_ref, bf16[8,128,256]{2,1,0:T(8,128)(2,1)} %copy-done.2, f32[1,1920]{1,0:T(1,128)} %broadcast_in_dim.44.gain_ref, bf16[1920,768]{1,0:T(8,128)(2,1)} %bitcast.26, ...), custom_call_target="tpu_custom_call" | custom-call | flops 4000000000 | bytes 20971520 | tf_op jit(solution)/shard_map/frames/pallas_call | solution.py:319
  223.1 6.8 %own.1 = (f32[2,4,256,256]{3,2,1,0:T(8,128)}, f32[2,4,256,1]{3,2,1,0:T(8,128)}) custom-call(bf16[512,256]{1,0:T(8,128)(2,1)} %get-tuple-element.64.q0_ref, bf16[512,256]{1,0:T(8,128)(2,1)} %get-tuple-element.67.q1_ref, bf16[512,512]{1,0:T(8,128)(2,1)} %get-tuple-element.65.kv0_ref, bf16[512,512]{1,0:T(8,128)(2,1)} %get-tuple-element.68.kv1_ref), custom_call_target="tpu_custom_call" | custom-call | flops 1000000000 | bytes 4194304 | tf_op jit(solution)/shard_map/own/pallas_call | solution.py:562
  230.7 8.1 %past.1 = (f32[2,4,256,256]{3,2,1,0:T(8,128)}, f32[2,4,256,1]{3,2,1,0:T(8,128)}) custom-call(s32[6]{0:T(128)} %stack.27.info, bf16[512,256]{1,0:T(8,128)(2,1)} %get-tuple-element.64.q0_ref, bf16[512,256]{1,0:T(8,128)(2,1)} %get-tuple-element.67.q1_ref, bf16[512,512]{1,0:T(8,128)(2,1)} %copy-done.8, bf16[512,512]{1,0:T(8,128)(2,1)} %copy-done.12, ...), custom_call_target="tpu_custom_call" | custom-call | flops 1000000000 | bytes 4194304 | tf_op jit(solution)/shard_map/past/pallas_call | solution.py:564
  242.4 7.4 %past_end.1 = bf16[1024,256]{1,0:T(8,128)(2,1)} custom-call(s32[6]{0:T(128)} %stack.27.info, bf16[512,256]{1,0:T(8,128)(2,1)} %get-tuple-element.64.q0_ref, bf16[512,256]{1,0:T(8,128)(2,1)} %get-tuple-element.67.q1_ref, bf16[512,512]{1,0:T(8,128)(2,1)} %copy-done.14, bf16[512,512]{1,0:T(8,128)(2,1)} %copy-done.21, ...), custom_call_target="tpu_custom_call" | custom-call | flops 2000000000 | bytes 4194304 | tf_op jit(solution)/shard_map/past_end/pallas_call | solution.py:569
  (90 shorter events, 42.1 us)
Async XLA Ops:
  7.2 8.8 %copy-start.16 = (s32[256]{0:T(256)S(1)}, s32[256]{0:T(256)}, u32[]{:S(2)}) copy-start(s32[256]{0:T(256)} %param.9) | copy-start | bytes 3076
  10.5 18.7 %collective-permute-start = (bf16[768,512]{1,0:T(8,128)(2,1)}, bf16[768,512]{1,0:T(8,128)(2,1)S(1)}, u32[]{:S(2)}, u32[]{:S(2)}) collective-permute-start(bf16[768,512]{1,0:T(8,128)(2,1)} %get-tuple-element.42), channel_id=1, source_target_pairs={{0,68},{1,69},{2,70},{3,71},{4,64},{5,65},{6,66},{7,67},{8,76},{9,... | collective-permute-start | bytes 2359304 | tf_op jit(solution)/shard_map/ppermute | solution.py:482
  11.8 14.9 %all-to-all-start = ((bf16[4,46,16,128]{3,2,1,0:T(8,128)(2,1)}), bf16[4,46,16,128]{3,2,1,0:T(8,128)(2,1)S(1)}, u32[]{:S(2)}, u32[]{:S(2)}) async-start(bf16[4,46,16,128]{3,2,1,0:T(8,128)(2,1)} %get-tuple-element.41), calls=%async_computation | async-start | bytes 1507328 | tf_op jit(solution)/shard_map/all_to_all | solution.py:448
  15.9 172.2 %all-gather.3.cloned.1.call-start = ((), (), s32[]{:S(2)}) async-start(), calls=%async_computation.10 | async-start | bytes 25624576 | tf_op jit(solution)/shard_map/all_gather | solution.py:514
  16.0 5.4 %collective-permute-start.1 = (s32[40]{0:T(128)S(1)}, s32[40]{0:T(128)S(1)}, u32[]{:S(2)}, u32[]{:S(2)}) collective-permute-start(s32[40]{0:T(128)S(1)} %broadcast_select_fusion.3), channel_id=1, source_target_pairs={{0,8},{1,9},{2,10},{3,11},{8,16},{9,17},{10,18},{11,19},{16,24},{1... | collective-permute-start | bytes 488 | tf_op jit(solution)/shard_map/ppermute | solution.py:485
  26.7 15.4 %copy-start.11 = (bf16[4,46,16,128]{3,2,1,0:T(8,128)(2,1)}, bf16[4,46,16,128]{3,2,1,0:T(8,128)(2,1)S(1)}, u32[]{:S(2)}) copy-start(bf16[4,46,16,128]{3,2,1,0:T(8,128)(2,1)S(1)} %all-to-all-done.mine) | copy-start | bytes 2260996
  29.2 7.3 %copy-start.3 = (bf16[768,512]{1,0:T(8,128)(2,1)}, bf16[768,512]{1,0:T(8,128)(2,1)S(1)}, u32[]{:S(2)}) copy-start(bf16[768,512]{1,0:T(8,128)(2,1)S(1)} %collective-permute-done.got_ref.got_hbm) | copy-start | bytes 2359300
  29.2 7.3 %collective-permute-start.3 = (bf16[768,512]{1,0:T(8,128)(2,1)S(1)}, bf16[768,512]{1,0:T(8,128)(2,1)S(1)}, u32[]{:S(2)}, u32[]{:S(2)}) collective-permute-start(bf16[768,512]{1,0:T(8,128)(2,1)S(1)} %collective-permute-done.got_ref.got_hbm), channel_id=1, source_target_pairs={{0,8},{8,0},{16,24},{24,16},{32,40},{40,32},{48,56},{56,48},{64,72... | collective-permute-start | bytes 2359304 | tf_op jit(solution)/shard_map/ppermute | solution.py:444
  30.7 18.5 %collective-permute-start.2 = (bf16[4,46,16,128]{3,2,1,0:T(8,128)(2,1)S(1)}, bf16[4,46,16,128]{3,2,1,0:T(8,128)(2,1)S(1)}, u32[]{:S(2)}, u32[]{:S(2)}) collective-permute-start(bf16[4,46,16,128]{3,2,1,0:T(8,128)(2,1)S(1)} %all-to-all-done.mine), channel_id=1, source_target_pairs={{0,68},{1,69},{2,70},{3,71},{4,64},{5,65},{6,66},{7,67},{8,76},{9,... | collective-permute-start | bytes 2261000 | tf_op jit(solution)/shard_map/ppermute | solution.py:487
  52.7 25.6 %copy-start.19 = (bf16[2,512,512]{2,1,0:T(8,128)(2,1)S(1)}, bf16[2,512,512]{2,1,0:T(8,128)(2,1)}, u32[]{:S(2)}) copy-start(bf16[2,512,512]{2,1,0:T(8,128)(2,1)} %get-tuple-element.51) | copy-start | bytes 3145732
  52.8 11.4 %all-to-all-start.1 = ((bf16[4,208,256]{2,1,0:T(8,128)(2,1)}), bf16[4,208,256]{2,1,0:T(8,128)(2,1)S(1)}, u32[]{:S(2)}, u32[]{:S(2)}) async-start(bf16[4,208,256]{2,1,0:T(8,128)(2,1)} %get-tuple-element.50), calls=%async_computation.1 | async-start | bytes 851968 | tf_op jit(solution)/shard_map/all_to_all | solution.py:448
  57.1 12.7 %collective-permute-start.4 = (bf16[512,512]{1,0:T(8,128)(2,1)}, bf16[512,512]{1,0:T(8,128)(2,1)S(1)}, u32[]{:S(2)}, u32[]{:S(2)}) collective-permute-start(bf16[512,512]{1,0:T(8,128)(2,1)} %get-tuple-element.48), channel_id=1, source_target_pairs={{0,68},{1,69},{2,70},{3,71},{4,64},{5,65},{6,66},{7,67},{8,76},{9,... | collective-permute-start | bytes 1572872 | tf_op jit(solution)/shard_map/ppermute | solution.py:516
  65.1 9.9 %all-to-all-start.2 = ((bf16[4,208,256]{2,1,0:T(8,128)(2,1)}), bf16[4,208,256]{2,1,0:T(8,128)(2,1)S(1)}, u32[]{:S(2)}, u32[]{:S(2)}) async-start(bf16[4,208,256]{2,1,0:T(8,128)(2,1)} %broadcast_in_dim.37), calls=%async_computation.2 | async-start | bytes 851968 | tf_op jit(solution)/shard_map/all_to_all | solution.py:448
  69.8 10.1 %copy-start.6 = (bf16[512,512]{1,0:T(8,128)(2,1)}, bf16[512,512]{1,0:T(8,128)(2,1)S(1)}, u32[]{:S(2)}) copy-start(bf16[512,512]{1,0:T(8,128)(2,1)S(1)} %collective-permute-done.4.got1_hbm.got_hbm) | copy-start | bytes 1572868
  74.9 4.9 %copy-start.9 = (bf16[4,208,256]{2,1,0:T(8,128)(2,1)}, bf16[4,208,256]{2,1,0:T(8,128)(2,1)S(1)}, u32[]{:S(2)}) copy-start(bf16[4,208,256]{2,1,0:T(8,128)(2,1)S(1)} %all-to-all-done.2.r_ref) | copy-start | bytes 1277956
  74.9 4.9 %collective-permute-start.6 = (bf16[512,512]{1,0:T(8,128)(2,1)S(1)}, bf16[512,512]{1,0:T(8,128)(2,1)S(1)}, u32[]{:S(2)}, u32[]{:S(2)}) collective-permute-start(bf16[512,512]{1,0:T(8,128)(2,1)S(1)} %collective-permute-done.4.got1_hbm.got_hbm), channel_id=1, source_target_pairs={{0,8},{8,0},{16,24},{24,16},{32,40},{40,32},{48,56},{56,48},{64,72... | collective-permute-start | bytes 1572872 | tf_op jit(solution)/shard_map/ppermute | solution.py:444
  78.3 24.8 %collective-permute-start.5 = (bf16[2,512,512]{2,1,0:T(8,128)(2,1)S(1)}, bf16[2,512,512]{2,1,0:T(8,128)(2,1)S(1)}, u32[]{:S(2)}, u32[]{:S(2)}) collective-permute-start(bf16[2,512,512]{2,1,0:T(8,128)(2,1)S(1)} %copy-done.19), channel_id=1, source_target_pairs={{0,68},{1,69},{2,70},{3,71},{4,64},{5,65},{6,66},{7,67},{8,76},{9,... | collective-permute-start | bytes 3145736 | tf_op jit(solution)/shard_map/ppermute | solution.py:527
  97.2 10.2 %all-to-all-start.4 = ((bf16[4,208,256]{2,1,0:T(8,128)(2,1)}), bf16[4,208,256]{2,1,0:T(8,128)(2,1)S(1)}, u32[]{:S(2)}, u32[]{:S(2)}) async-start(bf16[4,208,256]{2,1,0:T(8,128)(2,1)} %broadcast_in_dim.39), calls=%async_computation.4 | async-start | bytes 851968 | tf_op jit(solution)/shard_map/all_to_all | solution.py:448
  103.2 9.1 %copy-start = (bf16[2,512,512]{2,1,0:T(8,128)(2,1)}, bf16[2,512,512]{2,1,0:T(8,128)(2,1)S(1)}, u32[]{:S(2)}) copy-start(bf16[2,512,512]{2,1,0:T(8,128)(2,1)S(1)} %collective-permute-done.5.got1_hbm.got_hbm) | copy-start | bytes 3145732
  107.4 4.9 %copy-start.10 = (bf16[4,208,256]{2,1,0:T(8,128)(2,1)}, bf16[4,208,256]{2,1,0:T(8,128)(2,1)S(1)}, u32[]{:S(2)}) copy-start(bf16[4,208,256]{2,1,0:T(8,128)(2,1)S(1)} %all-to-all-done.4.r_ref) | copy-start | bytes 1277956
  107.4 4.9 %collective-permute-start.7 = (bf16[2,512,512]{2,1,0:T(8,128)(2,1)S(1)}, bf16[2,512,512]{2,1,0:T(8,128)(2,1)S(1)}, u32[]{:S(2)}, u32[]{:S(2)}) collective-permute-start(bf16[2,512,512]{2,1,0:T(8,128)(2,1)S(1)} %collective-permute-done.5.got1_hbm.got_hbm), channel_id=1, source_target_pairs={{0,8},{8,0},{16,24},{24,16},{32,40},{40,32},{48,56},{56,48},{64,72... | collective-permute-start | bytes 3145736 | tf_op jit(solution)/shard_map/ppermute | solution.py:444
  151.8 18.5 %copy-start.17 = (f32[1920]{0:T(1024)S(1)}, f32[1920]{0:T(1024)}, u32[]{:S(2)}) copy-start(f32[1920]{0:T(1024)} %param.16) | copy-start | bytes 23044
  151.8 19.1 %copy-start.18 = (s32[1024]{0:T(1024)S(1)}, s32[1024]{0:T(1024)}, u32[]{:S(2)}) copy-start(s32[1024]{0:T(1024)} %param.10) | copy-start | bytes 12292
  151.9 20.8 %copy-start.5 = (bf16[1920,2,384]{2,1,0:T(2,128)(2,1)S(1)}, bf16[1920,2,384]{2,1,0:T(2,128)(2,1)}, u32[]{:S(2)}) copy-start(bf16[1920,2,384]{2,1,0:T(2,128)(2,1)} %param.17) | copy-start | bytes 8847364
  164.0 20.0 %all-to-all-start.9 = ((bf16[8,128,256]{2,1,0:T(8,128)(2,1)}), bf16[8,128,256]{2,1,0:T(8,128)(2,1)S(1)}, u32[]{:S(2)}, u32[]{:S(2)}) async-start(bf16[8,128,256]{2,1,0:T(8,128)(2,1)} %cond_end.1), calls=%async_computation.9 | async-start | bytes 1048576 | tf_op jit(solution)/shard_map/all_to_all | solution.py:448
  202.2 16.3 %collective-permute-start.8 = (bf16[512,512]{1,0:T(8,128)(2,1)}, bf16[512,512]{1,0:T(8,128)(2,1)S(1)}, u32[]{:S(2)}, u32[]{:S(2)}) collective-permute-start(bf16[512,512]{1,0:T(8,128)(2,1)} %get-tuple-element.65.kv0_ref), channel_id=1, source_target_pairs={{0,16},{8,24},{16,32},{24,40},{32,48},{40,56},{48,64},{56,72},{64,... | collective-permute-start | bytes 1572872 | tf_op jit(solution)/shard_map/ppermute | solution.py:553
  204.3 14.2 %copy-start.15 = (bf16[512,512]{1,0:T(8,128)(2,1)S(1)}, bf16[512,512]{1,0:T(8,128)(2,1)}, u32[]{:S(2)}) copy-start(bf16[512,512]{1,0:T(8,128)(2,1)} %get-tuple-element.65.kv0_ref) | copy-start | bytes 1572868
  218.5 11.4 %copy-start.8 = (bf16[512,512]{1,0:T(8,128)(2,1)}, bf16[512,512]{1,0:T(8,128)(2,1)S(1)}, u32[]{:S(2)}) copy-start(bf16[512,512]{1,0:T(8,128)(2,1)S(1)} %collective-permute-done.8.far_ref) | copy-start | bytes 1572868
  218.6 11.3 %collective-permute-start.10 = (bf16[512,512]{1,0:T(8,128)(2,1)S(1)}, bf16[512,512]{1,0:T(8,128)(2,1)S(1)}, u32[]{:S(2)}, u32[]{:S(2)}) collective-permute-start(bf16[512,512]{1,0:T(8,128)(2,1)S(1)} %broadcast_select_fusion.1), channel_id=1, source_target_pairs={{0,8},{8,0},{16,24},{24,16},{32,40},{40,32},{48,56},{56,48},{64,72... | collective-permute-start | bytes 1572872 | tf_op jit(solution)/shard_map/ppermute | solution.py:444
  221.1 18.1 %collective-permute-start.9 = (bf16[512,512]{1,0:T(8,128)(2,1)}, bf16[512,512]{1,0:T(8,128)(2,1)S(1)}, u32[]{:S(2)}, u32[]{:S(2)}) collective-permute-start(bf16[512,512]{1,0:T(8,128)(2,1)} %get-tuple-element.68.kv1_ref), channel_id=1, source_target_pairs={{0,16},{8,24},{16,32},{24,40},{32,48},{40,56},{48,64},{56,72},{64,... | collective-permute-start | bytes 1572872 | tf_op jit(solution)/shard_map/ppermute | solution.py:553
  229.9 9.4 %copy-start.13 = (bf16[512,512]{1,0:T(8,128)(2,1)S(1)}, bf16[512,512]{1,0:T(8,128)(2,1)}, u32[]{:S(2)}) copy-start(bf16[512,512]{1,0:T(8,128)(2,1)} %get-tuple-element.68.kv1_ref) | copy-start | bytes 1572868
  239.3 2.3 collective-permute-start.11
  (8 other events, 11.6 us)
Sparse Core Ops, SparseCore 0:
  52.9 135.1 all-gather.2

commit v4 on v3

--- a/solution.py
+++ b/solution.py
@@ -201,11 +201,6 @@
     finish(copies)
 
 
-def join_kernel(mine, others, out):
-    out[:4] = mine[...]
-    out[4:] = others[...]
-
-
 def call(body, outs, scratch=(), smem=1, n=0, hbm=0, after=0, flops=10**9, name=None):
     def spec(space):
         return pl.BlockSpec(memory_space=space)
@@ -231,21 +226,22 @@
 CHUNKS = ((0, 4), (4, 4), (8, 4), (12, 3))
 
 
-def frames_kernel(pair, info, codes_ref, hf_ref, gain_ref, qkv_hbm, full_ref, q_ref, kv_ref, weights, table, qkv, hf, rows, x, xn, sems, table_sems, qkv_sem):
+def frames_kernel(pair, info, codes_ref, hf_ref, gain_ref, qkv_hbm, own_hbm, other_hbm, q_ref, kv_ref, weights, table, qkv, hf, rows, x, xn, sems, table_sems, qkv_sem):
     def weight_copies(phase):
         return [
             pltpu.make_async_copy(
-                full_ref.at[pl.ds(part * 4 ^ info[3], 4), pair, t ^ info[3], pl.ds(phase * BLOCKS, BLOCKS)],
-                weights.at[phase, t, pl.ds(part * 4, 4)],
-                sems.at[phase, part, t],
+                full.at[pl.ds(part * 4 ^ info[3], 4), pair, y, pl.ds(phase * BLOCKS, BLOCKS)],
+                weights.at[phase, half, y, pl.ds(part * 4, 4)],
+                sems.at[phase, half, part, y],
             )
+            for half, full in enumerate((own_hbm, other_hbm))
             for part in range(2)
-            for t in range(8)
+            for y in range(4)
         ]
 
     def product(phase):
         for first, size in CHUNKS:
-            w = [weights[phase, :, :, block].reshape(C, 128) for block in range(first, first + size)]
+            w = [weights[phase, :, :, :, block].reshape(C, 128) for block in range(first, first + size)]
             x[phase, :, first * 128 : (first + size) * 128] = dot(hf[...], jnp.concatenate(w, axis=1))
 
     def norm(phase):
@@ -277,8 +273,9 @@
 
     table_copies = [
         pltpu.make_async_copy(
-            full_ref.at[:, part, :, pl.ds(UP_BLOCKS, 16)], table.at[:, part], table_sems.at[part]
+            full.at[:, part, :, pl.ds(UP_BLOCKS, 16)], table.at[half, :, part], table_sems.at[half, part]
         )
+        for half, full in enumerate((own_hbm, other_hbm))
         for part in range(2)
     ]
     qkv_copy = pltpu.make_async_copy(qkv_hbm, qkv, qkv_sem)
@@ -286,57 +283,59 @@
     start(weight_copies(0))
     start(weight_copies(1))
     qkv_copy.start()
-    for half in range(2):
-        for j in range(8):
-            at = 0 if j // 4 == half else 128
-            hf[half * 128 : half * 128 + 128, j * 128 : j * 128 + 128] = hf_ref[
-                half * 4 + j % 4, :, at : at + 128
-            ]
+    for rows_of in range(2):
+        for half in range(2):
+            at = pl.multiple_of(((info[3] // 4) ^ half ^ rows_of) * 128, 128)
+            for y in range(4):
+                j = half * 4 + y
+                hf[rows_of * 128 : rows_of * 128 + 128, j * 128 : j * 128 + 128] = hf_ref[
+                    rows_of * 4 + y, :, pl.ds(at, 128)
+                ]
     flat = table.reshape(VOCAB, 16, 128)
+
+    def look_up(phase):
+        for row in range(phase * 256, phase * 256 + 256):
+            rows[row] = flat[codes_ref[pair * 512 + row]].astype(F32)
+
     finish(table_copies)
-
-    def look_up(i, carry):
-        for j in range(8):
-            row = i * 8 + j
-            rows[row] = flat[codes_ref[pair * 512 + row]].astype(F32)
-        return carry
-
-    lax.fori_loop(0, 64, look_up, 0)
     finish(weight_copies(0))
+    look_up(0)
     product(0)
     finish(weight_copies(1))
     qkv_copy.wait()
+    look_up(1)
+    product(1)
     norm(0)
-    product(1)
     project(0)
     norm(1)
     project(1)
 
 
-def frames(pair, info, codes, hf, gain, qkv, full):
+def frames(pair, info, codes, hf, gain, qkv, full_own, full_other):
     vm = pl.BlockSpec(memory_space=pltpu.VMEM)
     sm = pl.BlockSpec(memory_space=pltpu.SMEM)
+    any_space = pl.BlockSpec(memory_space=pl.ANY)
     return pl.pallas_call(
         functools.partial(frames_kernel, pair),
         out_shape=(shape(512, 256), shape(512, 512)),
-        in_specs=[sm, sm, vm, vm, pl.BlockSpec(memory_space=pl.ANY), pl.BlockSpec(memory_space=pltpu.HBM)],
+        in_specs=[sm, sm, vm, vm, any_space, any_space, any_space],
         out_specs=(vm, vm),
         scratch_shapes=[
-            pltpu.VMEM((2, 8, 8, BLOCKS, 16, 128), BF),
-            pltpu.VMEM((8, 2, 8, 16, 16, 128), BF),
+            pltpu.VMEM((2, 2, 4, 8, BLOCKS, 16, 128), BF),
+            pltpu.VMEM((2, 8, 2, 4, 16, 16, 128), BF),
             pltpu.VMEM((D, 768), BF),
             pltpu.VMEM((256, C), BF),
             pltpu.VMEM((512, 16, 128), F32),
             pltpu.VMEM((2, 256, D), F32),
             pltpu.VMEM((2, 256, D), BF),
-            pltpu.SemaphoreType.DMA((2, 2, 8)),
-            pltpu.SemaphoreType.DMA((2,)),
+            pltpu.SemaphoreType.DMA((2, 2, 2, 4)),
+            pltpu.SemaphoreType.DMA((2, 2)),
             pltpu.SemaphoreType.DMA,
         ],
         compiler_params=params(),
         cost_estimate=cost(4 * 10**9, 20 << 20),
         name="frames",
-    )(info, codes, hf, gain, qkv, full)
+    )(info, codes, hf, gain, qkv, full_own, full_other)
 
 
 SCALE = 128**-0.5 * 1.4426950408889634
@@ -347,11 +346,11 @@
 
 
 def fold(q_refs, kv, seen_of, old_of, put):
-    def body(head, carry):
-        k = kv[:, pl.ds(pl.multiple_of(head * 128, 128), 128)]
-        v = kv[:, pl.ds(pl.multiple_of(256 + head * 128, 128), 128)]
+    for head in range(2):
+        cols = slice(head * 128, head * 128 + 128)
+        k = kv[:, cols]
+        v = kv[:, 256 + head * 128 : 384 + head * 128]
         v = jnp.concatenate([v, jnp.ones(v.shape, BF)], axis=1)
-        cols = pl.ds(pl.multiple_of(head * 128, 128), 128)
         for phase in range(4):
             s = scores_of(q_refs[phase // 2][phase % 2 * 256 : phase % 2 * 256 + 256, cols], k)
             s = jnp.where(seen_of(phase), s, -1e30)
@@ -363,9 +362,6 @@
                 top = jnp.maximum(old[0], top)
                 p = jnp.exp2((s - top) * SCALE).astype(BF)
                 put(head, phase, top, old[1] * jnp.exp2((old[0] - top) * SCALE) + dot(p, v))
-        return carry
-
-    lax.fori_loop(0, 2, body, 0)
 
 
 def join_keys(kv, first, second):
@@ -446,6 +442,10 @@
 
 def exchange(value, axis="tensor", groups=None):
     return lax.all_to_all(value, axis, 0, 0, axis_index_groups=groups, tiled=True)
+
+
+def gathered(parts):
+    return lax.all_gather(parts, "song", axis=0, tiled=False).reshape(8, 2, 4, PART, 16, 128)
 
 
 def on_device(
@@ -484,6 +484,7 @@
     edge = jnp.where(x_hi == 0, upper_codes[-40:], upper_codes[:40])
     edge = lax.ppermute(edge, EVERY, song_neighbours())
     mine, got0, edge = lax.optimization_barrier((mine, got0, edge))
+    full_own = gathered(mine)
     others = lax.ppermute(mine, EVERY, other_half())
     sib0 = to_sibling(got0)
     codes = jnp.where(
@@ -509,13 +510,12 @@
         name="pack_later",
     )(info, dilated_weight, mixing_weight)
 
-    others, pack1, terms = lax.optimization_barrier((others, pack1, terms))
-    both = call(join_kernel, shape(8, PART, 16, 128), smem=0, n=2, name="join")(mine, others)
-    full = lax.all_gather(both, "song", axis=0, tiled=False)
-    full = full.reshape(8, 2, 8, PART, 16, 128)
-    got1 = lax.ppermute(pack1, EVERY, other_half())
     for level in range(4):
         terms = exchange(terms, groups=Y_GROUPS)
+        if level == 0:
+            others, pack1, terms = lax.optimization_barrier((others, pack1, terms))
+            full_other = gathered(others)
+            got1 = lax.ppermute(pack1, EVERY, other_half())
         total = terms[0].astype(F32)
         for y in range(1, 4):
             total = total + terms[y].astype(F32)
@@ -545,16 +545,18 @@
     hf = exchange(spread)
 
     mid = middle_codes.reshape(256, 4).T.reshape(1024)
-    mid = ((mid % 256) // 16 * 128 + mid // 256 * 16 + mid % 16) ^ (x_hi * (8 * 128 + 4 * 16))
+    mid = (mid // 1024 * 1024 + mid % 256 // 16 * 64 + mid // 256 % 4 * 16 + mid % 16) ^ (
+        x_hi * (1024 + 8 * 64)
+    )
     gain = norm_gain[None]
     qkv = qkv_weight.reshape(D, 768)
 
     def from_two_back(value):
         return lax.ppermute(value, "song", [(i, i + 2) for i in range(14)])
 
-    q0, kv0 = frames(0, info, mid, hf, gain, qkv, full)
+    q0, kv0 = frames(0, info, mid, hf, gain, qkv, full_own, full_other)
     far0 = from_two_back(kv0)
-    q1, kv1 = frames(1, info, mid, hf, gain, qkv, full)
+    q1, kv1 = frames(1, info, mid, hf, gain, qkv, full_own, full_other)
     far1 = from_two_back(kv1)
     state = (shape(2, 4, 256, 256, dtype=F32), shape(2, 4, 256, 1, dtype=F32))
     keys = pltpu.VMEM((1024, 512), BF)

time: 260 us -> 249 us (0.958)
  blocking collectives: 50.5 us -> 62 us
  waiting for transfers between devices: 51.8 us -> 43.2 us
  starting transfers between devices: 46.2 us -> 40.4 us
  Pallas kernels: 80.3 us -> 76.2 us
    all_to_all x5 -> x6, blocking collectives: 50.5 us -> 62 us  [exchange(): lax.all_to_all(value, axis, 0, 0, axis_index_groups=groups, tiled=True)]
    all_to_all x5 -> x4, waiting for transfers between devices: 29 us -> 19 us  [exchange(): lax.all_to_all(value, axis, 0, 0, axis_index_groups=groups, tiled=True)]
    ppermute x1, waiting for transfers between devices: 7.1 us -> 3.28 us  [on_device(): others = lax.ppermute(mine, EVERY, other_half())]
    all_gather x1 -> x2, waiting for transfers between devices: 4.14 us -> 7.6 us  [gathered(): lax.all_gather(parts, 'song', axis=0, tiled=False)]
    all_to_all x5 -> x4, starting transfers between devices: 21.8 us -> 18.9 us  [exchange(): lax.all_to_all(value, axis, 0, 0, axis_index_groups=groups, tiled=True)]
    pallas_call x1 -> x0, Pallas kernels: 2.66 us -> none  [on_device(): call(join_kernel, shape(8, PART, 16, 128), smem=0, n=2, name='join')]
    unnamed x46 -> x42, local copies, waits for them, and re-layouts: 7.47 us -> 6.5 us
  transfers between devices with their start and end apart: 18 -> 18, of which waited for: 15 -> 14; matrix products, arithmetic and copies ran while one was open for 3% -> 3% of each run, Pallas kernels for 21% -> 21%
where the time goes in v4:
time: 249 us; the launch traced here: 248 us
  Pallas kernels  76.2 us (31%)
  blocking collectives  62 us (25%)
  waiting for transfers between devices  43.2 us (17%)
  starting transfers between devices  40.4 us (16%)
  between operations  13.7 us (6%)
  local copies, waits for them, and re-layouts  10.7 us (4%)
    all_to_all x6, blocking collectives, exchange(): lax.all_to_all(value, axis, 0, 0, axis_index_groups=groups, tiled=True)  62 us
    pallas_call x2, Pallas kernels, frames(): pl.pallas_call(functools.partial(frames_kernel, pair), out_shape=(shape(5...  28.9 us
    all_to_all x4, waiting for transfers between devices, exchange(): lax.all_to_all(value, axis, 0, 0, axis_index_groups=groups, tiled=True)  19 us
    all_to_all x4, starting transfers between devices, exchange(): lax.all_to_all(value, axis, 0, 0, axis_index_groups=groups, tiled=True)  18.9 us
    pallas_call x3, Pallas kernels, on_device(): call(functools.partial(middle_kernel, level), (shape(ROWS[level + 1], 256...  12.3 us
    ppermute x5, starting transfers between devices, to_sibling(): return lax.ppermute(value, 'song', [(i, i ^ 1) for i in range(16)])  8.42 us
    all_gather x2, waiting for transfers between devices, gathered(): lax.all_gather(parts, 'song', axis=0, tiled=False)  7.6 us
    pallas_call x1, Pallas kernels, on_device(): call(functools.partial(past_kernel, False), state, [keys], n=6, flops=10...  7.54 us
  transfers between devices with their start and end apart: 18, of which 14 were waited for; matrix products, arithmetic and copies ran while one was open for 3% of the time, Pallas kernels for 21%

profile of v4, /device:TPU:3, one launch (start us, length us, event | category | flops | bytes accessed | tf_op | source)
XLA Modules:
  0.0 247.9 jit_solution(4102117214174753928)
XLA Ops:
  7.2 3.3 %pack.1 = (bf16[768,512]{1,0:T(8,128)(2,1)}, bf16[4,46,16,128]{3,2,1,0:T(8,128)(2,1)}) custom-call(s32[6]{0:T(128)} %stack.27.info, bf16[4,3,128,1024]{3,2,1,0:T(8,128)(2,1)} %dil_hbm.11, bf16[4,1024,128]{2,1,0:T(8,128)(2,1)} %mix_hbm.11, bf16[2048,128]{1,0:T(8,128)(2,1)} %table_ref.1, bf16[128,7680]{1,0:T(8,128)(2,1)} %up_hbm.1, bf16[256,1920]{1,0:T(8,128)(2,1)} %mid_hbm.1), custom_call_target="tpu_custom_call" | custom-call | flops 1000000000 | bytes 4194304 | tf_op jit(solution)/shard_map/pack/pallas_call | solution.py:470
  11.8 4.2 %all-to-all-start = ((bf16[4,46,16,128]{3,2,1,0:T(8,128)(2,1)}), bf16[4,46,16,128]{3,2,1,0:T(8,128)(2,1)S(1)}, u32[]{:S(2)}, u32[]{:S(2)}) async-start(bf16[4,46,16,128]{3,2,1,0:T(8,128)(2,1)} %get-tuple-element.41), calls=%async_computation | async-start | bytes 1507328 | tf_op jit(solution)/shard_map/all_to_all | solution.py:444
  16.1 4.7 %collective-permute-start.1 = (s32[40]{0:T(128)S(1)}, s32[40]{0:T(128)S(1)}, u32[]{:S(2)}, u32[]{:S(2)}) collective-permute-start(s32[40]{0:T(128)S(1)} %broadcast_select_fusion.3), channel_id=1, source_target_pairs={{0,8},{1,9},{2,10},{3,11},{8,16},{9,17},{10,18},{11,19},{16,24},{1... | collective-permute-start | bytes 488 | tf_op jit(solution)/shard_map/ppermute | solution.py:485
  21.4 5.3 %all-to-all-done = bf16[4,46,16,128]{3,2,1,0:T(8,128)(2,1)S(1)} async-done(((bf16[4,46,16,128]{3,2,1,0:T(8,128)(2,1)}), bf16[4,46,16,128]{3,2,1,0:T(8,128)(2,1)S(1)}, u32[]{:S(2)}, u32[]{:S(2)}) %all-to-all-start) | async-done | bytes 753696 | tf_op jit(solution)/shard_map/all_to_all | solution.py:444
  26.7 2.5 %collective-permute-done.got_ref.got_hbm = bf16[768,512]{1,0:T(8,128)(2,1)S(1)} collective-permute-done((bf16[768,512]{1,0:T(8,128)(2,1)}, bf16[768,512]{1,0:T(8,128)(2,1)S(1)}, u32[]{:S(2)}, u32[]{:S(2)}) %collective-permute-start) | collective-permute-done | bytes 786464 | tf_op jit(solution)/shard_map/ppermute | solution.py:482
  34.1 4.7 %cond0.1 = (f32[208,256]{1,0:T(8,128)}, bf16[4,208,256]{2,1,0:T(8,128)(2,1)}) custom-call(s32[6]{0:T(128)} %stack.27.info, s32[208,1]{1,0:T(8,128)} %broadcast_select_fusion.2.codes_ref, bf16[2048,128]{1,0:T(8,128)(2,1)} %table_ref.1, bf16[4,3,128,1024]{3,2,1,0:T(8,128)(2,1)} %dil_hbm.11, bf16[768,512]{1,0:T(8,128)(2,1)} %copy-done.3, bf16[768,512]{1,0:T(8,128)(2,1)} %copy-done.4), custom_call_target="tpu_custom_call" | custom-call | flops 1000000000 | bytes 4194304 | tf_op jit(solution)/shard_map/cond0/pallas_call | solution.py:496
  38.8 4.2 %all-to-all-start.1 = ((bf16[4,208,256]{2,1,0:T(8,128)(2,1)}), bf16[4,208,256]{2,1,0:T(8,128)(2,1)S(1)}, u32[]{:S(2)}, u32[]{:S(2)}) async-start(bf16[4,208,256]{2,1,0:T(8,128)(2,1)} %get-tuple-element.47), calls=%async_computation.1 | async-start | bytes 851968 | tf_op jit(solution)/shard_map/all_to_all | solution.py:444
  43.0 3.4 %pack_later.1 = (bf16[512,512]{1,0:T(8,128)(2,1)}, bf16[2,512,512]{2,1,0:T(8,128)(2,1)}) custom-call(s32[6]{0:T(128)} %stack.27.info, bf16[4,3,128,1024]{3,2,1,0:T(8,128)(2,1)} %dil_hbm.11, bf16[4,1024,128]{2,1,0:T(8,128)(2,1)} %mix_hbm.11), custom_call_target="tpu_custom_call" | custom-call | flops 1000000000 | bytes 4194304 | tf_op jit(solution)/shard_map/pack_later/pallas_call | solution.py:505
  46.4 3.3 %collective-permute-done.2 = bf16[4,46,16,128]{3,2,1,0:T(8,128)(2,1)S(1)} collective-permute-done((bf16[4,46,16,128]{3,2,1,0:T(8,128)(2,1)}, bf16[4,46,16,128]{3,2,1,0:T(8,128)(2,1)S(1)}, u32[]{:S(2)}, u32[]{:S(2)}) %collective-permute-start.2) | collective-permute-done | bytes 753696 | tf_op jit(solution)/shard_map/ppermute | solution.py:488
  52.0 11.3 %all_to_all.50.r_ref = bf16[4,208,256]{2,1,0:T(8,128)(2,1)} all-to-all(bf16[4,208,256]{2,1,0:T(8,128)(2,1)S(1)} %broadcast_in_dim.37), channel_id=1, replica_groups={{0,1,2,3},{4,5,6,7},{8,9,10,11},{12,13,14,15},{16,17,18,19},{20,21,22,2..., dimensions={0} | all-to-all | bytes 851968 | tf_op jit(solution)/shard_map/all_to_all | solution.py:444
  67.9 4.2 %cond.3 = (f32[208,256]{1,0:T(8,128)}, bf16[4,208,256]{2,1,0:T(8,128)(2,1)}) custom-call(s32[6]{0:T(128)} %stack.27.info, bf16[4,208,256]{2,1,0:T(8,128)(2,1)} %all_to_all.50.r_ref, f32[208,256]{1,0:T(8,128)} %get-tuple-element.53.h_ref, bf16[4,1024,128]{2,1,0:T(8,128)(2,1)} %mix_hbm.11, bf16[768,512]{1,0:T(8,128)(2,1)} %copy-done.3, ...), custom_call_target="tpu_custom_call" | custom-call | flops 1000000000 | bytes 4194304 | tf_op jit(solution)/shard_map/cond/pallas_call | solution.py:533
  72.1 11.7 %all_to_all.51 = bf16[4,208,256]{2,1,0:T(8,128)(2,1)S(1)} all-to-all(bf16[4,208,256]{2,1,0:T(8,128)(2,1)} %get-tuple-element.55), channel_id=1, replica_groups={{0,1,2,3},{4,5,6,7},{8,9,10,11},{12,13,14,15},{16,17,18,19},{20,21,22,2..., dimensions={0} | all-to-all | bytes 851968 | tf_op jit(solution)/shard_map/all_to_all | solution.py:444
  84.7 3.5 %all-to-all-start.4 = ((bf16[4,208,256]{2,1,0:T(8,128)(2,1)}), bf16[4,208,256]{2,1,0:T(8,128)(2,1)S(1)}, u32[]{:S(2)}, u32[]{:S(2)}) async-start(bf16[4,208,256]{2,1,0:T(8,128)(2,1)} %broadcast_in_dim.39), calls=%async_computation.4 | async-start | bytes 851968 | tf_op jit(solution)/shard_map/all_to_all | solution.py:444
  88.2 2.5 %collective-permute-done.5.got1_hbm.got_hbm = bf16[2,512,512]{2,1,0:T(8,128)(2,1)S(1)} collective-permute-done((bf16[2,512,512]{2,1,0:T(8,128)(2,1)}, bf16[2,512,512]{2,1,0:T(8,128)(2,1)S(1)}, u32[]{:S(2)}, u32[]{:S(2)}) %collective-permute-start.5) | collective-permute-done | bytes 1048608 | tf_op jit(solution)/shard_map/ppermute | solution.py:527
  90.7 4.0 %all-to-all-done.4.r_ref = bf16[4,208,256]{2,1,0:T(8,128)(2,1)S(1)} async-done(((bf16[4,208,256]{2,1,0:T(8,128)(2,1)}), bf16[4,208,256]{2,1,0:T(8,128)(2,1)S(1)}, u32[]{:S(2)}, u32[]{:S(2)}) %all-to-all-start.4) | async-done | bytes 426016 | tf_op jit(solution)/shard_map/all_to_all | solution.py:444
  94.7 2.8 %collective-permute-start.7 = (bf16[2,512,512]{2,1,0:T(8,128)(2,1)S(1)}, bf16[2,512,512]{2,1,0:T(8,128)(2,1)S(1)}, u32[]{:S(2)}, u32[]{:S(2)}) collective-permute-start(bf16[2,512,512]{2,1,0:T(8,128)(2,1)S(1)} %collective-permute-done.5.got1_hbm.got_hbm), channel_id=1, source_target_pairs={{0,8},{8,0},{16,24},{24,16},{32,40},{40,32},{48,56},{56,48},{64,72... | collective-permute-start | bytes 3145736 | tf_op jit(solution)/shard_map/ppermute | solution.py:440
  97.5 2.6 %collective-permute-done.7.sib1_hbm.sib_hbm = bf16[2,512,512]{2,1,0:T(8,128)(2,1)S(1)} collective-permute-done((bf16[2,512,512]{2,1,0:T(8,128)(2,1)S(1)}, bf16[2,512,512]{2,1,0:T(8,128)(2,1)S(1)}, u32[]{:S(2)}, u32[]{:S(2)}) %collective-permute-start.7) | collective-permute-done | bytes 1048608 | tf_op jit(solution)/shard_map/ppermute | solution.py:440
  101.0 4.1 %cond.4 = (f32[208,256]{1,0:T(8,128)}, bf16[4,192,256]{2,1,0:T(8,128)(2,1)}) custom-call(s32[6]{0:T(128)} %stack.27.info, bf16[4,208,256]{2,1,0:T(8,128)(2,1)} %copy-done.10, f32[208,256]{1,0:T(8,128)} %get-tuple-element.57.h_ref, bf16[4,1024,128]{2,1,0:T(8,128)(2,1)} %mix_hbm.11, bf16[512,512]{1,0:T(8,128)(2,1)} %copy-done.7, bf16[512,512]{1,0:T(8,128)(2,1)} %copy-done.8, ...), custom_call_target="tpu_custom_call" | custom-call | flops 1000000000 | bytes 4194304 | tf_op jit(solution)/shard_map/cond/pallas_call | solution.py:533
  105.2 11.3 %all_to_all.52 = bf16[4,192,256]{2,1,0:T(8,128)(2,1)S(1)} all-to-all(bf16[4,192,256]{2,1,0:T(8,128)(2,1)} %get-tuple-element.59), channel_id=1, replica_groups={{0,1,2,3},{4,5,6,7},{8,9,10,11},{12,13,14,15},{16,17,18,19},{20,21,22,2..., dimensions={0} | all-to-all | bytes 786432 | tf_op jit(solution)/shard_map/all_to_all | solution.py:444
  116.5 10.0 %all_to_all.53.r_ref = bf16[4,192,256]{2,1,0:T(8,128)(2,1)} all-to-all(bf16[4,192,256]{2,1,0:T(8,128)(2,1)S(1)} %broadcast_in_dim.41), channel_id=1, replica_groups={{0,1,2,3},{4,5,6,7},{8,9,10,11},{12,13,14,15},{16,17,18,19},{20,21,22,2..., dimensions={0} | all-to-all | bytes 786432 | tf_op jit(solution)/shard_map/all_to_all | solution.py:444
  126.5 4.0 %cond.5 = (f32[192,256]{1,0:T(8,128)}, bf16[4,128,256]{2,1,0:T(8,128)(2,1)}) custom-call(s32[6]{0:T(128)} %stack.27.info, bf16[4,192,256]{2,1,0:T(8,128)(2,1)} %all_to_all.53.r_ref, f32[208,256]{1,0:T(8,128)} %get-tuple-element.60.h_ref, bf16[4,1024,128]{2,1,0:T(8,128)(2,1)} %mix_hbm.11, bf16[2,512,512]{2,1,0:T(8,128)(2,1)} %copy-done, ...), custom_call_target="tpu_custom_call" | custom-call | flops 1000000000 | bytes 4194304 | tf_op jit(solution)/shard_map/cond/pallas_call | solution.py:533
  130.5 8.9 %all_to_all.54 = bf16[4,128,256]{2,1,0:T(8,128)(2,1)S(1)} all-to-all(bf16[4,128,256]{2,1,0:T(8,128)(2,1)} %get-tuple-element.61), channel_id=1, replica_groups={{0,1,2,3},{4,5,6,7},{8,9,10,11},{12,13,14,15},{16,17,18,19},{20,21,22,2..., dimensions={0} | all-to-all | bytes 524288 | tf_op jit(solution)/shard_map/all_to_all | solution.py:444
  139.5 8.8 %all_to_all.55.r_ref = bf16[4,128,256]{2,1,0:T(8,128)(2,1)} all-to-all(bf16[4,128,256]{2,1,0:T(8,128)(2,1)S(1)} %broadcast_in_dim.43), channel_id=1, replica_groups={{0,1,2,3},{4,5,6,7},{8,9,10,11},{12,13,14,15},{16,17,18,19},{20,21,22,2..., dimensions={0} | all-to-all | bytes 524288 | tf_op jit(solution)/shard_map/all_to_all | solution.py:444
  148.4 3.2 %cond_end.1 = bf16[8,128,256]{2,1,0:T(8,128)(2,1)} custom-call(s32[6]{0:T(128)} %stack.27.info, bf16[4,128,256]{2,1,0:T(8,128)(2,1)} %all_to_all.55.r_ref, f32[192,256]{1,0:T(8,128)} %get-tuple-element.62.h_ref, bf16[4,1024,128]{2,1,0:T(8,128)(2,1)} %mix_hbm.11, bf16[2,512,512]{2,1,0:T(8,128)(2,1)} %copy-done, bf16[2,512,512]{2,1,0:T(8,128)(2,1)} %copy-done.1), custom_call_target="tpu_custom_call" | custom-call | flops 1000000000 | bytes 4194304 | tf_op jit(solution)/shard_map/cond_end/pallas_call | solution.py:542
  151.6 7.1 %all-to-all-start.9 = ((bf16[8,128,256]{2,1,0:T(8,128)(2,1)}), bf16[8,128,256]{2,1,0:T(8,128)(2,1)S(1)}, u32[]{:S(2)}, u32[]{:S(2)}) async-start(bf16[8,128,256]{2,1,0:T(8,128)(2,1)} %cond_end.1), calls=%async_computation.9 | async-start | bytes 1048576 | tf_op jit(solution)/shard_map/all_to_all | solution.py:444
  163.9 8.5 %all-to-all-done.9.hf_ref = bf16[8,128,256]{2,1,0:T(8,128)(2,1)S(1)} async-done(((bf16[8,128,256]{2,1,0:T(8,128)(2,1)}), bf16[8,128,256]{2,1,0:T(8,128)(2,1)S(1)}, u32[]{:S(2)}, u32[]{:S(2)}) %all-to-all-start.9) | async-done | bytes 524320 | tf_op jit(solution)/shard_map/all_to_all | solution.py:444
  172.4 7.6 %all-gather.7.cloned.1.call-done = bf16[64,46,16,128]{3,2,1,0:T(8,128)(2,1)} async-done(((bf16[4,46,16,128]{3,2,1,0:T(8,128)(2,1)}), bf16[64,46,16,128]{3,2,1,0:T(8,128)(2,1)}) %all-gather.7.cloned.1.call-update) | async-done | bytes 12058640 | tf_op jit(solution)/shard_map/all_gather | solution.py:448
  180.0 14.4 %frames.2 = (bf16[512,256]{1,0:T(8,128)(2,1)}, bf16[512,512]{1,0:T(8,128)(2,1)}) custom-call(s32[6]{0:T(128)} %stack.27.info, s32[1024]{0:T(1024)} %fusion.9.codes_ref, bf16[8,128,256]{2,1,0:T(8,128)(2,1)} %copy-done.2, f32[1,1920]{1,0:T(1,128)} %broadcast_in_dim.44.gain_ref, bf16[1920,768]{1,0:T(8,128)(2,1)} %bitcast.28, ...), custom_call_target="tpu_custom_call" | custom-call | flops 4000000000 | bytes 20971520 | tf_op jit(solution)/shard_map/frames/pallas_call | solution.py:318
  196.6 14.5 %frames.3 = (bf16[512,256]{1,0:T(8,128)(2,1)}, bf16[512,512]{1,0:T(8,128)(2,1)}) custom-call(s32[6]{0:T(128)} %stack.27.info, s32[1024]{0:T(1024)} %fusion.9.codes_ref, bf16[8,128,256]{2,1,0:T(8,128)(2,1)} %copy-done.2, f32[1,1920]{1,0:T(1,128)} %broadcast_in_dim.44.gain_ref, bf16[1920,768]{1,0:T(8,128)(2,1)} %bitcast.29, ...), custom_call_target="tpu_custom_call" | custom-call | flops 4000000000 | bytes 20971520 | tf_op jit(solution)/shard_map/frames/pallas_call | solution.py:318
  215.3 6.1 %own.1 = (f32[2,4,256,256]{3,2,1,0:T(8,128)}, f32[2,4,256,1]{3,2,1,0:T(8,128)}) custom-call(bf16[512,256]{1,0:T(8,128)(2,1)} %get-tuple-element.64.q0_ref, bf16[512,256]{1,0:T(8,128)(2,1)} %get-tuple-element.67.q1_ref, bf16[512,512]{1,0:T(8,128)(2,1)} %get-tuple-element.65.kv0_ref, bf16[512,512]{1,0:T(8,128)(2,1)} %get-tuple-element.68.kv1_ref), custom_call_target="tpu_custom_call" | custom-call | flops 1000000000 | bytes 4194304 | tf_op jit(solution)/shard_map/own/pallas_call | solution.py:564
  222.2 7.5 %past.1 = (f32[2,4,256,256]{3,2,1,0:T(8,128)}, f32[2,4,256,1]{3,2,1,0:T(8,128)}) custom-call(s32[6]{0:T(128)} %stack.27.info, bf16[512,256]{1,0:T(8,128)(2,1)} %get-tuple-element.64.q0_ref, bf16[512,256]{1,0:T(8,128)(2,1)} %get-tuple-element.67.q1_ref, bf16[512,512]{1,0:T(8,128)(2,1)} %copy-done.9, bf16[512,512]{1,0:T(8,128)(2,1)} %copy-done.12, ...), custom_call_target="tpu_custom_call" | custom-call | flops 1000000000 | bytes 4194304 | tf_op jit(solution)/shard_map/past/pallas_call | solution.py:566
  234.4 6.7 %past_end.1 = bf16[1024,256]{1,0:T(8,128)(2,1)} custom-call(s32[6]{0:T(128)} %stack.27.info, bf16[512,256]{1,0:T(8,128)(2,1)} %get-tuple-element.64.q0_ref, bf16[512,256]{1,0:T(8,128)(2,1)} %get-tuple-element.67.q1_ref, bf16[512,512]{1,0:T(8,128)(2,1)} %copy-done.14, bf16[512,512]{1,0:T(8,128)(2,1)} %copy-done.19, ...), custom_call_target="tpu_custom_call" | custom-call | flops 2000000000 | bytes 4194304 | tf_op jit(solution)/shard_map/past_end/pallas_call | solution.py:571
  (87 shorter events, 33.5 us)
Async XLA Ops:
  7.2 8.8 %copy-start.16 = (s32[256]{0:T(256)S(1)}, s32[256]{0:T(256)}, u32[]{:S(2)}) copy-start(s32[256]{0:T(256)} %param.9) | copy-start | bytes 3076
  10.5 18.7 %collective-permute-start = (bf16[768,512]{1,0:T(8,128)(2,1)}, bf16[768,512]{1,0:T(8,128)(2,1)S(1)}, u32[]{:S(2)}, u32[]{:S(2)}) collective-permute-start(bf16[768,512]{1,0:T(8,128)(2,1)} %get-tuple-element.42), channel_id=1, source_target_pairs={{0,68},{1,69},{2,70},{3,71},{4,64},{5,65},{6,66},{7,67},{8,76},{9,... | collective-permute-start | bytes 2359304 | tf_op jit(solution)/shard_map/ppermute | solution.py:482
  11.8 14.9 %all-to-all-start = ((bf16[4,46,16,128]{3,2,1,0:T(8,128)(2,1)}), bf16[4,46,16,128]{3,2,1,0:T(8,128)(2,1)S(1)}, u32[]{:S(2)}, u32[]{:S(2)}) async-start(bf16[4,46,16,128]{3,2,1,0:T(8,128)(2,1)} %get-tuple-element.41), calls=%async_computation | async-start | bytes 1507328 | tf_op jit(solution)/shard_map/all_to_all | solution.py:444
  16.0 156.4 %all-gather.5.cloned.1.call-start = ((), (), s32[]{:S(2)}) async-start(), calls=%async_computation.10 | async-start | bytes 12812288 | tf_op jit(solution)/shard_map/all_gather | solution.py:448
  16.1 5.4 %collective-permute-start.1 = (s32[40]{0:T(128)S(1)}, s32[40]{0:T(128)S(1)}, u32[]{:S(2)}, u32[]{:S(2)}) collective-permute-start(s32[40]{0:T(128)S(1)} %broadcast_select_fusion.3), channel_id=1, source_target_pairs={{0,8},{1,9},{2,10},{3,11},{8,16},{9,17},{10,18},{11,19},{16,24},{1... | collective-permute-start | bytes 488 | tf_op jit(solution)/shard_map/ppermute | solution.py:485
  26.7 2.5 %copy-start.5 = (bf16[4,46,16,128]{3,2,1,0:T(8,128)(2,1)}, bf16[4,46,16,128]{3,2,1,0:T(8,128)(2,1)S(1)}, u32[]{:S(2)}) copy-start(bf16[4,46,16,128]{3,2,1,0:T(8,128)(2,1)S(1)} %all-to-all-done) | copy-start | bytes 2260996
  29.2 4.0 %copy-start.3 = (bf16[768,512]{1,0:T(8,128)(2,1)}, bf16[768,512]{1,0:T(8,128)(2,1)S(1)}, u32[]{:S(2)}) copy-start(bf16[768,512]{1,0:T(8,128)(2,1)S(1)} %collective-permute-done.got_ref.got_hbm) | copy-start | bytes 2359300
  29.2 3.9 %collective-permute-start.3 = (bf16[768,512]{1,0:T(8,128)(2,1)S(1)}, bf16[768,512]{1,0:T(8,128)(2,1)S(1)}, u32[]{:S(2)}, u32[]{:S(2)}) collective-permute-start(bf16[768,512]{1,0:T(8,128)(2,1)S(1)} %collective-permute-done.got_ref.got_hbm), channel_id=1, source_target_pairs={{0,8},{8,0},{16,24},{24,16},{32,40},{40,32},{48,56},{56,48},{64,72... | collective-permute-start | bytes 2359304 | tf_op jit(solution)/shard_map/ppermute | solution.py:440
  30.9 18.7 %collective-permute-start.2 = (bf16[4,46,16,128]{3,2,1,0:T(8,128)(2,1)}, bf16[4,46,16,128]{3,2,1,0:T(8,128)(2,1)S(1)}, u32[]{:S(2)}, u32[]{:S(2)}) collective-permute-start(bf16[4,46,16,128]{3,2,1,0:T(8,128)(2,1)} %copy-done.5), channel_id=1, source_target_pairs={{0,68},{1,69},{2,70},{3,71},{4,64},{5,65},{6,66},{7,67},{8,76},{9,... | collective-permute-start | bytes 2261000 | tf_op jit(solution)/shard_map/ppermute | solution.py:488
  38.8 12.1 %all-to-all-start.1 = ((bf16[4,208,256]{2,1,0:T(8,128)(2,1)}), bf16[4,208,256]{2,1,0:T(8,128)(2,1)S(1)}, u32[]{:S(2)}, u32[]{:S(2)}) async-start(bf16[4,208,256]{2,1,0:T(8,128)(2,1)} %get-tuple-element.47), calls=%async_computation.1 | async-start | bytes 851968 | tf_op jit(solution)/shard_map/all_to_all | solution.py:444
  43.0 137.0 %all-gather.7.cloned.1.call-start = ((), (), s32[]{:S(2)}) async-start(), calls=%async_computation.11 | async-start | bytes 12812288 | tf_op jit(solution)/shard_map/all_gather | solution.py:448
  51.0 12.4 %collective-permute-start.4 = (bf16[512,512]{1,0:T(8,128)(2,1)}, bf16[512,512]{1,0:T(8,128)(2,1)S(1)}, u32[]{:S(2)}, u32[]{:S(2)}) collective-permute-start(bf16[512,512]{1,0:T(8,128)(2,1)} %get-tuple-element.48), channel_id=1, source_target_pairs={{0,68},{1,69},{2,70},{3,71},{4,64},{5,65},{6,66},{7,67},{8,76},{9,... | collective-permute-start | bytes 1572872 | tf_op jit(solution)/shard_map/ppermute | solution.py:518
  63.3 3.8 %copy-start.7 = (bf16[512,512]{1,0:T(8,128)(2,1)}, bf16[512,512]{1,0:T(8,128)(2,1)S(1)}, u32[]{:S(2)}) copy-start(bf16[512,512]{1,0:T(8,128)(2,1)S(1)} %collective-permute-done.4.got1_hbm.got_hbm) | copy-start | bytes 1572868
  63.3 3.8 %collective-permute-start.6 = (bf16[512,512]{1,0:T(8,128)(2,1)S(1)}, bf16[512,512]{1,0:T(8,128)(2,1)S(1)}, u32[]{:S(2)}, u32[]{:S(2)}) collective-permute-start(bf16[512,512]{1,0:T(8,128)(2,1)S(1)} %collective-permute-done.4.got1_hbm.got_hbm), channel_id=1, source_target_pairs={{0,8},{8,0},{16,24},{24,16},{32,40},{40,32},{48,56},{56,48},{64,72... | collective-permute-start | bytes 1572872 | tf_op jit(solution)/shard_map/ppermute | solution.py:440
  65.6 25.1 %collective-permute-start.5 = (bf16[2,512,512]{2,1,0:T(8,128)(2,1)}, bf16[2,512,512]{2,1,0:T(8,128)(2,1)S(1)}, u32[]{:S(2)}, u32[]{:S(2)}) collective-permute-start(bf16[2,512,512]{2,1,0:T(8,128)(2,1)} %get-tuple-element.51), channel_id=1, source_target_pairs={{0,68},{1,69},{2,70},{3,71},{4,64},{5,65},{6,66},{7,67},{8,76},{9,... | collective-permute-start | bytes 3145736 | tf_op jit(solution)/shard_map/ppermute | solution.py:527
  84.7 10.0 %all-to-all-start.4 = ((bf16[4,208,256]{2,1,0:T(8,128)(2,1)}), bf16[4,208,256]{2,1,0:T(8,128)(2,1)S(1)}, u32[]{:S(2)}, u32[]{:S(2)}) async-start(bf16[4,208,256]{2,1,0:T(8,128)(2,1)} %broadcast_in_dim.39), calls=%async_computation.4 | async-start | bytes 851968 | tf_op jit(solution)/shard_map/all_to_all | solution.py:444
  90.7 9.4 %copy-start = (bf16[2,512,512]{2,1,0:T(8,128)(2,1)}, bf16[2,512,512]{2,1,0:T(8,128)(2,1)S(1)}, u32[]{:S(2)}) copy-start(bf16[2,512,512]{2,1,0:T(8,128)(2,1)S(1)} %collective-permute-done.5.got1_hbm.got_hbm) | copy-start | bytes 3145732
  94.7 5.3 %copy-start.10 = (bf16[4,208,256]{2,1,0:T(8,128)(2,1)}, bf16[4,208,256]{2,1,0:T(8,128)(2,1)S(1)}, u32[]{:S(2)}) copy-start(bf16[4,208,256]{2,1,0:T(8,128)(2,1)S(1)} %all-to-all-done.4.r_ref) | copy-start | bytes 1277956
  94.7 5.3 %collective-permute-start.7 = (bf16[2,512,512]{2,1,0:T(8,128)(2,1)S(1)}, bf16[2,512,512]{2,1,0:T(8,128)(2,1)S(1)}, u32[]{:S(2)}, u32[]{:S(2)}) collective-permute-start(bf16[2,512,512]{2,1,0:T(8,128)(2,1)S(1)} %collective-permute-done.5.got1_hbm.got_hbm), channel_id=1, source_target_pairs={{0,8},{8,0},{16,24},{24,16},{32,40},{40,32},{48,56},{56,48},{64,72... | collective-permute-start | bytes 3145736 | tf_op jit(solution)/shard_map/ppermute | solution.py:440
  139.5 19.2 %copy-start.17 = (f32[1920]{0:T(1024)S(1)}, f32[1920]{0:T(1024)}, u32[]{:S(2)}) copy-start(f32[1920]{0:T(1024)} %param.16) | copy-start | bytes 23044
  139.5 19.8 %copy-start.18 = (s32[1024]{0:T(1024)S(1)}, s32[1024]{0:T(1024)}, u32[]{:S(2)}) copy-start(s32[1024]{0:T(1024)} %param.10) | copy-start | bytes 12292
  139.5 21.6 %copy-start.6 = (bf16[1920,2,384]{2,1,0:T(2,128)(2,1)S(1)}, bf16[1920,2,384]{2,1,0:T(2,128)(2,1)}, u32[]{:S(2)}) copy-start(bf16[1920,2,384]{2,1,0:T(2,128)(2,1)} %param.17) | copy-start | bytes 8847364
  151.6 20.7 %all-to-all-start.9 = ((bf16[8,128,256]{2,1,0:T(8,128)(2,1)}), bf16[8,128,256]{2,1,0:T(8,128)(2,1)S(1)}, u32[]{:S(2)}, u32[]{:S(2)}) async-start(bf16[8,128,256]{2,1,0:T(8,128)(2,1)} %cond_end.1), calls=%async_computation.9 | async-start | bytes 1048576 | tf_op jit(solution)/shard_map/all_to_all | solution.py:444
  172.4 7.6 %copy-start.2 = (bf16[8,128,256]{2,1,0:T(8,128)(2,1)}, bf16[8,128,256]{2,1,0:T(8,128)(2,1)S(1)}, u32[]{:S(2)}) copy-start(bf16[8,128,256]{2,1,0:T(8,128)(2,1)S(1)} %all-to-all-done.9.hf_ref) | copy-start | bytes 1572868
  194.4 18.0 %collective-permute-start.8 = (bf16[512,512]{1,0:T(8,128)(2,1)}, bf16[512,512]{1,0:T(8,128)(2,1)S(1)}, u32[]{:S(2)}, u32[]{:S(2)}) collective-permute-start(bf16[512,512]{1,0:T(8,128)(2,1)} %get-tuple-element.65.kv0_ref), channel_id=1, source_target_pairs={{0,16},{8,24},{16,32},{24,40},{32,48},{40,56},{48,64},{56,72},{64,... | collective-permute-start | bytes 1572872 | tf_op jit(solution)/shard_map/ppermute | solution.py:555
  196.6 15.9 %copy-start.15 = (bf16[512,512]{1,0:T(8,128)(2,1)S(1)}, bf16[512,512]{1,0:T(8,128)(2,1)}, u32[]{:S(2)}) copy-start(bf16[512,512]{1,0:T(8,128)(2,1)} %get-tuple-element.65.kv0_ref) | copy-start | bytes 1572868
  212.4 9.0 %copy-start.9 = (bf16[512,512]{1,0:T(8,128)(2,1)}, bf16[512,512]{1,0:T(8,128)(2,1)S(1)}, u32[]{:S(2)}) copy-start(bf16[512,512]{1,0:T(8,128)(2,1)S(1)} %collective-permute-done.8.far_ref) | copy-start | bytes 1572868
  212.5 8.9 %collective-permute-start.10 = (bf16[512,512]{1,0:T(8,128)(2,1)S(1)}, bf16[512,512]{1,0:T(8,128)(2,1)S(1)}, u32[]{:S(2)}, u32[]{:S(2)}) collective-permute-start(bf16[512,512]{1,0:T(8,128)(2,1)S(1)} %broadcast_select_fusion.1), channel_id=1, source_target_pairs={{0,8},{8,0},{16,24},{24,16},{32,40},{40,32},{48,56},{56,48},{64,72... | collective-permute-start | bytes 1572872 | tf_op jit(solution)/shard_map/ppermute | solution.py:440
  213.4 17.7 %collective-permute-start.9 = (bf16[512,512]{1,0:T(8,128)(2,1)}, bf16[512,512]{1,0:T(8,128)(2,1)S(1)}, u32[]{:S(2)}, u32[]{:S(2)}) collective-permute-start(bf16[512,512]{1,0:T(8,128)(2,1)} %get-tuple-element.68.kv1_ref), channel_id=1, source_target_pairs={{0,16},{8,24},{16,32},{24,40},{32,48},{40,56},{48,64},{56,72},{64,... | collective-permute-start | bytes 1572872 | tf_op jit(solution)/shard_map/ppermute | solution.py:555
  221.4 9.7 %copy-start.13 = (bf16[512,512]{1,0:T(8,128)(2,1)S(1)}, bf16[512,512]{1,0:T(8,128)(2,1)}, u32[]{:S(2)}) copy-start(bf16[512,512]{1,0:T(8,128)(2,1)} %get-tuple-element.68.kv1_ref) | copy-start | bytes 1572868
  231.1 2.5 %copy-start.14 = (bf16[512,512]{1,0:T(8,128)(2,1)}, bf16[512,512]{1,0:T(8,128)(2,1)S(1)}, u32[]{:S(2)}) copy-start(bf16[512,512]{1,0:T(8,128)(2,1)S(1)} %collective-permute-done.9.far_ref) | copy-start | bytes 1572868
  231.2 2.4 collective-permute-start.11
  (6 other events, 5.5 us)
Sparse Core Ops, SparseCore 0:
  29.4 73.8 all-gather.4
  105.0 74.9 all-gather.6

commit v5 on v4

--- a/solution.py
+++ b/solution.py
@@ -16,7 +16,6 @@
 HALF = 128
 HALO = (40, 39, 36, 27, 0)
 ROWS = (208, 208, 208, 192, 128)
-VMEM_LIMIT = 60 << 20
 
 BLOCKS = D // 128
 UP_BLOCKS = 2 * BLOCKS
@@ -25,8 +24,8 @@
 Y_GROUPS = [[0, 1, 2, 3], [4, 5, 6, 7]]
 
 
-def params(**kw):
-    return pltpu.CompilerParams(vmem_limit_bytes=VMEM_LIMIT, **kw)
+def params(mib):
+    return pltpu.CompilerParams(vmem_limit_bytes=mib << 20)
 
 
 def cost(flops, nbytes, trans=0):
@@ -201,19 +200,19 @@
     finish(copies)
 
 
-def call(body, outs, scratch=(), smem=1, n=0, hbm=0, after=0, flops=10**9, name=None):
+def call(body, outs, scratch=(), smem=1, n=0, hbm=0, after=0, flops=10**9, name=None, mib=12, space=pl.ANY):
     def spec(space):
         return pl.BlockSpec(memory_space=space)
 
     specs = [spec(pltpu.SMEM)] * smem + [spec(pltpu.VMEM)] * n
-    specs += [spec(pl.ANY)] * hbm + [spec(pltpu.VMEM)] * after
+    specs += [spec(space)] * hbm + [spec(pltpu.VMEM)] * after
     return pl.pallas_call(
         body,
         out_shape=outs,
         in_specs=specs,
         out_specs=jax.tree.map(lambda _: spec(pltpu.VMEM), outs),
         scratch_shapes=list(scratch),
-        compiler_params=params(),
+        compiler_params=params(mib),
         cost_estimate=cost(flops, 4 << 20),
         name=name,
     )
@@ -279,8 +278,8 @@
         for part in range(2)
     ]
     qkv_copy = pltpu.make_async_copy(qkv_hbm, qkv, qkv_sem)
+    start(weight_copies(0))
     start(table_copies)
-    start(weight_copies(0))
     start(weight_copies(1))
     qkv_copy.start()
     for rows_of in range(2):
@@ -293,19 +292,21 @@
                 ]
     flat = table.reshape(VOCAB, 16, 128)
 
-    def look_up(phase):
-        for row in range(phase * 256, phase * 256 + 256):
+    finish(weight_copies(0))
+    product(0)
+    finish(table_copies)
+
+    def look_up(i, carry):
+        for j in range(16):
+            row = i * 16 + j
             rows[row] = flat[codes_ref[pair * 512 + row]].astype(F32)
-
-    finish(table_copies)
-    finish(weight_copies(0))
-    look_up(0)
-    product(0)
+        return carry
+
+    lax.fori_loop(0, 32, look_up, 0)
     finish(weight_copies(1))
     qkv_copy.wait()
-    look_up(1)
+    norm(0)
     product(1)
-    norm(0)
     project(0)
     norm(1)
     project(1)
@@ -332,7 +333,7 @@
             pltpu.SemaphoreType.DMA((2, 2)),
             pltpu.SemaphoreType.DMA,
         ],
-        compiler_params=params(),
+        compiler_params=params(40),
         cost_estimate=cost(4 * 10**9, 20 << 20),
         name="frames",
     )(info, codes, hf, gain, qkv, full_own, full_other)
@@ -345,23 +346,26 @@
     return lax.dot_general(q, k, (((1,), (1,)), ((), ())), preferred_element_type=F32)
 
 
-def fold(q_refs, kv, seen_of, old_of, put):
+def fold(tiles, kv, old_of, put):
     for head in range(2):
         cols = slice(head * 128, head * 128 + 128)
         k = kv[:, cols]
         v = kv[:, 256 + head * 128 : 384 + head * 128]
         v = jnp.concatenate([v, jnp.ones(v.shape, BF)], axis=1)
-        for phase in range(4):
-            s = scores_of(q_refs[phase // 2][phase % 2 * 256 : phase % 2 * 256 + 256, cols], k)
-            s = jnp.where(seen_of(phase), s, -1e30)
+        for tile, (queries, seen) in enumerate(tiles):
+            s = jnp.where(seen, scores_of(queries[:, cols], k), -1e30)
             top = jnp.max(s, axis=1, keepdims=True)
-            old = old_of(head, phase)
+            old = old_of(head, tile)
             if old is None:
-                put(head, phase, top, dot(jnp.exp2((s - top) * SCALE).astype(BF), v))
+                put(head, tile, top, dot(jnp.exp2((s - top) * SCALE).astype(BF), v))
             else:
                 top = jnp.maximum(old[0], top)
                 p = jnp.exp2((s - top) * SCALE).astype(BF)
-                put(head, phase, top, old[1] * jnp.exp2((old[0] - top) * SCALE) + dot(p, v))
+                put(head, tile, top, old[1] * jnp.exp2((old[0] - top) * SCALE) + dot(p, v))
+
+
+def phase_tiles(q0_ref, q1_ref, seen):
+    return [(ref[at : at + 256], seen) for ref in (q0_ref, q1_ref) for at in (0, 256)]
 
 
 def join_keys(kv, first, second):
@@ -370,15 +374,25 @@
 
 
 def own_kernel(q0_ref, q1_ref, kv0_ref, kv1_ref, acc_ref, top_ref, kv):
-    join_keys(kv, kv0_ref, kv1_ref)
-    col = lax.broadcasted_iota(jnp.int32, (256, 1024), 1)
-    ahead = (col & 255) * 4 + (col >> 8) - 4 * lax.broadcasted_iota(jnp.int32, (256, 1024), 0)
-
-    def put(head, phase, top, acc):
-        top_ref[head, phase] = top
-        acc_ref[head, phase] = acc
-
-    fold((q0_ref, q1_ref), kv, lambda p: ahead <= p, lambda head, phase: None, put)
+    for part in range(2):
+        keys = 128 * (part + 1)
+        for phase, ref in enumerate((kv0_ref, kv0_ref, kv1_ref, kv1_ref)):
+            kv[phase * keys : (phase + 1) * keys] = ref[phase % 2 * 256 : phase % 2 * 256 + keys]
+        col = lax.broadcasted_iota(jnp.int32, (256, 4 * keys), 1)
+        row = lax.broadcasted_iota(jnp.int32, (256, 4 * keys), 0)
+        ahead = col % keys * 4 + col // keys - (part * 512 + row % 128 * 4 + row // 128)
+        tiles = []
+        for pair, ref in enumerate((q0_ref, q1_ref)):
+            lines = slice(part * 128, part * 128 + 128), slice(256 + part * 128, 384 + part * 128)
+            tiles.append((jnp.concatenate([ref[at, :] for at in lines]), ahead <= 2 * pair))
+
+        def put(head, tile, top, acc):
+            lines = slice(part * 128, part * 128 + 128)
+            for i in range(2):
+                top_ref[head, tile * 2 + i, lines] = top[i * 128 : i * 128 + 128]
+                acc_ref[head, tile * 2 + i, lines] = acc[i * 128 : i * 128 + 128]
+
+        fold(tiles, kv[: 4 * keys], lambda head, tile: None, put)
 
 
 def past_kernel(last, info, q0_ref, q1_ref, far_ref, near_ref, acc_ref, top_ref, *refs):
@@ -404,9 +418,8 @@
             acc[head, phase] = total
 
         fold(
-            (q0_ref, q1_ref),
-            kv,
-            lambda p: seen,
+            phase_tiles(q0_ref, q1_ref, seen),
+            kv[...],
             lambda head, phase: (top_ref[head, phase], acc_ref[head, phase]),
             put,
         )
@@ -478,13 +491,15 @@
         ],
         hbm=5,
         name="pack",
+        space=pltpu.HBM,
     )(info, dilated_weight, mixing_weight, upper_table, upsample_weight, middle_table)
     got0 = lax.ppermute(pack0, EVERY, other_half())
     mine = exchange(part, groups=Y_GROUPS)
     edge = jnp.where(x_hi == 0, upper_codes[-40:], upper_codes[:40])
     edge = lax.ppermute(edge, EVERY, song_neighbours())
-    mine, got0, edge = lax.optimization_barrier((mine, got0, edge))
+    mine, edge = lax.optimization_barrier((mine, edge))
     full_own = gathered(mine)
+    mine, got0 = lax.optimization_barrier((mine, got0))
     others = lax.ppermute(mine, EVERY, other_half())
     sib0 = to_sibling(got0)
     codes = jnp.where(
@@ -508,6 +523,7 @@
         [pltpu.SemaphoreType.DMA((21,))],
         hbm=2,
         name="pack_later",
+        space=pltpu.HBM,
     )(info, dilated_weight, mixing_weight)
 
     for level in range(4):
@@ -561,9 +577,9 @@
     state = (shape(2, 4, 256, 256, dtype=F32), shape(2, 4, 256, 1, dtype=F32))
     keys = pltpu.VMEM((1024, 512), BF)
     far0, q1 = lax.optimization_barrier((far0, q1))
-    kept = call(own_kernel, state, [keys], smem=0, n=4, flops=10**9, name="own")(q0, q1, kv0, kv1)
+    kept = call(own_kernel, state, [keys], smem=0, n=4, flops=10**9, name="own", mib=24)(q0, q1, kv0, kv1)
     near0 = to_sibling(jnp.where(core == 0, kv0, far0))
-    kept = call(functools.partial(past_kernel, False), state, [keys], n=6, flops=10**9, name="past")(
+    kept = call(functools.partial(past_kernel, False), state, [keys], n=6, flops=10**9, name="past", mib=24)(
         info, q0, q1, far0, near0, *kept
     )
     far1, kept = lax.optimization_barrier((far1, kept))
@@ -580,6 +596,7 @@
         n=6,
         flops=2 * 10**9,
         name="past_end",
+        mib=24,
     )(info, q0, q1, far1, near1, *kept)
 
 

time: 249 us -> 253 us (1.016)
  Pallas kernels: 76.2 us -> 54.1 us
  local copies, waits for them, and re-layouts: 10.7 us -> 24.7 us
  starting transfers between devices: 40.4 us -> 49.5 us
  waiting for transfers between devices: 43.2 us -> 51.9 us
  blocking collectives: 62 us -> 54.9 us
    unnamed x42 -> x56, local copies, waits for them, and re-layouts: 6.5 us -> 23.2 us
    ppermute x1, waiting for transfers between devices: 2.49 us -> 16.3 us  [on_device(): got0 = lax.ppermute(pack0, EVERY, other_half())]
    all_gather x2, waiting for transfers between devices: 7.6 us -> 0.01 us  [gathered(): lax.all_gather(parts, 'song', axis=0, tiled=False)]
    all_to_all x6, blocking collectives: 62 us -> 54.9 us  [exchange(): lax.all_to_all(value, axis, 0, 0, axis_index_groups=groups, tiled=True)]
    ppermute x5, starting transfers between devices: 8.42 us -> 14.4 us  [to_sibling(): return lax.ppermute(value, 'song', [(i, i ^ 1) for i in range(16)])]
    pallas_call x3, Pallas kernels: 12.3 us -> 7.78 us  [on_device(): call(functools.partial(middle_kernel, level), (shape(ROWS[level + 1], 256...]
    pallas_call x2, Pallas kernels: 28.9 us -> 24.5 us  [frames(): pl.pallas_call(functools.partial(frames_kernel, pair), out_shape=(shape(5...]
    ppermute x2, starting transfers between devices: 4.05 us -> 7.35 us  [from_two_back(): return lax.ppermute(value, 'song', [(i, i + 2) for i in range(14)])]
  transfers between devices with their start and end apart: 18 -> 18, of which waited for: 14 -> 14; matrix products, arithmetic and copies ran while one was open for 3% -> 2% of each run, Pallas kernels for 21% -> 14%
where the time goes in v5:
time: 253 us; the launch traced here: 252 us
  blocking collectives  54.9 us (22%)
  Pallas kernels  54.1 us (21%)
  waiting for transfers between devices  51.9 us (21%)
  starting transfers between devices  49.5 us (20%)
  local copies, waits for them, and re-layouts  24.7 us (10%)
  between operations  13.8 us (5%)
  other arithmetic  2.64 us (1%)
    all_to_all x6, blocking collectives, exchange(): lax.all_to_all(value, axis, 0, 0, axis_index_groups=groups, tiled=True)  54.9 us
    pallas_call x2, Pallas kernels, frames(): pl.pallas_call(functools.partial(frames_kernel, pair), out_shape=(shape(5...  24.5 us
    unnamed x56, local copies, waits for them, and re-layouts  23.2 us
    all_to_all x4, starting transfers between devices, exchange(): lax.all_to_all(value, axis, 0, 0, axis_index_groups=groups, tiled=True)  18.5 us
    all_to_all x4, waiting for transfers between devices, exchange(): lax.all_to_all(value, axis, 0, 0, axis_index_groups=groups, tiled=True)  17.7 us
    ppermute x1, waiting for transfers between devices, on_device(): got0 = lax.ppermute(pack0, EVERY, other_half())  16.3 us
    ppermute x5, starting transfers between devices, to_sibling(): return lax.ppermute(value, 'song', [(i, i ^ 1) for i in range(16)])  14.4 us
    pallas_call x3, Pallas kernels, on_device(): call(functools.partial(middle_kernel, level), (shape(ROWS[level + 1], 256...  7.78 us
  transfers between devices with their start and end apart: 18, of which 14 were waited for; matrix products, arithmetic and copies ran while one was open for 2% of the time, Pallas kernels for 14%

profile of v5, /device:TPU:3, one launch (start us, length us, event | category | flops | bytes accessed | tf_op | source)
XLA Modules:
  0.0 251.6 jit_solution(6187757295741150422)
XLA Ops:
  16.5 4.2 %all-to-all-start = ((bf16[4,46,16,128]{3,2,1,0:T(8,128)(2,1)}), bf16[4,46,16,128]{3,2,1,0:T(8,128)(2,1)}, u32[]{:S(2)}, u32[]{:S(2)}) async-start(bf16[4,46,16,128]{3,2,1,0:T(8,128)(2,1)} %copy-done.15), calls=%async_computation | async-start | bytes 1507328 | tf_op jit(solution)/shard_map/all_to_all | solution.py:457
  20.9 4.3 %collective-permute-start = (s32[40]{0:T(128)S(1)}, s32[40]{0:T(128)S(1)}, u32[]{:S(2)}, u32[]{:S(2)}) collective-permute-start(s32[40]{0:T(128)S(1)} %broadcast_select_fusion.3), channel_id=1, source_target_pairs={{0,8},{1,9},{2,10},{3,11},{8,16},{9,17},{10,18},{11,19},{16,24},{1... | collective-permute-start | bytes 488 | tf_op jit(solution)/shard_map/ppermute | solution.py:499
  25.9 6.0 %all-to-all-done = bf16[4,46,16,128]{3,2,1,0:T(8,128)(2,1)} async-done(((bf16[4,46,16,128]{3,2,1,0:T(8,128)(2,1)}), bf16[4,46,16,128]{3,2,1,0:T(8,128)(2,1)}, u32[]{:S(2)}, u32[]{:S(2)}) %all-to-all-start) | async-done | bytes 753696 | tf_op jit(solution)/shard_map/all_to_all | solution.py:457
  33.2 16.3 %collective-permute-done.1.got_ref.got_hbm = bf16[768,512]{1,0:T(8,128)(2,1)} collective-permute-done((bf16[768,512]{1,0:T(8,128)(2,1)}, bf16[768,512]{1,0:T(8,128)(2,1)}, u32[]{:S(2)}, u32[]{:S(2)}) %collective-permute-start.1) | collective-permute-done | bytes 786464 | tf_op jit(solution)/shard_map/ppermute | solution.py:496
  49.4 2.8 %collective-permute-start.3 = (bf16[768,512]{1,0:T(8,128)(2,1)}, bf16[768,512]{1,0:T(8,128)(2,1)}, u32[]{:S(2)}, u32[]{:S(2)}) collective-permute-start(bf16[768,512]{1,0:T(8,128)(2,1)} %collective-permute-done.1.got_ref.got_hbm), channel_id=1, source_target_pairs={{0,8},{8,0},{16,24},{24,16},{32,40},{40,32},{48,56},{56,48},{64,72... | collective-permute-start | bytes 2359304 | tf_op jit(solution)/shard_map/ppermute | solution.py:453
  55.5 3.9 %cond0.1 = (f32[208,256]{1,0:T(8,128)S(1)}, bf16[4,208,256]{2,1,0:T(8,128)(2,1)S(1)}) custom-call(s32[6]{0:T(128)S(1)} %stack.27.info, s32[208,1]{1,0:T(8,128)S(1)} %broadcast_select_fusion.2.codes_ref, bf16[2048,128]{1,0:T(8,128)(2,1)S(1)} %copy-done.12, bf16[4,3,128,1024]{3,2,1,0:T(8,128)(2,1)S(1)} %copy-done.1, ...), custom_call_target="tpu_custom_call" | custom-call | flops 1000000000 | bytes 4194304 | tf_op jit(solution)/shard_map/cond0/pallas_call | solution.py:511
  60.8 4.1 %all-to-all-start.1 = ((bf16[4,208,256]{2,1,0:T(8,128)(2,1)}), bf16[4,208,256]{2,1,0:T(8,128)(2,1)}, u32[]{:S(2)}, u32[]{:S(2)}) async-start(bf16[4,208,256]{2,1,0:T(8,128)(2,1)} %copy-done.16), calls=%async_computation.1 | async-start | bytes 851968 | tf_op jit(solution)/shard_map/all_to_all | solution.py:457
  75.6 9.0 %all_to_all.50.r_ref = bf16[4,208,256]{2,1,0:T(8,128)(2,1)S(1)} all-to-all(bf16[4,208,256]{2,1,0:T(8,128)(2,1)S(1)} %broadcast_in_dim.37), channel_id=1, replica_groups={{0,1,2,3},{4,5,6,7},{8,9,10,11},{12,13,14,15},{16,17,18,19},{20,21,22,2..., dimensions={0} | all-to-all | bytes 851968 | tf_op jit(solution)/shard_map/all_to_all | solution.py:457
  91.7 2.7 %cond.3 = (f32[208,256]{1,0:T(8,128)S(1)}, bf16[4,208,256]{2,1,0:T(8,128)(2,1)S(1)}) custom-call(s32[6]{0:T(128)S(1)} %stack.27.info, bf16[4,208,256]{2,1,0:T(8,128)(2,1)S(1)} %all_to_all.50.r_ref, f32[208,256]{1,0:T(8,128)S(1)} %copy-done.20, bf16[4,1024,128]{2,1,0:T(8,128)(2,1)S(1)} %copy-done.4, bf16[768,512]{1,0:T(8,128)(2,1)} %collective-permute-done.1.got_ref.got_hbm, ...), custom_call_target="tpu_custom_call" | custom-call | flops 1000000000 | bytes 4194304 | tf_op jit(solution)/shard_map/cond/pallas_call | solution.py:549
  94.4 10.4 %all_to_all.51 = bf16[4,208,256]{2,1,0:T(8,128)(2,1)S(1)} all-to-all(bf16[4,208,256]{2,1,0:T(8,128)(2,1)S(1)} %get-tuple-element.57), channel_id=1, replica_groups={{0,1,2,3},{4,5,6,7},{8,9,10,11},{12,13,14,15},{16,17,18,19},{20,21,22,2..., dimensions={0} | all-to-all | bytes 851968 | tf_op jit(solution)/shard_map/all_to_all | solution.py:457
  105.7 4.1 %all-to-all-start.4 = ((bf16[4,208,256]{2,1,0:T(8,128)(2,1)}), bf16[4,208,256]{2,1,0:T(8,128)(2,1)}, u32[]{:S(2)}, u32[]{:S(2)}) async-start(bf16[4,208,256]{2,1,0:T(8,128)(2,1)} %broadcast_in_dim.39), calls=%async_computation.4 | async-start | bytes 851968 | tf_op jit(solution)/shard_map/all_to_all | solution.py:457
  109.8 3.1 %collective-permute-done.5.got1_hbm.got_hbm = bf16[2,512,512]{2,1,0:T(8,128)(2,1)} collective-permute-done((bf16[2,512,512]{2,1,0:T(8,128)(2,1)}, bf16[2,512,512]{2,1,0:T(8,128)(2,1)}, u32[]{:S(2)}, u32[]{:S(2)}) %collective-permute-start.5) | collective-permute-done | bytes 1048608 | tf_op jit(solution)/shard_map/ppermute | solution.py:543
  112.9 3.7 %all-to-all-done.4.r_ref = bf16[4,208,256]{2,1,0:T(8,128)(2,1)} async-done(((bf16[4,208,256]{2,1,0:T(8,128)(2,1)}), bf16[4,208,256]{2,1,0:T(8,128)(2,1)}, u32[]{:S(2)}, u32[]{:S(2)}) %all-to-all-start.4) | async-done | bytes 426016 | tf_op jit(solution)/shard_map/all_to_all | solution.py:457
  116.7 2.6 %collective-permute-start.7 = (bf16[2,512,512]{2,1,0:T(8,128)(2,1)}, bf16[2,512,512]{2,1,0:T(8,128)(2,1)S(1)}, u32[]{:S(2)}, u32[]{:S(2)}) collective-permute-start(bf16[2,512,512]{2,1,0:T(8,128)(2,1)} %collective-permute-done.5.got1_hbm.got_hbm), channel_id=1, source_target_pairs={{0,8},{8,0},{16,24},{24,16},{32,40},{40,32},{48,56},{56,48},{64,72... | collective-permute-start | bytes 3145736 | tf_op jit(solution)/shard_map/ppermute | solution.py:453
  119.3 2.6 %collective-permute-done.7.sib1_hbm.sib_hbm = bf16[2,512,512]{2,1,0:T(8,128)(2,1)S(1)} collective-permute-done((bf16[2,512,512]{2,1,0:T(8,128)(2,1)}, bf16[2,512,512]{2,1,0:T(8,128)(2,1)S(1)}, u32[]{:S(2)}, u32[]{:S(2)}) %collective-permute-start.7) | collective-permute-done | bytes 1048608 | tf_op jit(solution)/shard_map/ppermute | solution.py:453
  125.3 2.9 %cond.4 = (f32[208,256]{1,0:T(8,128)S(1)}, bf16[4,192,256]{2,1,0:T(8,128)(2,1)S(1)}) custom-call(s32[6]{0:T(128)S(1)} %stack.27.info, bf16[4,208,256]{2,1,0:T(8,128)(2,1)} %all-to-all-done.4.r_ref, f32[208,256]{1,0:T(8,128)S(1)} %get-tuple-element.59.h_ref, bf16[4,1024,128]{2,1,0:T(8,128)(2,1)S(1)} %copy-done.5, bf16[512,512]{1,0:T(8,128)(2,1)S(1)} %copy-done.8, ...), custom_call_target="tpu_custom_call" | custom-call | flops 1000000000 | bytes 4194304 | tf_op jit(solution)/shard_map/cond/pallas_call | solution.py:549
  128.1 10.4 %all_to_all.52 = bf16[4,192,256]{2,1,0:T(8,128)(2,1)S(1)} all-to-all(bf16[4,192,256]{2,1,0:T(8,128)(2,1)S(1)} %get-tuple-element.61), channel_id=1, replica_groups={{0,1,2,3},{4,5,6,7},{8,9,10,11},{12,13,14,15},{16,17,18,19},{20,21,22,2..., dimensions={0} | all-to-all | bytes 786432 | tf_op jit(solution)/shard_map/all_to_all | solution.py:457
  138.6 9.3 %all_to_all.53.r_ref = bf16[4,192,256]{2,1,0:T(8,128)(2,1)S(1)} all-to-all(bf16[4,192,256]{2,1,0:T(8,128)(2,1)S(1)} %broadcast_in_dim.41), channel_id=1, replica_groups={{0,1,2,3},{4,5,6,7},{8,9,10,11},{12,13,14,15},{16,17,18,19},{20,21,22,2..., dimensions={0} | all-to-all | bytes 786432 | tf_op jit(solution)/shard_map/all_to_all | solution.py:457
  150.3 7.9 %all_to_all.54 = bf16[4,128,256]{2,1,0:T(8,128)(2,1)S(1)} all-to-all(bf16[4,128,256]{2,1,0:T(8,128)(2,1)S(1)} %get-tuple-element.63), channel_id=1, replica_groups={{0,1,2,3},{4,5,6,7},{8,9,10,11},{12,13,14,15},{16,17,18,19},{20,21,22,2..., dimensions={0} | all-to-all | bytes 524288 | tf_op jit(solution)/shard_map/all_to_all | solution.py:457
  158.3 7.9 %all_to_all.55.r_ref = bf16[4,128,256]{2,1,0:T(8,128)(2,1)S(1)} all-to-all(bf16[4,128,256]{2,1,0:T(8,128)(2,1)S(1)} %broadcast_in_dim.43), channel_id=1, replica_groups={{0,1,2,3},{4,5,6,7},{8,9,10,11},{12,13,14,15},{16,17,18,19},{20,21,22,2..., dimensions={0} | all-to-all | bytes 524288 | tf_op jit(solution)/shard_map/all_to_all | solution.py:457
  166.2 2.5 %cond_end.1 = bf16[8,128,256]{2,1,0:T(8,128)(2,1)} custom-call(s32[6]{0:T(128)S(1)} %stack.27.info, bf16[4,128,256]{2,1,0:T(8,128)(2,1)S(1)} %all_to_all.55.r_ref, f32[192,256]{1,0:T(8,128)S(1)} %get-tuple-element.64.h_ref, bf16[4,1024,128]{2,1,0:T(8,128)(2,1)S(1)} %copy-done.6, bf16[2,512,512]{2,1,0:T(8,128)(2,1)} %collective-permute-done.5.got1_hbm.got_hbm, ...), custom_call_target="tpu_custom_call" | custom-call | flops 1000000000 | bytes 4194304 | tf_op jit(solution)/shard_map/cond_end/pallas_call | solution.py:558
  168.7 6.1 %all-to-all-start.9 = ((bf16[8,128,256]{2,1,0:T(8,128)(2,1)}), bf16[8,128,256]{2,1,0:T(8,128)(2,1)S(1)}, u32[]{:S(2)}, u32[]{:S(2)}) async-start(bf16[8,128,256]{2,1,0:T(8,128)(2,1)} %cond_end.1), calls=%async_computation.9 | async-start | bytes 1048576 | tf_op jit(solution)/shard_map/all_to_all | solution.py:457
  177.5 5.9 %all-to-all-done.9.hf_ref = bf16[8,128,256]{2,1,0:T(8,128)(2,1)S(1)} async-done(((bf16[8,128,256]{2,1,0:T(8,128)(2,1)}), bf16[8,128,256]{2,1,0:T(8,128)(2,1)S(1)}, u32[]{:S(2)}, u32[]{:S(2)}) %all-to-all-start.9) | async-done | bytes 524320 | tf_op jit(solution)/shard_map/all_to_all | solution.py:457
  183.4 12.6 %frames.2 = (bf16[512,256]{1,0:T(8,128)(2,1)S(1)}, bf16[512,512]{1,0:T(8,128)(2,1)}) custom-call(s32[6]{0:T(128)S(1)} %stack.27.info, s32[1024]{0:T(1024)S(1)} %fusion.9.codes_ref, bf16[8,128,256]{2,1,0:T(8,128)(2,1)S(1)} %all-to-all-done.9.hf_ref, f32[1,1920]{1,0:T(1,128)S(1)} %broadcast_in_dim.44.gain_ref, bf16[1920,768]{1,0:T(8,128)(2,1)S(1)} %bitcast.24, ...), custom_call_target="tpu_custom_call" | custom-call | flops 4000000000 | bytes 20971520 | tf_op jit(solution)/shard_map/frames/pallas_call | solution.py:319
  196.8 4.0 %collective-permute-start.8 = (bf16[512,512]{1,0:T(8,128)(2,1)}, bf16[512,512]{1,0:T(8,128)(2,1)}, u32[]{:S(2)}, u32[]{:S(2)}) collective-permute-start(bf16[512,512]{1,0:T(8,128)(2,1)} %get-tuple-element.67.kv0_ref), channel_id=1, source_target_pairs={{0,16},{8,24},{16,32},{24,40},{32,48},{40,56},{48,64},{56,72},{64,... | collective-permute-start | bytes 1572872 | tf_op jit(solution)/shard_map/ppermute | solution.py:571
  200.8 11.9 %frames.3 = (bf16[512,256]{1,0:T(8,128)(2,1)S(1)}, bf16[512,512]{1,0:T(8,128)(2,1)S(1)}) custom-call(s32[6]{0:T(128)S(1)} %stack.27.info, s32[1024]{0:T(1024)S(1)} %fusion.9.codes_ref, bf16[8,128,256]{2,1,0:T(8,128)(2,1)S(1)} %all-to-all-done.9.hf_ref, f32[1,1920]{1,0:T(1,128)S(1)} %broadcast_in_dim.44.gain_ref, bf16[1920,768]{1,0:T(8,128)(2,1)S(1)} %bitcast.25, ...), custom_call_target="tpu_custom_call" | custom-call | flops 4000000000 | bytes 20971520 | tf_op jit(solution)/shard_map/frames/pallas_call | solution.py:319
  213.8 6.1 %collective-permute-start.10 = (bf16[512,512]{1,0:T(8,128)(2,1)S(1)}, bf16[512,512]{1,0:T(8,128)(2,1)S(1)}, u32[]{:S(2)}, u32[]{:S(2)}) collective-permute-start(bf16[512,512]{1,0:T(8,128)(2,1)S(1)} %broadcast_select_fusion.1), channel_id=1, source_target_pairs={{0,8},{8,0},{16,24},{24,16},{32,40},{40,32},{48,56},{56,48},{64,72... | collective-permute-start | bytes 1572872 | tf_op jit(solution)/shard_map/ppermute | solution.py:453
  219.9 3.3 %collective-permute-start.9 = (bf16[512,512]{1,0:T(8,128)(2,1)S(1)}, bf16[512,512]{1,0:T(8,128)(2,1)S(1)}, u32[]{:S(2)}, u32[]{:S(2)}) collective-permute-start(bf16[512,512]{1,0:T(8,128)(2,1)S(1)} %get-tuple-element.70.kv1_ref), channel_id=1, source_target_pairs={{0,16},{8,24},{16,32},{24,40},{32,48},{40,56},{48,64},{56,72},{64,... | collective-permute-start | bytes 1572872 | tf_op jit(solution)/shard_map/ppermute | solution.py:571
  223.2 3.9 %own.1 = (f32[2,4,256,256]{3,2,1,0:T(8,128)S(1)}, f32[2,4,256,1]{3,2,1,0:T(8,128)S(1)}) custom-call(bf16[512,256]{1,0:T(8,128)(2,1)S(1)} %copy-done.18, bf16[512,256]{1,0:T(8,128)(2,1)S(1)} %get-tuple-element.69.q1_ref, bf16[512,512]{1,0:T(8,128)(2,1)} %get-tuple-element.67.kv0_ref, bf16[512,512]{1,0:T(8,128)(2,1)S(1)} %get-tuple-element.70.kv1_ref), custom_call_target="tpu_custom_call" | custom-call | flops 1000000000 | bytes 4194304 | tf_op jit(solution)/shard_map/own/pallas_call | solution.py:580
  227.2 4.6 %past.1 = (f32[2,4,256,256]{3,2,1,0:T(8,128)S(1)}, f32[2,4,256,1]{3,2,1,0:T(8,128)S(1)}) custom-call(s32[6]{0:T(128)S(1)} %stack.27.info, bf16[512,256]{1,0:T(8,128)(2,1)S(1)} %copy-done.18, bf16[512,256]{1,0:T(8,128)(2,1)S(1)} %get-tuple-element.69.q1_ref, bf16[512,512]{1,0:T(8,128)(2,1)} %collective-permute-done.8.far_ref, ...), custom_call_target="tpu_custom_call" | custom-call | flops 1000000000 | bytes 4194304 | tf_op jit(solution)/shard_map/past/pallas_call | solution.py:582
  231.8 5.7 %collective-permute-done.9.far_ref = bf16[512,512]{1,0:T(8,128)(2,1)S(1)} collective-permute-done((bf16[512,512]{1,0:T(8,128)(2,1)S(1)}, bf16[512,512]{1,0:T(8,128)(2,1)S(1)}, u32[]{:S(2)}, u32[]{:S(2)}) %collective-permute-start.9) | collective-permute-done | bytes 524320 | tf_op jit(solution)/shard_map/ppermute | solution.py:571
  239.9 4.8 %past_end.1 = bf16[1024,256]{1,0:T(8,128)(2,1)} custom-call(s32[6]{0:T(128)S(1)} %stack.27.info, bf16[512,256]{1,0:T(8,128)(2,1)S(1)} %copy-done.18, bf16[512,256]{1,0:T(8,128)(2,1)S(1)} %get-tuple-element.69.q1_ref, bf16[512,512]{1,0:T(8,128)(2,1)S(1)} %collective-permute-done.9.far_ref, bf16[512,512]{1,0:T(8,128)(2,1)S(1)} %collective-permute-done.11.near_ref, ...), custom_call_target="tpu_custom_call" | custom-call | flops 2000000000 | bytes 4194304 | tf_op jit(solution)/shard_map/past_end/pallas_call | solution.py:587
  (101 shorter events, 48.2 us)
Async XLA Ops:
  6.6 1.9 copy-start
  8.5 1.2 copy-start.2
  10.8 1.5 copy-start.13
  13.5 7.2 %copy-start.24 = (s32[256]{0:T(256)S(1)}, s32[256]{0:T(256)}, u32[]{:S(2)}) copy-start(s32[256]{0:T(256)} %param.9) | copy-start | bytes 3076
  13.5 40.9 %copy-start.1 = (bf16[4,3,128,1024]{3,2,1,0:T(8,128)(2,1)S(1)}, bf16[4,3,128,1024]{3,2,1,0:T(8,128)(2,1)}, u32[]{:S(2)}) copy-start(bf16[4,3,128,1024]{3,2,1,0:T(8,128)(2,1)} %dil_hbm.11) | copy-start | bytes 9437188
  16.5 15.3 %all-to-all-start = ((bf16[4,46,16,128]{3,2,1,0:T(8,128)(2,1)}), bf16[4,46,16,128]{3,2,1,0:T(8,128)(2,1)}, u32[]{:S(2)}, u32[]{:S(2)}) async-start(bf16[4,46,16,128]{3,2,1,0:T(8,128)(2,1)} %copy-done.15), calls=%async_computation | async-start | bytes 1507328 | tf_op jit(solution)/shard_map/all_to_all | solution.py:457
  20.7 162.7 %all-gather.5.cloned.1.call-start = ((), (), s32[]{:S(2)}) async-start(), calls=%async_computation.10 | async-start | bytes 12812288 | tf_op jit(solution)/shard_map/all_gather | solution.py:461
  20.9 5.0 %collective-permute-start = (s32[40]{0:T(128)S(1)}, s32[40]{0:T(128)S(1)}, u32[]{:S(2)}, u32[]{:S(2)}) collective-permute-start(s32[40]{0:T(128)S(1)} %broadcast_select_fusion.3), channel_id=1, source_target_pairs={{0,8},{1,9},{2,10},{3,11},{8,16},{9,17},{10,18},{11,19},{16,24},{1... | collective-permute-start | bytes 488 | tf_op jit(solution)/shard_map/ppermute | solution.py:499
  31.9 17.6 %collective-permute-start.1 = (bf16[768,512]{1,0:T(8,128)(2,1)}, bf16[768,512]{1,0:T(8,128)(2,1)}, u32[]{:S(2)}, u32[]{:S(2)}) collective-permute-start(bf16[768,512]{1,0:T(8,128)(2,1)} %copy-done.22), channel_id=1, source_target_pairs={{0,68},{1,69},{2,70},{3,71},{4,64},{5,65},{6,66},{7,67},{8,76},{9,... | collective-permute-start | bytes 2359304 | tf_op jit(solution)/shard_map/ppermute | solution.py:496
  49.4 5.0 %collective-permute-start.3 = (bf16[768,512]{1,0:T(8,128)(2,1)}, bf16[768,512]{1,0:T(8,128)(2,1)}, u32[]{:S(2)}, u32[]{:S(2)}) collective-permute-start(bf16[768,512]{1,0:T(8,128)(2,1)} %collective-permute-done.1.got_ref.got_hbm), channel_id=1, source_target_pairs={{0,8},{8,0},{16,24},{24,16},{32,40},{40,32},{48,56},{56,48},{64,72... | collective-permute-start | bytes 2359304 | tf_op jit(solution)/shard_map/ppermute | solution.py:453
  52.3 18.8 %collective-permute-start.2 = (bf16[4,46,16,128]{3,2,1,0:T(8,128)(2,1)}, bf16[4,46,16,128]{3,2,1,0:T(8,128)(2,1)}, u32[]{:S(2)}, u32[]{:S(2)}) collective-permute-start(bf16[4,46,16,128]{3,2,1,0:T(8,128)(2,1)} %all-to-all-done), channel_id=1, source_target_pairs={{0,68},{1,69},{2,70},{3,71},{4,64},{5,65},{6,66},{7,67},{8,76},{9,... | collective-permute-start | bytes 2261000 | tf_op jit(solution)/shard_map/ppermute | solution.py:503
  60.8 12.3 %all-to-all-start.1 = ((bf16[4,208,256]{2,1,0:T(8,128)(2,1)}), bf16[4,208,256]{2,1,0:T(8,128)(2,1)}, u32[]{:S(2)}, u32[]{:S(2)}) async-start(bf16[4,208,256]{2,1,0:T(8,128)(2,1)} %copy-done.16), calls=%async_computation.1 | async-start | bytes 851968 | tf_op jit(solution)/shard_map/all_to_all | solution.py:457
  65.0 118.5 %all-gather.7.cloned.1.call-start = ((), (), s32[]{:S(2)}) async-start(), calls=%async_computation.11 | async-start | bytes 12812288 | tf_op jit(solution)/shard_map/all_gather | solution.py:461
  65.0 1.2 copy-start.3
  73.2 12.6 %collective-permute-start.4 = (bf16[512,512]{1,0:T(8,128)(2,1)}, bf16[512,512]{1,0:T(8,128)(2,1)S(1)}, u32[]{:S(2)}, u32[]{:S(2)}) collective-permute-start(bf16[512,512]{1,0:T(8,128)(2,1)} %copy-done.23), channel_id=1, source_target_pairs={{0,68},{1,69},{2,70},{3,71},{4,64},{5,65},{6,66},{7,67},{8,76},{9,... | collective-permute-start | bytes 1572872 | tf_op jit(solution)/shard_map/ppermute | solution.py:534
  85.8 8.6 %copy-start.7 = (bf16[512,512]{1,0:T(8,128)(2,1)}, bf16[512,512]{1,0:T(8,128)(2,1)S(1)}, u32[]{:S(2)}) copy-start(bf16[512,512]{1,0:T(8,128)(2,1)S(1)} %collective-permute-done.4.got1_hbm.got_hbm) | copy-start | bytes 1572868
  85.8 3.6 %collective-permute-start.6 = (bf16[512,512]{1,0:T(8,128)(2,1)S(1)}, bf16[512,512]{1,0:T(8,128)(2,1)S(1)}, u32[]{:S(2)}, u32[]{:S(2)}) collective-permute-start(bf16[512,512]{1,0:T(8,128)(2,1)S(1)} %collective-permute-done.4.got1_hbm.got_hbm), channel_id=1, source_target_pairs={{0,8},{8,0},{16,24},{24,16},{32,40},{40,32},{48,56},{56,48},{64,72... | collective-permute-start | bytes 1572872 | tf_op jit(solution)/shard_map/ppermute | solution.py:453
  87.8 25.1 %collective-permute-start.5 = (bf16[2,512,512]{2,1,0:T(8,128)(2,1)}, bf16[2,512,512]{2,1,0:T(8,128)(2,1)}, u32[]{:S(2)}, u32[]{:S(2)}) collective-permute-start(bf16[2,512,512]{2,1,0:T(8,128)(2,1)} %copy-done.21), channel_id=1, source_target_pairs={{0,68},{1,69},{2,70},{3,71},{4,64},{5,65},{6,66},{7,67},{8,76},{9,... | collective-permute-start | bytes 3145736 | tf_op jit(solution)/shard_map/ppermute | solution.py:543
  89.4 5.0 %copy-start.9 = (bf16[512,512]{1,0:T(8,128)(2,1)}, bf16[512,512]{1,0:T(8,128)(2,1)S(1)}, u32[]{:S(2)}) copy-start(bf16[512,512]{1,0:T(8,128)(2,1)S(1)} %collective-permute-done.6.sib1_hbm.sib_hbm) | copy-start | bytes 1572868
  89.4 1.4 copy-start.4
  105.7 11.0 %all-to-all-start.4 = ((bf16[4,208,256]{2,1,0:T(8,128)(2,1)}), bf16[4,208,256]{2,1,0:T(8,128)(2,1)}, u32[]{:S(2)}, u32[]{:S(2)}) async-start(bf16[4,208,256]{2,1,0:T(8,128)(2,1)} %broadcast_in_dim.39), calls=%async_computation.4 | async-start | bytes 851968 | tf_op jit(solution)/shard_map/all_to_all | solution.py:457
  116.7 5.2 %collective-permute-start.7 = (bf16[2,512,512]{2,1,0:T(8,128)(2,1)}, bf16[2,512,512]{2,1,0:T(8,128)(2,1)S(1)}, u32[]{:S(2)}, u32[]{:S(2)}) collective-permute-start(bf16[2,512,512]{2,1,0:T(8,128)(2,1)} %collective-permute-done.5.got1_hbm.got_hbm), channel_id=1, source_target_pairs={{0,8},{8,0},{16,24},{24,16},{32,40},{40,32},{48,56},{56,48},{64,72... | collective-permute-start | bytes 3145736 | tf_op jit(solution)/shard_map/ppermute | solution.py:453
  121.9 1.3 copy-start.5
  128.1 19.9 %copy-start.6 = (bf16[4,1024,128]{2,1,0:T(8,128)(2,1)S(1)}, bf16[4,1024,128]{2,1,0:T(8,128)(2,1)}, u32[]{:S(2)}) copy-start(bf16[4,1024,128]{2,1,0:T(8,128)(2,1)} %mix_hbm.11) | copy-start | bytes 3145732
  158.2 16.6 %copy-start.25 = (f32[1920]{0:T(1024)S(1)}, f32[1920]{0:T(1024)}, u32[]{:S(2)}) copy-start(f32[1920]{0:T(1024)} %param.16) | copy-start | bytes 23044
  158.2 16.6 %copy-start.26 = (s32[1024]{0:T(1024)S(1)}, s32[1024]{0:T(1024)}, u32[]{:S(2)}) copy-start(s32[1024]{0:T(1024)} %param.10) | copy-start | bytes 12292
  168.7 14.7 %all-to-all-start.9 = ((bf16[8,128,256]{2,1,0:T(8,128)(2,1)}), bf16[8,128,256]{2,1,0:T(8,128)(2,1)S(1)}, u32[]{:S(2)}, u32[]{:S(2)}) async-start(bf16[8,128,256]{2,1,0:T(8,128)(2,1)} %cond_end.1), calls=%async_computation.9 | async-start | bytes 1048576 | tf_op jit(solution)/shard_map/all_to_all | solution.py:457
  196.8 15.9 %collective-permute-start.8 = (bf16[512,512]{1,0:T(8,128)(2,1)}, bf16[512,512]{1,0:T(8,128)(2,1)}, u32[]{:S(2)}, u32[]{:S(2)}) collective-permute-start(bf16[512,512]{1,0:T(8,128)(2,1)} %get-tuple-element.67.kv0_ref), channel_id=1, source_target_pairs={{0,16},{8,24},{16,32},{24,40},{32,48},{40,56},{48,64},{56,72},{64,... | collective-permute-start | bytes 1572872 | tf_op jit(solution)/shard_map/ppermute | solution.py:571
  200.8 22.4 %copy-start.18 = (bf16[512,256]{1,0:T(8,128)(2,1)S(1)}, bf16[512,256]{1,0:T(8,128)(2,1)}, u32[]{:S(2)}) copy-start(bf16[512,256]{1,0:T(8,128)(2,1)} %copy-done.17) | copy-start | bytes 786436
  213.8 13.4 %collective-permute-start.10 = (bf16[512,512]{1,0:T(8,128)(2,1)S(1)}, bf16[512,512]{1,0:T(8,128)(2,1)S(1)}, u32[]{:S(2)}, u32[]{:S(2)}) collective-permute-start(bf16[512,512]{1,0:T(8,128)(2,1)S(1)} %broadcast_select_fusion.1), channel_id=1, source_target_pairs={{0,8},{8,0},{16,24},{24,16},{32,40},{40,32},{48,56},{56,48},{64,72... | collective-permute-start | bytes 1572872 | tf_op jit(solution)/shard_map/ppermute | solution.py:453
  219.9 17.5 %collective-permute-start.9 = (bf16[512,512]{1,0:T(8,128)(2,1)S(1)}, bf16[512,512]{1,0:T(8,128)(2,1)S(1)}, u32[]{:S(2)}, u32[]{:S(2)}) collective-permute-start(bf16[512,512]{1,0:T(8,128)(2,1)S(1)} %get-tuple-element.70.kv1_ref), channel_id=1, source_target_pairs={{0,16},{8,24},{16,32},{24,40},{32,48},{40,56},{48,64},{56,72},{64,... | collective-permute-start | bytes 1572872 | tf_op jit(solution)/shard_map/ppermute | solution.py:571
  237.5 2.4 collective-permute-start.11
  (13 other events, 12.2 us)
Sparse Core Ops, SparseCore 0:
  32.0 71.2 all-gather.4
  105.0 70.4 all-gather.6

commit v6 on v5

--- a/solution.py
+++ b/solution.py
@@ -200,12 +200,12 @@
     finish(copies)
 
 
-def call(body, outs, scratch=(), smem=1, n=0, hbm=0, after=0, flops=10**9, name=None, mib=12, space=pl.ANY):
+def call(body, outs, scratch=(), smem=1, n=0, hbm=0, after=0, flops=10**9, name=None, mib=12):
     def spec(space):
         return pl.BlockSpec(memory_space=space)
 
     specs = [spec(pltpu.SMEM)] * smem + [spec(pltpu.VMEM)] * n
-    specs += [spec(space)] * hbm + [spec(pltpu.VMEM)] * after
+    specs += [spec(pl.ANY)] * hbm + [spec(pltpu.VMEM)] * after
     return pl.pallas_call(
         body,
         out_shape=outs,
@@ -478,6 +478,8 @@
     x_hi = rank // 4
     begin = song * 256 + x_hi * HALF
     share = song ^ (8 * x_hi)
+    dilated_weight = pltpu.with_memory_space_constraint(dilated_weight, pltpu.HBM)
+    mixing_weight = pltpu.with_memory_space_constraint(mixing_weight, pltpu.HBM)
     info = jnp.stack([core, begin, song, x_hi * 4, share // 2, share]).astype(jnp.int32)
 
     pack0, part = call(
@@ -491,15 +493,22 @@
         ],
         hbm=5,
         name="pack",
-        space=pltpu.HBM,
+        mib=60,
     )(info, dilated_weight, mixing_weight, upper_table, upsample_weight, middle_table)
     got0 = lax.ppermute(pack0, EVERY, other_half())
     mine = exchange(part, groups=Y_GROUPS)
     edge = jnp.where(x_hi == 0, upper_codes[-40:], upper_codes[:40])
     edge = lax.ppermute(edge, EVERY, song_neighbours())
-    mine, edge = lax.optimization_barrier((mine, edge))
+    pack1, pack2 = call(
+        later_kernel,
+        (shape(512, 512), shape(2, 512, 512)),
+        [pltpu.SemaphoreType.DMA((21,))],
+        hbm=2,
+        name="pack_later",
+        mib=60,
+    )(info, dilated_weight, mixing_weight)
+    mine, got0, edge, pack1, pack2 = lax.optimization_barrier((mine, got0, edge, pack1, pack2))
     full_own = gathered(mine)
-    mine, got0 = lax.optimization_barrier((mine, got0))
     others = lax.ppermute(mine, EVERY, other_half())
     sib0 = to_sibling(got0)
     codes = jnp.where(
@@ -517,15 +526,6 @@
         after=2,
         name="cond0",
     )(info, codes, upper_table, dilated_weight, got0, sib0)
-    pack1, pack2 = call(
-        later_kernel,
-        (shape(512, 512), shape(2, 512, 512)),
-        [pltpu.SemaphoreType.DMA((21,))],
-        hbm=2,
-        name="pack_later",
-        space=pltpu.HBM,
-    )(info, dilated_weight, mixing_weight)
-
     for level in range(4):
         terms = exchange(terms, groups=Y_GROUPS)
         if level == 0:

time: 253 us -> 246 us (0.972)
  local copies, waits for them, and re-layouts: 24.7 us -> 7.23 us
  waiting for transfers between devices: 51.9 us -> 63.8 us
  starting transfers between devices: 49.5 us -> 40.6 us
  Pallas kernels: 54.1 us -> 59.9 us
  blocking collectives: 54.9 us -> 58.3 us
    unnamed x56 -> x28, local copies, waits for them, and re-layouts: 23.2 us -> 5.26 us
    all_gather x2, waiting for transfers between devices: 0.01 us -> 16.4 us  [gathered(): lax.all_gather(parts, 'song', axis=0, tiled=False)]
    ppermute x1, waiting for transfers between devices: 16.3 us -> 2.49 us  [on_device(): got0 = lax.ppermute(pack0, EVERY, other_half())]
    ppermute x1, waiting for transfers between devices: 1.9 us -> 8.97 us  [on_device(): others = lax.ppermute(mine, EVERY, other_half())]
    ppermute x5, starting transfers between devices: 14.4 us -> 7.73 us  [to_sibling(): return lax.ppermute(value, 'song', [(i, i ^ 1) for i in range(16)])]
    ppermute x2, waiting for transfers between devices: 5.67 us -> 10.9 us  [from_two_back(): return lax.ppermute(value, 'song', [(i, i + 2) for i in range(14)])]
    all_to_all x6, blocking collectives: 54.9 us -> 58.3 us  [exchange(): lax.all_to_all(value, axis, 0, 0, axis_index_groups=groups, tiled=True)]
    ppermute x2, starting transfers between devices: 7.35 us -> 4.04 us  [from_two_back(): return lax.ppermute(value, 'song', [(i, i + 2) for i in range(14)])]
  transfers between devices with their start and end apart: 18 -> 18, of which waited for: 14 -> 14; matrix products, arithmetic and copies ran while one was open for 2% -> 2% of each run, Pallas kernels for 14% -> 16%
where the time goes in v6:
time: 246 us; the launch traced here: 245 us
  waiting for transfers between devices  63.8 us (26%)
  Pallas kernels  59.9 us (24%)
  blocking collectives  58.3 us (24%)
  starting transfers between devices  40.6 us (17%)
  between operations  13.7 us (6%)
  local copies, waits for them, and re-layouts  7.23 us (3%)
    all_to_all x6, blocking collectives, exchange(): lax.all_to_all(value, axis, 0, 0, axis_index_groups=groups, tiled=True)  58.3 us
    pallas_call x2, Pallas kernels, frames(): pl.pallas_call(functools.partial(frames_kernel, pair), out_shape=(shape(5...  24.5 us
    all_to_all x4, starting transfers between devices, exchange(): lax.all_to_all(value, axis, 0, 0, axis_index_groups=groups, tiled=True)  19.2 us
    all_to_all x4, waiting for transfers between devices, exchange(): lax.all_to_all(value, axis, 0, 0, axis_index_groups=groups, tiled=True)  16.6 us
    all_gather x2, waiting for transfers between devices, gathered(): lax.all_gather(parts, 'song', axis=0, tiled=False)  16.4 us
    ppermute x2, waiting for transfers between devices, from_two_back(): return lax.ppermute(value, 'song', [(i, i + 2) for i in range(14)])  10.9 us
    ppermute x1, waiting for transfers between devices, on_device(): others = lax.ppermute(mine, EVERY, other_half())  8.97 us
    pallas_call x3, Pallas kernels, on_device(): call(functools.partial(middle_kernel, level), (shape(ROWS[level + 1], 256...  8.41 us
  transfers between devices with their start and end apart: 18, of which 14 were waited for; matrix products, arithmetic and copies ran while one was open for 2% of the time, Pallas kernels for 16%

profile of v6, /device:TPU:3, one launch (start us, length us, event | category | flops | bytes accessed | tf_op | source)
XLA Modules:
  0.0 245.2 jit_solution(14184235460024111022)
XLA Ops:
  7.1 3.3 %pack.1 = (bf16[768,512]{1,0:T(8,128)(2,1)}, bf16[4,46,16,128]{3,2,1,0:T(8,128)(2,1)}) custom-call(s32[6]{0:T(128)} %stack.27.info, bf16[4,3,128,1024]{3,2,1,0:T(8,128)(2,1)} %dil_hbm.11, bf16[4,1024,128]{2,1,0:T(8,128)(2,1)} %mix_hbm.11, bf16[2048,128]{1,0:T(8,128)(2,1)} %table_ref.1, bf16[128,7680]{1,0:T(8,128)(2,1)} %up_hbm.1, bf16[256,1920]{1,0:T(8,128)(2,1)} %mid_hbm.1), custom_call_target="tpu_custom_call" | custom-call | flops 1000000000 | bytes 4194304 | tf_op jit(solution)/shard_map/pack/pallas_call | solution.py:485
  11.7 4.2 %all-to-all-start = ((bf16[4,46,16,128]{3,2,1,0:T(8,128)(2,1)}), bf16[4,46,16,128]{3,2,1,0:T(8,128)(2,1)S(1)}, u32[]{:S(2)}, u32[]{:S(2)}) async-start(bf16[4,46,16,128]{3,2,1,0:T(8,128)(2,1)} %get-tuple-element.43), calls=%async_computation | async-start | bytes 1507328 | tf_op jit(solution)/shard_map/all_to_all | solution.py:457
  16.0 4.8 %collective-permute-start.1 = (s32[40]{0:T(128)S(1)}, s32[40]{0:T(128)S(1)}, u32[]{:S(2)}, u32[]{:S(2)}) collective-permute-start(s32[40]{0:T(128)S(1)} %broadcast_select_fusion.3), channel_id=1, source_target_pairs={{0,8},{1,9},{2,10},{3,11},{8,16},{9,17},{10,18},{11,19},{16,24},{1... | collective-permute-start | bytes 488 | tf_op jit(solution)/shard_map/ppermute | solution.py:501
  20.8 3.5 %pack_later.1 = (bf16[512,512]{1,0:T(8,128)(2,1)}, bf16[2,512,512]{2,1,0:T(8,128)(2,1)}) custom-call(s32[6]{0:T(128)} %stack.27.info, bf16[4,3,128,1024]{3,2,1,0:T(8,128)(2,1)} %dil_hbm.11, bf16[4,1024,128]{2,1,0:T(8,128)(2,1)} %mix_hbm.11), custom_call_target="tpu_custom_call" | custom-call | flops 1000000000 | bytes 4194304 | tf_op jit(solution)/shard_map/pack_later/pallas_call | solution.py:502
  32.7 3.7 %cond0.1 = (f32[208,256]{1,0:T(8,128)S(1)}, bf16[4,208,256]{2,1,0:T(8,128)(2,1)}) custom-call(s32[6]{0:T(128)S(1)} %copy-done.7, s32[208,1]{1,0:T(8,128)S(1)} %broadcast_select_fusion.2.codes_ref, bf16[2048,128]{1,0:T(8,128)(2,1)S(1)} %copy-done.2, bf16[4,3,128,1024]{3,2,1,0:T(8,128)(2,1)} %dil_hbm.11, ...), custom_call_target="tpu_custom_call" | custom-call | flops 1000000000 | bytes 4194304 | tf_op jit(solution)/shard_map/cond0/pallas_call | solution.py:520
  36.4 4.2 %all-to-all-start.1 = ((bf16[4,208,256]{2,1,0:T(8,128)(2,1)}), bf16[4,208,256]{2,1,0:T(8,128)(2,1)S(1)}, u32[]{:S(2)}, u32[]{:S(2)}) async-start(bf16[4,208,256]{2,1,0:T(8,128)(2,1)} %get-tuple-element.51), calls=%async_computation.1 | async-start | bytes 851968 | tf_op jit(solution)/shard_map/all_to_all | solution.py:457
  40.6 9.0 %collective-permute-done.2 = bf16[4,46,16,128]{3,2,1,0:T(8,128)(2,1)S(1)} collective-permute-done((bf16[4,46,16,128]{3,2,1,0:T(8,128)(2,1)}, bf16[4,46,16,128]{3,2,1,0:T(8,128)(2,1)S(1)}, u32[]{:S(2)}, u32[]{:S(2)}) %collective-permute-start.2) | collective-permute-done | bytes 753696 | tf_op jit(solution)/shard_map/ppermute | solution.py:512
  51.9 11.2 %all_to_all.50.r_ref = bf16[4,208,256]{2,1,0:T(8,128)(2,1)S(1)} all-to-all(bf16[4,208,256]{2,1,0:T(8,128)(2,1)S(1)} %broadcast_in_dim.37), channel_id=1, replica_groups={{0,1,2,3},{4,5,6,7},{8,9,10,11},{12,13,14,15},{16,17,18,19},{20,21,22,2..., dimensions={0} | all-to-all | bytes 851968 | tf_op jit(solution)/shard_map/all_to_all | solution.py:457
  68.0 2.8 %cond.3 = (f32[208,256]{1,0:T(8,128)S(1)}, bf16[4,208,256]{2,1,0:T(8,128)(2,1)S(1)}) custom-call(s32[6]{0:T(128)S(1)} %copy-done.7, bf16[4,208,256]{2,1,0:T(8,128)(2,1)S(1)} %all_to_all.50.r_ref, f32[208,256]{1,0:T(8,128)S(1)} %copy-done.6, bf16[4,1024,128]{2,1,0:T(8,128)(2,1)} %mix_hbm.11, bf16[768,512]{1,0:T(8,128)(2,1)S(1)} %collective-permute-done.got_ref.got_hbm, ...), custom_call_target="tpu_custom_call" | custom-call | flops 1000000000 | bytes 4194304 | tf_op jit(solution)/shard_map/cond/pallas_call | solution.py:549
  70.9 11.8 %all_to_all.51 = bf16[4,208,256]{2,1,0:T(8,128)(2,1)S(1)} all-to-all(bf16[4,208,256]{2,1,0:T(8,128)(2,1)S(1)} %get-tuple-element.59), channel_id=1, replica_groups={{0,1,2,3},{4,5,6,7},{8,9,10,11},{12,13,14,15},{16,17,18,19},{20,21,22,2..., dimensions={0} | all-to-all | bytes 851968 | tf_op jit(solution)/shard_map/all_to_all | solution.py:457
  83.6 3.5 %all-to-all-start.4 = ((bf16[4,208,256]{2,1,0:T(8,128)(2,1)}), bf16[4,208,256]{2,1,0:T(8,128)(2,1)S(1)}, u32[]{:S(2)}, u32[]{:S(2)}) async-start(bf16[4,208,256]{2,1,0:T(8,128)(2,1)} %broadcast_in_dim.39), calls=%async_computation.4 | async-start | bytes 851968 | tf_op jit(solution)/shard_map/all_to_all | solution.py:457
  87.1 3.2 %collective-permute-done.5.got1_hbm.got_hbm = bf16[2,512,512]{2,1,0:T(8,128)(2,1)S(1)} collective-permute-done((bf16[2,512,512]{2,1,0:T(8,128)(2,1)}, bf16[2,512,512]{2,1,0:T(8,128)(2,1)S(1)}, u32[]{:S(2)}, u32[]{:S(2)}) %collective-permute-start.5) | collective-permute-done | bytes 1048608 | tf_op jit(solution)/shard_map/ppermute | solution.py:543
  90.3 3.4 %all-to-all-done.4.r_ref = bf16[4,208,256]{2,1,0:T(8,128)(2,1)S(1)} async-done(((bf16[4,208,256]{2,1,0:T(8,128)(2,1)}), bf16[4,208,256]{2,1,0:T(8,128)(2,1)S(1)}, u32[]{:S(2)}, u32[]{:S(2)}) %all-to-all-start.4) | async-done | bytes 426016 | tf_op jit(solution)/shard_map/all_to_all | solution.py:457
  93.7 2.7 %collective-permute-start.7 = (bf16[2,512,512]{2,1,0:T(8,128)(2,1)S(1)}, bf16[2,512,512]{2,1,0:T(8,128)(2,1)S(1)}, u32[]{:S(2)}, u32[]{:S(2)}) collective-permute-start(bf16[2,512,512]{2,1,0:T(8,128)(2,1)S(1)} %collective-permute-done.5.got1_hbm.got_hbm), channel_id=1, source_target_pairs={{0,8},{8,0},{16,24},{24,16},{32,40},{40,32},{48,56},{56,48},{64,72... | collective-permute-start | bytes 3145736 | tf_op jit(solution)/shard_map/ppermute | solution.py:453
  98.7 2.8 %cond.4 = (f32[208,256]{1,0:T(8,128)S(1)}, bf16[4,192,256]{2,1,0:T(8,128)(2,1)S(1)}) custom-call(s32[6]{0:T(128)S(1)} %copy-done.7, bf16[4,208,256]{2,1,0:T(8,128)(2,1)S(1)} %all-to-all-done.4.r_ref, f32[208,256]{1,0:T(8,128)S(1)} %get-tuple-element.61.h_ref, bf16[4,1024,128]{2,1,0:T(8,128)(2,1)} %mix_hbm.11, ...), custom_call_target="tpu_custom_call" | custom-call | flops 1000000000 | bytes 4194304 | tf_op jit(solution)/shard_map/cond/pallas_call | solution.py:549
  101.5 10.2 %all_to_all.52 = bf16[4,192,256]{2,1,0:T(8,128)(2,1)S(1)} all-to-all(bf16[4,192,256]{2,1,0:T(8,128)(2,1)S(1)} %get-tuple-element.63), channel_id=1, replica_groups={{0,1,2,3},{4,5,6,7},{8,9,10,11},{12,13,14,15},{16,17,18,19},{20,21,22,2..., dimensions={0} | all-to-all | bytes 786432 | tf_op jit(solution)/shard_map/all_to_all | solution.py:457
  111.8 9.3 %all_to_all.53.r_ref = bf16[4,192,256]{2,1,0:T(8,128)(2,1)S(1)} all-to-all(bf16[4,192,256]{2,1,0:T(8,128)(2,1)S(1)} %broadcast_in_dim.41), channel_id=1, replica_groups={{0,1,2,3},{4,5,6,7},{8,9,10,11},{12,13,14,15},{16,17,18,19},{20,21,22,2..., dimensions={0} | all-to-all | bytes 786432 | tf_op jit(solution)/shard_map/all_to_all | solution.py:457
  121.1 2.7 %cond.5 = (f32[192,256]{1,0:T(8,128)S(1)}, bf16[4,128,256]{2,1,0:T(8,128)(2,1)S(1)}) custom-call(s32[6]{0:T(128)S(1)} %copy-done.7, bf16[4,192,256]{2,1,0:T(8,128)(2,1)S(1)} %all_to_all.53.r_ref, f32[208,256]{1,0:T(8,128)S(1)} %get-tuple-element.64.h_ref, bf16[4,1024,128]{2,1,0:T(8,128)(2,1)} %mix_hbm.11, ...), custom_call_target="tpu_custom_call" | custom-call | flops 1000000000 | bytes 4194304 | tf_op jit(solution)/shard_map/cond/pallas_call | solution.py:549
  123.9 7.9 %all_to_all.54 = bf16[4,128,256]{2,1,0:T(8,128)(2,1)S(1)} all-to-all(bf16[4,128,256]{2,1,0:T(8,128)(2,1)S(1)} %get-tuple-element.65), channel_id=1, replica_groups={{0,1,2,3},{4,5,6,7},{8,9,10,11},{12,13,14,15},{16,17,18,19},{20,21,22,2..., dimensions={0} | all-to-all | bytes 524288 | tf_op jit(solution)/shard_map/all_to_all | solution.py:457
  131.9 7.9 %all_to_all.55.r_ref = bf16[4,128,256]{2,1,0:T(8,128)(2,1)S(1)} all-to-all(bf16[4,128,256]{2,1,0:T(8,128)(2,1)S(1)} %broadcast_in_dim.43), channel_id=1, replica_groups={{0,1,2,3},{4,5,6,7},{8,9,10,11},{12,13,14,15},{16,17,18,19},{20,21,22,2..., dimensions={0} | all-to-all | bytes 524288 | tf_op jit(solution)/shard_map/all_to_all | solution.py:457
  139.8 2.7 %cond_end.1 = bf16[8,128,256]{2,1,0:T(8,128)(2,1)} custom-call(s32[6]{0:T(128)S(1)} %copy-done.7, bf16[4,128,256]{2,1,0:T(8,128)(2,1)S(1)} %all_to_all.55.r_ref, f32[192,256]{1,0:T(8,128)S(1)} %get-tuple-element.66.h_ref, bf16[4,1024,128]{2,1,0:T(8,128)(2,1)} %mix_hbm.11, bf16[2,512,512]{2,1,0:T(8,128)(2,1)S(1)} %collective-permute-done.5.got1_hbm.got_hbm, ...), custom_call_target="tpu_custom_call" | custom-call | flops 1000000000 | bytes 4194304 | tf_op jit(solution)/shard_map/cond_end/pallas_call | solution.py:558
  142.5 7.3 %all-to-all-start.9 = ((bf16[8,128,256]{2,1,0:T(8,128)(2,1)}), bf16[8,128,256]{2,1,0:T(8,128)(2,1)S(1)}, u32[]{:S(2)}, u32[]{:S(2)}) async-start(bf16[8,128,256]{2,1,0:T(8,128)(2,1)} %cond_end.1), calls=%async_computation.9 | async-start | bytes 1048576 | tf_op jit(solution)/shard_map/all_to_all | solution.py:457
  150.0 2.5 %copy.21 = bf16[240,8,2,384]{3,1,2,0:T(8,128)(2,1)S(1)} copy(bf16[240,8,2,384]{3,2,1,0:T(2,128)(2,1)} %bitcast.30) | data formatting | bytes 5898240
  152.6 10.9 %all-to-all-done.9.hf_ref = bf16[8,128,256]{2,1,0:T(8,128)(2,1)S(1)} async-done(((bf16[8,128,256]{2,1,0:T(8,128)(2,1)}), bf16[8,128,256]{2,1,0:T(8,128)(2,1)S(1)}, u32[]{:S(2)}, u32[]{:S(2)}) %all-to-all-start.9) | async-done | bytes 524320 | tf_op jit(solution)/shard_map/all_to_all | solution.py:457
  163.5 16.4 %all-gather.7.cloned.1.call-done = bf16[64,46,16,128]{3,2,1,0:T(8,128)(2,1)} async-done(((bf16[4,46,16,128]{3,2,1,0:T(8,128)(2,1)}), bf16[64,46,16,128]{3,2,1,0:T(8,128)(2,1)}) %all-gather.7.cloned.1.call-update) | async-done | bytes 12058640 | tf_op jit(solution)/shard_map/all_gather | solution.py:461
  179.9 12.6 %frames.2 = (bf16[512,256]{1,0:T(8,128)(2,1)S(1)}, bf16[512,512]{1,0:T(8,128)(2,1)}) custom-call(s32[6]{0:T(128)S(1)} %copy-done.7, s32[1024]{0:T(1024)S(1)} %fusion.9.codes_ref, bf16[8,128,256]{2,1,0:T(8,128)(2,1)S(1)} %all-to-all-done.9.hf_ref, f32[1,1920]{1,0:T(1,128)S(1)} %broadcast_in_dim.44.gain_ref, bf16[1920,768]{1,0:T(8,128)(2,1)S(1)} %bitcast.24, ...), custom_call_target="tpu_custom_call" | custom-call | flops 4000000000 | bytes 20971520 | tf_op jit(solution)/shard_map/frames/pallas_call | solution.py:319
  195.3 11.8 %frames.3 = (bf16[512,256]{1,0:T(8,128)(2,1)S(1)}, bf16[512,512]{1,0:T(8,128)(2,1)S(1)}) custom-call(s32[6]{0:T(128)S(1)} %copy-done.7, s32[1024]{0:T(1024)S(1)} %fusion.9.codes_ref, bf16[8,128,256]{2,1,0:T(8,128)(2,1)S(1)} %all-to-all-done.9.hf_ref, f32[1,1920]{1,0:T(1,128)S(1)} %broadcast_in_dim.44.gain_ref, bf16[1920,768]{1,0:T(8,128)(2,1)S(1)} %bitcast.25, ...), custom_call_target="tpu_custom_call" | custom-call | flops 4000000000 | bytes 20971520 | tf_op jit(solution)/shard_map/frames/pallas_call | solution.py:319
  207.2 4.1 %collective-permute-done.8.far_ref = bf16[512,512]{1,0:T(8,128)(2,1)} collective-permute-done((bf16[512,512]{1,0:T(8,128)(2,1)}, bf16[512,512]{1,0:T(8,128)(2,1)}, u32[]{:S(2)}, u32[]{:S(2)}) %collective-permute-start.8) | collective-permute-done | bytes 524320 | tf_op jit(solution)/shard_map/ppermute | solution.py:571
  215.2 4.0 %own.1 = (f32[2,4,256,256]{3,2,1,0:T(8,128)S(1)}, f32[2,4,256,1]{3,2,1,0:T(8,128)S(1)}) custom-call(bf16[512,256]{1,0:T(8,128)(2,1)S(1)} %copy-done.4, bf16[512,256]{1,0:T(8,128)(2,1)S(1)} %get-tuple-element.71.q1_ref, bf16[512,512]{1,0:T(8,128)(2,1)} %get-tuple-element.69.kv0_ref, bf16[512,512]{1,0:T(8,128)(2,1)S(1)} %get-tuple-element.72.kv1_ref), custom_call_target="tpu_custom_call" | custom-call | flops 1000000000 | bytes 4194304 | tf_op jit(solution)/shard_map/own/pallas_call | solution.py:580
  219.2 4.8 %past.1 = (f32[2,4,256,256]{3,2,1,0:T(8,128)S(1)}, f32[2,4,256,1]{3,2,1,0:T(8,128)S(1)}) custom-call(s32[6]{0:T(128)S(1)} %copy-done.7, bf16[512,256]{1,0:T(8,128)(2,1)S(1)} %copy-done.4, bf16[512,256]{1,0:T(8,128)(2,1)S(1)} %get-tuple-element.71.q1_ref, bf16[512,512]{1,0:T(8,128)(2,1)} %collective-permute-done.8.far_ref, ...), custom_call_target="tpu_custom_call" | custom-call | flops 1000000000 | bytes 4194304 | tf_op jit(solution)/shard_map/past/pallas_call | solution.py:582
  224.0 6.8 %collective-permute-done.9.far_ref = bf16[512,512]{1,0:T(8,128)(2,1)S(1)} collective-permute-done((bf16[512,512]{1,0:T(8,128)(2,1)S(1)}, bf16[512,512]{1,0:T(8,128)(2,1)S(1)}, u32[]{:S(2)}, u32[]{:S(2)}) %collective-permute-start.9) | collective-permute-done | bytes 524320 | tf_op jit(solution)/shard_map/ppermute | solution.py:571
  233.3 5.0 %past_end.1 = bf16[1024,256]{1,0:T(8,128)(2,1)} custom-call(s32[6]{0:T(128)S(1)} %copy-done.7, bf16[512,256]{1,0:T(8,128)(2,1)S(1)} %copy-done.4, bf16[512,256]{1,0:T(8,128)(2,1)S(1)} %get-tuple-element.71.q1_ref, bf16[512,512]{1,0:T(8,128)(2,1)S(1)} %collective-permute-done.9.far_ref, bf16[512,512]{1,0:T(8,128)(2,1)S(1)} %collective-permute-done.11.near_ref, ...), custom_call_target="tpu_custom_call" | custom-call | flops 2000000000 | bytes 4194304 | tf_op jit(solution)/shard_map/past_end/pallas_call | solution.py:587
  (73 shorter events, 30.3 us)
Async XLA Ops:
  7.1 8.8 %copy-start.10 = (s32[256]{0:T(256)S(1)}, s32[256]{0:T(256)}, u32[]{:S(2)}) copy-start(s32[256]{0:T(256)} %param.9) | copy-start | bytes 3076
  10.4 18.7 %collective-permute-start = (bf16[768,512]{1,0:T(8,128)(2,1)}, bf16[768,512]{1,0:T(8,128)(2,1)S(1)}, u32[]{:S(2)}, u32[]{:S(2)}) collective-permute-start(bf16[768,512]{1,0:T(8,128)(2,1)} %get-tuple-element.44), channel_id=1, source_target_pairs={{0,68},{1,69},{2,70},{3,71},{4,64},{5,65},{6,66},{7,67},{8,76},{9,... | collective-permute-start | bytes 2359304 | tf_op jit(solution)/shard_map/ppermute | solution.py:498
  11.7 14.9 %all-to-all-start = ((bf16[4,46,16,128]{3,2,1,0:T(8,128)(2,1)}), bf16[4,46,16,128]{3,2,1,0:T(8,128)(2,1)S(1)}, u32[]{:S(2)}, u32[]{:S(2)}) async-start(bf16[4,46,16,128]{3,2,1,0:T(8,128)(2,1)} %get-tuple-element.43), calls=%async_computation | async-start | bytes 1507328 | tf_op jit(solution)/shard_map/all_to_all | solution.py:457
  15.9 16.8 %copy-start.2 = (bf16[2048,128]{1,0:T(8,128)(2,1)S(1)}, bf16[2048,128]{1,0:T(8,128)(2,1)}, u32[]{:S(2)}) copy-start(bf16[2048,128]{1,0:T(8,128)(2,1)} %table_ref.1) | copy-start | bytes 1572868
  15.9 16.8 %copy-start.7 = (s32[6]{0:T(128)S(1)}, s32[6]{0:T(128)}, u32[]{:S(2)}) copy-start(s32[6]{0:T(128)} %stack.27.info) | copy-start | bytes 76
  15.9 147.6 %all-gather.5.cloned.1.call-start = ((), (), s32[]{:S(2)}) async-start(), calls=%async_computation.10 | async-start | bytes 12812288 | tf_op jit(solution)/shard_map/all_gather | solution.py:461
  16.0 8.3 %collective-permute-start.1 = (s32[40]{0:T(128)S(1)}, s32[40]{0:T(128)S(1)}, u32[]{:S(2)}, u32[]{:S(2)}) collective-permute-start(s32[40]{0:T(128)S(1)} %broadcast_select_fusion.3), channel_id=1, source_target_pairs={{0,8},{1,9},{2,10},{3,11},{8,16},{9,17},{10,18},{11,19},{16,24},{1... | collective-permute-start | bytes 488 | tf_op jit(solution)/shard_map/ppermute | solution.py:501
  26.6 2.5 %copy-start.8 = (bf16[4,46,16,128]{3,2,1,0:T(8,128)(2,1)}, bf16[4,46,16,128]{3,2,1,0:T(8,128)(2,1)S(1)}, u32[]{:S(2)}) copy-start(bf16[4,46,16,128]{3,2,1,0:T(8,128)(2,1)S(1)} %all-to-all-done) | copy-start | bytes 2260996
  29.1 3.5 %collective-permute-start.3 = (bf16[768,512]{1,0:T(8,128)(2,1)S(1)}, bf16[768,512]{1,0:T(8,128)(2,1)S(1)}, u32[]{:S(2)}, u32[]{:S(2)}) collective-permute-start(bf16[768,512]{1,0:T(8,128)(2,1)S(1)} %collective-permute-done.got_ref.got_hbm), channel_id=1, source_target_pairs={{0,8},{8,0},{16,24},{24,16},{32,40},{40,32},{48,56},{56,48},{64,72... | collective-permute-start | bytes 2359304 | tf_op jit(solution)/shard_map/ppermute | solution.py:453
  30.8 18.7 %collective-permute-start.2 = (bf16[4,46,16,128]{3,2,1,0:T(8,128)(2,1)}, bf16[4,46,16,128]{3,2,1,0:T(8,128)(2,1)S(1)}, u32[]{:S(2)}, u32[]{:S(2)}) collective-permute-start(bf16[4,46,16,128]{3,2,1,0:T(8,128)(2,1)} %copy-done.8), channel_id=1, source_target_pairs={{0,68},{1,69},{2,70},{3,71},{4,64},{5,65},{6,66},{7,67},{8,76},{9,... | collective-permute-start | bytes 2261000 | tf_op jit(solution)/shard_map/ppermute | solution.py:512
  36.4 27.2 %copy-start.5 = (f32[208,256]{1,0:T(8,128)}, f32[208,256]{1,0:T(8,128)S(1)}, u32[]{:S(2)}) copy-start(f32[208,256]{1,0:T(8,128)S(1)} %get-tuple-element.57.h_ref) | copy-start | bytes 638980
  36.4 13.2 %all-to-all-start.1 = ((bf16[4,208,256]{2,1,0:T(8,128)(2,1)}), bf16[4,208,256]{2,1,0:T(8,128)(2,1)S(1)}, u32[]{:S(2)}, u32[]{:S(2)}) async-start(bf16[4,208,256]{2,1,0:T(8,128)(2,1)} %get-tuple-element.51), calls=%async_computation.1 | async-start | bytes 851968 | tf_op jit(solution)/shard_map/all_to_all | solution.py:457
  40.6 139.3 %all-gather.7.cloned.1.call-start = ((), (), s32[]{:S(2)}) async-start(), calls=%async_computation.11 | async-start | bytes 12812288 | tf_op jit(solution)/shard_map/all_gather | solution.py:461
  49.6 0.9 copy-start.9
  50.5 13.1 %collective-permute-start.4 = (bf16[512,512]{1,0:T(8,128)(2,1)}, bf16[512,512]{1,0:T(8,128)(2,1)S(1)}, u32[]{:S(2)}, u32[]{:S(2)}) collective-permute-start(bf16[512,512]{1,0:T(8,128)(2,1)} %get-tuple-element.52), channel_id=1, source_target_pairs={{0,68},{1,69},{2,70},{3,71},{4,64},{5,65},{6,66},{7,67},{8,76},{9,... | collective-permute-start | bytes 1572872 | tf_op jit(solution)/shard_map/ppermute | solution.py:534
  63.6 3.3 %collective-permute-start.6 = (bf16[512,512]{1,0:T(8,128)(2,1)S(1)}, bf16[512,512]{1,0:T(8,128)(2,1)S(1)}, u32[]{:S(2)}, u32[]{:S(2)}) collective-permute-start(bf16[512,512]{1,0:T(8,128)(2,1)S(1)} %collective-permute-done.4.got1_hbm.got_hbm), channel_id=1, source_target_pairs={{0,8},{8,0},{16,24},{24,16},{32,40},{40,32},{48,56},{56,48},{64,72... | collective-permute-start | bytes 1572872 | tf_op jit(solution)/shard_map/ppermute | solution.py:453
  65.2 25.0 %collective-permute-start.5 = (bf16[2,512,512]{2,1,0:T(8,128)(2,1)}, bf16[2,512,512]{2,1,0:T(8,128)(2,1)S(1)}, u32[]{:S(2)}, u32[]{:S(2)}) collective-permute-start(bf16[2,512,512]{2,1,0:T(8,128)(2,1)} %get-tuple-element.55), channel_id=1, source_target_pairs={{0,68},{1,69},{2,70},{3,71},{4,64},{5,65},{6,66},{7,67},{8,76},{9,... | collective-permute-start | bytes 3145736 | tf_op jit(solution)/shard_map/ppermute | solution.py:543
  66.9 4.0 %copy-start = (bf16[512,512]{1,0:T(8,128)(2,1)}, bf16[512,512]{1,0:T(8,128)(2,1)S(1)}, u32[]{:S(2)}) copy-start(bf16[512,512]{1,0:T(8,128)(2,1)S(1)} %collective-permute-done.6.sib1_hbm.sib_hbm) | copy-start | bytes 1572868
  66.9 1.1 copy-start.6
  70.9 27.8 %copy-start.1 = (bf16[512,512]{1,0:T(8,128)(2,1)S(1)}, bf16[512,512]{1,0:T(8,128)(2,1)}, u32[]{:S(2)}) copy-start(bf16[512,512]{1,0:T(8,128)(2,1)} %copy-done) | copy-start | bytes 1572868
  83.6 10.1 %all-to-all-start.4 = ((bf16[4,208,256]{2,1,0:T(8,128)(2,1)}), bf16[4,208,256]{2,1,0:T(8,128)(2,1)S(1)}, u32[]{:S(2)}, u32[]{:S(2)}) async-start(bf16[4,208,256]{2,1,0:T(8,128)(2,1)} %broadcast_in_dim.39), calls=%async_computation.4 | async-start | bytes 851968 | tf_op jit(solution)/shard_map/all_to_all | solution.py:457
  93.7 5.0 %collective-permute-start.7 = (bf16[2,512,512]{2,1,0:T(8,128)(2,1)S(1)}, bf16[2,512,512]{2,1,0:T(8,128)(2,1)S(1)}, u32[]{:S(2)}, u32[]{:S(2)}) collective-permute-start(bf16[2,512,512]{2,1,0:T(8,128)(2,1)S(1)} %collective-permute-done.5.got1_hbm.got_hbm), channel_id=1, source_target_pairs={{0,8},{8,0},{16,24},{24,16},{32,40},{40,32},{48,56},{56,48},{64,72... | collective-permute-start | bytes 3145736 | tf_op jit(solution)/shard_map/ppermute | solution.py:453
  131.8 17.9 %copy-start.11 = (f32[1920]{0:T(1024)S(1)}, f32[1920]{0:T(1024)}, u32[]{:S(2)}) copy-start(f32[1920]{0:T(1024)} %param.16) | copy-start | bytes 23044
  131.9 17.9 %copy-start.12 = (s32[1024]{0:T(1024)S(1)}, s32[1024]{0:T(1024)}, u32[]{:S(2)}) copy-start(s32[1024]{0:T(1024)} %param.10) | copy-start | bytes 12292
  142.5 21.0 %all-to-all-start.9 = ((bf16[8,128,256]{2,1,0:T(8,128)(2,1)}), bf16[8,128,256]{2,1,0:T(8,128)(2,1)S(1)}, u32[]{:S(2)}, u32[]{:S(2)}) async-start(bf16[8,128,256]{2,1,0:T(8,128)(2,1)} %cond_end.1), calls=%async_computation.9 | async-start | bytes 1048576 | tf_op jit(solution)/shard_map/all_to_all | solution.py:457
  192.5 0.7 copy-start.3
  193.2 18.1 %collective-permute-start.8 = (bf16[512,512]{1,0:T(8,128)(2,1)}, bf16[512,512]{1,0:T(8,128)(2,1)}, u32[]{:S(2)}, u32[]{:S(2)}) collective-permute-start(bf16[512,512]{1,0:T(8,128)(2,1)} %get-tuple-element.69.kv0_ref), channel_id=1, source_target_pairs={{0,16},{8,24},{16,32},{24,40},{32,48},{40,56},{48,64},{56,72},{64,... | collective-permute-start | bytes 1572872 | tf_op jit(solution)/shard_map/ppermute | solution.py:571
  195.3 19.9 %copy-start.4 = (bf16[512,256]{1,0:T(8,128)(2,1)S(1)}, bf16[512,256]{1,0:T(8,128)(2,1)}, u32[]{:S(2)}) copy-start(bf16[512,256]{1,0:T(8,128)(2,1)} %copy-done.3) | copy-start | bytes 786436
  212.4 6.8 %collective-permute-start.10 = (bf16[512,512]{1,0:T(8,128)(2,1)S(1)}, bf16[512,512]{1,0:T(8,128)(2,1)S(1)}, u32[]{:S(2)}, u32[]{:S(2)}) collective-permute-start(bf16[512,512]{1,0:T(8,128)(2,1)S(1)} %broadcast_select_fusion.1), channel_id=1, source_target_pairs={{0,8},{8,0},{16,24},{24,16},{32,40},{40,32},{48,56},{56,48},{64,72... | collective-permute-start | bytes 1572872 | tf_op jit(solution)/shard_map/ppermute | solution.py:453
  213.3 17.5 %collective-permute-start.9 = (bf16[512,512]{1,0:T(8,128)(2,1)S(1)}, bf16[512,512]{1,0:T(8,128)(2,1)S(1)}, u32[]{:S(2)}, u32[]{:S(2)}) collective-permute-start(bf16[512,512]{1,0:T(8,128)(2,1)S(1)} %get-tuple-element.72.kv1_ref), channel_id=1, source_target_pairs={{0,16},{8,24},{16,32},{24,40},{32,48},{40,56},{48,64},{56,72},{64,... | collective-permute-start | bytes 1572872 | tf_op jit(solution)/shard_map/ppermute | solution.py:571
  230.9 2.4 collective-permute-start.11
Sparse Core Ops, SparseCore 0:
  29.3 73.8 all-gather.4
  104.9 74.9 all-gather.6

commit v7 on v6

--- a/solution.py
+++ b/solution.py
@@ -169,32 +169,30 @@
     return [pltpu.make_async_copy(a, b, sems.at[i]) for i, (a, b) in enumerate(pairs)]
 
 
-def pack_kernel(info, dil_hbm, mix_hbm, tab_hbm, up_hbm, mid_hbm, pack0, part_ref, up, mid, wide, sems):
+def share_kernel(info, up_hbm, mid_hbm, part_ref, up, mid, wide, sems):
     pairs = [
         (up_hbm.at[pl.ds(info[4] * 16, 16), pl.ds(pl.multiple_of(info[0] * 2 * D, 128), 2 * D)], up),
         (mid_hbm.at[pl.ds(info[5] * 16, 16), :], mid),
     ]
-    pairs += half_copies(info, 0, dil_hbm, mix_hbm, pack0)
-    for i in range(4):
-        rows = pl.ds(pl.multiple_of(info[0] * 1024 + i * 256, 256), 256)
-        pairs.append((tab_hbm.at[rows, :], pack0.at[pl.ds(512, 256), pl.ds(i * 128, 128)]))
     copies = copies_of(pairs, sems)
     start(copies)
-    finish(copies[:2])
     wide[...] = jnp.zeros_like(wide)
+    finish(copies)
     for block in range(BLOCKS):
         wide[:, block, :] = mid[:, block * 128 : block * 128 + 128].astype(F32)
     for y in range(4):
         for block in range(UP_BLOCKS):
             part_ref[y, block] = up[:, block * 128 : block * 128 + 128]
         part_ref[y, UP_BLOCKS:] = wide[...].astype(BF)
-    finish(copies[2:])
-
-
-def later_kernel(info, dil_hbm, mix_hbm, pack1, pack2, sems):
-    pairs = half_copies(info, 1, dil_hbm, mix_hbm, pack1)
+
+
+def pack_kernel(info, dil_hbm, mix_hbm, tab_hbm, pack0, pack1, pack2, sems):
+    pairs = half_copies(info, 0, dil_hbm, mix_hbm, pack0) + half_copies(info, 1, dil_hbm, mix_hbm, pack1)
     for i in range(2):
         pairs += half_copies(info, 2 + i, dil_hbm, mix_hbm, pack2.at[i])
+    for i in range(4):
+        rows = pl.ds(pl.multiple_of(info[0] * 1024 + i * 256, 256), 256)
+        pairs.append((tab_hbm.at[rows, :], pack0.at[pl.ds(512, 256), pl.ds(i * 128, 128)]))
     copies = copies_of(pairs, sems)
     start(copies)
     finish(copies)
@@ -482,35 +480,38 @@
     mixing_weight = pltpu.with_memory_space_constraint(mixing_weight, pltpu.HBM)
     info = jnp.stack([core, begin, song, x_hi * 4, share // 2, share]).astype(jnp.int32)
 
-    pack0, part = call(
-        pack_kernel,
-        (shape(768, 512), shape(4, PART, 16, 128)),
+    part = call(
+        share_kernel,
+        shape(4, PART, 16, 128),
         [
             pltpu.VMEM((16, 2 * D), BF),
             pltpu.VMEM((16, D), BF),
             pltpu.VMEM((16, 16, 128), F32),
-            pltpu.SemaphoreType.DMA((13,)),
+            pltpu.SemaphoreType.DMA((2,)),
         ],
-        hbm=5,
+        hbm=2,
+        name="share",
+        mib=60,
+    )(info, upsample_weight, middle_table)
+    mine = exchange(part, groups=Y_GROUPS)
+
+    pack0, pack1, pack2 = call(
+        pack_kernel,
+        (shape(768, 512), shape(512, 512), shape(2, 512, 512)),
+        [pltpu.SemaphoreType.DMA((32,))],
+        hbm=3,
         name="pack",
         mib=60,
-    )(info, dilated_weight, mixing_weight, upper_table, upsample_weight, middle_table)
+    )(info, dilated_weight, mixing_weight, upper_table)
     got0 = lax.ppermute(pack0, EVERY, other_half())
-    mine = exchange(part, groups=Y_GROUPS)
+
     edge = jnp.where(x_hi == 0, upper_codes[-40:], upper_codes[:40])
     edge = lax.ppermute(edge, EVERY, song_neighbours())
-    pack1, pack2 = call(
-        later_kernel,
-        (shape(512, 512), shape(2, 512, 512)),
-        [pltpu.SemaphoreType.DMA((21,))],
-        hbm=2,
-        name="pack_later",
-        mib=60,
-    )(info, dilated_weight, mixing_weight)
-    mine, got0, edge, pack1, pack2 = lax.optimization_barrier((mine, got0, edge, pack1, pack2))
+    mine, edge, pack1 = lax.optimization_barrier((mine, edge, pack1))
     full_own = gathered(mine)
-    others = lax.ppermute(mine, EVERY, other_half())
+    pack1, got0 = lax.optimization_barrier((pack1, got0))
     sib0 = to_sibling(got0)
+    got1 = lax.ppermute(pack1, EVERY, other_half())
     codes = jnp.where(
         x_hi == 0,
         jnp.concatenate([edge, upper_codes[: HALF + 40]]),
@@ -529,16 +530,16 @@
     for level in range(4):
         terms = exchange(terms, groups=Y_GROUPS)
         if level == 0:
-            others, pack1, terms = lax.optimization_barrier((others, pack1, terms))
-            full_other = gathered(others)
-            got1 = lax.ppermute(pack1, EVERY, other_half())
+            mine, terms = lax.optimization_barrier((mine, terms))
+            others = lax.ppermute(mine, EVERY, other_half())
         total = terms[0].astype(F32)
         for y in range(1, 4):
             total = total + terms[y].astype(F32)
         r = jnp.maximum(total, 0.0).astype(BF)
         r = exchange(jnp.broadcast_to(r[None], terms.shape), groups=Y_GROUPS)
         if level == 0:
-            got1, pack2, r = lax.optimization_barrier((got1, pack2, r))
+            got1, others, pack2, r = lax.optimization_barrier((got1, others, pack2, r))
+            full_other = gathered(others)
             sib1 = to_sibling(got1)
             got2 = lax.ppermute(pack2, EVERY, other_half())
             stacks = [(got0, sib0), (got1, sib1)]

time: 246 us -> 253 us (1.028)
  starting transfers between devices: 40.6 us -> 47.8 us
    ppermute x1, waiting for transfers between devices: 0.58 us -> 22.7 us  [on_device(): got1 = lax.ppermute(pack1, EVERY, other_half())]
    all_gather x2, waiting for transfers between devices: 16.4 us -> 0.01 us  [gathered(): lax.all_gather(parts, 'song', axis=0, tiled=False)]
    ppermute x1, waiting for transfers between devices: 2.49 us -> 16.3 us  [on_device(): got0 = lax.ppermute(pack0, EVERY, other_half())]
    ppermute x1, waiting for transfers between devices: 8.97 us -> 0.01 us  [on_device(): others = lax.ppermute(mine, EVERY, other_half())]
    ppermute x5, starting transfers between devices: 7.73 us -> 14.8 us  [to_sibling(): return lax.ppermute(value, 'song', [(i, i ^ 1) for i in range(16)])]
    ppermute x2, waiting for transfers between devices: 10.9 us -> 5.21 us  [from_two_back(): return lax.ppermute(value, 'song', [(i, i + 2) for i in range(14)])]
    all_to_all x4, waiting for transfers between devices: 16.6 us -> 11.5 us  [exchange(): lax.all_to_all(value, axis, 0, 0, axis_index_groups=groups, tiled=True)]
    ppermute x2, starting transfers between devices: 4.04 us -> 7.59 us  [from_two_back(): return lax.ppermute(value, 'song', [(i, i + 2) for i in range(14)])]
  transfers between devices with their start and end apart: 18 -> 18, of which waited for: 14 -> 11; matrix products, arithmetic and copies ran while one was open for 2% -> 2% of each run, Pallas kernels for 16% -> 15%
where the time goes in v7:
time: 253 us; the launch traced here: 252 us
  waiting for transfers between devices  65 us (26%)
  Pallas kernels  58.7 us (23%)
  blocking collectives  56.3 us (22%)
  starting transfers between devices  47.8 us (19%)
  between operations  13.8 us (5%)
  local copies, waits for them, and re-layouts  8.91 us (4%)
    all_to_all x6, blocking collectives, exchange(): lax.all_to_all(value, axis, 0, 0, axis_index_groups=groups, tiled=True)  56.3 us
    pallas_call x2, Pallas kernels, frames(): pl.pallas_call(functools.partial(frames_kernel, pair), out_shape=(shape(5...  24.4 us
    ppermute x1, waiting for transfers between devices, on_device(): got1 = lax.ppermute(pack1, EVERY, other_half())  22.7 us
    all_to_all x4, starting transfers between devices, exchange(): lax.all_to_all(value, axis, 0, 0, axis_index_groups=groups, tiled=True)  16.9 us
    ppermute x1, waiting for transfers between devices, on_device(): got0 = lax.ppermute(pack0, EVERY, other_half())  16.3 us
    ppermute x5, starting transfers between devices, to_sibling(): return lax.ppermute(value, 'song', [(i, i ^ 1) for i in range(16)])  14.8 us
    all_to_all x4, waiting for transfers between devices, exchange(): lax.all_to_all(value, axis, 0, 0, axis_index_groups=groups, tiled=True)  11.5 us
    pallas_call x3, Pallas kernels, on_device(): call(functools.partial(middle_kernel, level), (shape(ROWS[level + 1], 256...  8.41 us
  transfers between devices with their start and end apart: 18, of which 11 were waited for; matrix products, arithmetic and copies ran while one was open for 2% of the time, Pallas kernels for 15%

profile of v7, /device:TPU:3, one launch (start us, length us, event | category | flops | bytes accessed | tf_op | source)
XLA Modules:
  0.0 252.0 jit_solution(17954197510454916811)
XLA Ops:
  9.8 4.2 %all-to-all-start = ((bf16[4,46,16,128]{3,2,1,0:T(8,128)(2,1)}), bf16[4,46,16,128]{3,2,1,0:T(8,128)(2,1)}, u32[]{:S(2)}, u32[]{:S(2)}) async-start(bf16[4,46,16,128]{3,2,1,0:T(8,128)(2,1)} %share.1), calls=%async_computation | async-start | bytes 1507328 | tf_op jit(solution)/shard_map/all_to_all | solution.py:455
  14.1 4.4 %collective-permute-start = (s32[40]{0:T(128)S(1)}, s32[40]{0:T(128)S(1)}, u32[]{:S(2)}, u32[]{:S(2)}) collective-permute-start(s32[40]{0:T(128)S(1)} %broadcast_select_fusion.3), channel_id=1, source_target_pairs={{0,8},{1,9},{2,10},{3,11},{8,16},{9,17},{10,18},{11,19},{16,24},{1... | collective-permute-start | bytes 488 | tf_op jit(solution)/shard_map/ppermute | solution.py:509
  18.6 4.0 %pack.1 = (bf16[768,512]{1,0:T(8,128)(2,1)}, bf16[512,512]{1,0:T(8,128)(2,1)}, bf16[2,512,512]{2,1,0:T(8,128)(2,1)}) custom-call(s32[6]{0:T(128)} %stack.27.info, bf16[4,3,128,1024]{3,2,1,0:T(8,128)(2,1)} %dil_hbm.9, bf16[4,1024,128]{2,1,0:T(8,128)(2,1)} %mix_hbm.9, bf16[2048,128]{1,0:T(8,128)(2,1)} %table_ref.1), custom_call_target="tpu_custom_call" | custom-call | flops 1000000000 | bytes 4194304 | tf_op jit(solution)/shard_map/pack/pallas_call | solution.py:498
  26.4 16.3 %collective-permute-done.1.got_ref.got_hbm = bf16[768,512]{1,0:T(8,128)(2,1)S(1)} collective-permute-done((bf16[768,512]{1,0:T(8,128)(2,1)}, bf16[768,512]{1,0:T(8,128)(2,1)S(1)}, u32[]{:S(2)}, u32[]{:S(2)}) %collective-permute-start.1) | collective-permute-done | bytes 786464 | tf_op jit(solution)/shard_map/ppermute | solution.py:506
  42.7 2.7 %collective-permute-start.3 = (bf16[768,512]{1,0:T(8,128)(2,1)S(1)}, bf16[768,512]{1,0:T(8,128)(2,1)S(1)}, u32[]{:S(2)}, u32[]{:S(2)}) collective-permute-start(bf16[768,512]{1,0:T(8,128)(2,1)S(1)} %collective-permute-done.1.got_ref.got_hbm), channel_id=1, source_target_pairs={{0,8},{8,0},{16,24},{24,16},{32,40},{40,32},{48,56},{56,48},{64,72... | collective-permute-start | bytes 2359304 | tf_op jit(solution)/shard_map/ppermute | solution.py:451
  47.3 2.9 %cond0.1 = (f32[208,256]{1,0:T(8,128)S(1)}, bf16[4,208,256]{2,1,0:T(8,128)(2,1)S(1)}) custom-call(s32[6]{0:T(128)S(1)} %copy-done.9, s32[208,1]{1,0:T(8,128)S(1)} %broadcast_select_fusion.2.codes_ref, bf16[2048,128]{1,0:T(8,128)(2,1)S(1)} %copy-done.2, bf16[4,3,128,1024]{3,2,1,0:T(8,128)(2,1)} %dil_hbm.9, ...), custom_call_target="tpu_custom_call" | custom-call | flops 1000000000 | bytes 4194304 | tf_op jit(solution)/shard_map/cond0/pallas_call | solution.py:521
  50.2 10.4 %all_to_all.50 = bf16[4,208,256]{2,1,0:T(8,128)(2,1)S(1)} all-to-all(bf16[4,208,256]{2,1,0:T(8,128)(2,1)S(1)} %get-tuple-element.49), channel_id=1, replica_groups={{0,1,2,3},{4,5,6,7},{8,9,10,11},{12,13,14,15},{16,17,18,19},{20,21,22,2..., dimensions={0} | all-to-all | bytes 851968 | tf_op jit(solution)/shard_map/all_to_all | solution.py:455
  63.0 3.5 %all-to-all-start.2 = ((bf16[4,208,256]{2,1,0:T(8,128)(2,1)}), bf16[4,208,256]{2,1,0:T(8,128)(2,1)S(1)}, u32[]{:S(2)}, u32[]{:S(2)}) async-start(bf16[4,208,256]{2,1,0:T(8,128)(2,1)} %broadcast_in_dim.37), calls=%async_computation.2 | async-start | bytes 851968 | tf_op jit(solution)/shard_map/all_to_all | solution.py:455
  66.5 22.7 %collective-permute-done.2.got1_hbm.got_hbm = bf16[512,512]{1,0:T(8,128)(2,1)S(1)} collective-permute-done((bf16[512,512]{1,0:T(8,128)(2,1)}, bf16[512,512]{1,0:T(8,128)(2,1)S(1)}, u32[]{:S(2)}, u32[]{:S(2)}) %collective-permute-start.2) | collective-permute-done | bytes 524320 | tf_op jit(solution)/shard_map/ppermute | solution.py:514
  95.8 2.8 %cond.3 = (f32[208,256]{1,0:T(8,128)S(1)}, bf16[4,208,256]{2,1,0:T(8,128)(2,1)S(1)}) custom-call(s32[6]{0:T(128)S(1)} %copy-done.9, bf16[4,208,256]{2,1,0:T(8,128)(2,1)S(1)} %copy-done.4, f32[208,256]{1,0:T(8,128)S(1)} %copy-done.8, bf16[4,1024,128]{2,1,0:T(8,128)(2,1)} %mix_hbm.9, bf16[768,512]{1,0:T(8,128)(2,1)S(1)} %collective-permute-done.1.got_ref.got_hbm, ...), custom_call_target="tpu_custom_call" | custom-call | flops 1000000000 | bytes 4194304 | tf_op jit(solution)/shard_map/cond/pallas_call | solution.py:550
  98.7 10.5 %all_to_all.51 = bf16[4,208,256]{2,1,0:T(8,128)(2,1)S(1)} all-to-all(bf16[4,208,256]{2,1,0:T(8,128)(2,1)S(1)} %get-tuple-element.57), channel_id=1, replica_groups={{0,1,2,3},{4,5,6,7},{8,9,10,11},{12,13,14,15},{16,17,18,19},{20,21,22,2..., dimensions={0} | all-to-all | bytes 851968 | tf_op jit(solution)/shard_map/all_to_all | solution.py:455
  110.1 3.5 %all-to-all-start.4 = ((bf16[4,208,256]{2,1,0:T(8,128)(2,1)}), bf16[4,208,256]{2,1,0:T(8,128)(2,1)S(1)}, u32[]{:S(2)}, u32[]{:S(2)}) async-start(bf16[4,208,256]{2,1,0:T(8,128)(2,1)} %broadcast_in_dim.39), calls=%async_computation.4 | async-start | bytes 851968 | tf_op jit(solution)/shard_map/all_to_all | solution.py:455
  113.6 3.7 %collective-permute-done.5.got1_hbm.got_hbm = bf16[2,512,512]{2,1,0:T(8,128)(2,1)S(1)} collective-permute-done((bf16[2,512,512]{2,1,0:T(8,128)(2,1)}, bf16[2,512,512]{2,1,0:T(8,128)(2,1)S(1)}, u32[]{:S(2)}, u32[]{:S(2)}) %collective-permute-start.5) | collective-permute-done | bytes 1048608 | tf_op jit(solution)/shard_map/ppermute | solution.py:544
  117.2 3.1 %all-to-all-done.4.r_ref = bf16[4,208,256]{2,1,0:T(8,128)(2,1)S(1)} async-done(((bf16[4,208,256]{2,1,0:T(8,128)(2,1)}), bf16[4,208,256]{2,1,0:T(8,128)(2,1)S(1)}, u32[]{:S(2)}, u32[]{:S(2)}) %all-to-all-start.4) | async-done | bytes 426016 | tf_op jit(solution)/shard_map/all_to_all | solution.py:455
  125.2 2.8 %cond.4 = (f32[208,256]{1,0:T(8,128)S(1)}, bf16[4,192,256]{2,1,0:T(8,128)(2,1)S(1)}) custom-call(s32[6]{0:T(128)S(1)} %copy-done.9, bf16[4,208,256]{2,1,0:T(8,128)(2,1)S(1)} %all-to-all-done.4.r_ref, f32[208,256]{1,0:T(8,128)S(1)} %get-tuple-element.59.h_ref, bf16[4,1024,128]{2,1,0:T(8,128)(2,1)} %mix_hbm.9, ...), custom_call_target="tpu_custom_call" | custom-call | flops 1000000000 | bytes 4194304 | tf_op jit(solution)/shard_map/cond/pallas_call | solution.py:550
  128.0 10.2 %all_to_all.52 = bf16[4,192,256]{2,1,0:T(8,128)(2,1)S(1)} all-to-all(bf16[4,192,256]{2,1,0:T(8,128)(2,1)S(1)} %get-tuple-element.61), channel_id=1, replica_groups={{0,1,2,3},{4,5,6,7},{8,9,10,11},{12,13,14,15},{16,17,18,19},{20,21,22,2..., dimensions={0} | all-to-all | bytes 786432 | tf_op jit(solution)/shard_map/all_to_all | solution.py:455
  138.4 9.3 %all_to_all.53.r_ref = bf16[4,192,256]{2,1,0:T(8,128)(2,1)S(1)} all-to-all(bf16[4,192,256]{2,1,0:T(8,128)(2,1)S(1)} %broadcast_in_dim.41), channel_id=1, replica_groups={{0,1,2,3},{4,5,6,7},{8,9,10,11},{12,13,14,15},{16,17,18,19},{20,21,22,2..., dimensions={0} | all-to-all | bytes 786432 | tf_op jit(solution)/shard_map/all_to_all | solution.py:455
  147.6 2.7 %cond.5 = (f32[192,256]{1,0:T(8,128)S(1)}, bf16[4,128,256]{2,1,0:T(8,128)(2,1)S(1)}) custom-call(s32[6]{0:T(128)S(1)} %copy-done.9, bf16[4,192,256]{2,1,0:T(8,128)(2,1)S(1)} %all_to_all.53.r_ref, f32[208,256]{1,0:T(8,128)S(1)} %get-tuple-element.62.h_ref, bf16[4,1024,128]{2,1,0:T(8,128)(2,1)} %mix_hbm.9, ...), custom_call_target="tpu_custom_call" | custom-call | flops 1000000000 | bytes 4194304 | tf_op jit(solution)/shard_map/cond/pallas_call | solution.py:550
  150.4 7.9 %all_to_all.54 = bf16[4,128,256]{2,1,0:T(8,128)(2,1)S(1)} all-to-all(bf16[4,128,256]{2,1,0:T(8,128)(2,1)S(1)} %get-tuple-element.63), channel_id=1, replica_groups={{0,1,2,3},{4,5,6,7},{8,9,10,11},{12,13,14,15},{16,17,18,19},{20,21,22,2..., dimensions={0} | all-to-all | bytes 524288 | tf_op jit(solution)/shard_map/all_to_all | solution.py:455
  158.4 7.9 %all_to_all.55.r_ref = bf16[4,128,256]{2,1,0:T(8,128)(2,1)S(1)} all-to-all(bf16[4,128,256]{2,1,0:T(8,128)(2,1)S(1)} %broadcast_in_dim.43), channel_id=1, replica_groups={{0,1,2,3},{4,5,6,7},{8,9,10,11},{12,13,14,15},{16,17,18,19},{20,21,22,2..., dimensions={0} | all-to-all | bytes 524288 | tf_op jit(solution)/shard_map/all_to_all | solution.py:455
  166.3 2.7 %cond_end.1 = bf16[8,128,256]{2,1,0:T(8,128)(2,1)} custom-call(s32[6]{0:T(128)S(1)} %copy-done.9, bf16[4,128,256]{2,1,0:T(8,128)(2,1)S(1)} %all_to_all.55.r_ref, f32[192,256]{1,0:T(8,128)S(1)} %get-tuple-element.64.h_ref, bf16[4,1024,128]{2,1,0:T(8,128)(2,1)} %mix_hbm.9, bf16[2,512,512]{2,1,0:T(8,128)(2,1)S(1)} %collective-permute-done.5.got1_hbm.got_hbm, ...), custom_call_target="tpu_custom_call" | custom-call | flops 1000000000 | bytes 4194304 | tf_op jit(solution)/shard_map/cond_end/pallas_call | solution.py:559
  169.0 5.7 %all-to-all-start.9 = ((bf16[8,128,256]{2,1,0:T(8,128)(2,1)}), bf16[8,128,256]{2,1,0:T(8,128)(2,1)S(1)}, u32[]{:S(2)}, u32[]{:S(2)}) async-start(bf16[8,128,256]{2,1,0:T(8,128)(2,1)} %cond_end.1), calls=%async_computation.9 | async-start | bytes 1048576 | tf_op jit(solution)/shard_map/all_to_all | solution.py:455
  177.5 5.9 %all-to-all-done.9.hf_ref = bf16[8,128,256]{2,1,0:T(8,128)(2,1)S(1)} async-done(((bf16[8,128,256]{2,1,0:T(8,128)(2,1)}), bf16[8,128,256]{2,1,0:T(8,128)(2,1)S(1)}, u32[]{:S(2)}, u32[]{:S(2)}) %all-to-all-start.9) | async-done | bytes 524320 | tf_op jit(solution)/shard_map/all_to_all | solution.py:455
  183.4 12.6 %frames.2 = (bf16[512,256]{1,0:T(8,128)(2,1)S(1)}, bf16[512,512]{1,0:T(8,128)(2,1)}) custom-call(s32[6]{0:T(128)S(1)} %copy-done.9, s32[1024]{0:T(1024)S(1)} %fusion.9.codes_ref, bf16[8,128,256]{2,1,0:T(8,128)(2,1)S(1)} %all-to-all-done.9.hf_ref, f32[1,1920]{1,0:T(1,128)S(1)} %broadcast_in_dim.44.gain_ref, bf16[1920,768]{1,0:T(8,128)(2,1)S(1)} %bitcast.24, ...), custom_call_target="tpu_custom_call" | custom-call | flops 4000000000 | bytes 20971520 | tf_op jit(solution)/shard_map/frames/pallas_call | solution.py:317
  196.7 3.9 %collective-permute-start.8 = (bf16[512,512]{1,0:T(8,128)(2,1)}, bf16[512,512]{1,0:T(8,128)(2,1)}, u32[]{:S(2)}, u32[]{:S(2)}) collective-permute-start(bf16[512,512]{1,0:T(8,128)(2,1)} %get-tuple-element.67.kv0_ref), channel_id=1, source_target_pairs={{0,16},{8,24},{16,32},{24,40},{32,48},{40,56},{48,64},{56,72},{64,... | collective-permute-start | bytes 1572872 | tf_op jit(solution)/shard_map/ppermute | solution.py:572
  200.6 11.8 %frames.3 = (bf16[512,256]{1,0:T(8,128)(2,1)S(1)}, bf16[512,512]{1,0:T(8,128)(2,1)S(1)}) custom-call(s32[6]{0:T(128)S(1)} %copy-done.9, s32[1024]{0:T(1024)S(1)} %fusion.9.codes_ref, bf16[8,128,256]{2,1,0:T(8,128)(2,1)S(1)} %all-to-all-done.9.hf_ref, f32[1,1920]{1,0:T(1,128)S(1)} %broadcast_in_dim.44.gain_ref, bf16[1920,768]{1,0:T(8,128)(2,1)S(1)} %bitcast.25, ...), custom_call_target="tpu_custom_call" | custom-call | flops 4000000000 | bytes 20971520 | tf_op jit(solution)/shard_map/frames/pallas_call | solution.py:317
  213.6 6.5 %collective-permute-start.10 = (bf16[512,512]{1,0:T(8,128)(2,1)S(1)}, bf16[512,512]{1,0:T(8,128)(2,1)S(1)}, u32[]{:S(2)}, u32[]{:S(2)}) collective-permute-start(bf16[512,512]{1,0:T(8,128)(2,1)S(1)} %broadcast_select_fusion.1), channel_id=1, source_target_pairs={{0,8},{8,0},{16,24},{24,16},{32,40},{40,32},{48,56},{56,48},{64,72... | collective-permute-start | bytes 1572872 | tf_op jit(solution)/shard_map/ppermute | solution.py:451
  220.1 3.7 %collective-permute-start.9 = (bf16[512,512]{1,0:T(8,128)(2,1)S(1)}, bf16[512,512]{1,0:T(8,128)(2,1)S(1)}, u32[]{:S(2)}, u32[]{:S(2)}) collective-permute-start(bf16[512,512]{1,0:T(8,128)(2,1)S(1)} %get-tuple-element.70.kv1_ref), channel_id=1, source_target_pairs={{0,16},{8,24},{16,32},{24,40},{32,48},{40,56},{48,64},{56,72},{64,... | collective-permute-start | bytes 1572872 | tf_op jit(solution)/shard_map/ppermute | solution.py:572
  223.8 4.0 %own.1 = (f32[2,4,256,256]{3,2,1,0:T(8,128)S(1)}, f32[2,4,256,1]{3,2,1,0:T(8,128)S(1)}) custom-call(bf16[512,256]{1,0:T(8,128)(2,1)S(1)} %copy-done.6, bf16[512,256]{1,0:T(8,128)(2,1)S(1)} %get-tuple-element.69.q1_ref, bf16[512,512]{1,0:T(8,128)(2,1)} %get-tuple-element.67.kv0_ref, bf16[512,512]{1,0:T(8,128)(2,1)S(1)} %get-tuple-element.70.kv1_ref), custom_call_target="tpu_custom_call" | custom-call | flops 1000000000 | bytes 4194304 | tf_op jit(solution)/shard_map/own/pallas_call | solution.py:581
  227.8 4.7 %past.1 = (f32[2,4,256,256]{3,2,1,0:T(8,128)S(1)}, f32[2,4,256,1]{3,2,1,0:T(8,128)S(1)}) custom-call(s32[6]{0:T(128)S(1)} %copy-done.9, bf16[512,256]{1,0:T(8,128)(2,1)S(1)} %copy-done.6, bf16[512,256]{1,0:T(8,128)(2,1)S(1)} %get-tuple-element.69.q1_ref, bf16[512,512]{1,0:T(8,128)(2,1)} %collective-permute-done.8.far_ref, ...), custom_call_target="tpu_custom_call" | custom-call | flops 1000000000 | bytes 4194304 | tf_op jit(solution)/shard_map/past/pallas_call | solution.py:583
  232.4 5.2 %collective-permute-done.9.far_ref = bf16[512,512]{1,0:T(8,128)(2,1)S(1)} collective-permute-done((bf16[512,512]{1,0:T(8,128)(2,1)S(1)}, bf16[512,512]{1,0:T(8,128)(2,1)S(1)}, u32[]{:S(2)}, u32[]{:S(2)}) %collective-permute-start.9) | collective-permute-done | bytes 524320 | tf_op jit(solution)/shard_map/ppermute | solution.py:572
  240.1 5.0 %past_end.1 = bf16[1024,256]{1,0:T(8,128)(2,1)} custom-call(s32[6]{0:T(128)S(1)} %copy-done.9, bf16[512,256]{1,0:T(8,128)(2,1)S(1)} %copy-done.6, bf16[512,256]{1,0:T(8,128)(2,1)S(1)} %get-tuple-element.69.q1_ref, bf16[512,512]{1,0:T(8,128)(2,1)S(1)} %collective-permute-done.9.far_ref, bf16[512,512]{1,0:T(8,128)(2,1)S(1)} %collective-permute-done.11.near_ref, ...), custom_call_target="tpu_custom_call" | custom-call | flops 2000000000 | bytes 4194304 | tf_op jit(solution)/shard_map/past_end/pallas_call | solution.py:588
  (73 shorter events, 30.9 us)
Async XLA Ops:
  6.5 7.5 %copy-start.10 = (s32[256]{0:T(256)S(1)}, s32[256]{0:T(256)}, u32[]{:S(2)}) copy-start(s32[256]{0:T(256)} %param.9) | copy-start | bytes 3076
  9.8 15.3 %all-to-all-start = ((bf16[4,46,16,128]{3,2,1,0:T(8,128)(2,1)}), bf16[4,46,16,128]{3,2,1,0:T(8,128)(2,1)}, u32[]{:S(2)}, u32[]{:S(2)}) async-start(bf16[4,46,16,128]{3,2,1,0:T(8,128)(2,1)} %share.1), calls=%async_computation | async-start | bytes 1507328 | tf_op jit(solution)/shard_map/all_to_all | solution.py:455
  14.0 169.4 %all-gather.5.cloned.1.call-start = ((), (), s32[]{:S(2)}) async-start(), calls=%async_computation.10 | async-start | bytes 12812288 | tf_op jit(solution)/shard_map/all_gather | solution.py:459
  14.1 33.2 %copy-start.2 = (bf16[2048,128]{1,0:T(8,128)(2,1)S(1)}, bf16[2048,128]{1,0:T(8,128)(2,1)}, u32[]{:S(2)}) copy-start(bf16[2048,128]{1,0:T(8,128)(2,1)} %table_ref.1) | copy-start | bytes 1572868
  14.1 33.2 %copy-start.9 = (s32[6]{0:T(128)S(1)}, s32[6]{0:T(128)}, u32[]{:S(2)}) copy-start(s32[6]{0:T(128)} %stack.27.info) | copy-start | bytes 76
  14.1 8.5 %collective-permute-start = (s32[40]{0:T(128)S(1)}, s32[40]{0:T(128)S(1)}, u32[]{:S(2)}, u32[]{:S(2)}) collective-permute-start(s32[40]{0:T(128)S(1)} %broadcast_select_fusion.3), channel_id=1, source_target_pairs={{0,8},{1,9},{2,10},{3,11},{8,16},{9,17},{10,18},{11,19},{16,24},{1... | collective-permute-start | bytes 488 | tf_op jit(solution)/shard_map/ppermute | solution.py:509
  25.1 17.6 %collective-permute-start.1 = (bf16[768,512]{1,0:T(8,128)(2,1)}, bf16[768,512]{1,0:T(8,128)(2,1)S(1)}, u32[]{:S(2)}, u32[]{:S(2)}) collective-permute-start(bf16[768,512]{1,0:T(8,128)(2,1)} %get-tuple-element.44), channel_id=1, source_target_pairs={{0,68},{1,69},{2,70},{3,71},{4,64},{5,65},{6,66},{7,67},{8,76},{9,... | collective-permute-start | bytes 2359304 | tf_op jit(solution)/shard_map/ppermute | solution.py:506
  42.7 4.6 %collective-permute-start.3 = (bf16[768,512]{1,0:T(8,128)(2,1)S(1)}, bf16[768,512]{1,0:T(8,128)(2,1)S(1)}, u32[]{:S(2)}, u32[]{:S(2)}) collective-permute-start(bf16[768,512]{1,0:T(8,128)(2,1)S(1)} %collective-permute-done.1.got_ref.got_hbm), channel_id=1, source_target_pairs={{0,8},{8,0},{16,24},{24,16},{32,40},{40,32},{48,56},{56,48},{64,72... | collective-permute-start | bytes 2359304 | tf_op jit(solution)/shard_map/ppermute | solution.py:451
  50.2 39.0 %copy-start.7 = (f32[208,256]{1,0:T(8,128)}, f32[208,256]{1,0:T(8,128)S(1)}, u32[]{:S(2)}) copy-start(f32[208,256]{1,0:T(8,128)S(1)} %get-tuple-element.55.h_ref) | copy-start | bytes 638980
  60.6 28.5 %collective-permute-start.4 = (bf16[4,46,16,128]{3,2,1,0:T(8,128)(2,1)}, bf16[4,46,16,128]{3,2,1,0:T(8,128)(2,1)}, u32[]{:S(2)}, u32[]{:S(2)}) collective-permute-start(bf16[4,46,16,128]{3,2,1,0:T(8,128)(2,1)} %all-to-all-done), channel_id=1, source_target_pairs={{0,68},{1,69},{2,70},{3,71},{4,64},{5,65},{6,66},{7,67},{8,76},{9,... | collective-permute-start | bytes 2261000 | tf_op jit(solution)/shard_map/ppermute | solution.py:534
  61.8 27.3 %collective-permute-start.2 = (bf16[512,512]{1,0:T(8,128)(2,1)}, bf16[512,512]{1,0:T(8,128)(2,1)S(1)}, u32[]{:S(2)}, u32[]{:S(2)}) collective-permute-start(bf16[512,512]{1,0:T(8,128)(2,1)} %get-tuple-element.45), channel_id=1, source_target_pairs={{0,68},{1,69},{2,70},{3,71},{4,64},{5,65},{6,66},{7,67},{8,76},{9,... | collective-permute-start | bytes 1572872 | tf_op jit(solution)/shard_map/ppermute | solution.py:514
  63.0 26.2 %all-to-all-start.2 = ((bf16[4,208,256]{2,1,0:T(8,128)(2,1)}), bf16[4,208,256]{2,1,0:T(8,128)(2,1)S(1)}, u32[]{:S(2)}, u32[]{:S(2)}) async-start(bf16[4,208,256]{2,1,0:T(8,128)(2,1)} %broadcast_in_dim.37), calls=%async_computation.2 | async-start | bytes 851968 | tf_op jit(solution)/shard_map/all_to_all | solution.py:455
  66.4 116.9 %all-gather.7.cloned.1.call-start = ((), (), s32[]{:S(2)}) async-start(), calls=%async_computation.11 | async-start | bytes 12812288 | tf_op jit(solution)/shard_map/all_gather | solution.py:459
  89.2 0.8 copy-start.3
  89.9 3.7 %collective-permute-start.6 = (bf16[512,512]{1,0:T(8,128)(2,1)S(1)}, bf16[512,512]{1,0:T(8,128)(2,1)S(1)}, u32[]{:S(2)}, u32[]{:S(2)}) collective-permute-start(bf16[512,512]{1,0:T(8,128)(2,1)S(1)} %collective-permute-done.2.got1_hbm.got_hbm), channel_id=1, source_target_pairs={{0,8},{8,0},{16,24},{24,16},{32,40},{40,32},{48,56},{56,48},{64,72... | collective-permute-start | bytes 1572872 | tf_op jit(solution)/shard_map/ppermute | solution.py:451
  92.1 25.1 %collective-permute-start.5 = (bf16[2,512,512]{2,1,0:T(8,128)(2,1)}, bf16[2,512,512]{2,1,0:T(8,128)(2,1)S(1)}, u32[]{:S(2)}, u32[]{:S(2)}) collective-permute-start(bf16[2,512,512]{2,1,0:T(8,128)(2,1)} %get-tuple-element.53), channel_id=1, source_target_pairs={{0,68},{1,69},{2,70},{3,71},{4,64},{5,65},{6,66},{7,67},{8,76},{9,... | collective-permute-start | bytes 3145736 | tf_op jit(solution)/shard_map/ppermute | solution.py:544
  93.7 5.0 %copy-start = (bf16[512,512]{1,0:T(8,128)(2,1)}, bf16[512,512]{1,0:T(8,128)(2,1)S(1)}, u32[]{:S(2)}) copy-start(bf16[512,512]{1,0:T(8,128)(2,1)S(1)} %collective-permute-done.6.sib1_hbm.sib_hbm) | copy-start | bytes 1572868
  93.7 1.2 copy-start.4
  94.9 1.0 copy-start.8
  98.7 26.5 %copy-start.1 = (bf16[512,512]{1,0:T(8,128)(2,1)S(1)}, bf16[512,512]{1,0:T(8,128)(2,1)}, u32[]{:S(2)}) copy-start(bf16[512,512]{1,0:T(8,128)(2,1)} %copy-done) | copy-start | bytes 1572868
  110.1 10.2 %all-to-all-start.4 = ((bf16[4,208,256]{2,1,0:T(8,128)(2,1)}), bf16[4,208,256]{2,1,0:T(8,128)(2,1)S(1)}, u32[]{:S(2)}, u32[]{:S(2)}) async-start(bf16[4,208,256]{2,1,0:T(8,128)(2,1)} %broadcast_in_dim.39), calls=%async_computation.4 | async-start | bytes 851968 | tf_op jit(solution)/shard_map/all_to_all | solution.py:455
  120.3 4.9 %collective-permute-start.7 = (bf16[2,512,512]{2,1,0:T(8,128)(2,1)S(1)}, bf16[2,512,512]{2,1,0:T(8,128)(2,1)S(1)}, u32[]{:S(2)}, u32[]{:S(2)}) collective-permute-start(bf16[2,512,512]{2,1,0:T(8,128)(2,1)S(1)} %collective-permute-done.5.got1_hbm.got_hbm), channel_id=1, source_target_pairs={{0,8},{8,0},{16,24},{24,16},{32,40},{40,32},{48,56},{56,48},{64,72... | collective-permute-start | bytes 3145736 | tf_op jit(solution)/shard_map/ppermute | solution.py:451
  158.4 16.4 %copy-start.11 = (f32[1920]{0:T(1024)S(1)}, f32[1920]{0:T(1024)}, u32[]{:S(2)}) copy-start(f32[1920]{0:T(1024)} %param.16) | copy-start | bytes 23044
  158.4 16.4 %copy-start.12 = (s32[1024]{0:T(1024)S(1)}, s32[1024]{0:T(1024)}, u32[]{:S(2)}) copy-start(s32[1024]{0:T(1024)} %param.10) | copy-start | bytes 12292
  169.0 14.4 %all-to-all-start.9 = ((bf16[8,128,256]{2,1,0:T(8,128)(2,1)}), bf16[8,128,256]{2,1,0:T(8,128)(2,1)S(1)}, u32[]{:S(2)}, u32[]{:S(2)}) async-start(bf16[8,128,256]{2,1,0:T(8,128)(2,1)} %cond_end.1), calls=%async_computation.9 | async-start | bytes 1048576 | tf_op jit(solution)/shard_map/all_to_all | solution.py:455
  196.0 0.7 copy-start.5
  196.7 15.8 %collective-permute-start.8 = (bf16[512,512]{1,0:T(8,128)(2,1)}, bf16[512,512]{1,0:T(8,128)(2,1)}, u32[]{:S(2)}, u32[]{:S(2)}) collective-permute-start(bf16[512,512]{1,0:T(8,128)(2,1)} %get-tuple-element.67.kv0_ref), channel_id=1, source_target_pairs={{0,16},{8,24},{16,32},{24,40},{32,48},{40,56},{48,64},{56,72},{64,... | collective-permute-start | bytes 1572872 | tf_op jit(solution)/shard_map/ppermute | solution.py:572
  200.6 23.2 %copy-start.6 = (bf16[512,256]{1,0:T(8,128)(2,1)S(1)}, bf16[512,256]{1,0:T(8,128)(2,1)}, u32[]{:S(2)}) copy-start(bf16[512,256]{1,0:T(8,128)(2,1)} %copy-done.5) | copy-start | bytes 786436
  213.6 14.2 %collective-permute-start.10 = (bf16[512,512]{1,0:T(8,128)(2,1)S(1)}, bf16[512,512]{1,0:T(8,128)(2,1)S(1)}, u32[]{:S(2)}, u32[]{:S(2)}) collective-permute-start(bf16[512,512]{1,0:T(8,128)(2,1)S(1)} %broadcast_select_fusion.1), channel_id=1, source_target_pairs={{0,8},{8,0},{16,24},{24,16},{32,40},{40,32},{48,56},{56,48},{64,72... | collective-permute-start | bytes 1572872 | tf_op jit(solution)/shard_map/ppermute | solution.py:451
  220.1 17.5 %collective-permute-start.9 = (bf16[512,512]{1,0:T(8,128)(2,1)S(1)}, bf16[512,512]{1,0:T(8,128)(2,1)S(1)}, u32[]{:S(2)}, u32[]{:S(2)}) collective-permute-start(bf16[512,512]{1,0:T(8,128)(2,1)S(1)} %get-tuple-element.70.kv1_ref), channel_id=1, source_target_pairs={{0,16},{8,24},{16,32},{24,40},{32,48},{40,56},{48,64},{56,72},{64,... | collective-permute-start | bytes 1572872 | tf_op jit(solution)/shard_map/ppermute | solution.py:572
  237.7 2.4 collective-permute-start.11
Sparse Core Ops, SparseCore 0:
  25.2 71.2 all-gather.4
  98.2 70.4 all-gather.6

commit v8 on v7

--- a/solution.py
+++ b/solution.py
@@ -530,17 +530,17 @@
     for level in range(4):
         terms = exchange(terms, groups=Y_GROUPS)
         if level == 0:
-            mine, terms = lax.optimization_barrier((mine, terms))
+            got1, mine, terms = lax.optimization_barrier((got1, mine, terms))
             others = lax.ppermute(mine, EVERY, other_half())
+            sib1 = to_sibling(got1)
         total = terms[0].astype(F32)
         for y in range(1, 4):
             total = total + terms[y].astype(F32)
         r = jnp.maximum(total, 0.0).astype(BF)
         r = exchange(jnp.broadcast_to(r[None], terms.shape), groups=Y_GROUPS)
         if level == 0:
-            got1, others, pack2, r = lax.optimization_barrier((got1, others, pack2, r))
+            others, pack2, r = lax.optimization_barrier((others, pack2, r))
             full_other = gathered(others)
-            sib1 = to_sibling(got1)
             got2 = lax.ppermute(pack2, EVERY, other_half())
             stacks = [(got0, sib0), (got1, sib1)]
         if level == 1:

time: 253 us -> 240 us (0.949)
  waiting for transfers between devices: 65 us -> 51.4 us
  blocking collectives: 56.3 us -> 64.4 us
  starting transfers between devices: 47.8 us -> 43.4 us
  local copies, waits for them, and re-layouts: 8.91 us -> 5.33 us
    ppermute x1, waiting for transfers between devices: 22.7 us -> 5.21 us  [on_device(): got1 = lax.ppermute(pack1, EVERY, other_half())]
    all_to_all x6 -> x7, blocking collectives: 56.3 us -> 64.4 us  [exchange(): lax.all_to_all(value, axis, 0, 0, axis_index_groups=groups, tiled=True)]
    ppermute x1, waiting for transfers between devices: 0.01 us -> 6.89 us  [on_device(): others = lax.ppermute(mine, EVERY, other_half())]
    ppermute x1, waiting for transfers between devices: 3.66 us -> 0.55 us  [on_device(): got2 = lax.ppermute(pack2, EVERY, other_half())]
    all_to_all x4 -> x3, starting transfers between devices: 16.9 us -> 14.1 us  [exchange(): lax.all_to_all(value, axis, 0, 0, axis_index_groups=groups, tiled=True)]
    unnamed x28 -> x18, local copies, waits for them, and re-layouts: 6.09 us -> 4.11 us
    all_to_all x4 -> x3, waiting for transfers between devices: 11.5 us -> 12.5 us  [exchange(): lax.all_to_all(value, axis, 0, 0, axis_index_groups=groups, tiled=True)]
  transfers between devices with their start and end apart: 18 -> 17, of which waited for: 11 -> 12; matrix products, arithmetic and copies ran while one was open for 2% -> 1% of each run, Pallas kernels for 15% -> 16%
where the time goes in v8:
time: 240 us; the launch traced here: 239 us
  blocking collectives  64.4 us (27%)
  Pallas kernels  59.3 us (25%)
  waiting for transfers between devices  51.4 us (21%)
  starting transfers between devices  43.4 us (18%)
  between operations  13.7 us (6%)
  local copies, waits for them, and re-layouts  5.33 us (2%)
    all_to_all x7, blocking collectives, exchange(): lax.all_to_all(value, axis, 0, 0, axis_index_groups=groups, tiled=True)  64.4 us
    pallas_call x2, Pallas kernels, frames(): pl.pallas_call(functools.partial(frames_kernel, pair), out_shape=(shape(5...  24.5 us
    ppermute x1, waiting for transfers between devices, on_device(): got0 = lax.ppermute(pack0, EVERY, other_half())  16.3 us
    all_to_all x3, starting transfers between devices, exchange(): lax.all_to_all(value, axis, 0, 0, axis_index_groups=groups, tiled=True)  14.1 us
    ppermute x5, starting transfers between devices, to_sibling(): return lax.ppermute(value, 'song', [(i, i ^ 1) for i in range(16)])  13.6 us
    all_to_all x3, waiting for transfers between devices, exchange(): lax.all_to_all(value, axis, 0, 0, axis_index_groups=groups, tiled=True)  12.5 us
    pallas_call x3, Pallas kernels, on_device(): call(functools.partial(middle_kernel, level), (shape(ROWS[level + 1], 256...  8.44 us
    ppermute x1, waiting for transfers between devices, on_device(): others = lax.ppermute(mine, EVERY, other_half())  6.89 us
  transfers between devices with their start and end apart: 17, of which 12 were waited for; matrix products, arithmetic and copies ran while one was open for 1% of the time, Pallas kernels for 16%

profile of v8, /device:TPU:3, one launch (start us, length us, event | category | flops | bytes accessed | tf_op | source)
XLA Modules:
  0.0 239.2 jit_solution(6474279949887045843)
XLA Ops:
  7.1 2.6 %share.1 = bf16[4,46,16,128]{3,2,1,0:T(8,128)(2,1)} custom-call(s32[6]{0:T(128)} %stack.27.info, bf16[128,7680]{1,0:T(8,128)(2,1)} %up_hbm.1, bf16[256,1920]{1,0:T(8,128)(2,1)} %mid_hbm.1), custom_call_target="tpu_custom_call" | custom-call | flops 1000000000 | bytes 4194304 | tf_op jit(solution)/shard_map/share/pallas_call | solution.py:483
  9.8 4.2 %all-to-all-start = ((bf16[4,46,16,128]{3,2,1,0:T(8,128)(2,1)}), bf16[4,46,16,128]{3,2,1,0:T(8,128)(2,1)S(1)}, u32[]{:S(2)}, u32[]{:S(2)}) async-start(bf16[4,46,16,128]{3,2,1,0:T(8,128)(2,1)} %share.1), calls=%async_computation | async-start | bytes 1507328 | tf_op jit(solution)/shard_map/all_to_all | solution.py:455
  14.0 4.5 %collective-permute-start = (s32[40]{0:T(128)S(1)}, s32[40]{0:T(128)S(1)}, u32[]{:S(2)}, u32[]{:S(2)}) collective-permute-start(s32[40]{0:T(128)S(1)} %broadcast_select_fusion.3), channel_id=1, source_target_pairs={{0,8},{1,9},{2,10},{3,11},{8,16},{9,17},{10,18},{11,19},{16,24},{1... | collective-permute-start | bytes 488 | tf_op jit(solution)/shard_map/ppermute | solution.py:509
  18.5 4.1 %pack.1 = (bf16[768,512]{1,0:T(8,128)(2,1)}, bf16[512,512]{1,0:T(8,128)(2,1)}, bf16[2,512,512]{2,1,0:T(8,128)(2,1)}) custom-call(s32[6]{0:T(128)} %stack.27.info, bf16[4,3,128,1024]{3,2,1,0:T(8,128)(2,1)} %dil_hbm.9, bf16[4,1024,128]{2,1,0:T(8,128)(2,1)} %mix_hbm.9, bf16[2048,128]{1,0:T(8,128)(2,1)} %table_ref.1), custom_call_target="tpu_custom_call" | custom-call | flops 1000000000 | bytes 4194304 | tf_op jit(solution)/shard_map/pack/pallas_call | solution.py:498
  27.2 16.3 %collective-permute-done.1.got_ref.got_hbm = bf16[768,512]{1,0:T(8,128)(2,1)S(1)} collective-permute-done((bf16[768,512]{1,0:T(8,128)(2,1)}, bf16[768,512]{1,0:T(8,128)(2,1)S(1)}, u32[]{:S(2)}, u32[]{:S(2)}) %collective-permute-start.1) | collective-permute-done | bytes 786464 | tf_op jit(solution)/shard_map/ppermute | solution.py:506
  43.5 2.7 %collective-permute-start.3 = (bf16[768,512]{1,0:T(8,128)(2,1)S(1)}, bf16[768,512]{1,0:T(8,128)(2,1)S(1)}, u32[]{:S(2)}, u32[]{:S(2)}) collective-permute-start(bf16[768,512]{1,0:T(8,128)(2,1)S(1)} %collective-permute-done.1.got_ref.got_hbm), channel_id=1, source_target_pairs={{0,8},{8,0},{16,24},{24,16},{32,40},{40,32},{48,56},{56,48},{64,72... | collective-permute-start | bytes 2359304 | tf_op jit(solution)/shard_map/ppermute | solution.py:451
  48.1 3.7 %cond0.1 = (f32[208,256]{1,0:T(8,128)S(1)}, bf16[4,208,256]{2,1,0:T(8,128)(2,1)}) custom-call(s32[6]{0:T(128)S(1)} %copy-done.3, s32[208,1]{1,0:T(8,128)S(1)} %broadcast_select_fusion.2.codes_ref, bf16[2048,128]{1,0:T(8,128)(2,1)S(1)} %copy-done, bf16[4,3,128,1024]{3,2,1,0:T(8,128)(2,1)} %dil_hbm.9, ...), custom_call_target="tpu_custom_call" | custom-call | flops 1000000000 | bytes 4194304 | tf_op jit(solution)/shard_map/cond0/pallas_call | solution.py:521
  51.8 3.5 %all-to-all-start.1 = ((bf16[4,208,256]{2,1,0:T(8,128)(2,1)}), bf16[4,208,256]{2,1,0:T(8,128)(2,1)S(1)}, u32[]{:S(2)}, u32[]{:S(2)}) async-start(bf16[4,208,256]{2,1,0:T(8,128)(2,1)} %get-tuple-element.49), calls=%async_computation.1 | async-start | bytes 851968 | tf_op jit(solution)/shard_map/all_to_all | solution.py:455
  55.3 5.2 %collective-permute-done.2.got1_hbm.got_hbm = bf16[512,512]{1,0:T(8,128)(2,1)S(1)} collective-permute-done((bf16[512,512]{1,0:T(8,128)(2,1)}, bf16[512,512]{1,0:T(8,128)(2,1)S(1)}, u32[]{:S(2)}, u32[]{:S(2)}) %collective-permute-start.2) | collective-permute-done | bytes 524320 | tf_op jit(solution)/shard_map/ppermute | solution.py:514
  60.5 2.9 %all-to-all-done.1 = bf16[4,208,256]{2,1,0:T(8,128)(2,1)S(1)} async-done(((bf16[4,208,256]{2,1,0:T(8,128)(2,1)}), bf16[4,208,256]{2,1,0:T(8,128)(2,1)S(1)}, u32[]{:S(2)}, u32[]{:S(2)}) %all-to-all-start.1) | async-done | bytes 426016 | tf_op jit(solution)/shard_map/all_to_all | solution.py:455
  64.8 9.1 %all_to_all.50.r_ref = bf16[4,208,256]{2,1,0:T(8,128)(2,1)S(1)} all-to-all(bf16[4,208,256]{2,1,0:T(8,128)(2,1)S(1)} %broadcast_in_dim.37), channel_id=1, replica_groups={{0,1,2,3},{4,5,6,7},{8,9,10,11},{12,13,14,15},{16,17,18,19},{20,21,22,2..., dimensions={0} | all-to-all | bytes 851968 | tf_op jit(solution)/shard_map/all_to_all | solution.py:455
  73.9 6.9 %collective-permute-done.4 = bf16[4,46,16,128]{3,2,1,0:T(8,128)(2,1)} collective-permute-done((bf16[4,46,16,128]{3,2,1,0:T(8,128)(2,1)}, bf16[4,46,16,128]{3,2,1,0:T(8,128)(2,1)}, u32[]{:S(2)}, u32[]{:S(2)}) %collective-permute-start.4) | collective-permute-done | bytes 753696 | tf_op jit(solution)/shard_map/ppermute | solution.py:534
  84.6 2.9 %cond.3 = (f32[208,256]{1,0:T(8,128)S(1)}, bf16[4,208,256]{2,1,0:T(8,128)(2,1)S(1)}) custom-call(s32[6]{0:T(128)S(1)} %copy-done.3, bf16[4,208,256]{2,1,0:T(8,128)(2,1)S(1)} %all_to_all.50.r_ref, f32[208,256]{1,0:T(8,128)S(1)} %get-tuple-element.55.h_ref, bf16[4,1024,128]{2,1,0:T(8,128)(2,1)} %mix_hbm.9, ...), custom_call_target="tpu_custom_call" | custom-call | flops 1000000000 | bytes 4194304 | tf_op jit(solution)/shard_map/cond/pallas_call | solution.py:550
  87.5 10.4 %all_to_all.51 = bf16[4,208,256]{2,1,0:T(8,128)(2,1)S(1)} all-to-all(bf16[4,208,256]{2,1,0:T(8,128)(2,1)S(1)} %get-tuple-element.57), channel_id=1, replica_groups={{0,1,2,3},{4,5,6,7},{8,9,10,11},{12,13,14,15},{16,17,18,19},{20,21,22,2..., dimensions={0} | all-to-all | bytes 851968 | tf_op jit(solution)/shard_map/all_to_all | solution.py:455
  98.0 9.5 %all_to_all.52.r_ref = bf16[4,208,256]{2,1,0:T(8,128)(2,1)S(1)} all-to-all(bf16[4,208,256]{2,1,0:T(8,128)(2,1)S(1)} %broadcast_in_dim.39), channel_id=1, replica_groups={{0,1,2,3},{4,5,6,7},{8,9,10,11},{12,13,14,15},{16,17,18,19},{20,21,22,2..., dimensions={0} | all-to-all | bytes 851968 | tf_op jit(solution)/shard_map/all_to_all | solution.py:455
  112.2 2.9 %cond.4 = (f32[208,256]{1,0:T(8,128)S(1)}, bf16[4,192,256]{2,1,0:T(8,128)(2,1)S(1)}) custom-call(s32[6]{0:T(128)S(1)} %copy-done.3, bf16[4,208,256]{2,1,0:T(8,128)(2,1)S(1)} %all_to_all.52.r_ref, f32[208,256]{1,0:T(8,128)S(1)} %get-tuple-element.59.h_ref, bf16[4,1024,128]{2,1,0:T(8,128)(2,1)} %mix_hbm.9, ...), custom_call_target="tpu_custom_call" | custom-call | flops 1000000000 | bytes 4194304 | tf_op jit(solution)/shard_map/cond/pallas_call | solution.py:550
  115.0 10.3 %all_to_all.53 = bf16[4,192,256]{2,1,0:T(8,128)(2,1)S(1)} all-to-all(bf16[4,192,256]{2,1,0:T(8,128)(2,1)S(1)} %get-tuple-element.61), channel_id=1, replica_groups={{0,1,2,3},{4,5,6,7},{8,9,10,11},{12,13,14,15},{16,17,18,19},{20,21,22,2..., dimensions={0} | all-to-all | bytes 786432 | tf_op jit(solution)/shard_map/all_to_all | solution.py:455
  125.4 9.3 %all_to_all.54.r_ref = bf16[4,192,256]{2,1,0:T(8,128)(2,1)S(1)} all-to-all(bf16[4,192,256]{2,1,0:T(8,128)(2,1)S(1)} %broadcast_in_dim.41), channel_id=1, replica_groups={{0,1,2,3},{4,5,6,7},{8,9,10,11},{12,13,14,15},{16,17,18,19},{20,21,22,2..., dimensions={0} | all-to-all | bytes 786432 | tf_op jit(solution)/shard_map/all_to_all | solution.py:455
  134.7 2.7 %cond.5 = (f32[192,256]{1,0:T(8,128)S(1)}, bf16[4,128,256]{2,1,0:T(8,128)(2,1)S(1)}) custom-call(s32[6]{0:T(128)S(1)} %copy-done.3, bf16[4,192,256]{2,1,0:T(8,128)(2,1)S(1)} %all_to_all.54.r_ref, f32[208,256]{1,0:T(8,128)S(1)} %get-tuple-element.62.h_ref, bf16[4,1024,128]{2,1,0:T(8,128)(2,1)} %mix_hbm.9, ...), custom_call_target="tpu_custom_call" | custom-call | flops 1000000000 | bytes 4194304 | tf_op jit(solution)/shard_map/cond/pallas_call | solution.py:550
  137.5 7.9 %all_to_all.55 = bf16[4,128,256]{2,1,0:T(8,128)(2,1)S(1)} all-to-all(bf16[4,128,256]{2,1,0:T(8,128)(2,1)S(1)} %get-tuple-element.63), channel_id=1, replica_groups={{0,1,2,3},{4,5,6,7},{8,9,10,11},{12,13,14,15},{16,17,18,19},{20,21,22,2..., dimensions={0} | all-to-all | bytes 524288 | tf_op jit(solution)/shard_map/all_to_all | solution.py:455
  145.5 7.9 %all_to_all.56.r_ref = bf16[4,128,256]{2,1,0:T(8,128)(2,1)S(1)} all-to-all(bf16[4,128,256]{2,1,0:T(8,128)(2,1)S(1)} %broadcast_in_dim.43), channel_id=1, replica_groups={{0,1,2,3},{4,5,6,7},{8,9,10,11},{12,13,14,15},{16,17,18,19},{20,21,22,2..., dimensions={0} | all-to-all | bytes 524288 | tf_op jit(solution)/shard_map/all_to_all | solution.py:455
  153.4 2.7 %cond_end.1 = bf16[8,128,256]{2,1,0:T(8,128)(2,1)} custom-call(s32[6]{0:T(128)S(1)} %copy-done.3, bf16[4,128,256]{2,1,0:T(8,128)(2,1)S(1)} %all_to_all.56.r_ref, f32[192,256]{1,0:T(8,128)S(1)} %get-tuple-element.64.h_ref, bf16[4,1024,128]{2,1,0:T(8,128)(2,1)} %mix_hbm.9, bf16[2,512,512]{2,1,0:T(8,128)(2,1)S(1)} %collective-permute-done.5.got1_hbm.got_hbm, ...), custom_call_target="tpu_custom_call" | custom-call | flops 1000000000 | bytes 4194304 | tf_op jit(solution)/shard_map/cond_end/pallas_call | solution.py:559
  156.1 6.5 %all-to-all-start.9 = ((bf16[8,128,256]{2,1,0:T(8,128)(2,1)}), bf16[8,128,256]{2,1,0:T(8,128)(2,1)S(1)}, u32[]{:S(2)}, u32[]{:S(2)}) async-start(bf16[8,128,256]{2,1,0:T(8,128)(2,1)} %cond_end.1), calls=%async_computation.9 | async-start | bytes 1048576 | tf_op jit(solution)/shard_map/all_to_all | solution.py:455
  165.2 7.3 %all-to-all-done.9.hf_ref = bf16[8,128,256]{2,1,0:T(8,128)(2,1)S(1)} async-done(((bf16[8,128,256]{2,1,0:T(8,128)(2,1)}), bf16[8,128,256]{2,1,0:T(8,128)(2,1)S(1)}, u32[]{:S(2)}, u32[]{:S(2)}) %all-to-all-start.9) | async-done | bytes 524320 | tf_op jit(solution)/shard_map/all_to_all | solution.py:455
  172.6 12.6 %frames.2 = (bf16[512,256]{1,0:T(8,128)(2,1)S(1)}, bf16[512,512]{1,0:T(8,128)(2,1)}) custom-call(s32[6]{0:T(128)S(1)} %copy-done.3, s32[1024]{0:T(1024)S(1)} %fusion.9.codes_ref, bf16[8,128,256]{2,1,0:T(8,128)(2,1)S(1)} %all-to-all-done.9.hf_ref, f32[1,1920]{1,0:T(1,128)S(1)} %broadcast_in_dim.44.gain_ref, bf16[1920,768]{1,0:T(8,128)(2,1)S(1)} %bitcast.24, ...), custom_call_target="tpu_custom_call" | custom-call | flops 4000000000 | bytes 20971520 | tf_op jit(solution)/shard_map/frames/pallas_call | solution.py:317
  188.4 11.9 %frames.3 = (bf16[512,256]{1,0:T(8,128)(2,1)S(1)}, bf16[512,512]{1,0:T(8,128)(2,1)S(1)}) custom-call(s32[6]{0:T(128)S(1)} %copy-done.3, s32[1024]{0:T(1024)S(1)} %fusion.9.codes_ref, bf16[8,128,256]{2,1,0:T(8,128)(2,1)S(1)} %all-to-all-done.9.hf_ref, f32[1,1920]{1,0:T(1,128)S(1)} %broadcast_in_dim.44.gain_ref, bf16[1920,768]{1,0:T(8,128)(2,1)S(1)} %bitcast.25, ...), custom_call_target="tpu_custom_call" | custom-call | flops 4000000000 | bytes 20971520 | tf_op jit(solution)/shard_map/frames/pallas_call | solution.py:317
  201.4 6.1 %collective-permute-start.10 = (bf16[512,512]{1,0:T(8,128)(2,1)S(1)}, bf16[512,512]{1,0:T(8,128)(2,1)S(1)}, u32[]{:S(2)}, u32[]{:S(2)}) collective-permute-start(bf16[512,512]{1,0:T(8,128)(2,1)S(1)} %broadcast_select_fusion.1), channel_id=1, source_target_pairs={{0,8},{8,0},{16,24},{24,16},{32,40},{40,32},{48,56},{56,48},{64,72... | collective-permute-start | bytes 1572872 | tf_op jit(solution)/shard_map/ppermute | solution.py:451
  207.5 3.4 %collective-permute-start.9 = (bf16[512,512]{1,0:T(8,128)(2,1)S(1)}, bf16[512,512]{1,0:T(8,128)(2,1)S(1)}, u32[]{:S(2)}, u32[]{:S(2)}) collective-permute-start(bf16[512,512]{1,0:T(8,128)(2,1)S(1)} %get-tuple-element.70.kv1_ref), channel_id=1, source_target_pairs={{0,16},{8,24},{16,32},{24,40},{32,48},{40,56},{48,64},{56,72},{64,... | collective-permute-start | bytes 1572872 | tf_op jit(solution)/shard_map/ppermute | solution.py:572
  210.9 3.9 %own.1 = (f32[2,4,256,256]{3,2,1,0:T(8,128)S(1)}, f32[2,4,256,1]{3,2,1,0:T(8,128)S(1)}) custom-call(bf16[512,256]{1,0:T(8,128)(2,1)S(1)} %copy-done.2, bf16[512,256]{1,0:T(8,128)(2,1)S(1)} %get-tuple-element.69.q1_ref, bf16[512,512]{1,0:T(8,128)(2,1)} %get-tuple-element.67.kv0_ref, bf16[512,512]{1,0:T(8,128)(2,1)S(1)} %get-tuple-element.70.kv1_ref), custom_call_target="tpu_custom_call" | custom-call | flops 1000000000 | bytes 4194304 | tf_op jit(solution)/shard_map/own/pallas_call | solution.py:581
  214.9 4.6 %past.1 = (f32[2,4,256,256]{3,2,1,0:T(8,128)S(1)}, f32[2,4,256,1]{3,2,1,0:T(8,128)S(1)}) custom-call(s32[6]{0:T(128)S(1)} %copy-done.3, bf16[512,256]{1,0:T(8,128)(2,1)S(1)} %copy-done.2, bf16[512,256]{1,0:T(8,128)(2,1)S(1)} %get-tuple-element.69.q1_ref, bf16[512,512]{1,0:T(8,128)(2,1)} %collective-permute-done.8.far_ref, ...), custom_call_target="tpu_custom_call" | custom-call | flops 1000000000 | bytes 4194304 | tf_op jit(solution)/shard_map/past/pallas_call | solution.py:583
  219.5 5.6 %collective-permute-done.9.far_ref = bf16[512,512]{1,0:T(8,128)(2,1)S(1)} collective-permute-done((bf16[512,512]{1,0:T(8,128)(2,1)S(1)}, bf16[512,512]{1,0:T(8,128)(2,1)S(1)}, u32[]{:S(2)}, u32[]{:S(2)}) %collective-permute-start.9) | collective-permute-done | bytes 524320 | tf_op jit(solution)/shard_map/ppermute | solution.py:572
  227.5 4.8 %past_end.1 = bf16[1024,256]{1,0:T(8,128)(2,1)} custom-call(s32[6]{0:T(128)S(1)} %copy-done.3, bf16[512,256]{1,0:T(8,128)(2,1)S(1)} %copy-done.2, bf16[512,256]{1,0:T(8,128)(2,1)S(1)} %get-tuple-element.69.q1_ref, bf16[512,512]{1,0:T(8,128)(2,1)S(1)} %collective-permute-done.9.far_ref, bf16[512,512]{1,0:T(8,128)(2,1)S(1)} %collective-permute-done.11.near_ref, ...), custom_call_target="tpu_custom_call" | custom-call | flops 2000000000 | bytes 4194304 | tf_op jit(solution)/shard_map/past_end/pallas_call | solution.py:588
  (62 shorter events, 26.8 us)
Async XLA Ops:
  6.5 7.4 %copy-start.5 = (s32[256]{0:T(256)S(1)}, s32[256]{0:T(256)}, u32[]{:S(2)}) copy-start(s32[256]{0:T(256)} %param.9) | copy-start | bytes 3076
  9.8 15.2 %all-to-all-start = ((bf16[4,46,16,128]{3,2,1,0:T(8,128)(2,1)}), bf16[4,46,16,128]{3,2,1,0:T(8,128)(2,1)S(1)}, u32[]{:S(2)}, u32[]{:S(2)}) async-start(bf16[4,46,16,128]{3,2,1,0:T(8,128)(2,1)} %share.1), calls=%async_computation | async-start | bytes 1507328 | tf_op jit(solution)/shard_map/all_to_all | solution.py:455
  13.9 158.6 %all-gather.5.cloned.1.call-start = ((), (), s32[]{:S(2)}) async-start(), calls=%async_computation.10 | async-start | bytes 12812288 | tf_op jit(solution)/shard_map/all_gather | solution.py:459
  14.0 34.0 %copy-start = (bf16[2048,128]{1,0:T(8,128)(2,1)S(1)}, bf16[2048,128]{1,0:T(8,128)(2,1)}, u32[]{:S(2)}) copy-start(bf16[2048,128]{1,0:T(8,128)(2,1)} %table_ref.1) | copy-start | bytes 1572868
  14.0 34.0 %copy-start.3 = (s32[6]{0:T(128)S(1)}, s32[6]{0:T(128)}, u32[]{:S(2)}) copy-start(s32[6]{0:T(128)} %stack.27.info) | copy-start | bytes 76
  14.0 8.6 %collective-permute-start = (s32[40]{0:T(128)S(1)}, s32[40]{0:T(128)S(1)}, u32[]{:S(2)}, u32[]{:S(2)}) collective-permute-start(s32[40]{0:T(128)S(1)} %broadcast_select_fusion.3), channel_id=1, source_target_pairs={{0,8},{1,9},{2,10},{3,11},{8,16},{9,17},{10,18},{11,19},{16,24},{1... | collective-permute-start | bytes 488 | tf_op jit(solution)/shard_map/ppermute | solution.py:509
  25.0 0.9 copy-start.4
  25.9 17.6 %collective-permute-start.1 = (bf16[768,512]{1,0:T(8,128)(2,1)}, bf16[768,512]{1,0:T(8,128)(2,1)S(1)}, u32[]{:S(2)}, u32[]{:S(2)}) collective-permute-start(bf16[768,512]{1,0:T(8,128)(2,1)} %get-tuple-element.44), channel_id=1, source_target_pairs={{0,68},{1,69},{2,70},{3,71},{4,64},{5,65},{6,66},{7,67},{8,76},{9,... | collective-permute-start | bytes 2359304 | tf_op jit(solution)/shard_map/ppermute | solution.py:506
  43.5 4.6 %collective-permute-start.3 = (bf16[768,512]{1,0:T(8,128)(2,1)S(1)}, bf16[768,512]{1,0:T(8,128)(2,1)S(1)}, u32[]{:S(2)}, u32[]{:S(2)}) collective-permute-start(bf16[768,512]{1,0:T(8,128)(2,1)S(1)} %collective-permute-done.1.got_ref.got_hbm), channel_id=1, source_target_pairs={{0,8},{8,0},{16,24},{24,16},{32,40},{40,32},{48,56},{56,48},{64,72... | collective-permute-start | bytes 2359304 | tf_op jit(solution)/shard_map/ppermute | solution.py:451
  46.6 13.9 %collective-permute-start.2 = (bf16[512,512]{1,0:T(8,128)(2,1)}, bf16[512,512]{1,0:T(8,128)(2,1)S(1)}, u32[]{:S(2)}, u32[]{:S(2)}) collective-permute-start(bf16[512,512]{1,0:T(8,128)(2,1)} %get-tuple-element.45), channel_id=1, source_target_pairs={{0,68},{1,69},{2,70},{3,71},{4,64},{5,65},{6,66},{7,67},{8,76},{9,... | collective-permute-start | bytes 1572872 | tf_op jit(solution)/shard_map/ppermute | solution.py:514
  51.8 11.6 %all-to-all-start.1 = ((bf16[4,208,256]{2,1,0:T(8,128)(2,1)}), bf16[4,208,256]{2,1,0:T(8,128)(2,1)S(1)}, u32[]{:S(2)}, u32[]{:S(2)}) async-start(bf16[4,208,256]{2,1,0:T(8,128)(2,1)} %get-tuple-element.49), calls=%async_computation.1 | async-start | bytes 851968 | tf_op jit(solution)/shard_map/all_to_all | solution.py:455
  55.3 117.3 %all-gather.7.cloned.1.call-start = ((), (), s32[]{:S(2)}) async-start(), calls=%async_computation.11 | async-start | bytes 12812288 | tf_op jit(solution)/shard_map/all_gather | solution.py:459
  63.4 17.4 %collective-permute-start.4 = (bf16[4,46,16,128]{3,2,1,0:T(8,128)(2,1)}, bf16[4,46,16,128]{3,2,1,0:T(8,128)(2,1)}, u32[]{:S(2)}, u32[]{:S(2)}) collective-permute-start(bf16[4,46,16,128]{3,2,1,0:T(8,128)(2,1)} %copy-done.4), channel_id=1, source_target_pairs={{0,68},{1,69},{2,70},{3,71},{4,64},{5,65},{6,66},{7,67},{8,76},{9,... | collective-permute-start | bytes 2261000 | tf_op jit(solution)/shard_map/ppermute | solution.py:534
  80.9 3.7 %collective-permute-start.6 = (bf16[512,512]{1,0:T(8,128)(2,1)S(1)}, bf16[512,512]{1,0:T(8,128)(2,1)S(1)}, u32[]{:S(2)}, u32[]{:S(2)}) collective-permute-start(bf16[512,512]{1,0:T(8,128)(2,1)S(1)} %collective-permute-done.2.got1_hbm.got_hbm), channel_id=1, source_target_pairs={{0,8},{8,0},{16,24},{24,16},{32,40},{40,32},{48,56},{56,48},{64,72... | collective-permute-start | bytes 1572872 | tf_op jit(solution)/shard_map/ppermute | solution.py:451
  83.1 24.9 %collective-permute-start.5 = (bf16[2,512,512]{2,1,0:T(8,128)(2,1)}, bf16[2,512,512]{2,1,0:T(8,128)(2,1)S(1)}, u32[]{:S(2)}, u32[]{:S(2)}) collective-permute-start(bf16[2,512,512]{2,1,0:T(8,128)(2,1)} %get-tuple-element.53), channel_id=1, source_target_pairs={{0,68},{1,69},{2,70},{3,71},{4,64},{5,65},{6,66},{7,67},{8,76},{9,... | collective-permute-start | bytes 3145736 | tf_op jit(solution)/shard_map/ppermute | solution.py:544
  108.0 4.2 %collective-permute-start.7 = (bf16[2,512,512]{2,1,0:T(8,128)(2,1)S(1)}, bf16[2,512,512]{2,1,0:T(8,128)(2,1)S(1)}, u32[]{:S(2)}, u32[]{:S(2)}) collective-permute-start(bf16[2,512,512]{2,1,0:T(8,128)(2,1)S(1)} %collective-permute-done.5.got1_hbm.got_hbm), channel_id=1, source_target_pairs={{0,8},{8,0},{16,24},{24,16},{32,40},{40,32},{48,56},{56,48},{64,72... | collective-permute-start | bytes 3145736 | tf_op jit(solution)/shard_map/ppermute | solution.py:451
  145.4 17.1 %copy-start.6 = (f32[1920]{0:T(1024)S(1)}, f32[1920]{0:T(1024)}, u32[]{:S(2)}) copy-start(f32[1920]{0:T(1024)} %param.16) | copy-start | bytes 23044
  145.4 17.1 %copy-start.7 = (s32[1024]{0:T(1024)S(1)}, s32[1024]{0:T(1024)}, u32[]{:S(2)}) copy-start(s32[1024]{0:T(1024)} %param.10) | copy-start | bytes 12292
  156.1 16.5 %all-to-all-start.9 = ((bf16[8,128,256]{2,1,0:T(8,128)(2,1)}), bf16[8,128,256]{2,1,0:T(8,128)(2,1)S(1)}, u32[]{:S(2)}, u32[]{:S(2)}) async-start(bf16[8,128,256]{2,1,0:T(8,128)(2,1)} %cond_end.1), calls=%async_computation.9 | async-start | bytes 1048576 | tf_op jit(solution)/shard_map/all_to_all | solution.py:455
  185.2 0.7 copy-start.1
  185.9 14.4 %collective-permute-start.8 = (bf16[512,512]{1,0:T(8,128)(2,1)}, bf16[512,512]{1,0:T(8,128)(2,1)}, u32[]{:S(2)}, u32[]{:S(2)}) collective-permute-start(bf16[512,512]{1,0:T(8,128)(2,1)} %get-tuple-element.67.kv0_ref), channel_id=1, source_target_pairs={{0,16},{8,24},{16,32},{24,40},{32,48},{40,56},{48,64},{56,72},{64,... | collective-permute-start | bytes 1572872 | tf_op jit(solution)/shard_map/ppermute | solution.py:572
  188.4 22.5 %copy-start.2 = (bf16[512,256]{1,0:T(8,128)(2,1)S(1)}, bf16[512,256]{1,0:T(8,128)(2,1)}, u32[]{:S(2)}) copy-start(bf16[512,256]{1,0:T(8,128)(2,1)} %copy-done.1) | copy-start | bytes 786436
  201.4 13.4 %collective-permute-start.10 = (bf16[512,512]{1,0:T(8,128)(2,1)S(1)}, bf16[512,512]{1,0:T(8,128)(2,1)S(1)}, u32[]{:S(2)}, u32[]{:S(2)}) collective-permute-start(bf16[512,512]{1,0:T(8,128)(2,1)S(1)} %broadcast_select_fusion.1), channel_id=1, source_target_pairs={{0,8},{8,0},{16,24},{24,16},{32,40},{40,32},{48,56},{56,48},{64,72... | collective-permute-start | bytes 1572872 | tf_op jit(solution)/shard_map/ppermute | solution.py:451
  207.5 17.5 %collective-permute-start.9 = (bf16[512,512]{1,0:T(8,128)(2,1)S(1)}, bf16[512,512]{1,0:T(8,128)(2,1)S(1)}, u32[]{:S(2)}, u32[]{:S(2)}) collective-permute-start(bf16[512,512]{1,0:T(8,128)(2,1)S(1)} %get-tuple-element.70.kv1_ref), channel_id=1, source_target_pairs={{0,16},{8,24},{16,32},{24,40},{32,48},{40,56},{48,64},{56,72},{64,... | collective-permute-start | bytes 1572872 | tf_op jit(solution)/shard_map/ppermute | solution.py:572
  225.1 2.4 %collective-permute-start.11 = (bf16[512,512]{1,0:T(8,128)(2,1)S(1)}, bf16[512,512]{1,0:T(8,128)(2,1)S(1)}, u32[]{:S(2)}, u32[]{:S(2)}) collective-permute-start(bf16[512,512]{1,0:T(8,128)(2,1)S(1)} %broadcast_select_fusion), channel_id=1, source_target_pairs={{0,8},{8,0},{16,24},{24,16},{32,40},{40,32},{48,56},{56,48},{64,72... | collective-permute-start | bytes 1572872 | tf_op jit(solution)/shard_map/ppermute | solution.py:451
Sparse Core Ops, SparseCore 0:
  26.0 71.2 all-gather.4
  99.0 70.4 all-gather.6

commit v9 on v8

--- a/solution.py
+++ b/solution.py
@@ -528,6 +528,9 @@
         name="cond0",
     )(info, codes, upper_table, dilated_weight, got0, sib0)
     for level in range(4):
+        if level == 1:
+            others, terms = lax.optimization_barrier((others, terms))
+            full_other = gathered(others)
         terms = exchange(terms, groups=Y_GROUPS)
         if level == 0:
             got1, mine, terms = lax.optimization_barrier((got1, mine, terms))
@@ -539,8 +542,7 @@
         r = jnp.maximum(total, 0.0).astype(BF)
         r = exchange(jnp.broadcast_to(r[None], terms.shape), groups=Y_GROUPS)
         if level == 0:
-            others, pack2, r = lax.optimization_barrier((others, pack2, r))
-            full_other = gathered(others)
+            pack2, r = lax.optimization_barrier((pack2, r))
             got2 = lax.ppermute(pack2, EVERY, other_half())
             stacks = [(got0, sib0), (got1, sib1)]
         if level == 1:

time: 240 us -> 238 us (level)
  blocking collectives: 64.4 us -> 55.1 us
  waiting for transfers between devices: 51.4 us -> 56.2 us
    all_to_all x7 -> x6, blocking collectives: 64.4 us -> 55.1 us  [exchange(): lax.all_to_all(value, axis, 0, 0, axis_index_groups=groups, tiled=True)]
    ppermute x1, waiting for transfers between devices: 0.55 us -> 8.27 us  [on_device(): got2 = lax.ppermute(pack2, EVERY, other_half())]
    ppermute x1, waiting for transfers between devices: 6.89 us -> 0.77 us  [on_device(): others = lax.ppermute(mine, EVERY, other_half())]
    all_to_all x3 -> x4, starting transfers between devices: 14.1 us -> 17.7 us  [exchange(): lax.all_to_all(value, axis, 0, 0, axis_index_groups=groups, tiled=True)]
    all_to_all x3 -> x4, waiting for transfers between devices: 12.5 us -> 15.1 us  [exchange(): lax.all_to_all(value, axis, 0, 0, axis_index_groups=groups, tiled=True)]
  transfers between devices with their start and end apart: 17 -> 18, of which waited for: 12 -> 12; matrix products, arithmetic and copies ran while one was open for 1% -> 2% of each run, Pallas kernels for 16% -> 17%
where the time goes in v9:
time: 238 us; the launch traced here: 237 us
  Pallas kernels  59.3 us (25%)
  waiting for transfers between devices  56.2 us (24%)
  blocking collectives  55.1 us (23%)
  starting transfers between devices  45.3 us (19%)
  between operations  13.7 us (6%)
  local copies, waits for them, and re-layouts  6.25 us (3%)
    all_to_all x6, blocking collectives, exchange(): lax.all_to_all(value, axis, 0, 0, axis_index_groups=groups, tiled=True)  55.1 us
    pallas_call x2, Pallas kernels, frames(): pl.pallas_call(functools.partial(frames_kernel, pair), out_shape=(shape(5...  24.5 us
    all_to_all x4, starting transfers between devices, exchange(): lax.all_to_all(value, axis, 0, 0, axis_index_groups=groups, tiled=True)  17.7 us
    ppermute x1, waiting for transfers between devices, on_device(): got0 = lax.ppermute(pack0, EVERY, other_half())  16.3 us
    all_to_all x4, waiting for transfers between devices, exchange(): lax.all_to_all(value, axis, 0, 0, axis_index_groups=groups, tiled=True)  15.1 us
    ppermute x5, starting transfers between devices, to_sibling(): return lax.ppermute(value, 'song', [(i, i ^ 1) for i in range(16)])  12.5 us
    pallas_call x3, Pallas kernels, on_device(): call(functools.partial(middle_kernel, level), (shape(ROWS[level + 1], 256...  8.42 us
    ppermute x1, waiting for transfers between devices, on_device(): got2 = lax.ppermute(pack2, EVERY, other_half())  8.27 us
  transfers between devices with their start and end apart: 18, of which 12 were waited for; matrix products, arithmetic and copies ran while one was open for 2% of the time, Pallas kernels for 17%

profile of v9, /device:TPU:3, one launch (start us, length us, event | category | flops | bytes accessed | tf_op | source)
XLA Modules:
  0.0 237.4 jit_solution(14810789882122429577)
XLA Ops:
  9.8 4.2 %all-to-all-start = ((bf16[4,46,16,128]{3,2,1,0:T(8,128)(2,1)}), bf16[4,46,16,128]{3,2,1,0:T(8,128)(2,1)S(1)}, u32[]{:S(2)}, u32[]{:S(2)}) async-start(bf16[4,46,16,128]{3,2,1,0:T(8,128)(2,1)} %share.1), calls=%async_computation | async-start | bytes 1507328 | tf_op jit(solution)/shard_map/all_to_all | solution.py:455
  14.1 4.5 %collective-permute-start = (s32[40]{0:T(128)S(1)}, s32[40]{0:T(128)S(1)}, u32[]{:S(2)}, u32[]{:S(2)}) collective-permute-start(s32[40]{0:T(128)S(1)} %broadcast_select_fusion.3), channel_id=1, source_target_pairs={{0,8},{1,9},{2,10},{3,11},{8,16},{9,17},{10,18},{11,19},{16,24},{1... | collective-permute-start | bytes 488 | tf_op jit(solution)/shard_map/ppermute | solution.py:509
  18.6 4.1 %pack.1 = (bf16[768,512]{1,0:T(8,128)(2,1)}, bf16[512,512]{1,0:T(8,128)(2,1)}, bf16[2,512,512]{2,1,0:T(8,128)(2,1)}) custom-call(s32[6]{0:T(128)} %stack.27.info, bf16[4,3,128,1024]{3,2,1,0:T(8,128)(2,1)} %dil_hbm.9, bf16[4,1024,128]{2,1,0:T(8,128)(2,1)} %mix_hbm.9, bf16[2048,128]{1,0:T(8,128)(2,1)} %table_ref.1), custom_call_target="tpu_custom_call" | custom-call | flops 1000000000 | bytes 4194304 | tf_op jit(solution)/shard_map/pack/pallas_call | solution.py:498
  27.3 16.3 %collective-permute-done.1.got_ref.got_hbm = bf16[768,512]{1,0:T(8,128)(2,1)S(1)} collective-permute-done((bf16[768,512]{1,0:T(8,128)(2,1)}, bf16[768,512]{1,0:T(8,128)(2,1)S(1)}, u32[]{:S(2)}, u32[]{:S(2)}) %collective-permute-start.1) | collective-permute-done | bytes 786464 | tf_op jit(solution)/shard_map/ppermute | solution.py:506
  43.6 2.7 %collective-permute-start.3 = (bf16[768,512]{1,0:T(8,128)(2,1)S(1)}, bf16[768,512]{1,0:T(8,128)(2,1)S(1)}, u32[]{:S(2)}, u32[]{:S(2)}) collective-permute-start(bf16[768,512]{1,0:T(8,128)(2,1)S(1)} %collective-permute-done.1.got_ref.got_hbm), channel_id=1, source_target_pairs={{0,8},{8,0},{16,24},{24,16},{32,40},{40,32},{48,56},{56,48},{64,72... | collective-permute-start | bytes 2359304 | tf_op jit(solution)/shard_map/ppermute | solution.py:451
  48.2 3.7 %cond0.1 = (f32[208,256]{1,0:T(8,128)S(1)}, bf16[4,208,256]{2,1,0:T(8,128)(2,1)}) custom-call(s32[6]{0:T(128)S(1)} %copy-done.3, s32[208,1]{1,0:T(8,128)S(1)} %broadcast_select_fusion.2.codes_ref, bf16[2048,128]{1,0:T(8,128)(2,1)S(1)} %copy-done, bf16[4,3,128,1024]{3,2,1,0:T(8,128)(2,1)} %dil_hbm.9, ...), custom_call_target="tpu_custom_call" | custom-call | flops 1000000000 | bytes 4194304 | tf_op jit(solution)/shard_map/cond0/pallas_call | solution.py:521
  51.9 3.5 %all-to-all-start.1 = ((bf16[4,208,256]{2,1,0:T(8,128)(2,1)}), bf16[4,208,256]{2,1,0:T(8,128)(2,1)S(1)}, u32[]{:S(2)}, u32[]{:S(2)}) async-start(bf16[4,208,256]{2,1,0:T(8,128)(2,1)} %get-tuple-element.51), calls=%async_computation.1 | async-start | bytes 851968 | tf_op jit(solution)/shard_map/all_to_all | solution.py:455
  55.4 5.2 %collective-permute-done.2.got1_hbm.got_hbm = bf16[512,512]{1,0:T(8,128)(2,1)S(1)} collective-permute-done((bf16[512,512]{1,0:T(8,128)(2,1)}, bf16[512,512]{1,0:T(8,128)(2,1)S(1)}, u32[]{:S(2)}, u32[]{:S(2)}) %collective-permute-start.2) | collective-permute-done | bytes 524320 | tf_op jit(solution)/shard_map/ppermute | solution.py:514
  60.6 2.9 %all-to-all-done.1 = bf16[4,208,256]{2,1,0:T(8,128)(2,1)S(1)} async-done(((bf16[4,208,256]{2,1,0:T(8,128)(2,1)}), bf16[4,208,256]{2,1,0:T(8,128)(2,1)S(1)}, u32[]{:S(2)}, u32[]{:S(2)}) %all-to-all-start.1) | async-done | bytes 426016 | tf_op jit(solution)/shard_map/all_to_all | solution.py:455
  66.4 11.0 %all_to_all.50.r_ref = bf16[4,208,256]{2,1,0:T(8,128)(2,1)S(1)} all-to-all(bf16[4,208,256]{2,1,0:T(8,128)(2,1)S(1)} %broadcast_in_dim.37), channel_id=1, replica_groups={{0,1,2,3},{4,5,6,7},{8,9,10,11},{12,13,14,15},{16,17,18,19},{20,21,22,2..., dimensions={0} | all-to-all | bytes 851968 | tf_op jit(solution)/shard_map/all_to_all | solution.py:455
  77.3 2.9 %cond.3 = (f32[208,256]{1,0:T(8,128)S(1)}, bf16[4,208,256]{2,1,0:T(8,128)(2,1)S(1)}) custom-call(s32[6]{0:T(128)S(1)} %copy-done.3, bf16[4,208,256]{2,1,0:T(8,128)(2,1)S(1)} %all_to_all.50.r_ref, f32[208,256]{1,0:T(8,128)S(1)} %get-tuple-element.56.h_ref, bf16[4,1024,128]{2,1,0:T(8,128)(2,1)} %mix_hbm.9, ...), custom_call_target="tpu_custom_call" | custom-call | flops 1000000000 | bytes 4194304 | tf_op jit(solution)/shard_map/cond/pallas_call | solution.py:552
  82.4 8.8 %all_to_all.51 = bf16[4,208,256]{2,1,0:T(8,128)(2,1)S(1)} all-to-all(bf16[4,208,256]{2,1,0:T(8,128)(2,1)S(1)} %get-tuple-element.59), channel_id=1, replica_groups={{0,1,2,3},{4,5,6,7},{8,9,10,11},{12,13,14,15},{16,17,18,19},{20,21,22,2..., dimensions={0} | all-to-all | bytes 851968 | tf_op jit(solution)/shard_map/all_to_all | solution.py:455
  92.1 3.5 %all-to-all-start.4 = ((bf16[4,208,256]{2,1,0:T(8,128)(2,1)}), bf16[4,208,256]{2,1,0:T(8,128)(2,1)S(1)}, u32[]{:S(2)}, u32[]{:S(2)}) async-start(bf16[4,208,256]{2,1,0:T(8,128)(2,1)} %broadcast_in_dim.39), calls=%async_computation.4 | async-start | bytes 851968 | tf_op jit(solution)/shard_map/all_to_all | solution.py:455
  95.5 8.3 %collective-permute-done.4.got1_hbm.got_hbm = bf16[2,512,512]{2,1,0:T(8,128)(2,1)S(1)} collective-permute-done((bf16[2,512,512]{2,1,0:T(8,128)(2,1)}, bf16[2,512,512]{2,1,0:T(8,128)(2,1)S(1)}, u32[]{:S(2)}, u32[]{:S(2)}) %collective-permute-start.4) | collective-permute-done | bytes 1048608 | tf_op jit(solution)/shard_map/ppermute | solution.py:546
  103.8 3.0 %collective-permute-start.7 = (bf16[2,512,512]{2,1,0:T(8,128)(2,1)S(1)}, bf16[2,512,512]{2,1,0:T(8,128)(2,1)S(1)}, u32[]{:S(2)}, u32[]{:S(2)}) collective-permute-start(bf16[2,512,512]{2,1,0:T(8,128)(2,1)S(1)} %collective-permute-done.4.got1_hbm.got_hbm), channel_id=1, source_target_pairs={{0,8},{8,0},{16,24},{24,16},{32,40},{40,32},{48,56},{56,48},{64,72... | collective-permute-start | bytes 3145736 | tf_op jit(solution)/shard_map/ppermute | solution.py:451
  109.1 2.8 %cond.4 = (f32[208,256]{1,0:T(8,128)S(1)}, bf16[4,192,256]{2,1,0:T(8,128)(2,1)S(1)}) custom-call(s32[6]{0:T(128)S(1)} %copy-done.3, bf16[4,208,256]{2,1,0:T(8,128)(2,1)S(1)} %all-to-all-done.4.r_ref, f32[208,256]{1,0:T(8,128)S(1)} %get-tuple-element.61.h_ref, bf16[4,1024,128]{2,1,0:T(8,128)(2,1)} %mix_hbm.9, ...), custom_call_target="tpu_custom_call" | custom-call | flops 1000000000 | bytes 4194304 | tf_op jit(solution)/shard_map/cond/pallas_call | solution.py:552
  112.0 10.2 %all_to_all.52 = bf16[4,192,256]{2,1,0:T(8,128)(2,1)S(1)} all-to-all(bf16[4,192,256]{2,1,0:T(8,128)(2,1)S(1)} %get-tuple-element.63), channel_id=1, replica_groups={{0,1,2,3},{4,5,6,7},{8,9,10,11},{12,13,14,15},{16,17,18,19},{20,21,22,2..., dimensions={0} | all-to-all | bytes 786432 | tf_op jit(solution)/shard_map/all_to_all | solution.py:455
  122.3 9.3 %all_to_all.53.r_ref = bf16[4,192,256]{2,1,0:T(8,128)(2,1)S(1)} all-to-all(bf16[4,192,256]{2,1,0:T(8,128)(2,1)S(1)} %broadcast_in_dim.41), channel_id=1, replica_groups={{0,1,2,3},{4,5,6,7},{8,9,10,11},{12,13,14,15},{16,17,18,19},{20,21,22,2..., dimensions={0} | all-to-all | bytes 786432 | tf_op jit(solution)/shard_map/all_to_all | solution.py:455
  131.6 2.7 %cond.5 = (f32[192,256]{1,0:T(8,128)S(1)}, bf16[4,128,256]{2,1,0:T(8,128)(2,1)S(1)}) custom-call(s32[6]{0:T(128)S(1)} %copy-done.3, bf16[4,192,256]{2,1,0:T(8,128)(2,1)S(1)} %all_to_all.53.r_ref, f32[208,256]{1,0:T(8,128)S(1)} %get-tuple-element.64.h_ref, bf16[4,1024,128]{2,1,0:T(8,128)(2,1)} %mix_hbm.9, ...), custom_call_target="tpu_custom_call" | custom-call | flops 1000000000 | bytes 4194304 | tf_op jit(solution)/shard_map/cond/pallas_call | solution.py:552
  134.3 7.9 %all_to_all.54 = bf16[4,128,256]{2,1,0:T(8,128)(2,1)S(1)} all-to-all(bf16[4,128,256]{2,1,0:T(8,128)(2,1)S(1)} %get-tuple-element.65), channel_id=1, replica_groups={{0,1,2,3},{4,5,6,7},{8,9,10,11},{12,13,14,15},{16,17,18,19},{20,21,22,2..., dimensions={0} | all-to-all | bytes 524288 | tf_op jit(solution)/shard_map/all_to_all | solution.py:455
  142.3 7.9 %all_to_all.55.r_ref = bf16[4,128,256]{2,1,0:T(8,128)(2,1)S(1)} all-to-all(bf16[4,128,256]{2,1,0:T(8,128)(2,1)S(1)} %broadcast_in_dim.43), channel_id=1, replica_groups={{0,1,2,3},{4,5,6,7},{8,9,10,11},{12,13,14,15},{16,17,18,19},{20,21,22,2..., dimensions={0} | all-to-all | bytes 524288 | tf_op jit(solution)/shard_map/all_to_all | solution.py:455
  150.3 2.7 %cond_end.1 = bf16[8,128,256]{2,1,0:T(8,128)(2,1)} custom-call(s32[6]{0:T(128)S(1)} %copy-done.3, bf16[4,128,256]{2,1,0:T(8,128)(2,1)S(1)} %all_to_all.55.r_ref, f32[192,256]{1,0:T(8,128)S(1)} %get-tuple-element.66.h_ref, bf16[4,1024,128]{2,1,0:T(8,128)(2,1)} %mix_hbm.9, bf16[2,512,512]{2,1,0:T(8,128)(2,1)S(1)} %collective-permute-done.4.got1_hbm.got_hbm, ...), custom_call_target="tpu_custom_call" | custom-call | flops 1000000000 | bytes 4194304 | tf_op jit(solution)/shard_map/cond_end/pallas_call | solution.py:561
  152.9 6.5 %all-to-all-start.9 = ((bf16[8,128,256]{2,1,0:T(8,128)(2,1)}), bf16[8,128,256]{2,1,0:T(8,128)(2,1)S(1)}, u32[]{:S(2)}, u32[]{:S(2)}) async-start(bf16[8,128,256]{2,1,0:T(8,128)(2,1)} %cond_end.1), calls=%async_computation.9 | async-start | bytes 1048576 | tf_op jit(solution)/shard_map/all_to_all | solution.py:455
  162.3 9.8 %all-to-all-done.9.hf_ref = bf16[8,128,256]{2,1,0:T(8,128)(2,1)S(1)} async-done(((bf16[8,128,256]{2,1,0:T(8,128)(2,1)}), bf16[8,128,256]{2,1,0:T(8,128)(2,1)S(1)}, u32[]{:S(2)}, u32[]{:S(2)}) %all-to-all-start.9) | async-done | bytes 524320 | tf_op jit(solution)/shard_map/all_to_all | solution.py:455
  172.1 12.6 %frames.2 = (bf16[512,256]{1,0:T(8,128)(2,1)S(1)}, bf16[512,512]{1,0:T(8,128)(2,1)}) custom-call(s32[6]{0:T(128)S(1)} %copy-done.3, s32[1024]{0:T(1024)S(1)} %fusion.9.codes_ref, bf16[8,128,256]{2,1,0:T(8,128)(2,1)S(1)} %all-to-all-done.9.hf_ref, f32[1,1920]{1,0:T(1,128)S(1)} %broadcast_in_dim.44.gain_ref, bf16[1920,768]{1,0:T(8,128)(2,1)S(1)} %bitcast.24, ...), custom_call_target="tpu_custom_call" | custom-call | flops 4000000000 | bytes 20971520 | tf_op jit(solution)/shard_map/frames/pallas_call | solution.py:317
  187.6 11.8 %frames.3 = (bf16[512,256]{1,0:T(8,128)(2,1)S(1)}, bf16[512,512]{1,0:T(8,128)(2,1)S(1)}) custom-call(s32[6]{0:T(128)S(1)} %copy-done.3, s32[1024]{0:T(1024)S(1)} %fusion.9.codes_ref, bf16[8,128,256]{2,1,0:T(8,128)(2,1)S(1)} %all-to-all-done.9.hf_ref, f32[1,1920]{1,0:T(1,128)S(1)} %broadcast_in_dim.44.gain_ref, bf16[1920,768]{1,0:T(8,128)(2,1)S(1)} %bitcast.25, ...), custom_call_target="tpu_custom_call" | custom-call | flops 4000000000 | bytes 20971520 | tf_op jit(solution)/shard_map/frames/pallas_call | solution.py:317
  201.2 4.5 %collective-permute-start.10 = (bf16[512,512]{1,0:T(8,128)(2,1)S(1)}, bf16[512,512]{1,0:T(8,128)(2,1)S(1)}, u32[]{:S(2)}, u32[]{:S(2)}) collective-permute-start(bf16[512,512]{1,0:T(8,128)(2,1)S(1)} %broadcast_select_fusion.1), channel_id=1, source_target_pairs={{0,8},{8,0},{16,24},{24,16},{32,40},{40,32},{48,56},{56,48},{64,72... | collective-permute-start | bytes 1572872 | tf_op jit(solution)/shard_map/ppermute | solution.py:451
  205.7 3.1 %collective-permute-start.9 = (bf16[512,512]{1,0:T(8,128)(2,1)S(1)}, bf16[512,512]{1,0:T(8,128)(2,1)S(1)}, u32[]{:S(2)}, u32[]{:S(2)}) collective-permute-start(bf16[512,512]{1,0:T(8,128)(2,1)S(1)} %get-tuple-element.72.kv1_ref), channel_id=1, source_target_pairs={{0,16},{8,24},{16,32},{24,40},{32,48},{40,56},{48,64},{56,72},{64,... | collective-permute-start | bytes 1572872 | tf_op jit(solution)/shard_map/ppermute | solution.py:574
  208.8 3.9 %own.1 = (f32[2,4,256,256]{3,2,1,0:T(8,128)S(1)}, f32[2,4,256,1]{3,2,1,0:T(8,128)S(1)}) custom-call(bf16[512,256]{1,0:T(8,128)(2,1)S(1)} %copy-done.2, bf16[512,256]{1,0:T(8,128)(2,1)S(1)} %get-tuple-element.71.q1_ref, bf16[512,512]{1,0:T(8,128)(2,1)} %get-tuple-element.69.kv0_ref, bf16[512,512]{1,0:T(8,128)(2,1)S(1)} %get-tuple-element.72.kv1_ref), custom_call_target="tpu_custom_call" | custom-call | flops 1000000000 | bytes 4194304 | tf_op jit(solution)/shard_map/own/pallas_call | solution.py:583
  212.8 4.6 %past.1 = (f32[2,4,256,256]{3,2,1,0:T(8,128)S(1)}, f32[2,4,256,1]{3,2,1,0:T(8,128)S(1)}) custom-call(s32[6]{0:T(128)S(1)} %copy-done.3, bf16[512,256]{1,0:T(8,128)(2,1)S(1)} %copy-done.2, bf16[512,256]{1,0:T(8,128)(2,1)S(1)} %get-tuple-element.71.q1_ref, bf16[512,512]{1,0:T(8,128)(2,1)} %collective-permute-done.8.far_ref, ...), custom_call_target="tpu_custom_call" | custom-call | flops 1000000000 | bytes 4194304 | tf_op jit(solution)/shard_map/past/pallas_call | solution.py:585
  217.3 5.9 %collective-permute-done.9.far_ref = bf16[512,512]{1,0:T(8,128)(2,1)S(1)} collective-permute-done((bf16[512,512]{1,0:T(8,128)(2,1)S(1)}, bf16[512,512]{1,0:T(8,128)(2,1)S(1)}, u32[]{:S(2)}, u32[]{:S(2)}) %collective-permute-start.9) | collective-permute-done | bytes 524320 | tf_op jit(solution)/shard_map/ppermute | solution.py:574
  225.7 4.8 %past_end.1 = bf16[1024,256]{1,0:T(8,128)(2,1)} custom-call(s32[6]{0:T(128)S(1)} %copy-done.3, bf16[512,256]{1,0:T(8,128)(2,1)S(1)} %copy-done.2, bf16[512,256]{1,0:T(8,128)(2,1)S(1)} %get-tuple-element.71.q1_ref, bf16[512,512]{1,0:T(8,128)(2,1)S(1)} %collective-permute-done.9.far_ref, bf16[512,512]{1,0:T(8,128)(2,1)S(1)} %collective-permute-done.11.near_ref, ...), custom_call_target="tpu_custom_call" | custom-call | flops 2000000000 | bytes 4194304 | tf_op jit(solution)/shard_map/past_end/pallas_call | solution.py:590
  (63 shorter events, 28.1 us)
Async XLA Ops:
  6.5 7.5 %copy-start.5 = (s32[256]{0:T(256)S(1)}, s32[256]{0:T(256)}, u32[]{:S(2)}) copy-start(s32[256]{0:T(256)} %param.9) | copy-start | bytes 3076
  9.8 15.2 %all-to-all-start = ((bf16[4,46,16,128]{3,2,1,0:T(8,128)(2,1)}), bf16[4,46,16,128]{3,2,1,0:T(8,128)(2,1)S(1)}, u32[]{:S(2)}, u32[]{:S(2)}) async-start(bf16[4,46,16,128]{3,2,1,0:T(8,128)(2,1)} %share.1), calls=%async_computation | async-start | bytes 1507328 | tf_op jit(solution)/shard_map/all_to_all | solution.py:455
  14.0 158.1 %all-gather.5.cloned.1.call-start = ((), (), s32[]{:S(2)}) async-start(), calls=%async_computation.10 | async-start | bytes 12812288 | tf_op jit(solution)/shard_map/all_gather | solution.py:459
  14.1 34.0 %copy-start = (bf16[2048,128]{1,0:T(8,128)(2,1)S(1)}, bf16[2048,128]{1,0:T(8,128)(2,1)}, u32[]{:S(2)}) copy-start(bf16[2048,128]{1,0:T(8,128)(2,1)} %table_ref.1) | copy-start | bytes 1572868
  14.1 34.0 %copy-start.3 = (s32[6]{0:T(128)S(1)}, s32[6]{0:T(128)}, u32[]{:S(2)}) copy-start(s32[6]{0:T(128)} %stack.27.info) | copy-start | bytes 76
  14.1 8.6 %collective-permute-start = (s32[40]{0:T(128)S(1)}, s32[40]{0:T(128)S(1)}, u32[]{:S(2)}, u32[]{:S(2)}) collective-permute-start(s32[40]{0:T(128)S(1)} %broadcast_select_fusion.3), channel_id=1, source_target_pairs={{0,8},{1,9},{2,10},{3,11},{8,16},{9,17},{10,18},{11,19},{16,24},{1... | collective-permute-start | bytes 488 | tf_op jit(solution)/shard_map/ppermute | solution.py:509
  25.1 0.9 copy-start.4
  26.0 17.6 %collective-permute-start.1 = (bf16[768,512]{1,0:T(8,128)(2,1)}, bf16[768,512]{1,0:T(8,128)(2,1)S(1)}, u32[]{:S(2)}, u32[]{:S(2)}) collective-permute-start(bf16[768,512]{1,0:T(8,128)(2,1)} %get-tuple-element.46), channel_id=1, source_target_pairs={{0,68},{1,69},{2,70},{3,71},{4,64},{5,65},{6,66},{7,67},{8,76},{9,... | collective-permute-start | bytes 2359304 | tf_op jit(solution)/shard_map/ppermute | solution.py:506
  43.6 4.6 %collective-permute-start.3 = (bf16[768,512]{1,0:T(8,128)(2,1)S(1)}, bf16[768,512]{1,0:T(8,128)(2,1)S(1)}, u32[]{:S(2)}, u32[]{:S(2)}) collective-permute-start(bf16[768,512]{1,0:T(8,128)(2,1)S(1)} %collective-permute-done.1.got_ref.got_hbm), channel_id=1, source_target_pairs={{0,8},{8,0},{16,24},{24,16},{32,40},{40,32},{48,56},{56,48},{64,72... | collective-permute-start | bytes 2359304 | tf_op jit(solution)/shard_map/ppermute | solution.py:451
  46.6 13.9 %collective-permute-start.2 = (bf16[512,512]{1,0:T(8,128)(2,1)}, bf16[512,512]{1,0:T(8,128)(2,1)S(1)}, u32[]{:S(2)}, u32[]{:S(2)}) collective-permute-start(bf16[512,512]{1,0:T(8,128)(2,1)} %get-tuple-element.47), channel_id=1, source_target_pairs={{0,68},{1,69},{2,70},{3,71},{4,64},{5,65},{6,66},{7,67},{8,76},{9,... | collective-permute-start | bytes 1572872 | tf_op jit(solution)/shard_map/ppermute | solution.py:514
  51.9 11.6 %all-to-all-start.1 = ((bf16[4,208,256]{2,1,0:T(8,128)(2,1)}), bf16[4,208,256]{2,1,0:T(8,128)(2,1)S(1)}, u32[]{:S(2)}, u32[]{:S(2)}) async-start(bf16[4,208,256]{2,1,0:T(8,128)(2,1)} %get-tuple-element.51), calls=%async_computation.1 | async-start | bytes 851968 | tf_op jit(solution)/shard_map/all_to_all | solution.py:455
  55.4 116.8 %all-gather.7.cloned.1.call-start = ((), (), s32[]{:S(2)}) async-start(), calls=%async_computation.11 | async-start | bytes 12812288 | tf_op jit(solution)/shard_map/all_gather | solution.py:459
  63.5 17.4 %collective-permute-start.5 = (bf16[4,46,16,128]{3,2,1,0:T(8,128)(2,1)}, bf16[4,46,16,128]{3,2,1,0:T(8,128)(2,1)}, u32[]{:S(2)}, u32[]{:S(2)}) collective-permute-start(bf16[4,46,16,128]{3,2,1,0:T(8,128)(2,1)} %copy-done.4), channel_id=1, source_target_pairs={{0,68},{1,69},{2,70},{3,71},{4,64},{5,65},{6,66},{7,67},{8,76},{9,... | collective-permute-start | bytes 2261000 | tf_op jit(solution)/shard_map/ppermute | solution.py:537
  64.8 12.5 %collective-permute-start.6 = (bf16[512,512]{1,0:T(8,128)(2,1)S(1)}, bf16[512,512]{1,0:T(8,128)(2,1)S(1)}, u32[]{:S(2)}, u32[]{:S(2)}) collective-permute-start(bf16[512,512]{1,0:T(8,128)(2,1)S(1)} %collective-permute-done.2.got1_hbm.got_hbm), channel_id=1, source_target_pairs={{0,8},{8,0},{16,24},{24,16},{32,40},{40,32},{48,56},{56,48},{64,72... | collective-permute-start | bytes 1572872 | tf_op jit(solution)/shard_map/ppermute | solution.py:451
  81.0 22.8 %collective-permute-start.4 = (bf16[2,512,512]{2,1,0:T(8,128)(2,1)}, bf16[2,512,512]{2,1,0:T(8,128)(2,1)S(1)}, u32[]{:S(2)}, u32[]{:S(2)}) collective-permute-start(bf16[2,512,512]{2,1,0:T(8,128)(2,1)} %get-tuple-element.53), channel_id=1, source_target_pairs={{0,68},{1,69},{2,70},{3,71},{4,64},{5,65},{6,66},{7,67},{8,76},{9,... | collective-permute-start | bytes 3145736 | tf_op jit(solution)/shard_map/ppermute | solution.py:546
  92.1 11.7 %all-to-all-start.4 = ((bf16[4,208,256]{2,1,0:T(8,128)(2,1)}), bf16[4,208,256]{2,1,0:T(8,128)(2,1)S(1)}, u32[]{:S(2)}, u32[]{:S(2)}) async-start(bf16[4,208,256]{2,1,0:T(8,128)(2,1)} %broadcast_in_dim.39), calls=%async_computation.4 | async-start | bytes 851968 | tf_op jit(solution)/shard_map/all_to_all | solution.py:455
  103.8 5.3 %collective-permute-start.7 = (bf16[2,512,512]{2,1,0:T(8,128)(2,1)S(1)}, bf16[2,512,512]{2,1,0:T(8,128)(2,1)S(1)}, u32[]{:S(2)}, u32[]{:S(2)}) collective-permute-start(bf16[2,512,512]{2,1,0:T(8,128)(2,1)S(1)} %collective-permute-done.4.got1_hbm.got_hbm), channel_id=1, source_target_pairs={{0,8},{8,0},{16,24},{24,16},{32,40},{40,32},{48,56},{56,48},{64,72... | collective-permute-start | bytes 3145736 | tf_op jit(solution)/shard_map/ppermute | solution.py:451
  142.3 17.2 %copy-start.6 = (f32[1920]{0:T(1024)S(1)}, f32[1920]{0:T(1024)}, u32[]{:S(2)}) copy-start(f32[1920]{0:T(1024)} %param.16) | copy-start | bytes 23044
  142.3 17.2 %copy-start.7 = (s32[1024]{0:T(1024)S(1)}, s32[1024]{0:T(1024)}, u32[]{:S(2)}) copy-start(s32[1024]{0:T(1024)} %param.10) | copy-start | bytes 12292
  152.9 19.2 %all-to-all-start.9 = ((bf16[8,128,256]{2,1,0:T(8,128)(2,1)}), bf16[8,128,256]{2,1,0:T(8,128)(2,1)S(1)}, u32[]{:S(2)}, u32[]{:S(2)}) async-start(bf16[8,128,256]{2,1,0:T(8,128)(2,1)} %cond_end.1), calls=%async_computation.9 | async-start | bytes 1048576 | tf_op jit(solution)/shard_map/all_to_all | solution.py:455
  184.7 0.7 copy-start.1
  185.5 14.7 %collective-permute-start.8 = (bf16[512,512]{1,0:T(8,128)(2,1)}, bf16[512,512]{1,0:T(8,128)(2,1)}, u32[]{:S(2)}, u32[]{:S(2)}) collective-permute-start(bf16[512,512]{1,0:T(8,128)(2,1)} %get-tuple-element.69.kv0_ref), channel_id=1, source_target_pairs={{0,16},{8,24},{16,32},{24,40},{32,48},{40,56},{48,64},{56,72},{64,... | collective-permute-start | bytes 1572872 | tf_op jit(solution)/shard_map/ppermute | solution.py:574
  187.6 21.2 %copy-start.2 = (bf16[512,256]{1,0:T(8,128)(2,1)S(1)}, bf16[512,256]{1,0:T(8,128)(2,1)}, u32[]{:S(2)}) copy-start(bf16[512,256]{1,0:T(8,128)(2,1)} %copy-done.1) | copy-start | bytes 786436
  201.2 11.5 %collective-permute-start.10 = (bf16[512,512]{1,0:T(8,128)(2,1)S(1)}, bf16[512,512]{1,0:T(8,128)(2,1)S(1)}, u32[]{:S(2)}, u32[]{:S(2)}) collective-permute-start(bf16[512,512]{1,0:T(8,128)(2,1)S(1)} %broadcast_select_fusion.1), channel_id=1, source_target_pairs={{0,8},{8,0},{16,24},{24,16},{32,40},{40,32},{48,56},{56,48},{64,72... | collective-permute-start | bytes 1572872 | tf_op jit(solution)/shard_map/ppermute | solution.py:451
  205.7 17.5 %collective-permute-start.9 = (bf16[512,512]{1,0:T(8,128)(2,1)S(1)}, bf16[512,512]{1,0:T(8,128)(2,1)S(1)}, u32[]{:S(2)}, u32[]{:S(2)}) collective-permute-start(bf16[512,512]{1,0:T(8,128)(2,1)S(1)} %get-tuple-element.72.kv1_ref), channel_id=1, source_target_pairs={{0,16},{8,24},{16,32},{24,40},{32,48},{40,56},{48,64},{56,72},{64,... | collective-permute-start | bytes 1572872 | tf_op jit(solution)/shard_map/ppermute | solution.py:574
  223.3 2.4 %collective-permute-start.11 = (bf16[512,512]{1,0:T(8,128)(2,1)S(1)}, bf16[512,512]{1,0:T(8,128)(2,1)S(1)}, u32[]{:S(2)}, u32[]{:S(2)}) collective-permute-start(bf16[512,512]{1,0:T(8,128)(2,1)S(1)} %broadcast_select_fusion), channel_id=1, source_target_pairs={{0,8},{8,0},{16,24},{24,16},{32,40},{40,32},{48,56},{56,48},{64,72... | collective-permute-start | bytes 1572872 | tf_op jit(solution)/shard_map/ppermute | solution.py:451
Sparse Core Ops, SparseCore 0:
  26.1 71.2 all-gather.4
  99.1 71.5 all-gather.6
